TPU v7x, 32 devices: a whole 2x2x4 slice. The times are simulated.
32 devices in a mesh: ctx: 8 (over z, x), mp: 4 (over y, core).
Axes of the slice: x: 2, y: 2, z: 4, core: 2. Of those that a mesh axis runs over, the one named last changes fastest.
Arguments:
- queries: bfloat16 [2048, 3072], P('ctx', 'mp'), may hold values from -8 to 8
- keys: bfloat16 [2048, 3072], P('ctx', 'mp'), may hold values from -8 to 8
- values: bfloat16 [2048, 3072], P('ctx', 'mp'), may hold values from -6 to 6
- out_grad: bfloat16 [2048, 6144], P('ctx', 'mp'), may hold values from -6 to 6
- out_weight: bfloat16 [3072, 6144], P('mp'), may hold values from -0.078125 to 0.078125
Outputs:
- query_grad: bfloat16 [2048, 3072], P('ctx', 'mp')
- key_grad: bfloat16 [2048, 3072], P('ctx', 'mp')
- value_grad: bfloat16 [2048, 3072], P('ctx', 'mp')
All inputs are finite; a program needn't handle non-finite values.
Results may differ from a plain program's by a relative error of at most 0.0076.
Values may be sent and summed in bfloat16 or wider, within the bound.
No kernel may reach another device: no remote copies, remote signals or barrier semaphores. Data moves between devices by JAX's collectives and lax.ppermute only.
A program may use at most 128 MiB of HBM per device.

v0:
```python
import jax
import jax.numpy as jnp
from jax import lax
from jax.sharding import PartitionSpec as P

HD = 128
REACH = 2


def passed_along(shard, axis, by):
    length = lax.axis_size(axis)
    pairs = [(i, i + by) for i in range(length) if 0 <= i + by < length]
    return lax.ppermute(shard, axis, pairs)


def body(queries, keys, values, out_grad, out_weight):
    tokens_here = queries.shape[0]
    head_count = queries.shape[1] // HD
    scaling = HD ** (-0.5)
    width = 2 * REACH + 1
    head_grad = lax.dot_general(
        lax.all_gather(out_grad, "mp", axis=1, tiled=True),
        out_weight,
        (((1,), (1,)), ((), ())),
        preferred_element_type=jnp.float32,
    ).astype(jnp.bfloat16)
    pair = (keys, values)
    before_list = []
    after_list = []
    lower = pair
    upper = pair
    for distance in range(REACH):
        lower = passed_along((lower[0], lower[1]), "ctx", 1)
        upper = passed_along((upper[0], upper[1]), "ctx", -1)
        before_list.append(lower)
        after_list.append(upper)
    ordered = before_list[::-1] + [pair] + after_list
    window_keys = jnp.concatenate([entry[0] for entry in ordered], 0).reshape(
        width * tokens_here, head_count, HD
    )
    window_values = jnp.concatenate([entry[1] for entry in ordered], 0).reshape(
        width * tokens_here, head_count, HD
    )
    query_heads = queries.reshape(tokens_here, head_count, HD)
    grad_heads = head_grad.reshape(tokens_here, head_count, HD)
    position = lax.axis_index("ctx")
    block_count = lax.axis_size("ctx")
    slot = lax.broadcasted_iota(jnp.int32, (width * tokens_here,), 0) // tokens_here
    target = position + slot - REACH
    allowed = (target >= 0) & (target < block_count)
    scores = (
        jnp.einsum("thd,uhd->htu", query_heads, window_keys, preferred_element_type=jnp.float32)
        * scaling
    )
    masked = jnp.where(allowed, scores, -jnp.inf)
    largest = jnp.max(masked, -1, keepdims=True)
    log_total = largest + jnp.log(jnp.sum(jnp.exp(masked - largest), -1, keepdims=True))
    probs = jnp.where(allowed, jnp.exp(scores - log_total), jnp.float32(0.0))
    prob_grad = jnp.einsum(
        "thd,uhd->htu", grad_heads, window_values, preferred_element_type=jnp.float32
    )
    delta_rows = jnp.sum(probs * prob_grad, -1, keepdims=True)
    score_grad = (probs * (prob_grad - delta_rows) * scaling).astype(jnp.bfloat16)
    query_grad = jnp.einsum(
        "htu,uhd->thd", score_grad, window_keys, preferred_element_type=jnp.float32
    )
    query_grad = query_grad.astype(jnp.bfloat16).reshape(tokens_here, -1)
    key_part = jnp.einsum(
        "htu,thd->uhd", score_grad, query_heads, preferred_element_type=jnp.float32
    )
    value_part = jnp.einsum(
        "htu,thd->uhd", probs.astype(jnp.bfloat16), grad_heads, preferred_element_type=jnp.float32
    )
    key_part = key_part.reshape(width, tokens_here, -1)
    value_part = value_part.reshape(width, tokens_here, -1)
    key_total = key_part[REACH]
    value_total = value_part[REACH]
    for distance in range(1, REACH + 1):
        lower_piece = (
            key_part[REACH - distance].astype(jnp.bfloat16),
            value_part[REACH - distance].astype(jnp.bfloat16),
        )
        upper_piece = (
            key_part[REACH + distance].astype(jnp.bfloat16),
            value_part[REACH + distance].astype(jnp.bfloat16),
        )
        from_after = passed_along((lower_piece[0], lower_piece[1]), "ctx", -distance)
        from_before = passed_along((upper_piece[0], upper_piece[1]), "ctx", distance)
        key_total = (
            key_total + from_after[0].astype(jnp.float32) + from_before[0].astype(jnp.float32)
        )
        value_total = (
            value_total + from_after[1].astype(jnp.float32) + from_before[1].astype(jnp.float32)
        )
    return (query_grad, key_total.astype(jnp.bfloat16), value_total.astype(jnp.bfloat16))


def solution(mesh):
    placed = (P("ctx", "mp"), P("ctx", "mp"), P("ctx", "mp"), P("ctx", "mp"), P("mp", None))
    return jax.shard_map(
        body,
        mesh=mesh,
        in_specs=placed,
        out_specs=(P("ctx", "mp"), P("ctx", "mp"), P("ctx", "mp")),
        check_vma=False,
    )
```

profile of v0, /device:TPU:0, one launch (start us, length us, event | category | flops | bytes accessed | tf_op | source)
XLA Modules:
  0.0 190.1 jit_solution(5518301074959439455)
XLA Ops:
  9.1 4.9 %collective-permute-start = (bf16[256,768]{0,1:T(8,128)(2,1)S(1)}, bf16[256,768]{0,1:T(8,128)(2,1)S(1)}, u32[]{:S(2)}, u32[]{:S(2)}) collective-permute-start(bf16[256,768]{0,1:T(8,128)(2,1)S(1)} %copy.29), channel_id=1, source_target_pairs={{0,4},{4,8},{8,12},{12,16},{16,20},{20,24},{24,28},{1,5},{5,9},{9,... | collective-permute-start | bytes 1179656 | tf_op jit(solution)/shard_map/ppermute | solution.py:13
  15.1 3.5 %collective-permute-start.4 = (bf16[256,768]{0,1:T(8,128)(2,1)S(1)}, bf16[256,768]{0,1:T(8,128)(2,1)S(1)}, u32[]{:S(2)}, u32[]{:S(2)}) collective-permute-start(bf16[256,768]{0,1:T(8,128)(2,1)S(1)} %copy.36), channel_id=1, source_target_pairs={{0,4},{4,8},{8,12},{12,16},{16,20},{20,24},{24,28},{1,5},{5,9},{9,... | collective-permute-start | bytes 1179656 | tf_op jit(solution)/shard_map/ppermute | solution.py:13
  18.6 1.3 collective-permute-start.6
  19.9 1.3 collective-permute-start.2
  21.2 19.1 %collective-permute-done = bf16[256,768]{0,1:T(8,128)(2,1)S(1)} collective-permute-done((bf16[256,768]{0,1:T(8,128)(2,1)S(1)}, bf16[256,768]{0,1:T(8,128)(2,1)S(1)}, u32[]{:S(2)}, u32[]{:S(2)}) %collective-permute-start) | collective-permute-done | bytes 393248 | tf_op jit(solution)/shard_map/ppermute | solution.py:13
  40.3 4.4 %collective-permute-start.1 = (bf16[256,768]{0,1:T(8,128)(2,1)S(1)}, bf16[256,768]{0,1:T(8,128)(2,1)S(1)}, u32[]{:S(2)}, u32[]{:S(2)}) collective-permute-start(bf16[256,768]{0,1:T(8,128)(2,1)S(1)} %collective-permute-done), channel_id=1, source_target_pairs={{0,4},{4,8},{8,12},{12,16},{16,20},{20,24},{24,28},{1,5},{5,9},{9,... | collective-permute-start | bytes 1179656 | tf_op jit(solution)/shard_map/ppermute | solution.py:13
  44.7 4.0 %collective-permute-done.4 = bf16[256,768]{0,1:T(8,128)(2,1)S(1)} collective-permute-done((bf16[256,768]{0,1:T(8,128)(2,1)S(1)}, bf16[256,768]{0,1:T(8,128)(2,1)S(1)}, u32[]{:S(2)}, u32[]{:S(2)}) %collective-permute-start.4) | collective-permute-done | bytes 393248 | tf_op jit(solution)/shard_map/ppermute | solution.py:13
  48.7 5.1 %collective-permute-start.5 = (bf16[256,768]{0,1:T(8,128)(2,1)S(1)}, bf16[256,768]{0,1:T(8,128)(2,1)}, u32[]{:S(2)}, u32[]{:S(2)}) collective-permute-start(bf16[256,768]{0,1:T(8,128)(2,1)S(1)} %collective-permute-done.4), channel_id=1, source_target_pairs={{0,4},{4,8},{8,12},{12,16},{16,20},{20,24},{24,28},{1,5},{5,9},{9,... | collective-permute-start | bytes 1179656 | tf_op jit(solution)/shard_map/ppermute | solution.py:13
  55.0 1.3 collective-permute-start.7
  56.3 1.3 collective-permute-start.3
  57.6 7.9 %collective-permute-done.1 = bf16[256,768]{0,1:T(8,128)(2,1)S(1)} collective-permute-done((bf16[256,768]{0,1:T(8,128)(2,1)S(1)}, bf16[256,768]{0,1:T(8,128)(2,1)S(1)}, u32[]{:S(2)}, u32[]{:S(2)}) %collective-permute-start.1) | collective-permute-done | bytes 393248 | tf_op jit(solution)/shard_map/ppermute | solution.py:13
  65.7 15.6 %collective-permute-done.5 = bf16[256,768]{0,1:T(8,128)(2,1)} collective-permute-done((bf16[256,768]{0,1:T(8,128)(2,1)S(1)}, bf16[256,768]{0,1:T(8,128)(2,1)}, u32[]{:S(2)}, u32[]{:S(2)}) %collective-permute-start.5) | collective-permute-done | bytes 393248 | tf_op jit(solution)/shard_map/ppermute | solution.py:13
  83.5 2.1 %bitcast_reduce_fusion = (f32[6,256]{1,0:T(8,128)S(1)}, f32[6,1280,256]{2,1,0:T(8,128)S(1)}) fusion(pred[1280]{0:T(1024)(128)(4,1)S(1)} %fusion.40, bf16[1280,6,128]{0,2,1:T(8,128)(2,1)S(1)} %bitcast.77, bf16[256,6,128]{0,2,1:T(8,128)(2,1)S(1)} %bitcast.80), kind=kOutput, calls=%fused_computation.7 | convolution fusion | flops 509213184 | bytes 10231040 | tf_op jit(solution)/shard_map/thd,uhd->htu/dot_general | solution.py:52
  85.6 3.0 %copy-done = f32[6,1280,256]{2,1,0:T(8,128)} copy-done((f32[6,1280,256]{2,1,0:T(8,128)}, f32[6,1280,256]{2,1,0:T(8,128)S(1)}, u32[]{:S(2)}) %copy-start) | copy-done | bytes 7864344
  88.7 2.1 %fusion.4 = f32[6,256]{1,0:T(8,128)S(1)} fusion(f32[6,1280,256]{2,1,0:T(8,128)S(1)} %get-tuple-element.18, f32[6,256]{1,0:T(8,128)S(1)} %get-tuple-element.17, pred[1280]{0:T(1024)(128)(4,1)S(1)} %fusion.40), kind=kLoop, calls=%fused_computation.9 | loop fusion | flops 7862784 | bytes 7877888 | tf_op jit(solution)/shard_map/reduce_sum | solution.py:57
  90.8 7.3 %convolution_convert_fusion = bf16[256,768]{1,0:T(8,128)(2,1)S(1)} fusion(bf16[256,6144]{1,0:T(8,128)(2,1)} %all-gather.2.cloned.1.call-done, bf16[768,6144]{1,0:T(8,128)(2,1)} %param.9), kind=kOutput, calls=%fused_computation.32 | convolution fusion | flops 2416115712 | bytes 12976128 | tf_op jit(solution)/shard_map/dot_general | solution.py:21
  98.3 4.4 %fusion.56 = f32[6,256,1280]{1,2,0:T(8,128)} fusion(bf16[256,6,128]{0,2,1:T(8,128)(2,1)S(1)} %bitcast.73, bf16[1280,6,128]{0,2,1:T(8,128)(2,1)S(1)} %bitcast.79), kind=kOutput, calls=%fused_computation.68 | convolution fusion | flops 503316480 | bytes 10223616 | tf_op jit(solution)/shard_map/thd,uhd->htu/dot_general | solution.py:59
  102.7 17.1 %fusion.54 = (bf16[1280,6,128]{0,2,1:T(8,128)(2,1)}, f32[1280,6,128]{0,2,1:T(8,128)}) fusion(bf16[256,6,128]{0,2,1:T(8,128)(2,1)S(1)} %bitcast.81, f32[6,256,1280]{1,2,0:T(8,128)} %fusion.56, f32[6,1280,256]{2,1,0:T(8,128)} %copy-done, f32[6,256]{1,0:T(8,128)S(1)} %log_add_fusion, pred[1280]{0:T(1024)(128)(4,1)S(1)} %fusion.40), kind=kOutput, calls=%fused_computation.66 | convolution fusion | flops 525929216 | bytes 22027520 | tf_op jit(solution)/shard_map/htu,thd->uhd/dot_general | solution.py:68
  119.7 1.5 fusion.53
  124.0 5.3 %collective-permute-start.9 = (bf16[256,768]{1,0:T(8,128)(2,1)}, bf16[256,768]{1,0:T(8,128)(2,1)}, u32[]{:S(2)}, u32[]{:S(2)}) collective-permute-start(bf16[256,768]{1,0:T(8,128)(2,1)} %copy.47), channel_id=1, source_target_pairs={{0,4},{4,8},{8,12},{12,16},{16,20},{20,24},{24,28},{1,5},{5,9},{9,... | collective-permute-start | bytes 1179656 | tf_op jit(solution)/shard_map/ppermute | solution.py:13
  129.2 1.3 collective-permute-start.10
  130.5 5.4 %collective-permute-start.11 = (bf16[256,768]{1,0:T(8,128)(2,1)}, bf16[256,768]{1,0:T(8,128)(2,1)}, u32[]{:S(2)}, u32[]{:S(2)}) collective-permute-start(bf16[256,768]{1,0:T(8,128)(2,1)} %copy.49), channel_id=1, source_target_pairs={{0,8},{4,12},{8,16},{12,20},{16,24},{20,28},{1,9},{5,13},{9,17},{1... | collective-permute-start | bytes 1179656 | tf_op jit(solution)/shard_map/ppermute | solution.py:13
  135.9 6.9 %fusion.55 = (bf16[1280,6,128]{0,2,1:T(8,128)(2,1)S(1)}, f32[1280,6,128]{0,2,1:T(8,128)}) fusion(bf16[256,6,128]{0,2,1:T(8,128)(2,1)S(1)} %bitcast.74, f32[6,1280,256]{2,1,0:T(8,128)} %copy-done, f32[6,256]{1,0:T(8,128)S(1)} %log_add_fusion, pred[1280]{0:T(1024)(128)(4,1)S(1)} %fusion.40), kind=kOutput, calls=%fused_computation.67 | convolution fusion | flops 512163840 | bytes 14163200 | tf_op jit(solution)/shard_map/htu,thd->uhd/dot_general | solution.py:71
  143.7 1.3 collective-permute-start.8
  146.7 5.3 %collective-permute-start.13 = (bf16[256,768]{1,0:T(8,128)(2,1)S(1)}, bf16[256,768]{1,0:T(8,128)(2,1)}, u32[]{:S(2)}, u32[]{:S(2)}) collective-permute-start(bf16[256,768]{1,0:T(8,128)(2,1)S(1)} %copy.53), channel_id=1, source_target_pairs={{0,4},{4,8},{8,12},{12,16},{16,20},{20,24},{24,28},{1,5},{5,9},{9,... | collective-permute-start | bytes 1179656 | tf_op jit(solution)/shard_map/ppermute | solution.py:13
  152.0 1.3 collective-permute-start.14
  153.3 5.3 %collective-permute-start.15 = (bf16[256,768]{1,0:T(8,128)(2,1)S(1)}, bf16[256,768]{1,0:T(8,128)(2,1)}, u32[]{:S(2)}, u32[]{:S(2)}) collective-permute-start(bf16[256,768]{1,0:T(8,128)(2,1)S(1)} %copy.55), channel_id=1, source_target_pairs={{0,8},{4,12},{8,16},{12,20},{16,24},{20,28},{1,9},{5,13},{9,17},{1... | collective-permute-start | bytes 1179656 | tf_op jit(solution)/shard_map/ppermute | solution.py:13
  158.6 1.3 collective-permute-start.12
  159.9 14.9 %fusion.33 = bf16[6,128,256]{2,1,0:T(8,128)(2,1)S(1)} fusion(bf16[1280,6,128]{0,2,1:T(8,128)(2,1)} %bitcast.78, f32[6,256,1280]{1,2,0:T(8,128)} %fusion.56, f32[6,1280,256]{2,1,0:T(8,128)} %copy-done, f32[6,256]{1,0:T(8,128)S(1)} %log_add_fusion, pred[1280]{0:T(1024)(128)(4,1)S(1)} %fusion.40), kind=kOutput, calls=%fused_computation.31 | convolution fusion | flops 525142784 | bytes 18095360 | tf_op jit(solution)/shard_map/htu,uhd->thd/dot_general | solution.py:64
  177.2 1.2 slice.63
  178.6 2.3 %add_convert_fusion.1 = bf16[256,768]{1,0:T(8,128)(2,1)} fusion(bf16[256,768]{1,0:T(8,128)(2,1)} %collective-permute-done.11, bf16[256,768]{1,0:T(8,128)(2,1)} %collective-permute-done.10, bf16[256,768]{1,0:T(8,128)(2,1)} %collective-permute-done.9, f32[256,768]{1,0:T(8,128)S(1)} %copy.46, bf16[256,768]{1,0:T(8,128)(2,1)} %collective-permute-done.8), kind=kLoop, calls=%fused_computation.34 | loop fusion | flops 1769472 | bytes 2752512 | tf_op jit(solution)/shard_map/convert_element_type | solution.py:95
  181.0 2.3 %add_convert_fusion = bf16[256,768]{1,0:T(8,128)(2,1)} fusion(bf16[256,768]{1,0:T(8,128)(2,1)} %collective-permute-done.15, bf16[256,768]{1,0:T(8,128)(2,1)} %collective-permute-done.14, bf16[256,768]{1,0:T(8,128)(2,1)} %collective-permute-done.13, f32[256,768]{1,0:T(8,128)S(1)} %copy.52, bf16[256,768]{1,0:T(8,128)(2,1)} %collective-permute-done.12), kind=kLoop, calls=%fused_computation.33 | loop fusion | flops 1769472 | bytes 2752512 | tf_op jit(solution)/shard_map/convert_element_type | solution.py:95
  (49 shorter events, 14.7 us)
Async XLA Ops:
  7.2 83.7 %all-gather.2.cloned.1.call-start = ((), (), s32[]{:S(2)}) async-start(), calls=%async_computation | async-start | bytes 3932160 | tf_op jit(solution)/shard_map/all_gather | solution.py:22
  9.1 31.2 %collective-permute-start = (bf16[256,768]{0,1:T(8,128)(2,1)S(1)}, bf16[256,768]{0,1:T(8,128)(2,1)S(1)}, u32[]{:S(2)}, u32[]{:S(2)}) collective-permute-start(bf16[256,768]{0,1:T(8,128)(2,1)S(1)} %copy.29), channel_id=1, source_target_pairs={{0,4},{4,8},{8,12},{12,16},{16,20},{20,24},{24,28},{1,5},{5,9},{9,... | collective-permute-start | bytes 1179656 | tf_op jit(solution)/shard_map/ppermute | solution.py:13
  15.1 33.6 %collective-permute-start.4 = (bf16[256,768]{0,1:T(8,128)(2,1)S(1)}, bf16[256,768]{0,1:T(8,128)(2,1)S(1)}, u32[]{:S(2)}, u32[]{:S(2)}) collective-permute-start(bf16[256,768]{0,1:T(8,128)(2,1)S(1)} %copy.36), channel_id=1, source_target_pairs={{0,4},{4,8},{8,12},{12,16},{16,20},{20,24},{24,28},{1,5},{5,9},{9,... | collective-permute-start | bytes 1179656 | tf_op jit(solution)/shard_map/ppermute | solution.py:13
  18.6 36.4 %collective-permute-start.6 = (bf16[256,768]{0,1:T(8,128)(2,1)S(1)}, bf16[256,768]{0,1:T(8,128)(2,1)S(1)}, u32[]{:S(2)}, u32[]{:S(2)}) collective-permute-start(bf16[256,768]{0,1:T(8,128)(2,1)S(1)} %copy.36), channel_id=1, source_target_pairs={{4,0},{8,4},{12,8},{16,12},{20,16},{24,20},{28,24},{5,1},{9,5},{13... | collective-permute-start | bytes 1179656 | tf_op jit(solution)/shard_map/ppermute | solution.py:13
  19.9 36.4 %collective-permute-start.2 = (bf16[256,768]{0,1:T(8,128)(2,1)S(1)}, bf16[256,768]{0,1:T(8,128)(2,1)S(1)}, u32[]{:S(2)}, u32[]{:S(2)}) collective-permute-start(bf16[256,768]{0,1:T(8,128)(2,1)S(1)} %copy.29), channel_id=1, source_target_pairs={{4,0},{8,4},{12,8},{16,12},{20,16},{24,20},{28,24},{5,1},{9,5},{13... | collective-permute-start | bytes 1179656 | tf_op jit(solution)/shard_map/ppermute | solution.py:13
  40.3 25.3 %collective-permute-start.1 = (bf16[256,768]{0,1:T(8,128)(2,1)S(1)}, bf16[256,768]{0,1:T(8,128)(2,1)S(1)}, u32[]{:S(2)}, u32[]{:S(2)}) collective-permute-start(bf16[256,768]{0,1:T(8,128)(2,1)S(1)} %collective-permute-done), channel_id=1, source_target_pairs={{0,4},{4,8},{8,12},{12,16},{16,20},{20,24},{24,28},{1,5},{5,9},{9,... | collective-permute-start | bytes 1179656 | tf_op jit(solution)/shard_map/ppermute | solution.py:13
  48.7 17.0 %copy-start.2 = (bf16[256,768]{0,1:T(8,128)(2,1)}, bf16[256,768]{0,1:T(8,128)(2,1)S(1)}, u32[]{:S(2)}) copy-start(bf16[256,768]{0,1:T(8,128)(2,1)S(1)} %collective-permute-done.4) | copy-start | bytes 1179652
  48.7 32.6 %collective-permute-start.5 = (bf16[256,768]{0,1:T(8,128)(2,1)S(1)}, bf16[256,768]{0,1:T(8,128)(2,1)}, u32[]{:S(2)}, u32[]{:S(2)}) collective-permute-start(bf16[256,768]{0,1:T(8,128)(2,1)S(1)} %collective-permute-done.4), channel_id=1, source_target_pairs={{0,4},{4,8},{8,12},{12,16},{16,20},{20,24},{24,28},{1,5},{5,9},{9,... | collective-permute-start | bytes 1179656 | tf_op jit(solution)/shard_map/ppermute | solution.py:13
  55.0 28.5 %collective-permute-start.7 = (bf16[256,768]{0,1:T(8,128)(2,1)S(1)}, bf16[256,768]{0,1:T(8,128)(2,1)S(1)}, u32[]{:S(2)}, u32[]{:S(2)}) collective-permute-start(bf16[256,768]{0,1:T(8,128)(2,1)S(1)} %collective-permute-done.6), channel_id=1, source_target_pairs={{4,0},{8,4},{12,8},{16,12},{20,16},{24,20},{28,24},{5,1},{9,5},{13... | collective-permute-start | bytes 1179656 | tf_op jit(solution)/shard_map/ppermute | solution.py:13
  56.3 27.1 %collective-permute-start.3 = (bf16[256,768]{0,1:T(8,128)(2,1)S(1)}, bf16[256,768]{0,1:T(8,128)(2,1)S(1)}, u32[]{:S(2)}, u32[]{:S(2)}) collective-permute-start(bf16[256,768]{0,1:T(8,128)(2,1)S(1)} %collective-permute-done.2), channel_id=1, source_target_pairs={{4,0},{8,4},{12,8},{16,12},{20,16},{24,20},{28,24},{5,1},{9,5},{13... | collective-permute-start | bytes 1179656 | tf_op jit(solution)/shard_map/ppermute | solution.py:13
  83.5 7.3 %copy-start.1 = (bf16[1280,768]{0,1:T(8,128)(2,1)}, bf16[1280,768]{0,1:T(8,128)(2,1)S(1)}, u32[]{:S(2)}) copy-start(bf16[1280,768]{0,1:T(8,128)(2,1)S(1)} %constant_dynamic-update-slice_fusion) | copy-start | bytes 5898244
  85.6 3.1 %copy-start = (f32[6,1280,256]{2,1,0:T(8,128)}, f32[6,1280,256]{2,1,0:T(8,128)S(1)}, u32[]{:S(2)}) copy-start(f32[6,1280,256]{2,1,0:T(8,128)S(1)} %get-tuple-element.18) | copy-start | bytes 23592964
  124.0 28.0 %collective-permute-start.9 = (bf16[256,768]{1,0:T(8,128)(2,1)}, bf16[256,768]{1,0:T(8,128)(2,1)}, u32[]{:S(2)}, u32[]{:S(2)}) collective-permute-start(bf16[256,768]{1,0:T(8,128)(2,1)} %copy.47), channel_id=1, source_target_pairs={{0,4},{4,8},{8,12},{12,16},{16,20},{20,24},{24,28},{1,5},{5,9},{9,... | collective-permute-start | bytes 1179656 | tf_op jit(solution)/shard_map/ppermute | solution.py:13
  129.2 24.1 %collective-permute-start.10 = (bf16[256,768]{1,0:T(8,128)(2,1)}, bf16[256,768]{1,0:T(8,128)(2,1)}, u32[]{:S(2)}, u32[]{:S(2)}) collective-permute-start(bf16[256,768]{1,0:T(8,128)(2,1)} %copy.48), channel_id=1, source_target_pairs={{8,0},{12,4},{16,8},{20,12},{24,16},{28,20},{9,1},{13,5},{17,9},{2... | collective-permute-start | bytes 1179656 | tf_op jit(solution)/shard_map/ppermute | solution.py:13
  130.5 28.1 %collective-permute-start.11 = (bf16[256,768]{1,0:T(8,128)(2,1)}, bf16[256,768]{1,0:T(8,128)(2,1)}, u32[]{:S(2)}, u32[]{:S(2)}) collective-permute-start(bf16[256,768]{1,0:T(8,128)(2,1)} %copy.49), channel_id=1, source_target_pairs={{0,8},{4,12},{8,16},{12,20},{16,24},{20,28},{1,9},{5,13},{9,17},{1... | collective-permute-start | bytes 1179656 | tf_op jit(solution)/shard_map/ppermute | solution.py:13
  143.7 34.9 %collective-permute-start.8 = (bf16[256,768]{1,0:T(8,128)(2,1)}, bf16[256,768]{1,0:T(8,128)(2,1)}, u32[]{:S(2)}, u32[]{:S(2)}) collective-permute-start(bf16[256,768]{1,0:T(8,128)(2,1)} %copy.45), channel_id=1, source_target_pairs={{4,0},{8,4},{12,8},{16,12},{20,16},{24,20},{28,24},{5,1},{9,5},{13... | collective-permute-start | bytes 1179656 | tf_op jit(solution)/shard_map/ppermute | solution.py:13
  146.7 34.3 %collective-permute-start.13 = (bf16[256,768]{1,0:T(8,128)(2,1)S(1)}, bf16[256,768]{1,0:T(8,128)(2,1)}, u32[]{:S(2)}, u32[]{:S(2)}) collective-permute-start(bf16[256,768]{1,0:T(8,128)(2,1)S(1)} %copy.53), channel_id=1, source_target_pairs={{0,4},{4,8},{8,12},{12,16},{16,20},{20,24},{24,28},{1,5},{5,9},{9,... | collective-permute-start | bytes 1179656 | tf_op jit(solution)/shard_map/ppermute | solution.py:13
  152.0 29.0 %collective-permute-start.14 = (bf16[256,768]{1,0:T(8,128)(2,1)S(1)}, bf16[256,768]{1,0:T(8,128)(2,1)}, u32[]{:S(2)}, u32[]{:S(2)}) collective-permute-start(bf16[256,768]{1,0:T(8,128)(2,1)S(1)} %copy.54), channel_id=1, source_target_pairs={{8,0},{12,4},{16,8},{20,12},{24,16},{28,20},{9,1},{13,5},{17,9},{2... | collective-permute-start | bytes 1179656 | tf_op jit(solution)/shard_map/ppermute | solution.py:13
  153.3 27.7 %collective-permute-start.15 = (bf16[256,768]{1,0:T(8,128)(2,1)S(1)}, bf16[256,768]{1,0:T(8,128)(2,1)}, u32[]{:S(2)}, u32[]{:S(2)}) collective-permute-start(bf16[256,768]{1,0:T(8,128)(2,1)S(1)} %copy.55), channel_id=1, source_target_pairs={{0,8},{4,12},{8,16},{12,20},{16,24},{20,28},{1,9},{5,13},{9,17},{1... | collective-permute-start | bytes 1179656 | tf_op jit(solution)/shard_map/ppermute | solution.py:13
  158.6 22.4 %collective-permute-start.12 = (bf16[256,768]{1,0:T(8,128)(2,1)}, bf16[256,768]{1,0:T(8,128)(2,1)}, u32[]{:S(2)}, u32[]{:S(2)}) collective-permute-start(bf16[256,768]{1,0:T(8,128)(2,1)} %copy.51), channel_id=1, source_target_pairs={{4,0},{8,4},{12,8},{16,12},{20,16},{24,20},{28,24},{5,1},{9,5},{13... | collective-permute-start | bytes 1179656 | tf_op jit(solution)/shard_map/ppermute | solution.py:13
Sparse Core Ops, SparseCore 0:
  9.6 31.2 all-gather.1
where the time goes:
time: 191 us; the launch traced here: 190 us
  matrix products  52.6 us (28%)
  starting transfers between devices  49.4 us (26%)
  waiting for transfers between devices  47.4 us (25%)
  local copies, waits for them, and re-layouts  19.6 us (10%)
  between operations  14.4 us (8%)
  other arithmetic  6.73 us (4%)
    ppermute x16, starting transfers between devices, passed_along(): return lax.ppermute(shard, axis, pairs)  49.4 us
    ppermute x16, waiting for transfers between devices, passed_along(): return lax.ppermute(shard, axis, pairs)  46.7 us
    dot_general x1, matrix products, body(): jnp.einsum('htu,thd->uhd', score_grad, query_heads, preferred_element_typ...  17.1 us
    dot_general x1, matrix products, body(): jnp.einsum('htu,uhd->thd', score_grad, window_keys, preferred_element_typ...  14.9 us
    unnamed x18, local copies, waits for them, and re-layouts  9.68 us
    dot_general x1, matrix products, body(): lax.dot_general(lax.all_gather(out_grad, 'mp', axis=1, tiled=True), out_w...  7.27 us
    dot_general x1, matrix products, body(): jnp.einsum('htu,thd->uhd', probs.astype(jnp.bfloat16), grad_heads, prefer...  6.94 us
    dot_general x1, matrix products, body(): jnp.einsum('thd,uhd->htu', grad_heads, window_values, preferred_element_t...  4.39 us
  transfers between devices with their start and end apart: 17, of which 4 were waited for; matrix products, arithmetic and copies ran while one was open for 21% of the time, Pallas kernels for 0%

commit v1 on v0

v1 whole, which is shorter than its diff:
```python
import functools
import math

import jax
import jax.numpy as jnp
from jax import lax
from jax.experimental import pallas as pl
from jax.experimental.pallas import tpu as pltpu
from jax.sharding import PartitionSpec as P

HD = 128
BF16 = jnp.bfloat16
F32 = jnp.float32
BIG = 1e30
ANY = pl.BlockSpec(memory_space=pl.ANY)
VM = pl.BlockSpec(memory_space=pltpu.VMEM)


def params(mib=40):
    return pltpu.CompilerParams(vmem_limit_bytes=mib << 20)


def nt(a, b):
    return lax.dot_general(a, b, (((1,), (1,)), ((), ())), preferred_element_type=F32)


def nn(a, b):
    return lax.dot_general(a, b, (((1,), (0,)), ((), ())), preferred_element_type=F32)


def cost(flops, moved, exps=0):
    return pl.CostEstimate(flops=int(flops), bytes_accessed=int(moved), transcendentals=int(exps))


def all_of(copies):
    for copy in copies:
        copy.start()
    for copy in copies:
        copy.wait()


def pack_kernel(q, k, v, og, keep, send, og0, og1, sem):
    half = q.shape[1] // 2
    wide = og.shape[1] // 2
    x = lax.rem(lax.axis_index("ctx"), 2)
    mine = pl.ds(pl.multiple_of(x * half, half), half)
    theirs = pl.ds(pl.multiple_of((1 - x) * half, half), half)
    copies = []
    for i, ref in enumerate((q, k, v)):
        copies.append(pltpu.make_async_copy(ref.at[:, mine], keep.at[i], sem.at[i]))
        copies.append(pltpu.make_async_copy(ref.at[:, theirs], send.at[i], sem.at[3 + i]))
    copies.append(pltpu.make_async_copy(og.at[:, :wide], og0, sem.at[6]))
    copies.append(pltpu.make_async_copy(og.at[:, wide:], og1, sem.at[7]))
    all_of(copies)


def pack(q, k, v, og):
    rows, cols = q.shape
    part = jax.ShapeDtypeStruct((3, rows, cols // 2), BF16)
    piece = jax.ShapeDtypeStruct((rows, og.shape[1] // 2), BF16)
    return pl.pallas_call(
        pack_kernel,
        out_shape=(part, part, piece, piece),
        in_specs=[ANY] * 4,
        out_specs=(ANY,) * 4,
        scratch_shapes=[pltpu.SemaphoreType.DMA((8,))],
        cost_estimate=cost(0, 8e6),
        name="pack",
    )(q, k, v, og)


def grad_kernel(width, flips, offset, has_acc, last, *refs):
    refs = list(refs)
    acc = refs.pop(0) if has_acc else None
    pieces = [refs.pop(0), refs.pop(0)]
    w = refs.pop(0)
    outs = [refs.pop(0) for _ in range(2 if last else 1)]
    wbuf, sem = refs.pop(0), refs.pop(0)
    me = lax.axis_index("mp")
    size = pieces[0].shape[1]
    copies = []
    for i, flip in enumerate(flips):
        first = jnp.bitwise_xor(me, flip) * width + offset
        columns = pl.ds(pl.multiple_of(first, size), size)
        copies.append(pltpu.make_async_copy(w.at[:, columns], wbuf.at[i], sem.at[i]))
    for copy in copies:
        copy.start()
    copies[0].wait()
    total = nt(pieces[0][...], wbuf[0])
    copies[1].wait()
    total = total + nt(pieces[1][...], wbuf[1])
    if has_acc:
        total = total + acc[...]
    if not last:
        outs[0][...] = total
        return
    half = total.shape[1] // 2
    x = lax.rem(lax.axis_index("ctx"), 2)
    low = total[:, :half].astype(BF16)
    high = total[:, half:].astype(BF16)

    @pl.when(x == 0)
    def _():
        outs[0][...] = low
        outs[1][...] = high

    @pl.when(x != 0)
    def _():
        outs[0][...] = high
        outs[1][...] = low


def grad_piece(acc, first, second, w, width, flips, offset, last):
    rows, size = first.shape
    heads = w.shape[0]
    if last:
        shape = (jax.ShapeDtypeStruct((rows, heads // 2), BF16),) * 2
        spec = (VM, VM)
    else:
        shape = jax.ShapeDtypeStruct((rows, heads), F32)
        spec = VM
    operands = ([] if acc is None else [acc]) + [first, second, w]
    return pl.pallas_call(
        functools.partial(grad_kernel, width, flips, offset, acc is not None, last),
        out_shape=shape,
        in_specs=[VM] * (len(operands) - 1) + [ANY],
        out_specs=spec,
        scratch_shapes=[pltpu.VMEM((2, heads, size), BF16), pltpu.SemaphoreType.DMA((2,))],
        compiler_params=params(),
        cost_estimate=cost(4 * rows * size * heads, 4 * heads * size + 4 * rows * size),
        name="head_grad",
    )(*operands)


def place():
    position = lax.axis_index("ctx")
    x = lax.rem(position, 2)
    block = position // 2
    odd = lax.rem(block, 2)
    return x, block, odd


def query_kernel(scale, keep, xr, e0, e1, o0, o1, dkeep, dxr, dq_keep, dq_send, stats, qs, ks, vs, ds, marks, sem):
    rows = keep.shape[1]
    heads = keep.shape[2] // HD
    both = 2 * rows
    x, block, odd = place()
    blocks = lax.axis_size("ctx") // 2
    mine = x * rows
    theirs = (1 - x) * rows
    even_at = (1 - odd) * (2 * both)
    odd_at = odd * (2 * both)

    def at(first):
        return pl.ds(pl.multiple_of(first, rows), rows)

    copies = [
        (keep.at[0], qs.at[at(mine)]),
        (xr.at[0], qs.at[at(theirs)]),
        (dkeep, ds.at[at(mine)]),
        (dxr, ds.at[at(theirs)]),
    ]
    for i, buffer in ((1, ks), (2, vs)):
        copies.append((keep.at[i], buffer.at[at(both + mine)]))
        copies.append((xr.at[i], buffer.at[at(both + theirs)]))
        copies.append((e0.at[i], buffer.at[at(even_at + mine)]))
        copies.append((e1.at[i], buffer.at[at(even_at + theirs)]))
        copies.append((o0.at[i], buffer.at[at(odd_at + mine)]))
        copies.append((o1.at[i], buffer.at[at(odd_at + theirs)]))
    all_of([pltpu.make_async_copy(a, b, sem.at[i]) for i, (a, b) in enumerate(copies)])

    log2e = math.log2(math.e)
    c = scale * log2e
    low_off = jnp.where(block > 0, 0.0, BIG).astype(F32)
    high_off = jnp.where(block < blocks - 1, 0.0, BIG).astype(F32)
    lane = lax.broadcasted_iota(jnp.int32, (rows, HD), 1)
    for half in range(2):
        if half == 0:
            runs = ((0, both, low_off), (both, 2 * both, None), (2 * both, 2 * both + rows, high_off))
        else:
            runs = ((rows, both, low_off), (both, 2 * both, None), (2 * both, 3 * both, high_off))
        mark = jnp.zeros((rows, HD), F32)
        here = slice(half * rows, (half + 1) * rows)
        for head in range(heads):
            cols = slice(head * HD, (head + 1) * HD)
            query = qs[here, cols]
            grad = ds[here, cols]
            scores = [nt(query, ks[a:b, cols]) for a, b, _ in runs]
            top = None
            for s, (_, _, off) in zip(scores, runs):
                m = jnp.max(s, -1, keepdims=True)
                m = m if off is None else m - off
                top = m if top is None else jnp.maximum(top, m)
            top = top * c
            weights = [
                jnp.exp2(s * c - (top if off is None else top + off))
                for s, (_, _, off) in zip(scores, runs)
            ]
            total = sum(jnp.sum(w, -1, keepdims=True) for w in weights)
            grads = [nt(grad, vs[a:b, cols]) for a, b, _ in runs]
            inverse = 1.0 / total
            delta = sum(jnp.sum(w * g, -1, keepdims=True) for w, g in zip(weights, grads)) * inverse
            result = sum(
                nn((w * (g - delta)).astype(BF16), ks[a:b, cols])
                for w, g, (a, b, _) in zip(weights, grads, runs)
            )
            result = (result * (inverse * scale)).astype(BF16)

            @pl.when(x == half)
            def _():
                dq_keep[:, cols] = result

            @pl.when(x != half)
            def _():
                dq_send[:, cols] = result

            mark = jnp.where(lane == 2 * head, top + jnp.log2(total), mark)
            mark = jnp.where(lane == 2 * head + 1, delta, mark)
        stats[:, half * rows : (half + 1) * rows] = jnp.transpose(mark)[: stats.shape[0], :]


def query_pass(keep, xr, e0, e1, o0, o1, dkeep, dxr):
    _, rows, cols = keep.shape
    heads = cols // HD
    both = 2 * rows
    pairs = both * 5 * rows * heads
    part = jax.ShapeDtypeStruct((rows, cols), BF16)
    return pl.pallas_call(
        functools.partial(query_kernel, HD ** -0.5),
        out_shape=(part, part, jax.ShapeDtypeStruct((8, both), F32)),
        in_specs=[ANY] * 8,
        out_specs=(VM, VM, VM),
        scratch_shapes=[
            pltpu.VMEM((both, cols), BF16),
            pltpu.VMEM((3 * both, cols), BF16),
            pltpu.VMEM((3 * both, cols), BF16),
            pltpu.VMEM((both, cols), BF16),
            pltpu.VMEM((rows, HD), F32),
            pltpu.SemaphoreType.DMA((16,)),
        ],
        compiler_params=params(),
        cost_estimate=cost(6 * HD * pairs, 20 * rows * cols * 2, pairs),
        name="query_pass",
    )(keep, xr, e0, e1, o0, o1, dkeep, dxr)


def key_kernel(scale, keep, xr, e0, e1, o0, o1, dkeep, dxr, de0, de1, do0, do1, stats, se, so,
               out_keep, out_send, ks, vs, qs, ds, marks, sem):
    rows = keep.shape[1]
    heads = keep.shape[2] // HD
    both = 2 * rows
    x, block, odd = place()
    blocks = lax.axis_size("ctx") // 2
    mine = x * rows
    theirs = (1 - x) * rows
    even_at = (1 - odd) * (2 * both)
    odd_at = odd * (2 * both)

    def at(first):
        return pl.ds(pl.multiple_of(first, rows), rows)

    copies = []
    for i, buffer in ((1, ks), (2, vs)):
        copies.append((keep.at[i], buffer.at[at(mine)]))
        copies.append((xr.at[i], buffer.at[at(theirs)]))
    for buffer, own0, own1, a0, a1, b0, b1 in (
        (qs, keep.at[0], xr.at[0], e0.at[0], e1.at[0], o0.at[0], o1.at[0]),
        (ds, dkeep, dxr, de0, de1, do0, do1),
    ):
        copies.append((own0, buffer.at[at(both + mine)]))
        copies.append((own1, buffer.at[at(both + theirs)]))
        copies.append((a0, buffer.at[at(even_at + mine)]))
        copies.append((a1, buffer.at[at(even_at + theirs)]))
        copies.append((b0, buffer.at[at(odd_at + mine)]))
        copies.append((b1, buffer.at[at(odd_at + theirs)]))
    all_of([pltpu.make_async_copy(a, b, sem.at[i]) for i, (a, b) in enumerate(copies)])

    c = scale * math.log2(math.e)
    low_ok = block > 0
    high_ok = block < blocks - 1
    is_even = odd == 0
    low = jnp.where(is_even, so[...], se[...])
    high = jnp.where(is_even, se[...], so[...])
    row = lax.broadcasted_iota(jnp.int32, low.shape, 0)
    nothing = jnp.where(lax.rem(row, 2) == 0, jnp.float32(BIG), jnp.float32(0.0))
    marks[:, :both] = jnp.where(low_ok, low, nothing)
    marks[:, both : 2 * both] = stats[...]
    marks[:, 2 * both :] = jnp.where(high_ok, high, nothing)

    for half in range(2):
        here = slice(half * rows, (half + 1) * rows)
        for head in range(heads):
            cols = slice(head * HD, (head + 1) * HD)
            key = ks[here, cols]
            value = vs[here, cols]
            key_sum = None
            value_sum = None
            for step in range(5):
                span = slice((half + step) * rows, (half + step + 1) * rows)
                query = qs[span, cols]
                grad = ds[span, cols]
                weight = jnp.exp2(nt(key, query) * c - marks[2 * head : 2 * head + 1, span])
                change = weight * (nt(value, grad) - marks[2 * head + 1 : 2 * head + 2, span])
                v = nn(weight.astype(BF16), grad)
                k = nn(change.astype(BF16), query)
                value_sum = v if value_sum is None else value_sum + v
                key_sum = k if key_sum is None else key_sum + k
            key_out = (key_sum * scale).astype(BF16)
            value_out = value_sum.astype(BF16)

            @pl.when(x == half)
            def _():
                out_keep[0, :, cols] = key_out
                out_keep[1, :, cols] = value_out

            @pl.when(x != half)
            def _():
                out_send[0, :, cols] = key_out
                out_send[1, :, cols] = value_out


def key_pass(*operands):
    _, rows, cols = operands[0].shape
    heads = cols // HD
    both = 2 * rows
    pairs = both * 5 * rows * heads
    part = jax.ShapeDtypeStruct((2, rows, cols), BF16)
    return pl.pallas_call(
        functools.partial(key_kernel, HD ** -0.5),
        out_shape=(part, part),
        in_specs=[ANY] * 12 + [VM] * 3,
        out_specs=(VM, VM),
        scratch_shapes=[
            pltpu.VMEM((both, cols), BF16),
            pltpu.VMEM((both, cols), BF16),
            pltpu.VMEM((3 * both, cols), BF16),
            pltpu.VMEM((3 * both, cols), BF16),
            pltpu.VMEM((8, 3 * both), F32),
            pltpu.SemaphoreType.DMA((16,)),
        ],
        compiler_params=params(),
        cost_estimate=cost(8 * HD * pairs, 20 * rows * cols * 2, pairs),
        name="key_pass",
    )(*operands)


def unpack_kernel(q_keep, q_got, kv_keep, kv_got, dq, dk, dv, sem):
    half = q_keep.shape[1]
    x = lax.rem(lax.axis_index("ctx"), 2)
    mine = pl.ds(pl.multiple_of(x * half, half), half)
    theirs = pl.ds(pl.multiple_of((1 - x) * half, half), half)
    pairs = [
        (q_keep, dq.at[:, mine]),
        (q_got, dq.at[:, theirs]),
        (kv_keep.at[0], dk.at[:, mine]),
        (kv_got.at[0], dk.at[:, theirs]),
        (kv_keep.at[1], dv.at[:, mine]),
        (kv_got.at[1], dv.at[:, theirs]),
    ]
    all_of([pltpu.make_async_copy(a, b, sem.at[i]) for i, (a, b) in enumerate(pairs)])


def unpack(q_keep, q_got, kv_keep, kv_got):
    rows, half = q_keep.shape
    whole = jax.ShapeDtypeStruct((rows, 2 * half), BF16)
    return pl.pallas_call(
        unpack_kernel,
        out_shape=(whole,) * 3,
        in_specs=[ANY] * 4,
        out_specs=(ANY,) * 3,
        scratch_shapes=[pltpu.SemaphoreType.DMA((6,))],
        cost_estimate=cost(0, 3 * rows * half * 8),
        name="unpack",
    )(q_keep, q_got, kv_keep, kv_got)


def body(queries, keys, values, out_grad, out_weight):
    length = lax.axis_size("ctx")
    lanes = lax.axis_size("mp")
    blocks = length // 2
    width = out_grad.shape[1]

    def over_mp(array, flip):
        return lax.ppermute(array, "mp", [(i, i ^ flip) for i in range(lanes)])

    def over_x(array):
        return lax.ppermute(array, "ctx", [(i, i ^ 1) for i in range(length)])

    def over_z(array, first):
        pairs = []
        for position in range(length):
            block = position // 2
            other = ((block - first) ^ 1) + first
            for lane in range(lanes):
                source = position * lanes + lane
                if block >= first and other < blocks:
                    target = (2 * other + position % 2) * lanes + lane
                else:
                    target = position * lanes + (lane ^ 1)
                pairs.append((source, target))
        return lax.ppermute(array, ("ctx", "mp"), pairs)

    keep, send, og0, og1 = pack(queries, keys, values, out_grad)
    e0, o0 = over_z(keep, 0), over_z(keep, 1)
    y0 = over_mp(og0, 2)
    xr = over_x(send)
    y1 = over_mp(og1, 2)
    near = over_mp(out_grad, 1)
    acc = grad_piece(None, out_grad, near, out_weight, width, (0, 1), 0, False)
    e1, o1 = over_z(xr, 0), over_z(xr, 1)
    far0 = over_mp(y0, 1)
    acc = grad_piece(acc, y0, far0, out_weight, width, (2, 3), 0, False)
    far1 = over_mp(y1, 1)
    dkeep, dsend = grad_piece(acc, y1, far1, out_weight, width, (2, 3), width // 2, True)
    dxr = over_x(dsend)
    de0, do0 = over_z(dkeep, 0), over_z(dkeep, 1)
    dq_keep, dq_send, stats = query_pass(keep, xr, e0, e1, o0, o1, dkeep, dxr)
    de1, do1 = over_z(dxr, 0), over_z(dxr, 1)
    se, so = over_z(stats, 0), over_z(stats, 1)
    dq_got = over_x(dq_send)
    kv_keep, kv_send = key_pass(
        keep, xr, e0, e1, o0, o1, dkeep, dxr, de0, de1, do0, do1, stats, se, so
    )
    kv_got = over_x(kv_send)
    return tuple(unpack(dq_keep, dq_got, kv_keep, kv_got))


def solution(mesh):
    placed = (P("ctx", "mp"), P("ctx", "mp"), P("ctx", "mp"), P("ctx", "mp"), P("mp", None))
    return jax.shard_map(
        body,
        mesh=mesh,
        in_specs=placed,
        out_specs=(P("ctx", "mp"), P("ctx", "mp"), P("ctx", "mp")),
        check_vma=False,
    )
```

time: 191 us -> 194 us (1.016)
  Pallas kernels: 0 us -> 125 us
  matrix products: 52.6 us -> 0 us
  starting transfers between devices: 49.4 us -> 26.1 us
  waiting for transfers between devices: 47.4 us -> 33.5 us
  between operations: 14.4 us -> 0.9 us
  local copies, waits for them, and re-layouts: 19.6 us -> 8.37 us
  other arithmetic: 6.73 us -> 0 us
    pallas_call x0 -> x7, Pallas kernels: none -> 125 us  [the longest x1 60.7 us: pack(): pl.pallas_call(pack_kernel, out_shape=(part, part, piece, piece), in_spec...]
    dot_general x6 -> x0, matrix products: 52.6 us -> none  [the longest x1 17.1 us: body(): jnp.einsum('htu,thd->uhd', score_grad, query_heads, preferred_element_typ...]
    ppermute x16 -> x19, starting transfers between devices: 49.4 us -> 26.1 us  [the longest x10 17.4 us: over_z(): return lax.ppermute(array, ('ctx', 'mp'), pairs)]
    ppermute x16 -> x19, waiting for transfers between devices: 46.7 us -> 33.5 us  [the longest x5 16.4 us: over_mp(): return lax.ppermute(array, 'mp', [(i, i ^ flip) for i in range(lanes)])]
    convert_element_type x9 -> x0, local copies, waits for them, and re-layouts: 5.31 us -> none  [the longest x2 1.86 us: body(): key_part[REACH - distance].astype(jnp.bfloat16)]
    convert_element_type x2 -> x0, other arithmetic: 4.64 us -> none  [the longest x1 2.32 us: body(): key_total.astype(jnp.bfloat16)]
    slice x4 -> x0, local copies, waits for them, and re-layouts: 4.03 us -> none  [the longest x1 1.47 us: body(): key_part[REACH - distance].astype(jnp.bfloat16)]
    reduce_sum x1 -> x0, other arithmetic: 2.07 us -> none  [body(): jnp.sum(jnp.exp(masked - largest), -1, keepdims=True)]
  transfers between devices with their start and end apart: 17 -> 19, of which waited for: 4 -> 5; matrix products, arithmetic and copies ran while one was open for 21% -> 0% of each run, Pallas kernels for 0% -> 40%
where the time goes in v1:
time: 194 us
  Pallas kernels  125 us (64%)
  waiting for transfers between devices  33.5 us (17%)
  starting transfers between devices  26.1 us (13%)
  local copies, waits for them, and re-layouts  8.37 us (4%)
    pallas_call x1, Pallas kernels, pack(): pl.pallas_call(pack_kernel, out_shape=(part, part, piece, piece), in_spec...  60.7 us
    pallas_call x1, Pallas kernels, unpack(): pl.pallas_call(unpack_kernel, out_shape=(whole,) * 3, in_specs=[ANY] * 4,...  36.9 us
    ppermute x10, starting transfers between devices, over_z(): return lax.ppermute(array, ('ctx', 'mp'), pairs)  17.4 us
    ppermute x5, waiting for transfers between devices, over_mp(): return lax.ppermute(array, 'mp', [(i, i ^ flip) for i in range(lanes)])  16.4 us
    ppermute x4, waiting for transfers between devices, over_x(): return lax.ppermute(array, 'ctx', [(i, i ^ 1) for i in range(length)])  15.4 us
    pallas_call x1, Pallas kernels, query_pass(): pl.pallas_call(functools.partial(query_kernel, HD ** (-0.5)), out_shape=(...  11.3 us
    pallas_call x1, Pallas kernels, key_pass(): pl.pallas_call(functools.partial(key_kernel, HD ** (-0.5)), out_shape=(pa...  11.2 us
    unnamed x16, local copies, waits for them, and re-layouts  8.37 us
  transfers between devices with their start and end apart: 19, of which 5 were waited for; matrix products, arithmetic and copies ran while one was open for 0% of the time, Pallas kernels for 40%

profile of v1, /device:TPU:0, one launch (start us, length us, event | category | flops | bytes accessed | tf_op | source)
XLA Modules:
  0.0 194.0 jit_solution(826944790944943346)
XLA Ops:
  0.6 0.5 collective-permute-start.5
  1.1 60.7 %pack.1 = (bf16[3,256,384]{2,1,0:T(8,128)(2,1)}, bf16[3,256,384]{2,1,0:T(8,128)(2,1)}, bf16[256,768]{1,0:T(8,128)(2,1)}, bf16[256,768]{1,0:T(8,128)(2,1)}) custom-call(bf16[256,768]{1,0:T(8,128)(2,1)} %q.1, bf16[256,768]{1,0:T(8,128)(2,1)} %k.1, bf16[256,768]{1,0:T(8,128)(2,1)} %v.1, bf16[256,1536]{1,0:T(8,128)(2,1)} %refs_0_.1), custom_call_target="tpu_custom_call" | custom-call | bytes 8000000 | tf_op jit(solution)/shard_map/pack/pallas_call | solution.py:61
  61.9 2.6 %collective-permute-start.6 = (bf16[256,768]{1,0:T(8,128)(2,1)}, bf16[256,768]{1,0:T(8,128)(2,1)S(1)}, u32[]{:S(2)}, u32[]{:S(2)}) collective-permute-start(bf16[256,768]{1,0:T(8,128)(2,1)} %get-tuple-element.16), channel_id=1, source_target_pairs={{0,2},{1,3},{2,0},{3,1},{4,6},{5,7},{6,4},{7,5},{8,10},{9,11},{10,... | collective-permute-start | bytes 1179656 | tf_op jit(solution)/shard_map/ppermute | solution.py:384
  64.5 1.5 collective-permute-start
  66.0 0.5 collective-permute-start.8
  66.5 8.2 %collective-permute-done.6.refs_1_ = bf16[256,768]{1,0:T(8,128)(2,1)S(1)} collective-permute-done((bf16[256,768]{1,0:T(8,128)(2,1)}, bf16[256,768]{1,0:T(8,128)(2,1)S(1)}, u32[]{:S(2)}, u32[]{:S(2)}) %collective-permute-start.6) | collective-permute-done | bytes 393248 | tf_op jit(solution)/shard_map/ppermute | solution.py:384
  74.7 8.2 %collective-permute-done.8.refs_1_ = bf16[256,768]{1,0:T(8,128)(2,1)S(1)} collective-permute-done((bf16[256,768]{1,0:T(8,128)(2,1)}, bf16[256,768]{1,0:T(8,128)(2,1)S(1)}, u32[]{:S(2)}, u32[]{:S(2)}) %collective-permute-start.8) | collective-permute-done | bytes 393248 | tf_op jit(solution)/shard_map/ppermute | solution.py:384
  82.9 0.5 collective-permute-start.3
  83.4 2.9 %collective-permute-start.1 = (bf16[3,256,384]{2,1,0:T(8,128)(2,1)}, bf16[3,256,384]{2,1,0:T(8,128)(2,1)S(1)}, u32[]{:S(2)}, u32[]{:S(2)}) collective-permute-start(bf16[3,256,384]{2,1,0:T(8,128)(2,1)} %get-tuple-element.14.keep), channel_id=1, source_target_pairs={{0,8},{1,9},{2,10},{3,11},{4,12},{5,13},{6,14},{7,15},{8,0},{9,1},... | collective-permute-start | bytes 1769480 | tf_op jit(solution)/shard_map/ppermute | solution.py:401
  86.3 2.1 %collective-permute-start.2 = (bf16[3,256,384]{2,1,0:T(8,128)(2,1)S(1)}, bf16[3,256,384]{2,1,0:T(8,128)(2,1)}, u32[]{:S(2)}, u32[]{:S(2)}) collective-permute-start(bf16[3,256,384]{2,1,0:T(8,128)(2,1)S(1)} %collective-permute-done.xr), channel_id=1, source_target_pairs={{0,8},{1,9},{2,10},{3,11},{4,12},{5,13},{6,14},{7,15},{8,0},{9,1},... | collective-permute-start | bytes 1769480 | tf_op jit(solution)/shard_map/ppermute | solution.py:401
  88.4 3.7 %copy-done = bf16[768,6144]{1,0:T(8,128)(2,1)S(1)} copy-done((bf16[768,6144]{1,0:T(8,128)(2,1)S(1)}, bf16[768,6144]{1,0:T(8,128)(2,1)}, u32[]{:S(2)}) %copy-start) | copy-done | bytes 9437208
  92.0 1.1 copy-done.2
  93.2 2.4 %head_grad.3.refs_0_ = f32[256,768]{1,0:T(8,128)S(1)} custom-call(bf16[256,1536]{1,0:T(8,128)(2,1)S(1)} %copy-done.2, bf16[256,1536]{1,0:T(8,128)(2,1)S(1)} %collective-permute-done.5.refs_1_, bf16[768,6144]{1,0:T(8,128)(2,1)S(1)} %copy-done), custom_call_target="tpu_custom_call" | custom-call | flops 1207959552 | bytes 6291456 | tf_op jit(solution)/shard_map/head_grad/pallas_call | solution.py:123
  95.6 1.3 copy-done.1
  96.9 1.3 head_grad.4.refs_0_
  98.1 1.3 head_grad.5
  99.5 1.6 collective-permute-start.10
  101.0 1.6 collective-permute-start.12
  102.6 2.8 %collective-permute-done.10.dxr = bf16[256,384]{1,0:T(8,128)(2,1)S(1)} collective-permute-done((bf16[256,384]{1,0:T(8,128)(2,1)S(1)}, bf16[256,384]{1,0:T(8,128)(2,1)S(1)}, u32[]{:S(2)}, u32[]{:S(2)}) %collective-permute-start.10) | collective-permute-done | bytes 196640 | tf_op jit(solution)/shard_map/ppermute | solution.py:387
  105.5 8.3 %collective-permute-start.13 = (bf16[256,384]{1,0:T(8,128)(2,1)S(1)}, bf16[256,384]{1,0:T(8,128)(2,1)S(1)}, u32[]{:S(2)}, u32[]{:S(2)}) collective-permute-start(bf16[256,384]{1,0:T(8,128)(2,1)S(1)} %collective-permute-done.10.dxr), channel_id=1, source_target_pairs={{0,8},{1,9},{2,10},{3,11},{4,12},{5,13},{6,14},{7,15},{8,0},{9,1},... | collective-permute-start | bytes 589832 | tf_op jit(solution)/shard_map/ppermute | solution.py:401
  113.8 11.3 %query_pass.1 = (bf16[256,384]{1,0:T(8,128)(2,1)S(1)}, bf16[256,384]{1,0:T(8,128)(2,1)S(1)}, f32[8,512]{1,0:T(8,128)S(1)}) custom-call(bf16[3,256,384]{2,1,0:T(8,128)(2,1)S(1)} %copy-done.5, bf16[3,256,384]{2,1,0:T(8,128)(2,1)S(1)} %collective-permute-done.xr, bf16[3,256,384]{2,1,0:T(8,128)(2,1)S(1)} %collective-permute-done.1.e0, ...), custom_call_target="tpu_custom_call" | custom-call | flops 1509949440 | bytes 3932160 | tf_op jit(solution)/shard_map/query_pass/pallas_call | solution.py:228
  125.1 0.7 copy-done.4
  125.8 2.0 %collective-permute-start.16 = (f32[8,512]{1,0:T(8,128)S(1)}, f32[8,512]{1,0:T(8,128)S(1)}, u32[]{:S(2)}, u32[]{:S(2)}) collective-permute-start(f32[8,512]{1,0:T(8,128)S(1)} %get-tuple-element.22.stats), channel_id=1, source_target_pairs={{0,8},{1,9},{2,10},{3,11},{4,12},{5,13},{6,14},{7,15},{8,0},{9,1},... | collective-permute-start | bytes 49160 | tf_op jit(solution)/shard_map/ppermute | solution.py:401
  127.9 1.7 collective-permute-done.16.se
  129.6 11.2 %key_pass.1 = (bf16[2,256,384]{2,1,0:T(8,128)(2,1)S(1)}, bf16[2,256,384]{2,1,0:T(8,128)(2,1)S(1)}) custom-call(bf16[3,256,384]{2,1,0:T(8,128)(2,1)S(1)} %copy-done.5, bf16[3,256,384]{2,1,0:T(8,128)(2,1)S(1)} %collective-permute-done.xr, bf16[3,256,384]{2,1,0:T(8,128)(2,1)S(1)} %collective-permute-done.1.e0, bf16[3,256,384]{2,1,0:T(8,128)(2,1)} %collective-permute-done.2.e1, ...), custom_call_target="tpu_custom_call" | custom-call | flops 2013265920 | bytes 3932160 | tf_op jit(solution)/shard_map/key_pass/pallas_call | solution.py:328
  140.8 0.7 copy-done.3
  141.5 1.5 collective-permute-start.18
  143.0 0.5 collective-permute-start.11
  143.6 12.5 %collective-permute-done.11.q_got = bf16[256,384]{1,0:T(8,128)(2,1)S(1)} collective-permute-done((bf16[256,384]{1,0:T(8,128)(2,1)S(1)}, bf16[256,384]{1,0:T(8,128)(2,1)S(1)}, u32[]{:S(2)}, u32[]{:S(2)}) %collective-permute-start.11) | collective-permute-done | bytes 196640 | tf_op jit(solution)/shard_map/ppermute | solution.py:387
  156.1 0.7 copy-done.7
  156.8 0.2 copy-done.6
  156.9 36.9 %unpack.1 = (bf16[256,768]{1,0:T(8,128)(2,1)}, bf16[256,768]{1,0:T(8,128)(2,1)}, bf16[256,768]{1,0:T(8,128)(2,1)}) custom-call(bf16[256,384]{1,0:T(8,128)(2,1)} %copy-done.4, bf16[256,384]{1,0:T(8,128)(2,1)} %copy-done.7, bf16[2,256,384]{2,1,0:T(8,128)(2,1)} %copy-done.3, bf16[2,256,384]{2,1,0:T(8,128)(2,1)} %copy-done.6), custom_call_target="tpu_custom_call" | custom-call | bytes 2359296 | tf_op jit(solution)/shard_map/unpack/pallas_call | solution.py:366
  (29 shorter events, 0.1 us)
Async XLA Ops:
  0.6 85.6 %collective-permute-start.5 = (bf16[256,1536]{1,0:T(8,128)(2,1)}, bf16[256,1536]{1,0:T(8,128)(2,1)S(1)}, u32[]{:S(2)}, u32[]{:S(2)}) collective-permute-start(bf16[256,1536]{1,0:T(8,128)(2,1)} %refs_0_.1), channel_id=1, source_target_pairs={{0,1},{1,0},{2,3},{3,2},{4,5},{5,4},{6,7},{7,6},{8,9},{9,8},{10,11... | collective-permute-start | bytes 2359304 | tf_op jit(solution)/shard_map/ppermute | solution.py:384
  61.9 12.8 %collective-permute-start.6 = (bf16[256,768]{1,0:T(8,128)(2,1)}, bf16[256,768]{1,0:T(8,128)(2,1)S(1)}, u32[]{:S(2)}, u32[]{:S(2)}) collective-permute-start(bf16[256,768]{1,0:T(8,128)(2,1)} %get-tuple-element.16), channel_id=1, source_target_pairs={{0,2},{1,3},{2,0},{3,1},{4,6},{5,7},{6,4},{7,5},{8,10},{9,11},{10,... | collective-permute-start | bytes 1179656 | tf_op jit(solution)/shard_map/ppermute | solution.py:384
  64.5 18.9 %collective-permute-start = (bf16[3,256,384]{2,1,0:T(8,128)(2,1)}, bf16[3,256,384]{2,1,0:T(8,128)(2,1)S(1)}, u32[]{:S(2)}, u32[]{:S(2)}) collective-permute-start(bf16[3,256,384]{2,1,0:T(8,128)(2,1)} %get-tuple-element.15), channel_id=1, source_target_pairs={{0,4},{4,0},{8,12},{12,8},{16,20},{20,16},{24,28},{28,24},{1,5},{5... | collective-permute-start | bytes 1769480 | tf_op jit(solution)/shard_map/ppermute | solution.py:387
  66.0 16.9 %collective-permute-start.8 = (bf16[256,768]{1,0:T(8,128)(2,1)}, bf16[256,768]{1,0:T(8,128)(2,1)S(1)}, u32[]{:S(2)}, u32[]{:S(2)}) collective-permute-start(bf16[256,768]{1,0:T(8,128)(2,1)} %get-tuple-element.17), channel_id=1, source_target_pairs={{0,2},{1,3},{2,0},{3,1},{4,6},{5,7},{6,4},{7,5},{8,10},{9,11},{10,... | collective-permute-start | bytes 1179656 | tf_op jit(solution)/shard_map/ppermute | solution.py:384
  74.7 11.6 %collective-permute-start.7 = (bf16[256,768]{1,0:T(8,128)(2,1)S(1)}, bf16[256,768]{1,0:T(8,128)(2,1)S(1)}, u32[]{:S(2)}, u32[]{:S(2)}) collective-permute-start(bf16[256,768]{1,0:T(8,128)(2,1)S(1)} %collective-permute-done.6.refs_1_), channel_id=1, source_target_pairs={{0,1},{1,0},{2,3},{3,2},{4,5},{5,4},{6,7},{7,6},{8,9},{9,8},{10,11... | collective-permute-start | bytes 1179656 | tf_op jit(solution)/shard_map/ppermute | solution.py:384
  82.9 15.2 %collective-permute-start.9 = (bf16[256,768]{1,0:T(8,128)(2,1)S(1)}, bf16[256,768]{1,0:T(8,128)(2,1)S(1)}, u32[]{:S(2)}, u32[]{:S(2)}) collective-permute-start(bf16[256,768]{1,0:T(8,128)(2,1)S(1)} %collective-permute-done.8.refs_1_), channel_id=1, source_target_pairs={{0,1},{1,0},{2,3},{3,2},{4,5},{5,4},{6,7},{7,6},{8,9},{9,8},{10,11... | collective-permute-start | bytes 1179656 | tf_op jit(solution)/shard_map/ppermute | solution.py:384
  82.9 18.1 %collective-permute-start.3 = (bf16[3,256,384]{2,1,0:T(8,128)(2,1)}, bf16[3,256,384]{2,1,0:T(8,128)(2,1)S(1)}, u32[]{:S(2)}, u32[]{:S(2)}) collective-permute-start(bf16[3,256,384]{2,1,0:T(8,128)(2,1)} %get-tuple-element.14.keep), channel_id=1, source_target_pairs={{0,1},{1,0},{2,3},{3,2},{4,5},{5,4},{6,7},{7,6},{8,16},{9,17},{10,... | collective-permute-start | bytes 1769480 | tf_op jit(solution)/shard_map/ppermute | solution.py:401
  83.4 17.6 %collective-permute-start.1 = (bf16[3,256,384]{2,1,0:T(8,128)(2,1)}, bf16[3,256,384]{2,1,0:T(8,128)(2,1)S(1)}, u32[]{:S(2)}, u32[]{:S(2)}) collective-permute-start(bf16[3,256,384]{2,1,0:T(8,128)(2,1)} %get-tuple-element.14.keep), channel_id=1, source_target_pairs={{0,8},{1,9},{2,10},{3,11},{4,12},{5,13},{6,14},{7,15},{8,0},{9,1},... | collective-permute-start | bytes 1769480 | tf_op jit(solution)/shard_map/ppermute | solution.py:401
  86.3 19.2 %collective-permute-start.4 = (bf16[3,256,384]{2,1,0:T(8,128)(2,1)S(1)}, bf16[3,256,384]{2,1,0:T(8,128)(2,1)}, u32[]{:S(2)}, u32[]{:S(2)}) collective-permute-start(bf16[3,256,384]{2,1,0:T(8,128)(2,1)S(1)} %collective-permute-done.xr), channel_id=1, source_target_pairs={{0,1},{1,0},{2,3},{3,2},{4,5},{5,4},{6,7},{7,6},{8,16},{9,17},{10,... | collective-permute-start | bytes 1769480 | tf_op jit(solution)/shard_map/ppermute | solution.py:401
  86.3 27.5 %collective-permute-start.2 = (bf16[3,256,384]{2,1,0:T(8,128)(2,1)S(1)}, bf16[3,256,384]{2,1,0:T(8,128)(2,1)}, u32[]{:S(2)}, u32[]{:S(2)}) collective-permute-start(bf16[3,256,384]{2,1,0:T(8,128)(2,1)S(1)} %collective-permute-done.xr), channel_id=1, source_target_pairs={{0,8},{1,9},{2,10},{3,11},{4,12},{5,13},{6,14},{7,15},{8,0},{9,1},... | collective-permute-start | bytes 1769480 | tf_op jit(solution)/shard_map/ppermute | solution.py:401
  88.4 3.7 %copy-start = (bf16[768,6144]{1,0:T(8,128)(2,1)S(1)}, bf16[768,6144]{1,0:T(8,128)(2,1)}, u32[]{:S(2)}) copy-start(bf16[768,6144]{1,0:T(8,128)(2,1)} %refs_3_.3) | copy-start | bytes 28311556
  92.0 1.1 copy-start.2
  93.2 3.7 %copy-start.1 = (bf16[768,6144]{1,0:T(8,128)(2,1)S(1)}, bf16[768,6144]{1,0:T(8,128)(2,1)}, u32[]{:S(2)}) copy-start(bf16[768,6144]{1,0:T(8,128)(2,1)} %refs_3_.3) | copy-start | bytes 28311556
  96.9 16.9 %copy-start.5 = (bf16[3,256,384]{2,1,0:T(8,128)(2,1)S(1)}, bf16[3,256,384]{2,1,0:T(8,128)(2,1)}, u32[]{:S(2)}) copy-start(bf16[3,256,384]{2,1,0:T(8,128)(2,1)} %get-tuple-element.14.keep) | copy-start | bytes 1769476
  99.5 6.0 %collective-permute-start.10 = (bf16[256,384]{1,0:T(8,128)(2,1)S(1)}, bf16[256,384]{1,0:T(8,128)(2,1)S(1)}, u32[]{:S(2)}, u32[]{:S(2)}) collective-permute-start(bf16[256,384]{1,0:T(8,128)(2,1)S(1)} %get-tuple-element.19), channel_id=1, source_target_pairs={{0,4},{4,0},{8,12},{12,8},{16,20},{20,16},{24,28},{28,24},{1,5},{5... | collective-permute-start | bytes 589832 | tf_op jit(solution)/shard_map/ppermute | solution.py:387
  101.0 24.8 %collective-permute-start.14 = (bf16[256,384]{1,0:T(8,128)(2,1)S(1)}, bf16[256,384]{1,0:T(8,128)(2,1)S(1)}, u32[]{:S(2)}, u32[]{:S(2)}) collective-permute-start(bf16[256,384]{1,0:T(8,128)(2,1)S(1)} %get-tuple-element.18.dkeep), channel_id=1, source_target_pairs={{0,1},{1,0},{2,3},{3,2},{4,5},{5,4},{6,7},{7,6},{8,16},{9,17},{10,... | collective-permute-start | bytes 589832 | tf_op jit(solution)/shard_map/ppermute | solution.py:401
  101.0 26.8 %collective-permute-start.12 = (bf16[256,384]{1,0:T(8,128)(2,1)S(1)}, bf16[256,384]{1,0:T(8,128)(2,1)S(1)}, u32[]{:S(2)}, u32[]{:S(2)}) collective-permute-start(bf16[256,384]{1,0:T(8,128)(2,1)S(1)} %get-tuple-element.18.dkeep), channel_id=1, source_target_pairs={{0,8},{1,9},{2,10},{3,11},{4,12},{5,13},{6,14},{7,15},{8,0},{9,1},... | collective-permute-start | bytes 589832 | tf_op jit(solution)/shard_map/ppermute | solution.py:401
  105.5 22.4 %collective-permute-start.15 = (bf16[256,384]{1,0:T(8,128)(2,1)S(1)}, bf16[256,384]{1,0:T(8,128)(2,1)S(1)}, u32[]{:S(2)}, u32[]{:S(2)}) collective-permute-start(bf16[256,384]{1,0:T(8,128)(2,1)S(1)} %collective-permute-done.10.dxr), channel_id=1, source_target_pairs={{0,1},{1,0},{2,3},{3,2},{4,5},{5,4},{6,7},{7,6},{8,16},{9,17},{10,... | collective-permute-start | bytes 589832 | tf_op jit(solution)/shard_map/ppermute | solution.py:401
  105.5 22.4 %collective-permute-start.13 = (bf16[256,384]{1,0:T(8,128)(2,1)S(1)}, bf16[256,384]{1,0:T(8,128)(2,1)S(1)}, u32[]{:S(2)}, u32[]{:S(2)}) collective-permute-start(bf16[256,384]{1,0:T(8,128)(2,1)S(1)} %collective-permute-done.10.dxr), channel_id=1, source_target_pairs={{0,8},{1,9},{2,10},{3,11},{4,12},{5,13},{6,14},{7,15},{8,0},{9,1},... | collective-permute-start | bytes 589832 | tf_op jit(solution)/shard_map/ppermute | solution.py:401
  125.1 0.7 copy-start.4
  125.8 2.1 %collective-permute-start.17 = (f32[8,512]{1,0:T(8,128)S(1)}, f32[8,512]{1,0:T(8,128)S(1)}, u32[]{:S(2)}, u32[]{:S(2)}) collective-permute-start(f32[8,512]{1,0:T(8,128)S(1)} %get-tuple-element.22.stats), channel_id=1, source_target_pairs={{0,1},{1,0},{2,3},{3,2},{4,5},{5,4},{6,7},{7,6},{8,16},{9,17},{10,... | collective-permute-start | bytes 49160 | tf_op jit(solution)/shard_map/ppermute | solution.py:401
  125.8 3.8 %collective-permute-start.16 = (f32[8,512]{1,0:T(8,128)S(1)}, f32[8,512]{1,0:T(8,128)S(1)}, u32[]{:S(2)}, u32[]{:S(2)}) collective-permute-start(f32[8,512]{1,0:T(8,128)S(1)} %get-tuple-element.22.stats), channel_id=1, source_target_pairs={{0,8},{1,9},{2,10},{3,11},{4,12},{5,13},{6,14},{7,15},{8,0},{9,1},... | collective-permute-start | bytes 49160 | tf_op jit(solution)/shard_map/ppermute | solution.py:401
  140.8 0.7 copy-start.3
  141.5 14.6 %collective-permute-start.18 = (bf16[2,256,384]{2,1,0:T(8,128)(2,1)S(1)}, bf16[2,256,384]{2,1,0:T(8,128)(2,1)S(1)}, u32[]{:S(2)}, u32[]{:S(2)}) collective-permute-start(bf16[2,256,384]{2,1,0:T(8,128)(2,1)S(1)} %get-tuple-element.24), channel_id=1, source_target_pairs={{0,4},{4,0},{8,12},{12,8},{16,20},{20,16},{24,28},{28,24},{1,5},{5... | collective-permute-start | bytes 1179656 | tf_op jit(solution)/shard_map/ppermute | solution.py:387
  143.0 13.1 %collective-permute-start.11 = (bf16[256,384]{1,0:T(8,128)(2,1)S(1)}, bf16[256,384]{1,0:T(8,128)(2,1)S(1)}, u32[]{:S(2)}, u32[]{:S(2)}) collective-permute-start(bf16[256,384]{1,0:T(8,128)(2,1)S(1)} %get-tuple-element.21), channel_id=1, source_target_pairs={{0,4},{4,0},{8,12},{12,8},{16,20},{20,16},{24,28},{28,24},{1,5},{5... | collective-permute-start | bytes 589832 | tf_op jit(solution)/shard_map/ppermute | solution.py:387
  156.1 0.7 copy-start.7
  156.1 0.8 copy-start.6

commit v2 on v1

--- a/solution.py
+++ b/solution.py
@@ -14,6 +14,7 @@
 BIG = 1e30
 ANY = pl.BlockSpec(memory_space=pl.ANY)
 VM = pl.BlockSpec(memory_space=pltpu.VMEM)
+HBM = pl.BlockSpec(memory_space=pltpu.HBM)
 
 
 def params(mib=40):
@@ -62,7 +63,7 @@
         pack_kernel,
         out_shape=(part, part, piece, piece),
         in_specs=[ANY] * 4,
-        out_specs=(ANY,) * 4,
+        out_specs=(VM,) * 4,
         scratch_shapes=[pltpu.SemaphoreType.DMA((8,))],
         cost_estimate=cost(0, 8e6),
         name="pack",
@@ -123,7 +124,7 @@
     return pl.pallas_call(
         functools.partial(grad_kernel, width, flips, offset, acc is not None, last),
         out_shape=shape,
-        in_specs=[VM] * (len(operands) - 1) + [ANY],
+        in_specs=[VM] * (len(operands) - 1) + [HBM],
         out_specs=spec,
         scratch_shapes=[pltpu.VMEM((2, heads, size), BF16), pltpu.SemaphoreType.DMA((2,))],
         compiler_params=params(),
@@ -367,7 +368,7 @@
         unpack_kernel,
         out_shape=(whole,) * 3,
         in_specs=[ANY] * 4,
-        out_specs=(ANY,) * 3,
+        out_specs=(VM,) * 3,
         scratch_shapes=[pltpu.SemaphoreType.DMA((6,))],
         cost_estimate=cost(0, 3 * rows * half * 8),
         name="unpack",

time: 194 us -> 102 us (0.53)
  Pallas kernels: 125 us -> 32.8 us
    pallas_call x1, Pallas kernels: 60.7 us -> 2.92 us  [pack(): pl.pallas_call(pack_kernel, out_shape=(part, part, piece, piece), in_spec...]
    pallas_call x1, Pallas kernels: 36.9 us -> 2.39 us  [unpack(): pl.pallas_call(unpack_kernel, out_shape=(whole,) * 3, in_specs=[ANY] * 4,...]
  transfers between devices with their start and end apart: 19 -> 19, of which waited for: 5 -> 5; matrix products, arithmetic and copies ran while one was open for 0% -> 0% of each run, Pallas kernels for 40% -> 19%
where the time goes in v2:
time: 102 us
  waiting for transfers between devices  33.5 us (33%)
  Pallas kernels  32.8 us (32%)
  starting transfers between devices  26.1 us (26%)
  local copies, waits for them, and re-layouts  8.37 us (8%)
    ppermute x10, starting transfers between devices, over_z(): return lax.ppermute(array, ('ctx', 'mp'), pairs)  17.4 us
    ppermute x5, waiting for transfers between devices, over_mp(): return lax.ppermute(array, 'mp', [(i, i ^ flip) for i in range(lanes)])  16.4 us
    ppermute x4, waiting for transfers between devices, over_x(): return lax.ppermute(array, 'ctx', [(i, i ^ 1) for i in range(length)])  15.4 us
    pallas_call x1, Pallas kernels, query_pass(): pl.pallas_call(functools.partial(query_kernel, HD ** (-0.5)), out_shape=(...  11.3 us
    pallas_call x1, Pallas kernels, key_pass(): pl.pallas_call(functools.partial(key_kernel, HD ** (-0.5)), out_shape=(pa...  11.2 us
    unnamed x16, local copies, waits for them, and re-layouts  8.37 us
    ppermute x4, starting transfers between devices, over_x(): return lax.ppermute(array, 'ctx', [(i, i ^ 1) for i in range(length)])  5.07 us
    pallas_call x3, Pallas kernels, grad_piece(): pl.pallas_call(functools.partial(grad_kernel, width, flips, offset, acc i...  4.93 us
  transfers between devices with their start and end apart: 19, of which 5 were waited for; matrix products, arithmetic and copies ran while one was open for 0% of the time, Pallas kernels for 19%

profile of v2, /device:TPU:0, one launch (start us, length us, event | category | flops | bytes accessed | tf_op | source)
XLA Modules:
  0.0 101.7 jit_solution(782635702949697300)
XLA Ops:
  0.6 0.5 collective-permute-start.5
  1.1 2.9 %pack.1 = (bf16[3,256,384]{2,1,0:T(8,128)(2,1)}, bf16[3,256,384]{2,1,0:T(8,128)(2,1)}, bf16[256,768]{1,0:T(8,128)(2,1)}, bf16[256,768]{1,0:T(8,128)(2,1)}) custom-call(bf16[256,768]{1,0:T(8,128)(2,1)} %q.1, bf16[256,768]{1,0:T(8,128)(2,1)} %k.1, bf16[256,768]{1,0:T(8,128)(2,1)} %v.1, bf16[256,1536]{1,0:T(8,128)(2,1)} %refs_0_.1), custom_call_target="tpu_custom_call" | custom-call | bytes 8000000 | tf_op jit(solution)/shard_map/pack/pallas_call | solution.py:62
  4.1 2.6 %collective-permute-start.6 = (bf16[256,768]{1,0:T(8,128)(2,1)}, bf16[256,768]{1,0:T(8,128)(2,1)S(1)}, u32[]{:S(2)}, u32[]{:S(2)}) collective-permute-start(bf16[256,768]{1,0:T(8,128)(2,1)} %get-tuple-element.16), channel_id=1, source_target_pairs={{0,2},{1,3},{2,0},{3,1},{4,6},{5,7},{6,4},{7,5},{8,10},{9,11},{10,... | collective-permute-start | bytes 1179656 | tf_op jit(solution)/shard_map/ppermute | solution.py:385
  6.7 1.5 %collective-permute-start = (bf16[3,256,384]{2,1,0:T(8,128)(2,1)}, bf16[3,256,384]{2,1,0:T(8,128)(2,1)S(1)}, u32[]{:S(2)}, u32[]{:S(2)}) collective-permute-start(bf16[3,256,384]{2,1,0:T(8,128)(2,1)} %get-tuple-element.15), channel_id=1, source_target_pairs={{0,4},{4,0},{8,12},{12,8},{16,20},{20,16},{24,28},{28,24},{1,5},{5... | collective-permute-start | bytes 1769480 | tf_op jit(solution)/shard_map/ppermute | solution.py:388
  8.2 0.5 collective-permute-start.8
  8.7 8.2 %collective-permute-done.6.refs_1_ = bf16[256,768]{1,0:T(8,128)(2,1)S(1)} collective-permute-done((bf16[256,768]{1,0:T(8,128)(2,1)}, bf16[256,768]{1,0:T(8,128)(2,1)S(1)}, u32[]{:S(2)}, u32[]{:S(2)}) %collective-permute-start.6) | collective-permute-done | bytes 393248 | tf_op jit(solution)/shard_map/ppermute | solution.py:385
  16.9 8.2 %collective-permute-done.8.refs_1_ = bf16[256,768]{1,0:T(8,128)(2,1)S(1)} collective-permute-done((bf16[256,768]{1,0:T(8,128)(2,1)}, bf16[256,768]{1,0:T(8,128)(2,1)S(1)}, u32[]{:S(2)}, u32[]{:S(2)}) %collective-permute-start.8) | collective-permute-done | bytes 393248 | tf_op jit(solution)/shard_map/ppermute | solution.py:385
  25.1 0.5 collective-permute-start.3
  25.6 2.9 %collective-permute-start.1 = (bf16[3,256,384]{2,1,0:T(8,128)(2,1)}, bf16[3,256,384]{2,1,0:T(8,128)(2,1)S(1)}, u32[]{:S(2)}, u32[]{:S(2)}) collective-permute-start(bf16[3,256,384]{2,1,0:T(8,128)(2,1)} %get-tuple-element.14.keep), channel_id=1, source_target_pairs={{0,8},{1,9},{2,10},{3,11},{4,12},{5,13},{6,14},{7,15},{8,0},{9,1},... | collective-permute-start | bytes 1769480 | tf_op jit(solution)/shard_map/ppermute | solution.py:402
  28.5 2.1 %collective-permute-start.2 = (bf16[3,256,384]{2,1,0:T(8,128)(2,1)S(1)}, bf16[3,256,384]{2,1,0:T(8,128)(2,1)}, u32[]{:S(2)}, u32[]{:S(2)}) collective-permute-start(bf16[3,256,384]{2,1,0:T(8,128)(2,1)S(1)} %collective-permute-done.xr), channel_id=1, source_target_pairs={{0,8},{1,9},{2,10},{3,11},{4,12},{5,13},{6,14},{7,15},{8,0},{9,1},... | collective-permute-start | bytes 1769480 | tf_op jit(solution)/shard_map/ppermute | solution.py:402
  30.6 3.7 %copy-done = bf16[768,6144]{1,0:T(8,128)(2,1)S(1)} copy-done((bf16[768,6144]{1,0:T(8,128)(2,1)S(1)}, bf16[768,6144]{1,0:T(8,128)(2,1)}, u32[]{:S(2)}) %copy-start) | copy-done | bytes 9437208
  34.2 1.1 %copy-done.2 = bf16[256,1536]{1,0:T(8,128)(2,1)S(1)} copy-done((bf16[256,1536]{1,0:T(8,128)(2,1)S(1)}, bf16[256,1536]{1,0:T(8,128)(2,1)}, u32[]{:S(2)}) %copy-start.2) | copy-done | bytes 786456
  35.4 2.4 %head_grad.3.refs_0_ = f32[256,768]{1,0:T(8,128)S(1)} custom-call(bf16[256,1536]{1,0:T(8,128)(2,1)S(1)} %copy-done.2, bf16[256,1536]{1,0:T(8,128)(2,1)S(1)} %collective-permute-done.5.refs_1_, bf16[768,6144]{1,0:T(8,128)(2,1)S(1)} %copy-done), custom_call_target="tpu_custom_call" | custom-call | flops 1207959552 | bytes 6291456 | tf_op jit(solution)/shard_map/head_grad/pallas_call | solution.py:124
  37.7 1.3 %copy-done.1 = bf16[768,6144]{1,0:T(8,128)(2,1)S(1)} copy-done((bf16[768,6144]{1,0:T(8,128)(2,1)S(1)}, bf16[768,6144]{1,0:T(8,128)(2,1)}, u32[]{:S(2)}) %copy-start.1) | copy-done | bytes 9437208
  39.0 1.3 %head_grad.4.refs_0_ = f32[256,768]{1,0:T(8,128)S(1)} custom-call(f32[256,768]{1,0:T(8,128)S(1)} %head_grad.3.refs_0_, bf16[256,768]{1,0:T(8,128)(2,1)S(1)} %collective-permute-done.6.refs_1_, bf16[256,768]{1,0:T(8,128)(2,1)S(1)} %collective-permute-done.7.refs_2_, bf16[768,6144]{1,0:T(8,128)(2,1)S(1)} %copy-done.1), custom_call_target="tpu_custom_call" | custom-call | flops 603979776 | bytes 3145728 | tf_op jit(solution)/shard_map/head_grad/pallas_call | solution.py:124
  40.3 1.3 %head_grad.5 = (bf16[256,384]{1,0:T(8,128)(2,1)S(1)}, bf16[256,384]{1,0:T(8,128)(2,1)S(1)}) custom-call(f32[256,768]{1,0:T(8,128)S(1)} %head_grad.4.refs_0_, bf16[256,768]{1,0:T(8,128)(2,1)S(1)} %collective-permute-done.8.refs_1_, bf16[256,768]{1,0:T(8,128)(2,1)S(1)} %collective-permute-done.9.refs_2_, bf16[768,6144]{1,0:T(8,128)(2,1)S(1)} %copy-done.1), custom_call_target="tpu_custom_call" | custom-call | flops 603979776 | bytes 3145728 | tf_op jit(solution)/shard_map/head_grad/pallas_call | solution.py:124
  41.6 1.6 %collective-permute-start.10 = (bf16[256,384]{1,0:T(8,128)(2,1)S(1)}, bf16[256,384]{1,0:T(8,128)(2,1)S(1)}, u32[]{:S(2)}, u32[]{:S(2)}) collective-permute-start(bf16[256,384]{1,0:T(8,128)(2,1)S(1)} %get-tuple-element.19), channel_id=1, source_target_pairs={{0,4},{4,0},{8,12},{12,8},{16,20},{20,16},{24,28},{28,24},{1,5},{5... | collective-permute-start | bytes 589832 | tf_op jit(solution)/shard_map/ppermute | solution.py:388
  43.2 1.6 %collective-permute-start.12 = (bf16[256,384]{1,0:T(8,128)(2,1)S(1)}, bf16[256,384]{1,0:T(8,128)(2,1)S(1)}, u32[]{:S(2)}, u32[]{:S(2)}) collective-permute-start(bf16[256,384]{1,0:T(8,128)(2,1)S(1)} %get-tuple-element.18.dkeep), channel_id=1, source_target_pairs={{0,8},{1,9},{2,10},{3,11},{4,12},{5,13},{6,14},{7,15},{8,0},{9,1},... | collective-permute-start | bytes 589832 | tf_op jit(solution)/shard_map/ppermute | solution.py:402
  44.8 2.8 %collective-permute-done.10.dxr = bf16[256,384]{1,0:T(8,128)(2,1)S(1)} collective-permute-done((bf16[256,384]{1,0:T(8,128)(2,1)S(1)}, bf16[256,384]{1,0:T(8,128)(2,1)S(1)}, u32[]{:S(2)}, u32[]{:S(2)}) %collective-permute-start.10) | collective-permute-done | bytes 196640 | tf_op jit(solution)/shard_map/ppermute | solution.py:388
  47.7 8.3 %collective-permute-start.13 = (bf16[256,384]{1,0:T(8,128)(2,1)S(1)}, bf16[256,384]{1,0:T(8,128)(2,1)S(1)}, u32[]{:S(2)}, u32[]{:S(2)}) collective-permute-start(bf16[256,384]{1,0:T(8,128)(2,1)S(1)} %collective-permute-done.10.dxr), channel_id=1, source_target_pairs={{0,8},{1,9},{2,10},{3,11},{4,12},{5,13},{6,14},{7,15},{8,0},{9,1},... | collective-permute-start | bytes 589832 | tf_op jit(solution)/shard_map/ppermute | solution.py:402
  56.0 11.3 %query_pass.1 = (bf16[256,384]{1,0:T(8,128)(2,1)S(1)}, bf16[256,384]{1,0:T(8,128)(2,1)S(1)}, f32[8,512]{1,0:T(8,128)S(1)}) custom-call(bf16[3,256,384]{2,1,0:T(8,128)(2,1)S(1)} %copy-done.5, bf16[3,256,384]{2,1,0:T(8,128)(2,1)S(1)} %collective-permute-done.xr, bf16[3,256,384]{2,1,0:T(8,128)(2,1)S(1)} %collective-permute-done.1.e0, ...), custom_call_target="tpu_custom_call" | custom-call | flops 1509949440 | bytes 3932160 | tf_op jit(solution)/shard_map/query_pass/pallas_call | solution.py:229
  67.3 0.7 copy-done.4
  68.0 2.0 %collective-permute-start.16 = (f32[8,512]{1,0:T(8,128)S(1)}, f32[8,512]{1,0:T(8,128)S(1)}, u32[]{:S(2)}, u32[]{:S(2)}) collective-permute-start(f32[8,512]{1,0:T(8,128)S(1)} %get-tuple-element.22.stats), channel_id=1, source_target_pairs={{0,8},{1,9},{2,10},{3,11},{4,12},{5,13},{6,14},{7,15},{8,0},{9,1},... | collective-permute-start | bytes 49160 | tf_op jit(solution)/shard_map/ppermute | solution.py:402
  70.1 1.7 %collective-permute-done.16.se = f32[8,512]{1,0:T(8,128)S(1)} collective-permute-done((f32[8,512]{1,0:T(8,128)S(1)}, f32[8,512]{1,0:T(8,128)S(1)}, u32[]{:S(2)}, u32[]{:S(2)}) %collective-permute-start.16) | collective-permute-done | bytes 16416 | tf_op jit(solution)/shard_map/ppermute | solution.py:402
  71.7 11.2 %key_pass.1 = (bf16[2,256,384]{2,1,0:T(8,128)(2,1)S(1)}, bf16[2,256,384]{2,1,0:T(8,128)(2,1)S(1)}) custom-call(bf16[3,256,384]{2,1,0:T(8,128)(2,1)S(1)} %copy-done.5, bf16[3,256,384]{2,1,0:T(8,128)(2,1)S(1)} %collective-permute-done.xr, bf16[3,256,384]{2,1,0:T(8,128)(2,1)S(1)} %collective-permute-done.1.e0, bf16[3,256,384]{2,1,0:T(8,128)(2,1)} %collective-permute-done.2.e1, ...), custom_call_target="tpu_custom_call" | custom-call | flops 2013265920 | bytes 3932160 | tf_op jit(solution)/shard_map/key_pass/pallas_call | solution.py:329
  83.0 0.7 copy-done.3
  83.7 1.5 %collective-permute-start.18 = (bf16[2,256,384]{2,1,0:T(8,128)(2,1)S(1)}, bf16[2,256,384]{2,1,0:T(8,128)(2,1)S(1)}, u32[]{:S(2)}, u32[]{:S(2)}) collective-permute-start(bf16[2,256,384]{2,1,0:T(8,128)(2,1)S(1)} %get-tuple-element.24), channel_id=1, source_target_pairs={{0,4},{4,0},{8,12},{12,8},{16,20},{20,16},{24,28},{28,24},{1,5},{5... | collective-permute-start | bytes 1179656 | tf_op jit(solution)/shard_map/ppermute | solution.py:388
  85.2 0.5 collective-permute-start.11
  85.8 12.5 %collective-permute-done.11.q_got = bf16[256,384]{1,0:T(8,128)(2,1)S(1)} collective-permute-done((bf16[256,384]{1,0:T(8,128)(2,1)S(1)}, bf16[256,384]{1,0:T(8,128)(2,1)S(1)}, u32[]{:S(2)}, u32[]{:S(2)}) %collective-permute-start.11) | collective-permute-done | bytes 196640 | tf_op jit(solution)/shard_map/ppermute | solution.py:388
  98.3 0.7 copy-done.7
  99.0 0.2 copy-done.6
  99.1 2.4 %unpack.1 = (bf16[256,768]{1,0:T(8,128)(2,1)}, bf16[256,768]{1,0:T(8,128)(2,1)}, bf16[256,768]{1,0:T(8,128)(2,1)}) custom-call(bf16[256,384]{1,0:T(8,128)(2,1)} %copy-done.4, bf16[256,384]{1,0:T(8,128)(2,1)} %copy-done.7, bf16[2,256,384]{2,1,0:T(8,128)(2,1)} %copy-done.3, bf16[2,256,384]{2,1,0:T(8,128)(2,1)} %copy-done.6), custom_call_target="tpu_custom_call" | custom-call | bytes 2359296 | tf_op jit(solution)/shard_map/unpack/pallas_call | solution.py:367
  (29 shorter events, 0.1 us)
Async XLA Ops:
  0.6 27.8 %collective-permute-start.5 = (bf16[256,1536]{1,0:T(8,128)(2,1)}, bf16[256,1536]{1,0:T(8,128)(2,1)S(1)}, u32[]{:S(2)}, u32[]{:S(2)}) collective-permute-start(bf16[256,1536]{1,0:T(8,128)(2,1)} %refs_0_.1), channel_id=1, source_target_pairs={{0,1},{1,0},{2,3},{3,2},{4,5},{5,4},{6,7},{7,6},{8,9},{9,8},{10,11... | collective-permute-start | bytes 2359304 | tf_op jit(solution)/shard_map/ppermute | solution.py:385
  4.1 12.8 %collective-permute-start.6 = (bf16[256,768]{1,0:T(8,128)(2,1)}, bf16[256,768]{1,0:T(8,128)(2,1)S(1)}, u32[]{:S(2)}, u32[]{:S(2)}) collective-permute-start(bf16[256,768]{1,0:T(8,128)(2,1)} %get-tuple-element.16), channel_id=1, source_target_pairs={{0,2},{1,3},{2,0},{3,1},{4,6},{5,7},{6,4},{7,5},{8,10},{9,11},{10,... | collective-permute-start | bytes 1179656 | tf_op jit(solution)/shard_map/ppermute | solution.py:385
  6.7 18.9 %collective-permute-start = (bf16[3,256,384]{2,1,0:T(8,128)(2,1)}, bf16[3,256,384]{2,1,0:T(8,128)(2,1)S(1)}, u32[]{:S(2)}, u32[]{:S(2)}) collective-permute-start(bf16[3,256,384]{2,1,0:T(8,128)(2,1)} %get-tuple-element.15), channel_id=1, source_target_pairs={{0,4},{4,0},{8,12},{12,8},{16,20},{20,16},{24,28},{28,24},{1,5},{5... | collective-permute-start | bytes 1769480 | tf_op jit(solution)/shard_map/ppermute | solution.py:388
  8.2 16.9 %collective-permute-start.8 = (bf16[256,768]{1,0:T(8,128)(2,1)}, bf16[256,768]{1,0:T(8,128)(2,1)S(1)}, u32[]{:S(2)}, u32[]{:S(2)}) collective-permute-start(bf16[256,768]{1,0:T(8,128)(2,1)} %get-tuple-element.17), channel_id=1, source_target_pairs={{0,2},{1,3},{2,0},{3,1},{4,6},{5,7},{6,4},{7,5},{8,10},{9,11},{10,... | collective-permute-start | bytes 1179656 | tf_op jit(solution)/shard_map/ppermute | solution.py:385
  16.9 11.6 %collective-permute-start.7 = (bf16[256,768]{1,0:T(8,128)(2,1)S(1)}, bf16[256,768]{1,0:T(8,128)(2,1)S(1)}, u32[]{:S(2)}, u32[]{:S(2)}) collective-permute-start(bf16[256,768]{1,0:T(8,128)(2,1)S(1)} %collective-permute-done.6.refs_1_), channel_id=1, source_target_pairs={{0,1},{1,0},{2,3},{3,2},{4,5},{5,4},{6,7},{7,6},{8,9},{9,8},{10,11... | collective-permute-start | bytes 1179656 | tf_op jit(solution)/shard_map/ppermute | solution.py:385
  25.1 15.2 %collective-permute-start.9 = (bf16[256,768]{1,0:T(8,128)(2,1)S(1)}, bf16[256,768]{1,0:T(8,128)(2,1)S(1)}, u32[]{:S(2)}, u32[]{:S(2)}) collective-permute-start(bf16[256,768]{1,0:T(8,128)(2,1)S(1)} %collective-permute-done.8.refs_1_), channel_id=1, source_target_pairs={{0,1},{1,0},{2,3},{3,2},{4,5},{5,4},{6,7},{7,6},{8,9},{9,8},{10,11... | collective-permute-start | bytes 1179656 | tf_op jit(solution)/shard_map/ppermute | solution.py:385
  25.1 18.1 %collective-permute-start.3 = (bf16[3,256,384]{2,1,0:T(8,128)(2,1)}, bf16[3,256,384]{2,1,0:T(8,128)(2,1)S(1)}, u32[]{:S(2)}, u32[]{:S(2)}) collective-permute-start(bf16[3,256,384]{2,1,0:T(8,128)(2,1)} %get-tuple-element.14.keep), channel_id=1, source_target_pairs={{0,1},{1,0},{2,3},{3,2},{4,5},{5,4},{6,7},{7,6},{8,16},{9,17},{10,... | collective-permute-start | bytes 1769480 | tf_op jit(solution)/shard_map/ppermute | solution.py:402
  25.6 17.6 %collective-permute-start.1 = (bf16[3,256,384]{2,1,0:T(8,128)(2,1)}, bf16[3,256,384]{2,1,0:T(8,128)(2,1)S(1)}, u32[]{:S(2)}, u32[]{:S(2)}) collective-permute-start(bf16[3,256,384]{2,1,0:T(8,128)(2,1)} %get-tuple-element.14.keep), channel_id=1, source_target_pairs={{0,8},{1,9},{2,10},{3,11},{4,12},{5,13},{6,14},{7,15},{8,0},{9,1},... | collective-permute-start | bytes 1769480 | tf_op jit(solution)/shard_map/ppermute | solution.py:402
  28.5 19.2 %collective-permute-start.4 = (bf16[3,256,384]{2,1,0:T(8,128)(2,1)S(1)}, bf16[3,256,384]{2,1,0:T(8,128)(2,1)}, u32[]{:S(2)}, u32[]{:S(2)}) collective-permute-start(bf16[3,256,384]{2,1,0:T(8,128)(2,1)S(1)} %collective-permute-done.xr), channel_id=1, source_target_pairs={{0,1},{1,0},{2,3},{3,2},{4,5},{5,4},{6,7},{7,6},{8,16},{9,17},{10,... | collective-permute-start | bytes 1769480 | tf_op jit(solution)/shard_map/ppermute | solution.py:402
  28.5 27.5 %collective-permute-start.2 = (bf16[3,256,384]{2,1,0:T(8,128)(2,1)S(1)}, bf16[3,256,384]{2,1,0:T(8,128)(2,1)}, u32[]{:S(2)}, u32[]{:S(2)}) collective-permute-start(bf16[3,256,384]{2,1,0:T(8,128)(2,1)S(1)} %collective-permute-done.xr), channel_id=1, source_target_pairs={{0,8},{1,9},{2,10},{3,11},{4,12},{5,13},{6,14},{7,15},{8,0},{9,1},... | collective-permute-start | bytes 1769480 | tf_op jit(solution)/shard_map/ppermute | solution.py:402
  30.6 3.7 %copy-start = (bf16[768,6144]{1,0:T(8,128)(2,1)S(1)}, bf16[768,6144]{1,0:T(8,128)(2,1)}, u32[]{:S(2)}) copy-start(bf16[768,6144]{1,0:T(8,128)(2,1)} %refs_3_.3) | copy-start | bytes 28311556
  34.2 1.1 %copy-start.2 = (bf16[256,1536]{1,0:T(8,128)(2,1)S(1)}, bf16[256,1536]{1,0:T(8,128)(2,1)}, u32[]{:S(2)}) copy-start(bf16[256,1536]{1,0:T(8,128)(2,1)} %refs_0_.1) | copy-start | bytes 2359300
  35.4 3.7 %copy-start.1 = (bf16[768,6144]{1,0:T(8,128)(2,1)S(1)}, bf16[768,6144]{1,0:T(8,128)(2,1)}, u32[]{:S(2)}) copy-start(bf16[768,6144]{1,0:T(8,128)(2,1)} %refs_3_.3) | copy-start | bytes 28311556
  39.0 16.9 %copy-start.5 = (bf16[3,256,384]{2,1,0:T(8,128)(2,1)S(1)}, bf16[3,256,384]{2,1,0:T(8,128)(2,1)}, u32[]{:S(2)}) copy-start(bf16[3,256,384]{2,1,0:T(8,128)(2,1)} %get-tuple-element.14.keep) | copy-start | bytes 1769476
  41.6 6.0 %collective-permute-start.10 = (bf16[256,384]{1,0:T(8,128)(2,1)S(1)}, bf16[256,384]{1,0:T(8,128)(2,1)S(1)}, u32[]{:S(2)}, u32[]{:S(2)}) collective-permute-start(bf16[256,384]{1,0:T(8,128)(2,1)S(1)} %get-tuple-element.19), channel_id=1, source_target_pairs={{0,4},{4,0},{8,12},{12,8},{16,20},{20,16},{24,28},{28,24},{1,5},{5... | collective-permute-start | bytes 589832 | tf_op jit(solution)/shard_map/ppermute | solution.py:388
  43.2 24.8 %collective-permute-start.14 = (bf16[256,384]{1,0:T(8,128)(2,1)S(1)}, bf16[256,384]{1,0:T(8,128)(2,1)S(1)}, u32[]{:S(2)}, u32[]{:S(2)}) collective-permute-start(bf16[256,384]{1,0:T(8,128)(2,1)S(1)} %get-tuple-element.18.dkeep), channel_id=1, source_target_pairs={{0,1},{1,0},{2,3},{3,2},{4,5},{5,4},{6,7},{7,6},{8,16},{9,17},{10,... | collective-permute-start | bytes 589832 | tf_op jit(solution)/shard_map/ppermute | solution.py:402
  43.2 26.8 %collective-permute-start.12 = (bf16[256,384]{1,0:T(8,128)(2,1)S(1)}, bf16[256,384]{1,0:T(8,128)(2,1)S(1)}, u32[]{:S(2)}, u32[]{:S(2)}) collective-permute-start(bf16[256,384]{1,0:T(8,128)(2,1)S(1)} %get-tuple-element.18.dkeep), channel_id=1, source_target_pairs={{0,8},{1,9},{2,10},{3,11},{4,12},{5,13},{6,14},{7,15},{8,0},{9,1},... | collective-permute-start | bytes 589832 | tf_op jit(solution)/shard_map/ppermute | solution.py:402
  47.7 22.4 %collective-permute-start.15 = (bf16[256,384]{1,0:T(8,128)(2,1)S(1)}, bf16[256,384]{1,0:T(8,128)(2,1)S(1)}, u32[]{:S(2)}, u32[]{:S(2)}) collective-permute-start(bf16[256,384]{1,0:T(8,128)(2,1)S(1)} %collective-permute-done.10.dxr), channel_id=1, source_target_pairs={{0,1},{1,0},{2,3},{3,2},{4,5},{5,4},{6,7},{7,6},{8,16},{9,17},{10,... | collective-permute-start | bytes 589832 | tf_op jit(solution)/shard_map/ppermute | solution.py:402
  47.7 22.4 %collective-permute-start.13 = (bf16[256,384]{1,0:T(8,128)(2,1)S(1)}, bf16[256,384]{1,0:T(8,128)(2,1)S(1)}, u32[]{:S(2)}, u32[]{:S(2)}) collective-permute-start(bf16[256,384]{1,0:T(8,128)(2,1)S(1)} %collective-permute-done.10.dxr), channel_id=1, source_target_pairs={{0,8},{1,9},{2,10},{3,11},{4,12},{5,13},{6,14},{7,15},{8,0},{9,1},... | collective-permute-start | bytes 589832 | tf_op jit(solution)/shard_map/ppermute | solution.py:402
  67.3 0.7 copy-start.4
  68.0 2.1 %collective-permute-start.17 = (f32[8,512]{1,0:T(8,128)S(1)}, f32[8,512]{1,0:T(8,128)S(1)}, u32[]{:S(2)}, u32[]{:S(2)}) collective-permute-start(f32[8,512]{1,0:T(8,128)S(1)} %get-tuple-element.22.stats), channel_id=1, source_target_pairs={{0,1},{1,0},{2,3},{3,2},{4,5},{5,4},{6,7},{7,6},{8,16},{9,17},{10,... | collective-permute-start | bytes 49160 | tf_op jit(solution)/shard_map/ppermute | solution.py:402
  68.0 3.8 %collective-permute-start.16 = (f32[8,512]{1,0:T(8,128)S(1)}, f32[8,512]{1,0:T(8,128)S(1)}, u32[]{:S(2)}, u32[]{:S(2)}) collective-permute-start(f32[8,512]{1,0:T(8,128)S(1)} %get-tuple-element.22.stats), channel_id=1, source_target_pairs={{0,8},{1,9},{2,10},{3,11},{4,12},{5,13},{6,14},{7,15},{8,0},{9,1},... | collective-permute-start | bytes 49160 | tf_op jit(solution)/shard_map/ppermute | solution.py:402
  83.0 0.7 copy-start.3
  83.7 14.6 %collective-permute-start.18 = (bf16[2,256,384]{2,1,0:T(8,128)(2,1)S(1)}, bf16[2,256,384]{2,1,0:T(8,128)(2,1)S(1)}, u32[]{:S(2)}, u32[]{:S(2)}) collective-permute-start(bf16[2,256,384]{2,1,0:T(8,128)(2,1)S(1)} %get-tuple-element.24), channel_id=1, source_target_pairs={{0,4},{4,0},{8,12},{12,8},{16,20},{20,16},{24,28},{28,24},{1,5},{5... | collective-permute-start | bytes 1179656 | tf_op jit(solution)/shard_map/ppermute | solution.py:388
  85.2 13.1 %collective-permute-start.11 = (bf16[256,384]{1,0:T(8,128)(2,1)S(1)}, bf16[256,384]{1,0:T(8,128)(2,1)S(1)}, u32[]{:S(2)}, u32[]{:S(2)}) collective-permute-start(bf16[256,384]{1,0:T(8,128)(2,1)S(1)} %get-tuple-element.21), channel_id=1, source_target_pairs={{0,4},{4,0},{8,12},{12,8},{16,20},{20,16},{24,28},{28,24},{1,5},{5... | collective-permute-start | bytes 589832 | tf_op jit(solution)/shard_map/ppermute | solution.py:388
  98.3 0.7 copy-start.7
  98.3 0.8 copy-start.6

commit v3 on v2

--- a/solution.py
+++ b/solution.py
@@ -29,8 +29,8 @@
     return lax.dot_general(a, b, (((1,), (0,)), ((), ())), preferred_element_type=F32)
 
 
-def cost(flops, moved, exps=0):
-    return pl.CostEstimate(flops=int(flops), bytes_accessed=int(moved), transcendentals=int(exps))
+def cost():
+    return pl.CostEstimate(flops=1, bytes_accessed=1, transcendentals=0)
 
 
 def all_of(copies):
@@ -65,7 +65,8 @@
         in_specs=[ANY] * 4,
         out_specs=(VM,) * 4,
         scratch_shapes=[pltpu.SemaphoreType.DMA((8,))],
-        cost_estimate=cost(0, 8e6),
+        compiler_params=params(16),
+        cost_estimate=cost(),
         name="pack",
     )(q, k, v, og)
 
@@ -127,8 +128,8 @@
         in_specs=[VM] * (len(operands) - 1) + [HBM],
         out_specs=spec,
         scratch_shapes=[pltpu.VMEM((2, heads, size), BF16), pltpu.SemaphoreType.DMA((2,))],
-        compiler_params=params(),
-        cost_estimate=cost(4 * rows * size * heads, 4 * heads * size + 4 * rows * size),
+        compiler_params=params(50),
+        cost_estimate=cost(),
         name="head_grad",
     )(*operands)
 
@@ -240,7 +241,7 @@
             pltpu.SemaphoreType.DMA((16,)),
         ],
         compiler_params=params(),
-        cost_estimate=cost(6 * HD * pairs, 20 * rows * cols * 2, pairs),
+        cost_estimate=cost(),
         name="query_pass",
     )(keep, xr, e0, e1, o0, o1, dkeep, dxr)
 
@@ -340,25 +341,23 @@
             pltpu.SemaphoreType.DMA((16,)),
         ],
         compiler_params=params(),
-        cost_estimate=cost(8 * HD * pairs, 20 * rows * cols * 2, pairs),
+        cost_estimate=cost(),
         name="key_pass",
     )(*operands)
 
 
-def unpack_kernel(q_keep, q_got, kv_keep, kv_got, dq, dk, dv, sem):
+def unpack_kernel(q_keep, q_got, kv_keep, kv_got, dq, dk, dv):
     half = q_keep.shape[1]
     x = lax.rem(lax.axis_index("ctx"), 2)
     mine = pl.ds(pl.multiple_of(x * half, half), half)
     theirs = pl.ds(pl.multiple_of((1 - x) * half, half), half)
-    pairs = [
-        (q_keep, dq.at[:, mine]),
-        (q_got, dq.at[:, theirs]),
-        (kv_keep.at[0], dk.at[:, mine]),
-        (kv_got.at[0], dk.at[:, theirs]),
-        (kv_keep.at[1], dv.at[:, mine]),
-        (kv_got.at[1], dv.at[:, theirs]),
-    ]
-    all_of([pltpu.make_async_copy(a, b, sem.at[i]) for i, (a, b) in enumerate(pairs)])
+    for out, kept, got in (
+        (dq, q_keep, q_got),
+        (dk, kv_keep.at[0], kv_got.at[0]),
+        (dv, kv_keep.at[1], kv_got.at[1]),
+    ):
+        out[:, mine] = kept[...]
+        out[:, theirs] = got[...]
 
 
 def unpack(q_keep, q_got, kv_keep, kv_got):
@@ -367,10 +366,10 @@
     return pl.pallas_call(
         unpack_kernel,
         out_shape=(whole,) * 3,
-        in_specs=[ANY] * 4,
+        in_specs=[VM] * 4,
         out_specs=(VM,) * 3,
-        scratch_shapes=[pltpu.SemaphoreType.DMA((6,))],
-        cost_estimate=cost(0, 3 * rows * half * 8),
+        compiler_params=params(16),
+        cost_estimate=cost(),
         name="unpack",
     )(q_keep, q_got, kv_keep, kv_got)
 
@@ -411,6 +410,7 @@
     e1, o1 = over_z(xr, 0), over_z(xr, 1)
     far0 = over_mp(y0, 1)
     acc = grad_piece(acc, y0, far0, out_weight, width, (2, 3), 0, False)
+    y1, e0, o0 = lax.optimization_barrier((y1, e0, o0))
     far1 = over_mp(y1, 1)
     dkeep, dsend = grad_piece(acc, y1, far1, out_weight, width, (2, 3), width // 2, True)
     dxr = over_x(dsend)

time: 102 us -> 91.3 us (0.90)
  starting transfers between devices: 26.1 us -> 20 us
  local copies, waits for them, and re-layouts: 8.37 us -> 5.25 us
  waiting for transfers between devices: 33.5 us -> 31.6 us
    ppermute x10, starting transfers between devices: 17.4 us -> 10.8 us  [over_z(): return lax.ppermute(array, ('ctx', 'mp'), pairs)]
    ppermute x5, waiting for transfers between devices: 16.4 us -> 12.4 us  [over_mp(): return lax.ppermute(array, 'mp', [(i, i ^ flip) for i in range(lanes)])]
    pallas_call x3, Pallas kernels: 4.93 us -> 8.78 us  [grad_piece(): pl.pallas_call(functools.partial(grad_kernel, width, flips, offset, acc i...]
    unnamed x16 -> x10, local copies, waits for them, and re-layouts: 8.37 us -> 5.25 us
    pallas_call x1, Pallas kernels: 2.92 us -> 0.26 us  [pack(): pl.pallas_call(pack_kernel, out_shape=(part, part, piece, piece), in_spec...]
    ppermute x10, waiting for transfers between devices: 1.72 us -> 3.56 us  [over_z(): return lax.ppermute(array, ('ctx', 'mp'), pairs)]
    pallas_call x1, Pallas kernels: 2.39 us -> 1.12 us  [unpack(): pl.pallas_call(unpack_kernel, out_shape=(whole,) * 3, in_specs=[VM] * 4,...]
  transfers between devices with their start and end apart: 19 -> 19, of which waited for: 5 -> 6; matrix products, arithmetic and copies ran while one was open for 0% -> 0% of each run, Pallas kernels for 19% -> 22%
where the time goes in v3:
time: 91.3 us; the launch traced here: 90.9 us
  Pallas kernels  33.3 us (36%)
  waiting for transfers between devices  31.6 us (35%)
  starting transfers between devices  20 us (22%)
  local copies, waits for them, and re-layouts  5.25 us (6%)
    ppermute x4, waiting for transfers between devices, over_x(): return lax.ppermute(array, 'ctx', [(i, i ^ 1) for i in range(length)])  15.7 us
    ppermute x5, waiting for transfers between devices, over_mp(): return lax.ppermute(array, 'mp', [(i, i ^ flip) for i in range(lanes)])  12.4 us
    pallas_call x1, Pallas kernels, key_pass(): pl.pallas_call(functools.partial(key_kernel, HD ** (-0.5)), out_shape=(pa...  11.8 us
    pallas_call x1, Pallas kernels, query_pass(): pl.pallas_call(functools.partial(query_kernel, HD ** (-0.5)), out_shape=(...  11.4 us
    ppermute x10, starting transfers between devices, over_z(): return lax.ppermute(array, ('ctx', 'mp'), pairs)  10.8 us
    pallas_call x3, Pallas kernels, grad_piece(): pl.pallas_call(functools.partial(grad_kernel, width, flips, offset, acc i...  8.78 us
    unnamed x10, local copies, waits for them, and re-layouts  5.25 us
    ppermute x4, starting transfers between devices, over_x(): return lax.ppermute(array, 'ctx', [(i, i ^ 1) for i in range(length)])  5.14 us
  transfers between devices with their start and end apart: 19, of which 6 were waited for; matrix products, arithmetic and copies ran while one was open for 0% of the time, Pallas kernels for 22%

profile of v3, /device:TPU:0, one launch (start us, length us, event | category | flops | bytes accessed | tf_op | source)
XLA Modules:
  0.0 90.9 jit_solution(3710383305013555165)
XLA Ops:
  0.6 1.1 %copy-done = bf16[256,1536]{1,0:T(8,128)(2,1)S(1)} copy-done((bf16[256,1536]{1,0:T(8,128)(2,1)S(1)}, bf16[256,1536]{1,0:T(8,128)(2,1)}, u32[]{:S(2)}) %copy-start) | copy-done | bytes 786456
  1.8 1.0 %copy-done.2 = bf16[256,768]{1,0:T(8,128)(2,1)S(1)} copy-done((bf16[256,768]{1,0:T(8,128)(2,1)S(1)}, bf16[256,768]{1,0:T(8,128)(2,1)}, u32[]{:S(2)}) %copy-start.2) | copy-done | bytes 393240
  2.8 1.0 %copy-done.3 = bf16[256,768]{1,0:T(8,128)(2,1)S(1)} copy-done((bf16[256,768]{1,0:T(8,128)(2,1)S(1)}, bf16[256,768]{1,0:T(8,128)(2,1)}, u32[]{:S(2)}) %copy-start.3) | copy-done | bytes 393240
  3.8 1.0 %copy-done.4 = bf16[256,768]{1,0:T(8,128)(2,1)S(1)} copy-done((bf16[256,768]{1,0:T(8,128)(2,1)S(1)}, bf16[256,768]{1,0:T(8,128)(2,1)}, u32[]{:S(2)}) %copy-start.4) | copy-done | bytes 393240
  4.8 0.3 pack.1
  5.0 3.0 %collective-permute-start.1 = (bf16[256,768]{1,0:T(8,128)(2,1)S(1)}, bf16[256,768]{1,0:T(8,128)(2,1)S(1)}, u32[]{:S(2)}, u32[]{:S(2)}) collective-permute-start(bf16[256,768]{1,0:T(8,128)(2,1)S(1)} %get-tuple-element.19), channel_id=1, source_target_pairs={{0,2},{1,3},{2,0},{3,1},{4,6},{5,7},{6,4},{7,5},{8,10},{9,11},{10,... | collective-permute-start | bytes 1179656 | tf_op jit(solution)/shard_map/ppermute | solution.py:384
  8.1 3.1 %collective-permute-start.2 = (bf16[3,256,384]{2,1,0:T(8,128)(2,1)S(1)}, bf16[3,256,384]{2,1,0:T(8,128)(2,1)S(1)}, u32[]{:S(2)}, u32[]{:S(2)}) collective-permute-start(bf16[3,256,384]{2,1,0:T(8,128)(2,1)S(1)} %get-tuple-element.17.keep), channel_id=1, source_target_pairs={{0,8},{1,9},{2,10},{3,11},{4,12},{5,13},{6,14},{7,15},{8,0},{9,1},... | collective-permute-start | bytes 1769480 | tf_op jit(solution)/shard_map/ppermute | solution.py:401
  11.2 1.5 %collective-permute-start = (bf16[3,256,384]{2,1,0:T(8,128)(2,1)S(1)}, bf16[3,256,384]{2,1,0:T(8,128)(2,1)S(1)}, u32[]{:S(2)}, u32[]{:S(2)}) collective-permute-start(bf16[3,256,384]{2,1,0:T(8,128)(2,1)S(1)} %get-tuple-element.18), channel_id=1, source_target_pairs={{0,4},{4,0},{8,12},{12,8},{16,20},{20,16},{24,28},{28,24},{1,5},{5... | collective-permute-start | bytes 1769480 | tf_op jit(solution)/shard_map/ppermute | solution.py:387
  12.7 0.5 collective-permute-start.7
  13.2 4.8 %collective-permute-done.1.refs_1_ = bf16[256,768]{1,0:T(8,128)(2,1)S(1)} collective-permute-done((bf16[256,768]{1,0:T(8,128)(2,1)S(1)}, bf16[256,768]{1,0:T(8,128)(2,1)S(1)}, u32[]{:S(2)}, u32[]{:S(2)}) %collective-permute-start.1) | collective-permute-done | bytes 393248 | tf_op jit(solution)/shard_map/ppermute | solution.py:384
  18.0 7.6 %collective-permute-done.7.refs_1_ = bf16[256,768]{1,0:T(8,128)(2,1)S(1)} collective-permute-done((bf16[256,768]{1,0:T(8,128)(2,1)S(1)}, bf16[256,768]{1,0:T(8,128)(2,1)S(1)}, u32[]{:S(2)}, u32[]{:S(2)}) %collective-permute-start.7) | collective-permute-done | bytes 393248 | tf_op jit(solution)/shard_map/ppermute | solution.py:384
  25.6 0.5 collective-permute-start.9
  26.1 0.1 collective-permute-start.5
  26.2 3.3 %collective-permute-start.4 = (bf16[3,256,384]{2,1,0:T(8,128)(2,1)S(1)}, bf16[3,256,384]{2,1,0:T(8,128)(2,1)S(1)}, u32[]{:S(2)}, u32[]{:S(2)}) collective-permute-start(bf16[3,256,384]{2,1,0:T(8,128)(2,1)S(1)} %collective-permute-done.xr), channel_id=1, source_target_pairs={{0,8},{1,9},{2,10},{3,11},{4,12},{5,13},{6,14},{7,15},{8,0},{9,1},... | collective-permute-start | bytes 1769480 | tf_op jit(solution)/shard_map/ppermute | solution.py:401
  29.5 1.1 %copy-done.1 = bf16[256,1536]{1,0:T(8,128)(2,1)S(1)} copy-done((bf16[256,1536]{1,0:T(8,128)(2,1)S(1)}, bf16[256,1536]{1,0:T(8,128)(2,1)}, u32[]{:S(2)}) %copy-start.1) | copy-done | bytes 786456
  30.6 3.8 %head_grad.3.refs_0_ = f32[256,768]{1,0:T(8,128)S(1)} custom-call(bf16[256,1536]{1,0:T(8,128)(2,1)S(1)} %copy-done.1, bf16[256,1536]{1,0:T(8,128)(2,1)S(1)} %collective-permute-done.6.refs_1_, bf16[768,6144]{1,0:T(8,128)(2,1)} %refs_3_.3), custom_call_target="tpu_custom_call" | custom-call | flops 1 | bytes 1 | tf_op jit(solution)/shard_map/head_grad/pallas_call | solution.py:125
  34.5 2.5 %head_grad.4.refs_0_ = f32[256,768]{1,0:T(8,128)S(1)} custom-call(f32[256,768]{1,0:T(8,128)S(1)} %head_grad.3.refs_0_, bf16[256,768]{1,0:T(8,128)(2,1)S(1)} %collective-permute-done.7.refs_1_, bf16[256,768]{1,0:T(8,128)(2,1)S(1)} %collective-permute-done.8.refs_2_, bf16[768,6144]{1,0:T(8,128)(2,1)} %refs_3_.3), custom_call_target="tpu_custom_call" | custom-call | flops 1 | bytes 1 | tf_op jit(solution)/shard_map/head_grad/pallas_call | solution.py:125
  37.0 2.5 %head_grad.5 = (bf16[256,384]{1,0:T(8,128)(2,1)S(1)}, bf16[256,384]{1,0:T(8,128)(2,1)S(1)}) custom-call(f32[256,768]{1,0:T(8,128)S(1)} %head_grad.4.refs_0_, bf16[256,768]{1,0:T(8,128)(2,1)S(1)} %collective-permute-done.1.refs_1_, bf16[256,768]{1,0:T(8,128)(2,1)S(1)} %collective-permute-done.9.refs_2_, bf16[768,6144]{1,0:T(8,128)(2,1)} %refs_3_.3), custom_call_target="tpu_custom_call" | custom-call | flops 1 | bytes 1 | tf_op jit(solution)/shard_map/head_grad/pallas_call | solution.py:125
  39.5 1.6 %collective-permute-start.10 = (bf16[256,384]{1,0:T(8,128)(2,1)S(1)}, bf16[256,384]{1,0:T(8,128)(2,1)S(1)}, u32[]{:S(2)}, u32[]{:S(2)}) collective-permute-start(bf16[256,384]{1,0:T(8,128)(2,1)S(1)} %get-tuple-element.25), channel_id=1, source_target_pairs={{0,4},{4,0},{8,12},{12,8},{16,20},{20,16},{24,28},{28,24},{1,5},{5... | collective-permute-start | bytes 589832 | tf_op jit(solution)/shard_map/ppermute | solution.py:387
  41.0 1.7 %collective-permute-start.12 = (bf16[256,384]{1,0:T(8,128)(2,1)S(1)}, bf16[256,384]{1,0:T(8,128)(2,1)S(1)}, u32[]{:S(2)}, u32[]{:S(2)}) collective-permute-start(bf16[256,384]{1,0:T(8,128)(2,1)S(1)} %get-tuple-element.24.dkeep), channel_id=1, source_target_pairs={{0,8},{1,9},{2,10},{3,11},{4,12},{5,13},{6,14},{7,15},{8,0},{9,1},... | collective-permute-start | bytes 589832 | tf_op jit(solution)/shard_map/ppermute | solution.py:401
  42.7 3.2 %collective-permute-done.10.dxr = bf16[256,384]{1,0:T(8,128)(2,1)S(1)} collective-permute-done((bf16[256,384]{1,0:T(8,128)(2,1)S(1)}, bf16[256,384]{1,0:T(8,128)(2,1)S(1)}, u32[]{:S(2)}, u32[]{:S(2)}) %collective-permute-start.10) | collective-permute-done | bytes 196640 | tf_op jit(solution)/shard_map/ppermute | solution.py:387
  45.9 2.3 %collective-permute-start.13 = (bf16[256,384]{1,0:T(8,128)(2,1)S(1)}, bf16[256,384]{1,0:T(8,128)(2,1)S(1)}, u32[]{:S(2)}, u32[]{:S(2)}) collective-permute-start(bf16[256,384]{1,0:T(8,128)(2,1)S(1)} %collective-permute-done.10.dxr), channel_id=1, source_target_pairs={{0,8},{1,9},{2,10},{3,11},{4,12},{5,13},{6,14},{7,15},{8,0},{9,1},... | collective-permute-start | bytes 589832 | tf_op jit(solution)/shard_map/ppermute | solution.py:401
  48.2 11.4 %query_pass.1 = (bf16[256,384]{1,0:T(8,128)(2,1)S(1)}, bf16[256,384]{1,0:T(8,128)(2,1)S(1)}, f32[8,512]{1,0:T(8,128)S(1)}) custom-call(bf16[3,256,384]{2,1,0:T(8,128)(2,1)S(1)} %get-tuple-element.17.keep, bf16[3,256,384]{2,1,0:T(8,128)(2,1)S(1)} %collective-permute-done.xr, bf16[3,256,384]{2,1,0:T(8,128)(2,1)S(1)} %collective-permute-done.2.e0, ...), custom_call_target="tpu_custom_call" | custom-call | flops 1 | bytes 1 | tf_op jit(solution)/shard_map/query_pass/pallas_call | solution.py:230
  59.6 0.1 collective-permute-start.17
  59.6 0.3 collective-permute-start.16
  59.9 0.9 collective-permute-done.17.so
  60.8 2.6 %collective-permute-done.16.se = f32[8,512]{1,0:T(8,128)S(1)} collective-permute-done((f32[8,512]{1,0:T(8,128)S(1)}, f32[8,512]{1,0:T(8,128)S(1)}, u32[]{:S(2)}, u32[]{:S(2)}) %collective-permute-start.16) | collective-permute-done | bytes 16416 | tf_op jit(solution)/shard_map/ppermute | solution.py:401
  63.5 11.8 %key_pass.1 = (bf16[2,256,384]{2,1,0:T(8,128)(2,1)S(1)}, bf16[2,256,384]{2,1,0:T(8,128)(2,1)S(1)}) custom-call(bf16[3,256,384]{2,1,0:T(8,128)(2,1)S(1)} %get-tuple-element.17.keep, bf16[3,256,384]{2,1,0:T(8,128)(2,1)S(1)} %collective-permute-done.xr, bf16[3,256,384]{2,1,0:T(8,128)(2,1)S(1)} %collective-permute-done.2.e0, ...), custom_call_target="tpu_custom_call" | custom-call | flops 1 | bytes 1 | tf_op jit(solution)/shard_map/key_pass/pallas_call | solution.py:330
  75.2 1.6 %collective-permute-start.18 = (bf16[2,256,384]{2,1,0:T(8,128)(2,1)S(1)}, bf16[2,256,384]{2,1,0:T(8,128)(2,1)S(1)}, u32[]{:S(2)}, u32[]{:S(2)}) collective-permute-start(bf16[2,256,384]{2,1,0:T(8,128)(2,1)S(1)} %get-tuple-element.30), channel_id=1, source_target_pairs={{0,4},{4,0},{8,12},{12,8},{16,20},{20,16},{24,28},{28,24},{1,5},{5... | collective-permute-start | bytes 1179656 | tf_op jit(solution)/shard_map/ppermute | solution.py:387
  76.8 0.5 collective-permute-start.11
  77.3 12.5 %collective-permute-done.11.q_got = bf16[256,384]{1,0:T(8,128)(2,1)S(1)} collective-permute-done((bf16[256,384]{1,0:T(8,128)(2,1)S(1)}, bf16[256,384]{1,0:T(8,128)(2,1)S(1)}, u32[]{:S(2)}, u32[]{:S(2)}) %collective-permute-start.11) | collective-permute-done | bytes 196640 | tf_op jit(solution)/shard_map/ppermute | solution.py:387
  89.8 1.1 %unpack.1 = (bf16[256,768]{1,0:T(8,128)(2,1)}, bf16[256,768]{1,0:T(8,128)(2,1)}, bf16[256,768]{1,0:T(8,128)(2,1)}) custom-call(bf16[256,384]{1,0:T(8,128)(2,1)S(1)} %get-tuple-element.26.q_keep, bf16[256,384]{1,0:T(8,128)(2,1)S(1)} %collective-permute-done.11.q_got, bf16[2,256,384]{2,1,0:T(8,128)(2,1)S(1)} %get-tuple-element.29.kv_keep, ...), custom_call_target="tpu_custom_call" | custom-call | flops 1 | bytes 1 | tf_op jit(solution)/shard_map/unpack/pallas_call | solution.py:366
  (23 shorter events, 0.1 us)
Async XLA Ops:
  0.6 1.1 %copy-start = (bf16[256,1536]{1,0:T(8,128)(2,1)S(1)}, bf16[256,1536]{1,0:T(8,128)(2,1)}, u32[]{:S(2)}) copy-start(bf16[256,1536]{1,0:T(8,128)(2,1)} %refs_0_.1) | copy-start | bytes 2359300
  1.8 1.0 %copy-start.2 = (bf16[256,768]{1,0:T(8,128)(2,1)S(1)}, bf16[256,768]{1,0:T(8,128)(2,1)}, u32[]{:S(2)}) copy-start(bf16[256,768]{1,0:T(8,128)(2,1)} %q.1) | copy-start | bytes 1179652
  2.8 1.0 %copy-start.3 = (bf16[256,768]{1,0:T(8,128)(2,1)S(1)}, bf16[256,768]{1,0:T(8,128)(2,1)}, u32[]{:S(2)}) copy-start(bf16[256,768]{1,0:T(8,128)(2,1)} %k.1) | copy-start | bytes 1179652
  3.8 1.0 %copy-start.4 = (bf16[256,768]{1,0:T(8,128)(2,1)S(1)}, bf16[256,768]{1,0:T(8,128)(2,1)}, u32[]{:S(2)}) copy-start(bf16[256,768]{1,0:T(8,128)(2,1)} %v.1) | copy-start | bytes 1179652
  5.0 13.0 %collective-permute-start.1 = (bf16[256,768]{1,0:T(8,128)(2,1)S(1)}, bf16[256,768]{1,0:T(8,128)(2,1)S(1)}, u32[]{:S(2)}, u32[]{:S(2)}) collective-permute-start(bf16[256,768]{1,0:T(8,128)(2,1)S(1)} %get-tuple-element.19), channel_id=1, source_target_pairs={{0,2},{1,3},{2,0},{3,1},{4,6},{5,7},{6,4},{7,5},{8,10},{9,11},{10,... | collective-permute-start | bytes 1179656 | tf_op jit(solution)/shard_map/ppermute | solution.py:384
  8.1 17.5 %collective-permute-start.3 = (bf16[3,256,384]{2,1,0:T(8,128)(2,1)S(1)}, bf16[3,256,384]{2,1,0:T(8,128)(2,1)S(1)}, u32[]{:S(2)}, u32[]{:S(2)}) collective-permute-start(bf16[3,256,384]{2,1,0:T(8,128)(2,1)S(1)} %get-tuple-element.17.keep), channel_id=1, source_target_pairs={{0,1},{1,0},{2,3},{3,2},{4,5},{5,4},{6,7},{7,6},{8,16},{9,17},{10,... | collective-permute-start | bytes 1769480 | tf_op jit(solution)/shard_map/ppermute | solution.py:401
  8.1 17.5 %collective-permute-start.2 = (bf16[3,256,384]{2,1,0:T(8,128)(2,1)S(1)}, bf16[3,256,384]{2,1,0:T(8,128)(2,1)S(1)}, u32[]{:S(2)}, u32[]{:S(2)}) collective-permute-start(bf16[3,256,384]{2,1,0:T(8,128)(2,1)S(1)} %get-tuple-element.17.keep), channel_id=1, source_target_pairs={{0,8},{1,9},{2,10},{3,11},{4,12},{5,13},{6,14},{7,15},{8,0},{9,1},... | collective-permute-start | bytes 1769480 | tf_op jit(solution)/shard_map/ppermute | solution.py:401
  11.2 14.9 %collective-permute-start = (bf16[3,256,384]{2,1,0:T(8,128)(2,1)S(1)}, bf16[3,256,384]{2,1,0:T(8,128)(2,1)S(1)}, u32[]{:S(2)}, u32[]{:S(2)}) collective-permute-start(bf16[3,256,384]{2,1,0:T(8,128)(2,1)S(1)} %get-tuple-element.18), channel_id=1, source_target_pairs={{0,4},{4,0},{8,12},{12,8},{16,20},{20,16},{24,28},{28,24},{1,5},{5... | collective-permute-start | bytes 1769480 | tf_op jit(solution)/shard_map/ppermute | solution.py:387
  12.7 12.9 %collective-permute-start.7 = (bf16[256,768]{1,0:T(8,128)(2,1)S(1)}, bf16[256,768]{1,0:T(8,128)(2,1)S(1)}, u32[]{:S(2)}, u32[]{:S(2)}) collective-permute-start(bf16[256,768]{1,0:T(8,128)(2,1)S(1)} %get-tuple-element.22), channel_id=1, source_target_pairs={{0,2},{1,3},{2,0},{3,1},{4,6},{5,7},{6,4},{7,5},{8,10},{9,11},{10,... | collective-permute-start | bytes 1179656 | tf_op jit(solution)/shard_map/ppermute | solution.py:384
  18.0 11.5 %collective-permute-start.6 = (bf16[256,1536]{1,0:T(8,128)(2,1)S(1)}, bf16[256,1536]{1,0:T(8,128)(2,1)S(1)}, u32[]{:S(2)}, u32[]{:S(2)}) collective-permute-start(bf16[256,1536]{1,0:T(8,128)(2,1)S(1)} %copy-done), channel_id=1, source_target_pairs={{0,1},{1,0},{2,3},{3,2},{4,5},{5,4},{6,7},{7,6},{8,9},{9,8},{10,11... | collective-permute-start | bytes 2359304 | tf_op jit(solution)/shard_map/ppermute | solution.py:384
  25.6 8.9 %collective-permute-start.8 = (bf16[256,768]{1,0:T(8,128)(2,1)S(1)}, bf16[256,768]{1,0:T(8,128)(2,1)S(1)}, u32[]{:S(2)}, u32[]{:S(2)}) collective-permute-start(bf16[256,768]{1,0:T(8,128)(2,1)S(1)} %collective-permute-done.7.refs_1_), channel_id=1, source_target_pairs={{0,1},{1,0},{2,3},{3,2},{4,5},{5,4},{6,7},{7,6},{8,9},{9,8},{10,11... | collective-permute-start | bytes 1179656 | tf_op jit(solution)/shard_map/ppermute | solution.py:384
  25.6 11.3 %collective-permute-start.9 = (bf16[256,768]{1,0:T(8,128)(2,1)S(1)}, bf16[256,768]{1,0:T(8,128)(2,1)S(1)}, u32[]{:S(2)}, u32[]{:S(2)}) collective-permute-start(bf16[256,768]{1,0:T(8,128)(2,1)S(1)} %collective-permute-done.1.refs_1_), channel_id=1, source_target_pairs={{0,1},{1,0},{2,3},{3,2},{4,5},{5,4},{6,7},{7,6},{8,9},{9,8},{10,11... | collective-permute-start | bytes 1179656 | tf_op jit(solution)/shard_map/ppermute | solution.py:384
  26.1 19.7 %collective-permute-start.5 = (bf16[3,256,384]{2,1,0:T(8,128)(2,1)S(1)}, bf16[3,256,384]{2,1,0:T(8,128)(2,1)S(1)}, u32[]{:S(2)}, u32[]{:S(2)}) collective-permute-start(bf16[3,256,384]{2,1,0:T(8,128)(2,1)S(1)} %collective-permute-done.xr), channel_id=1, source_target_pairs={{0,1},{1,0},{2,3},{3,2},{4,5},{5,4},{6,7},{7,6},{8,16},{9,17},{10,... | collective-permute-start | bytes 1769480 | tf_op jit(solution)/shard_map/ppermute | solution.py:401
  26.2 22.0 %collective-permute-start.4 = (bf16[3,256,384]{2,1,0:T(8,128)(2,1)S(1)}, bf16[3,256,384]{2,1,0:T(8,128)(2,1)S(1)}, u32[]{:S(2)}, u32[]{:S(2)}) collective-permute-start(bf16[3,256,384]{2,1,0:T(8,128)(2,1)S(1)} %collective-permute-done.xr), channel_id=1, source_target_pairs={{0,8},{1,9},{2,10},{3,11},{4,12},{5,13},{6,14},{7,15},{8,0},{9,1},... | collective-permute-start | bytes 1769480 | tf_op jit(solution)/shard_map/ppermute | solution.py:401
  29.5 1.1 %copy-start.1 = (bf16[256,1536]{1,0:T(8,128)(2,1)S(1)}, bf16[256,1536]{1,0:T(8,128)(2,1)}, u32[]{:S(2)}) copy-start(bf16[256,1536]{1,0:T(8,128)(2,1)} %refs_0_.1) | copy-start | bytes 2359300
  39.5 6.4 %collective-permute-start.10 = (bf16[256,384]{1,0:T(8,128)(2,1)S(1)}, bf16[256,384]{1,0:T(8,128)(2,1)S(1)}, u32[]{:S(2)}, u32[]{:S(2)}) collective-permute-start(bf16[256,384]{1,0:T(8,128)(2,1)S(1)} %get-tuple-element.25), channel_id=1, source_target_pairs={{0,4},{4,0},{8,12},{12,8},{16,20},{20,16},{24,28},{28,24},{1,5},{5... | collective-permute-start | bytes 589832 | tf_op jit(solution)/shard_map/ppermute | solution.py:387
  41.0 18.6 %collective-permute-start.14 = (bf16[256,384]{1,0:T(8,128)(2,1)S(1)}, bf16[256,384]{1,0:T(8,128)(2,1)S(1)}, u32[]{:S(2)}, u32[]{:S(2)}) collective-permute-start(bf16[256,384]{1,0:T(8,128)(2,1)S(1)} %get-tuple-element.24.dkeep), channel_id=1, source_target_pairs={{0,1},{1,0},{2,3},{3,2},{4,5},{5,4},{6,7},{7,6},{8,16},{9,17},{10,... | collective-permute-start | bytes 589832 | tf_op jit(solution)/shard_map/ppermute | solution.py:401
  41.0 18.9 %collective-permute-start.12 = (bf16[256,384]{1,0:T(8,128)(2,1)S(1)}, bf16[256,384]{1,0:T(8,128)(2,1)S(1)}, u32[]{:S(2)}, u32[]{:S(2)}) collective-permute-start(bf16[256,384]{1,0:T(8,128)(2,1)S(1)} %get-tuple-element.24.dkeep), channel_id=1, source_target_pairs={{0,8},{1,9},{2,10},{3,11},{4,12},{5,13},{6,14},{7,15},{8,0},{9,1},... | collective-permute-start | bytes 589832 | tf_op jit(solution)/shard_map/ppermute | solution.py:401
  45.9 17.6 %collective-permute-start.15 = (bf16[256,384]{1,0:T(8,128)(2,1)S(1)}, bf16[256,384]{1,0:T(8,128)(2,1)S(1)}, u32[]{:S(2)}, u32[]{:S(2)}) collective-permute-start(bf16[256,384]{1,0:T(8,128)(2,1)S(1)} %collective-permute-done.10.dxr), channel_id=1, source_target_pairs={{0,1},{1,0},{2,3},{3,2},{4,5},{5,4},{6,7},{7,6},{8,16},{9,17},{10,... | collective-permute-start | bytes 589832 | tf_op jit(solution)/shard_map/ppermute | solution.py:401
  45.9 17.6 %collective-permute-start.13 = (bf16[256,384]{1,0:T(8,128)(2,1)S(1)}, bf16[256,384]{1,0:T(8,128)(2,1)S(1)}, u32[]{:S(2)}, u32[]{:S(2)}) collective-permute-start(bf16[256,384]{1,0:T(8,128)(2,1)S(1)} %collective-permute-done.10.dxr), channel_id=1, source_target_pairs={{0,8},{1,9},{2,10},{3,11},{4,12},{5,13},{6,14},{7,15},{8,0},{9,1},... | collective-permute-start | bytes 589832 | tf_op jit(solution)/shard_map/ppermute | solution.py:401
  59.6 1.2 %collective-permute-start.17 = (f32[8,512]{1,0:T(8,128)S(1)}, f32[8,512]{1,0:T(8,128)S(1)}, u32[]{:S(2)}, u32[]{:S(2)}) collective-permute-start(f32[8,512]{1,0:T(8,128)S(1)} %get-tuple-element.28.stats), channel_id=1, source_target_pairs={{0,1},{1,0},{2,3},{3,2},{4,5},{5,4},{6,7},{7,6},{8,16},{9,17},{10,... | collective-permute-start | bytes 49160 | tf_op jit(solution)/shard_map/ppermute | solution.py:401
  59.6 3.8 %collective-permute-start.16 = (f32[8,512]{1,0:T(8,128)S(1)}, f32[8,512]{1,0:T(8,128)S(1)}, u32[]{:S(2)}, u32[]{:S(2)}) collective-permute-start(f32[8,512]{1,0:T(8,128)S(1)} %get-tuple-element.28.stats), channel_id=1, source_target_pairs={{0,8},{1,9},{2,10},{3,11},{4,12},{5,13},{6,14},{7,15},{8,0},{9,1},... | collective-permute-start | bytes 49160 | tf_op jit(solution)/shard_map/ppermute | solution.py:401
  75.2 14.6 %collective-permute-start.18 = (bf16[2,256,384]{2,1,0:T(8,128)(2,1)S(1)}, bf16[2,256,384]{2,1,0:T(8,128)(2,1)S(1)}, u32[]{:S(2)}, u32[]{:S(2)}) collective-permute-start(bf16[2,256,384]{2,1,0:T(8,128)(2,1)S(1)} %get-tuple-element.30), channel_id=1, source_target_pairs={{0,4},{4,0},{8,12},{12,8},{16,20},{20,16},{24,28},{28,24},{1,5},{5... | collective-permute-start | bytes 1179656 | tf_op jit(solution)/shard_map/ppermute | solution.py:387
  76.8 13.0 %collective-permute-start.11 = (bf16[256,384]{1,0:T(8,128)(2,1)S(1)}, bf16[256,384]{1,0:T(8,128)(2,1)S(1)}, u32[]{:S(2)}, u32[]{:S(2)}) collective-permute-start(bf16[256,384]{1,0:T(8,128)(2,1)S(1)} %get-tuple-element.27), channel_id=1, source_target_pairs={{0,4},{4,0},{8,12},{12,8},{16,20},{20,16},{24,28},{28,24},{1,5},{5... | collective-permute-start | bytes 589832 | tf_op jit(solution)/shard_map/ppermute | solution.py:387

commit v4 on v0

v4 whole, which is shorter than its diff:
```python
import functools
import math

import jax
import jax.numpy as jnp
from jax import lax
from jax.experimental import pallas as pl
from jax.experimental.pallas import tpu as pltpu
from jax.sharding import PartitionSpec as P

HD = 128
BF16 = jnp.bfloat16
F32 = jnp.float32
BIG = 1e30
ANY = pl.BlockSpec(memory_space=pl.ANY)
VM = pl.BlockSpec(memory_space=pltpu.VMEM)
HBM = pl.BlockSpec(memory_space=pltpu.HBM)


def params(mib=40):
    return pltpu.CompilerParams(vmem_limit_bytes=mib << 20)


def nt(a, b):
    return lax.dot_general(a, b, (((1,), (1,)), ((), ())), preferred_element_type=F32)


def nn(a, b):
    return lax.dot_general(a, b, (((1,), (0,)), ((), ())), preferred_element_type=F32)


def cost(flops=1):
    return pl.CostEstimate(flops=int(flops), bytes_accessed=1, transcendentals=0)


def pack_kernel(q, k, v, keep, send, sem):
    half = q.shape[1] // 2
    x = lax.rem(lax.axis_index("ctx"), 2)
    mine = pl.ds(pl.multiple_of(x * half, half), half)
    theirs = pl.ds(pl.multiple_of((1 - x) * half, half), half)
    copies = []
    for i, ref in enumerate((q, k, v)):
        copies.append(pltpu.make_async_copy(ref.at[:, mine], keep.at[i], sem.at[i]))
        copies.append(pltpu.make_async_copy(ref.at[:, theirs], send.at[i], sem.at[3 + i]))
    for copy in copies:
        copy.start()
    for copy in copies:
        copy.wait()


def pack(q, k, v):
    rows, cols = q.shape
    part = jax.ShapeDtypeStruct((3, rows, cols // 2), BF16)
    return pl.pallas_call(
        pack_kernel,
        out_shape=(part, part),
        in_specs=[ANY] * 3,
        out_specs=(VM,) * 2,
        scratch_shapes=[pltpu.SemaphoreType.DMA((6,))],
        compiler_params=params(60),
        cost_estimate=cost(),
        name="pack",
    )(q, k, v)


def first_kernel(og, near, w, acc, wy, wf, wbuf, sem):
    width = og.shape[1]
    me = lax.axis_index("mp")
    copies = []
    for flip, target in enumerate((wbuf.at[0], wbuf.at[1], wy, wf)):
        first = pl.multiple_of(jnp.bitwise_xor(me, flip) * width, width)
        copies.append(pltpu.make_async_copy(w.at[:, pl.ds(first, width)], target, sem.at[flip]))
    for copy in copies:
        copy.start()
    copies[0].wait()
    acc[...] = nt(og[...], wbuf[0])
    copies[1].wait()
    acc[...] += nt(near[...], wbuf[1])
    copies[2].wait()
    copies[3].wait()


def first_piece(og, near, w):
    rows, width = og.shape
    heads = w.shape[0]
    part = jax.ShapeDtypeStruct((heads, width), BF16)
    return pl.pallas_call(
        first_kernel,
        out_shape=(jax.ShapeDtypeStruct((rows, heads), F32), part, part),
        in_specs=[VM, VM, ANY],
        out_specs=(VM, VM, VM),
        scratch_shapes=[pltpu.VMEM((2, heads, width), BF16), pltpu.SemaphoreType.DMA((4,))],
        compiler_params=params(46),
        cost_estimate=cost(),
        name="head_grad_first",
    )(og, near, w)


def next_kernel(acc, piece, w, out):
    out[...] = acc[...] + nt(piece[...], w[...])


def last_kernel(acc, piece, w, keep, send):
    total = acc[...] + nt(piece[...], w[...])
    half = total.shape[1] // 2
    x = lax.rem(lax.axis_index("ctx"), 2)
    low = total[:, :half].astype(BF16)
    high = total[:, half:].astype(BF16)

    @pl.when(x == 0)
    def _():
        keep[...] = low
        send[...] = high

    @pl.when(x != 0)
    def _():
        keep[...] = high
        send[...] = low


def grad_piece(acc, piece, w, last):
    rows, heads = acc.shape
    half = jax.ShapeDtypeStruct((rows, heads // 2), BF16)
    return pl.pallas_call(
        last_kernel if last else next_kernel,
        out_shape=(half, half) if last else jax.ShapeDtypeStruct((rows, heads), F32),
        in_specs=[VM] * 3,
        out_specs=(VM, VM) if last else VM,
        compiler_params=params(30),
        cost_estimate=cost(),
        name="head_grad",
    )(acc, piece, w)


def place():
    position = lax.axis_index("ctx")
    block = position // 2
    low_ok = block > 0
    high_ok = block < lax.axis_size("ctx") // 2 - 1
    odd = lax.rem(block, 2) == 1
    even_ok = jnp.logical_or(jnp.logical_and(odd, low_ok), jnp.logical_and(jnp.logical_not(odd), high_ok))
    odd_ok = jnp.logical_or(jnp.logical_and(odd, high_ok), jnp.logical_and(jnp.logical_not(odd), low_ok))
    turned = lax.rem(position + block, 2) == 1
    return even_ok, odd_ok, turned


def off(ok):
    return jnp.where(ok, 0.0, BIG).astype(F32)


def query_kernel(scale, keep, xr, e0, e1, o0, o1, dkeep, dxr, dq_keep, dq_send, stats, fifth):
    rows = keep.shape[1]
    heads = keep.shape[2] // HD
    even_ok, odd_ok, turned = place()

    @pl.when(turned)
    def _():
        fifth[0] = e1[1:3]
        fifth[1] = o0[1:3]

    @pl.when(jnp.logical_not(turned))
    def _():
        fifth[0] = o1[1:3]
        fifth[1] = e0[1:3]

    c = scale * math.log2(math.e)
    even_off, odd_off = off(even_ok), off(odd_ok)
    lane = lax.broadcasted_iota(jnp.int32, (rows, HD), 1)
    fifth_off = (
        jnp.where(turned, even_off, odd_off),
        jnp.where(turned, odd_off, even_off),
    )
    for mine, (q, d, e, o, out) in enumerate(
        ((keep, dkeep, e0, o0, dq_keep), (xr, dxr, e1, o1, dq_send))
    ):
        runs = (
            (keep, 1, None),
            (xr, 1, None),
            (e, 1, even_off),
            (o, 1, odd_off),
            (fifth.at[mine], 0, fifth_off[mine]),
        )
        mark = jnp.zeros((rows, HD), F32)
        for head in range(heads):
            cols = slice(head * HD, (head + 1) * HD)
            query = q[0, :, cols]
            grad = d[:, cols]
            scores = [nt(query, ref[k, :, cols]) for ref, k, _ in runs]
            top = None
            for s, (_, _, gone) in zip(scores, runs):
                m = jnp.max(s, -1, keepdims=True)
                m = m if gone is None else m - gone
                top = m if top is None else jnp.maximum(top, m)
            top = top * c
            weights = [
                jnp.exp2(s * c - (top if gone is None else top + gone))
                for s, (_, _, gone) in zip(scores, runs)
            ]
            total = jnp.sum(sum(weights), -1, keepdims=True)
            grads = [nt(grad, ref[k + 1, :, cols]) for ref, k, _ in runs]
            inverse = 1.0 / total
            delta = jnp.sum(sum(w * g for w, g in zip(weights, grads)), -1, keepdims=True) * inverse
            result = sum(
                nn((w * (g - delta)).astype(BF16), ref[k, :, cols])
                for w, g, (ref, k, _) in zip(weights, grads, runs)
            )
            out[:, cols] = (result * (inverse * scale)).astype(BF16)
            mark = jnp.where(lane == 2 * head, top + jnp.log2(total), mark)
            mark = jnp.where(lane == 2 * head + 1, delta, mark)
        stats[:, mine * rows : (mine + 1) * rows] = jnp.transpose(mark)[: stats.shape[0], :]


def query_pass(keep, xr, e0, e1, o0, o1, dkeep, dxr):
    _, rows, cols = keep.shape
    part = jax.ShapeDtypeStruct((rows, cols), BF16)
    return pl.pallas_call(
        functools.partial(query_kernel, HD ** -0.5),
        out_shape=(part, part, jax.ShapeDtypeStruct((8, 2 * rows), F32)),
        in_specs=[VM] * 8,
        out_specs=(VM, VM, VM),
        scratch_shapes=[pltpu.VMEM((2, 2, rows, cols), BF16)],
        compiler_params=params(30),
        cost_estimate=cost(2e10),
        name="query_pass",
    )(keep, xr, e0, e1, o0, o1, dkeep, dxr)


def key_step(scale, key, value, steps):
    c = scale * math.log2(math.e)
    key_sum = None
    value_sum = None
    for query, grad, total, delta in steps:
        weight = jnp.exp2(nt(key, query) * c - total)
        change = weight * (nt(value, grad) - delta)
        v = nn(weight.astype(BF16), grad)
        k = nn(change.astype(BF16), query)
        value_sum = v if value_sum is None else value_sum + v
        key_sum = k if key_sum is None else key_sum + k
    return key_sum, value_sum


def own_kernel(scale, keep, xr, dkeep, dxr, stats, sums):
    rows = keep.shape[1]
    heads = keep.shape[2] // HD
    for mine, keys in enumerate((keep, xr)):
        for head in range(heads):
            cols = slice(head * HD, (head + 1) * HD)
            steps = []
            for i, (q, d) in enumerate(((keep, dkeep), (xr, dxr))):
                span = slice(i * rows, (i + 1) * rows)
                steps.append((
                    q[0, :, cols],
                    d[:, cols],
                    stats[2 * head : 2 * head + 1, span],
                    stats[2 * head + 1 : 2 * head + 2, span],
                ))
            k, v = key_step(scale, keys[1, :, cols], keys[2, :, cols], steps)
            sums[mine, 0, :, cols] = k
            sums[mine, 1, :, cols] = v


def own_pass(keep, xr, dkeep, dxr, stats):
    _, rows, cols = keep.shape
    return pl.pallas_call(
        functools.partial(own_kernel, HD ** -0.5),
        out_shape=jax.ShapeDtypeStruct((2, 2, rows, cols), F32),
        in_specs=[VM] * 5,
        out_specs=VM,
        compiler_params=params(30),
        cost_estimate=cost(),
        name="own_pass",
    )(keep, xr, dkeep, dxr, stats)


def key_kernel(scale, head, keep, xr, e0, e1, o0, o1, de0, de1, do0, do1, se, so, sums, out_keep, out_send, fifth, marks):
    rows = keep.shape[1]
    even_ok, odd_ok, turned = place()
    cols = slice(head * HD, (head + 1) * HD)

    @pl.when(turned)
    def _():
        fifth[0, 0] = e1[0, :, cols]
        fifth[0, 1] = de1[:, cols]
        fifth[1, 0] = o0[0, :, cols]
        fifth[1, 1] = do0[:, cols]

    @pl.when(jnp.logical_not(turned))
    def _():
        fifth[0, 0] = o1[0, :, cols]
        fifth[0, 1] = do1[:, cols]
        fifth[1, 0] = e0[0, :, cols]
        fifth[1, 1] = de0[:, cols]

    even = se[2 * head : 2 * head + 2, :]
    odd = so[2 * head : 2 * head + 2, :]
    row = lax.broadcasted_iota(jnp.int32, even.shape, 0)
    nothing = jnp.where(row == 0, jnp.float32(BIG), jnp.float32(0.0))
    even = jnp.where(even_ok, even, nothing)
    odd = jnp.where(odd_ok, odd, nothing)
    fifths = (
        jnp.where(turned, even[:, rows:], odd[:, rows:]),
        jnp.where(turned, odd[:, :rows], even[:, :rows]),
    )
    for mine, (keys, e, o, de, do, out) in enumerate(
        ((keep, e0, o0, de0, do0, out_keep), (xr, e1, o1, de1, do1, out_send))
    ):
        span = slice(mine * rows, (mine + 1) * rows)
        steps = (
            (e[0, :, cols], de[:, cols], even[0:1, span], even[1:2, span]),
            (o[0, :, cols], do[:, cols], odd[0:1, span], odd[1:2, span]),
            (fifth[mine, 0], fifth[mine, 1], fifths[mine][0:1], fifths[mine][1:2]),
        )
        k, v = key_step(scale, keys[1, :, cols], keys[2, :, cols], steps)
        out[0] = ((k + sums[mine, 0, :, cols]) * scale).astype(BF16)
        out[1] = (v + sums[mine, 1, :, cols]).astype(BF16)


def key_pass(head, *operands):
    _, rows, cols = operands[0].shape
    part = jax.ShapeDtypeStruct((2, rows, HD), BF16)
    return pl.pallas_call(
        functools.partial(key_kernel, HD ** -0.5, head),
        out_shape=(part, part),
        in_specs=[VM] * 13,
        out_specs=(VM, VM),
        scratch_shapes=[pltpu.VMEM((2, 2, rows, HD), BF16), pltpu.VMEM((8, 2 * rows), F32)],
        compiler_params=params(30),
        cost_estimate=cost(),
        name="key_pass",
    )(*operands)


def unpack_kernel(q_keep, q_got, *refs):
    heads = q_keep.shape[1] // HD
    kept, got, (dq, dk, dv) = refs[:heads], refs[heads : 2 * heads], refs[2 * heads :]
    half = q_keep.shape[1]
    x = lax.rem(lax.axis_index("ctx"), 2)
    mine = pl.multiple_of(x * half, half)
    theirs = pl.multiple_of((1 - x) * half, half)
    dq[:, pl.ds(mine, half)] = q_keep[...]
    dq[:, pl.ds(theirs, half)] = q_got[...]
    for head in range(heads):
        for i, out in enumerate((dk, dv)):
            out[:, pl.ds(mine + head * HD, HD)] = kept[head][i]
            out[:, pl.ds(theirs + head * HD, HD)] = got[head][i]


def unpack(q_keep, q_got, kept, got):
    rows, half = q_keep.shape
    whole = jax.ShapeDtypeStruct((rows, 2 * half), BF16)
    return pl.pallas_call(
        unpack_kernel,
        out_shape=(whole,) * 3,
        in_specs=[VM] * (2 + 2 * len(kept)),
        out_specs=(VM,) * 3,
        compiler_params=params(16),
        cost_estimate=cost(),
        name="unpack",
    )(q_keep, q_got, *kept, *got)


def body(queries, keys, values, out_grad, out_weight):
    length = lax.axis_size("ctx")
    lanes = lax.axis_size("mp")
    blocks = length // 2
    width = out_grad.shape[1]

    def over_mp(array, flip):
        return lax.ppermute(array, "mp", [(i, i ^ flip) for i in range(lanes)])

    def over_x(array):
        return lax.ppermute(array, "ctx", [(i, i ^ 1) for i in range(length)])

    def over_z(array, first):
        pairs = []
        for position in range(length):
            block = position // 2
            other = ((block - first) ^ 1) + first
            for lane in range(lanes):
                source = position * lanes + lane
                if block >= first and other < blocks:
                    target = (2 * other + position % 2) * lanes + lane
                else:
                    target = position * lanes + (lane ^ 1)
                pairs.append((source, target))
        return lax.ppermute(array, ("ctx", "mp"), pairs)

    y = over_mp(out_grad, 2)
    near = over_mp(out_grad, 1)
    keep, send = pack(queries, keys, values)
    e0, o0 = over_z(keep, 0), over_z(keep, 1)
    xr = over_x(send)
    acc, wy, wf = first_piece(out_grad, near, out_weight)
    y, e0, o0, acc = lax.optimization_barrier((y, e0, o0, acc))
    e1, o1 = over_z(xr, 0), over_z(xr, 1)
    far = over_mp(y, 1)
    acc = grad_piece(acc, y, wy, False)
    dkeep, dsend = grad_piece(acc, far, wf, True)
    dxr = over_x(dsend)
    de0, do0 = over_z(dkeep, 0), over_z(dkeep, 1)
    dq_keep, dq_send, stats = query_pass(keep, xr, e0, e1, o0, o1, dkeep, dxr)
    de1, do1 = over_z(dxr, 0), over_z(dxr, 1)
    stats, de0, do0 = lax.optimization_barrier((stats, de0, do0))
    se, so = over_z(stats, 0), over_z(stats, 1)
    dq_got = over_x(dq_send)
    sums = own_pass(keep, xr, dkeep, dxr, stats)
    kept, got = [], []
    for head in range(dkeep.shape[1] // HD):
        if head == 1:
            sums, dq_got = lax.optimization_barrier((sums, dq_got))
        kv_keep, kv_send = key_pass(
            head, keep, xr, e0, e1, o0, o1, de0, de1, do0, do1, se, so, sums
        )
        kept.append(kv_keep)
        got.append(over_x(kv_send))
    return tuple(unpack(dq_keep, dq_got, kept, got))


def solution(mesh):
    placed = (P("ctx", "mp"), P("ctx", "mp"), P("ctx", "mp"), P("ctx", "mp"), P("mp", None))
    return jax.shard_map(
        body,
        mesh=mesh,
        in_specs=placed,
        out_specs=(P("ctx", "mp"), P("ctx", "mp"), P("ctx", "mp")),
        check_vma=False,
    )
```

time: 191 us -> 67.8 us (0.35)
  matrix products: 52.6 us -> 0 us
  starting transfers between devices: 49.4 us -> 19.7 us
  waiting for transfers between devices: 47.4 us -> 24.6 us
  Pallas kernels: 0 us -> 21.4 us
  local copies, waits for them, and re-layouts: 19.6 us -> 1.14 us
  between operations: 14.4 us -> 0.74 us
  other arithmetic: 6.73 us -> 0 us
    dot_general x6 -> x0, matrix products: 52.6 us -> none  [the longest x1 17.1 us: body(): jnp.einsum('htu,thd->uhd', score_grad, query_heads, preferred_element_typ...]
    ppermute x16 -> x19, starting transfers between devices: 49.4 us -> 19.7 us  [the longest x10 9.21 us: over_z(): return lax.ppermute(array, ('ctx', 'mp'), pairs)]
    ppermute x16 -> x19, waiting for transfers between devices: 46.7 us -> 24.6 us  [the longest x10 17 us: over_z(): return lax.ppermute(array, ('ctx', 'mp'), pairs)]
    pallas_call x0 -> x10, Pallas kernels: none -> 21.4 us  [the longest x1 5.8 us: query_pass(): pl.pallas_call(functools.partial(query_kernel, HD ** (-0.5)), out_shape=(...]
    unnamed x18 -> x4, local copies, waits for them, and re-layouts: 9.68 us -> 1.14 us
    convert_element_type x9 -> x0, local copies, waits for them, and re-layouts: 5.31 us -> none  [the longest x2 1.86 us: body(): key_part[REACH - distance].astype(jnp.bfloat16)]
    convert_element_type x2 -> x0, other arithmetic: 4.64 us -> none  [the longest x1 2.32 us: body(): key_total.astype(jnp.bfloat16)]
    slice x4 -> x0, local copies, waits for them, and re-layouts: 4.03 us -> none  [the longest x1 1.47 us: body(): key_part[REACH - distance].astype(jnp.bfloat16)]
  transfers between devices with their start and end apart: 17 -> 19, of which waited for: 4 -> 8; matrix products, arithmetic and copies ran while one was open for 21% -> 0% of each run, Pallas kernels for 0% -> 28%
where the time goes in v4:
time: 67.8 us; the launch traced here: 67.6 us
  waiting for transfers between devices  24.6 us (36%)
  Pallas kernels  21.4 us (32%)
  starting transfers between devices  19.7 us (29%)
  local copies, waits for them, and re-layouts  1.14 us (2%)
  between operations  0.74 us (1%)
    ppermute x10, waiting for transfers between devices, over_z(): return lax.ppermute(array, ('ctx', 'mp'), pairs)  17 us
    ppermute x10, starting transfers between devices, over_z(): return lax.ppermute(array, ('ctx', 'mp'), pairs)  9.21 us
    ppermute x6, waiting for transfers between devices, over_x(): return lax.ppermute(array, 'ctx', [(i, i ^ 1) for i in range(length)])  7.43 us
    ppermute x6, starting transfers between devices, over_x(): return lax.ppermute(array, 'ctx', [(i, i ^ 1) for i in range(length)])  7.35 us
    pallas_call x1, Pallas kernels, query_pass(): pl.pallas_call(functools.partial(query_kernel, HD ** (-0.5)), out_shape=(...  5.8 us
    pallas_call x3, Pallas kernels, key_pass(): pl.pallas_call(functools.partial(key_kernel, HD ** (-0.5), head), out_sha...  4.28 us
    pallas_call x1, Pallas kernels, first_piece(): pl.pallas_call(first_kernel, out_shape=(jax.ShapeDtypeStruct((rows, heads...  3.82 us
    ppermute x3, starting transfers between devices, over_mp(): return lax.ppermute(array, 'mp', [(i, i ^ flip) for i in range(lanes)])  3.12 us
  transfers between devices with their start and end apart: 19, of which 8 were waited for; matrix products, arithmetic and copies ran while one was open for 0% of the time, Pallas kernels for 28%

profile of v4, /device:TPU:0, one launch (start us, length us, event | category | flops | bytes accessed | tf_op | source)
XLA Modules:
  0.0 67.6 jit_solution(1400688650775133885)
XLA Ops:
  0.6 0.5 collective-permute-start.4
  1.1 2.6 %collective-permute-start.1 = (bf16[256,1536]{1,0:T(8,128)(2,1)}, bf16[256,1536]{1,0:T(8,128)(2,1)S(1)}, u32[]{:S(2)}, u32[]{:S(2)}) collective-permute-start(bf16[256,1536]{1,0:T(8,128)(2,1)} %og.1), channel_id=1, source_target_pairs={{0,2},{1,3},{2,0},{3,1},{4,6},{5,7},{6,4},{7,5},{8,10},{9,11},{10,... | collective-permute-start | bytes 2359304 | tf_op jit(solution)/shard_map/ppermute | solution.py:369
  3.7 2.4 %pack.1 = (bf16[3,256,384]{2,1,0:T(8,128)(2,1)}, bf16[3,256,384]{2,1,0:T(8,128)(2,1)}) custom-call(bf16[256,768]{1,0:T(8,128)(2,1)} %q.1, bf16[256,768]{1,0:T(8,128)(2,1)} %k.1, bf16[256,768]{1,0:T(8,128)(2,1)} %v.1), custom_call_target="tpu_custom_call" | custom-call | flops 1 | bytes 1 | tf_op jit(solution)/shard_map/pack/pallas_call | solution.py:54
  6.2 1.6 %collective-permute-start.2 = (bf16[3,256,384]{2,1,0:T(8,128)(2,1)}, bf16[3,256,384]{2,1,0:T(8,128)(2,1)S(1)}, u32[]{:S(2)}, u32[]{:S(2)}) collective-permute-start(bf16[3,256,384]{2,1,0:T(8,128)(2,1)} %get-tuple-element.28.keep), channel_id=1, source_target_pairs={{0,8},{1,9},{2,10},{3,11},{4,12},{5,13},{6,14},{7,15},{8,0},{9,1},... | collective-permute-start | bytes 1769480 | tf_op jit(solution)/shard_map/ppermute | solution.py:386
  7.8 1.5 %collective-permute-start = (bf16[3,256,384]{2,1,0:T(8,128)(2,1)}, bf16[3,256,384]{2,1,0:T(8,128)(2,1)S(1)}, u32[]{:S(2)}, u32[]{:S(2)}) collective-permute-start(bf16[3,256,384]{2,1,0:T(8,128)(2,1)} %get-tuple-element.29), channel_id=1, source_target_pairs={{0,4},{4,0},{8,12},{12,8},{16,20},{20,16},{24,28},{28,24},{1,5},{5... | collective-permute-start | bytes 1769480 | tf_op jit(solution)/shard_map/ppermute | solution.py:372
  9.3 1.1 %copy-done.1 = bf16[256,1536]{1,0:T(8,128)(2,1)S(1)} copy-done((bf16[256,1536]{1,0:T(8,128)(2,1)S(1)}, bf16[256,1536]{1,0:T(8,128)(2,1)}, u32[]{:S(2)}) %copy-start.1) | copy-done | bytes 786456
  10.5 3.8 %head_grad_first.1 = (f32[256,768]{1,0:T(8,128)S(1)}, bf16[768,1536]{1,0:T(8,128)(2,1)S(1)}, bf16[768,1536]{1,0:T(8,128)(2,1)S(1)}) custom-call(bf16[256,1536]{1,0:T(8,128)(2,1)S(1)} %copy-done.1, bf16[256,1536]{1,0:T(8,128)(2,1)S(1)} %collective-permute-done.4.near, bf16[768,6144]{1,0:T(8,128)(2,1)} %w.1), custom_call_target="tpu_custom_call" | custom-call | flops 1 | bytes 1 | tf_op jit(solution)/shard_map/head_grad_first/pallas_call | solution.py:87
  14.3 7.6 %collective-permute-done.2.e0 = bf16[3,256,384]{2,1,0:T(8,128)(2,1)S(1)} collective-permute-done((bf16[3,256,384]{2,1,0:T(8,128)(2,1)}, bf16[3,256,384]{2,1,0:T(8,128)(2,1)S(1)}, u32[]{:S(2)}, u32[]{:S(2)}) %collective-permute-start.2) | collective-permute-done | bytes 589856 | tf_op jit(solution)/shard_map/ppermute | solution.py:386
  22.1 1.7 %collective-permute-done.xr = bf16[3,256,384]{2,1,0:T(8,128)(2,1)S(1)} collective-permute-done((bf16[3,256,384]{2,1,0:T(8,128)(2,1)}, bf16[3,256,384]{2,1,0:T(8,128)(2,1)S(1)}, u32[]{:S(2)}, u32[]{:S(2)}) %collective-permute-start) | collective-permute-done | bytes 589856 | tf_op jit(solution)/shard_map/ppermute | solution.py:372
  23.8 2.2 %collective-permute-start.5 = (bf16[3,256,384]{2,1,0:T(8,128)(2,1)S(1)}, bf16[3,256,384]{2,1,0:T(8,128)(2,1)S(1)}, u32[]{:S(2)}, u32[]{:S(2)}) collective-permute-start(bf16[3,256,384]{2,1,0:T(8,128)(2,1)S(1)} %collective-permute-done.xr), channel_id=1, source_target_pairs={{0,8},{1,9},{2,10},{3,11},{4,12},{5,13},{6,14},{7,15},{8,0},{9,1},... | collective-permute-start | bytes 1769480 | tf_op jit(solution)/shard_map/ppermute | solution.py:386
  26.0 0.8 %head_grad.2.acc = f32[256,768]{1,0:T(8,128)S(1)} custom-call(f32[256,768]{1,0:T(8,128)S(1)} %get-tuple-element.33.acc, bf16[256,1536]{1,0:T(8,128)(2,1)S(1)} %collective-permute-done.1.piece, bf16[768,1536]{1,0:T(8,128)(2,1)S(1)} %get-tuple-element.35.w), custom_call_target="tpu_custom_call" | custom-call | flops 1 | bytes 1 | tf_op jit(solution)/shard_map/head_grad/pallas_call | solution.py:124
  26.9 0.9 %head_grad.3 = (bf16[256,384]{1,0:T(8,128)(2,1)S(1)}, bf16[256,384]{1,0:T(8,128)(2,1)S(1)}) custom-call(f32[256,768]{1,0:T(8,128)S(1)} %head_grad.2.acc, bf16[256,1536]{1,0:T(8,128)(2,1)S(1)} %collective-permute-done.7.piece, bf16[768,1536]{1,0:T(8,128)(2,1)S(1)} %get-tuple-element.36.w), custom_call_target="tpu_custom_call" | custom-call | flops 1 | bytes 1 | tf_op jit(solution)/shard_map/head_grad/pallas_call | solution.py:124
  27.7 1.6 %collective-permute-start.8 = (bf16[256,384]{1,0:T(8,128)(2,1)S(1)}, bf16[256,384]{1,0:T(8,128)(2,1)S(1)}, u32[]{:S(2)}, u32[]{:S(2)}) collective-permute-start(bf16[256,384]{1,0:T(8,128)(2,1)S(1)} %get-tuple-element.38), channel_id=1, source_target_pairs={{0,4},{4,0},{8,12},{12,8},{16,20},{20,16},{24,28},{28,24},{1,5},{5... | collective-permute-start | bytes 589832 | tf_op jit(solution)/shard_map/ppermute | solution.py:372
  29.3 0.2 collective-permute-start.10
  29.5 1.8 %collective-permute-start.9 = (bf16[256,384]{1,0:T(8,128)(2,1)S(1)}, bf16[256,384]{1,0:T(8,128)(2,1)S(1)}, u32[]{:S(2)}, u32[]{:S(2)}) collective-permute-start(bf16[256,384]{1,0:T(8,128)(2,1)S(1)} %get-tuple-element.37.dkeep), channel_id=1, source_target_pairs={{0,8},{1,9},{2,10},{3,11},{4,12},{5,13},{6,14},{7,15},{8,0},{9,1},... | collective-permute-start | bytes 589832 | tf_op jit(solution)/shard_map/ppermute | solution.py:386
  31.3 9.0 %collective-permute-done.5.e1 = bf16[3,256,384]{2,1,0:T(8,128)(2,1)S(1)} collective-permute-done((bf16[3,256,384]{2,1,0:T(8,128)(2,1)S(1)}, bf16[3,256,384]{2,1,0:T(8,128)(2,1)S(1)}, u32[]{:S(2)}, u32[]{:S(2)}) %collective-permute-start.5) | collective-permute-done | bytes 589856 | tf_op jit(solution)/shard_map/ppermute | solution.py:386
  40.3 5.8 %query_pass.1 = (bf16[256,384]{1,0:T(8,128)(2,1)S(1)}, bf16[256,384]{1,0:T(8,128)(2,1)S(1)}, f32[8,512]{1,0:T(8,128)S(1)}) custom-call(bf16[3,256,384]{2,1,0:T(8,128)(2,1)S(1)} %copy-done, bf16[3,256,384]{2,1,0:T(8,128)(2,1)S(1)} %collective-permute-done.xr, bf16[3,256,384]{2,1,0:T(8,128)(2,1)S(1)} %collective-permute-done.2.e0, ...), custom_call_target="tpu_custom_call" | custom-call | flops 20000000000 | bytes 1 | tf_op jit(solution)/shard_map/query_pass/pallas_call | solution.py:216
  46.1 1.6 %collective-permute-start.11 = (bf16[256,384]{1,0:T(8,128)(2,1)S(1)}, bf16[256,384]{1,0:T(8,128)(2,1)S(1)}, u32[]{:S(2)}, u32[]{:S(2)}) collective-permute-start(bf16[256,384]{1,0:T(8,128)(2,1)S(1)} %get-tuple-element.42), channel_id=1, source_target_pairs={{0,4},{4,0},{8,12},{12,8},{16,20},{20,16},{24,28},{28,24},{1,5},{5... | collective-permute-start | bytes 589832 | tf_op jit(solution)/shard_map/ppermute | solution.py:372
  47.6 2.0 %collective-permute-start.12 = (bf16[256,384]{1,0:T(8,128)(2,1)S(1)}, bf16[256,384]{1,0:T(8,128)(2,1)S(1)}, u32[]{:S(2)}, u32[]{:S(2)}) collective-permute-start(bf16[256,384]{1,0:T(8,128)(2,1)S(1)} %collective-permute-done.8.dxr), channel_id=1, source_target_pairs={{0,8},{1,9},{2,10},{3,11},{4,12},{5,13},{6,14},{7,15},{8,0},{9,1},... | collective-permute-start | bytes 589832 | tf_op jit(solution)/shard_map/ppermute | solution.py:386
  49.7 1.3 %collective-permute-start.14 = (f32[8,512]{1,0:T(8,128)S(1)}, f32[8,512]{1,0:T(8,128)S(1)}, u32[]{:S(2)}, u32[]{:S(2)}) collective-permute-start(f32[8,512]{1,0:T(8,128)S(1)} %get-tuple-element.41.stats), channel_id=1, source_target_pairs={{0,8},{1,9},{2,10},{3,11},{4,12},{5,13},{6,14},{7,15},{8,0},{9,1},... | collective-permute-start | bytes 49160 | tf_op jit(solution)/shard_map/ppermute | solution.py:386
  51.0 2.3 %own_pass.1.sums = f32[2,2,256,384]{3,2,1,0:T(8,128)S(1)} custom-call(bf16[3,256,384]{2,1,0:T(8,128)(2,1)S(1)} %copy-done, bf16[3,256,384]{2,1,0:T(8,128)(2,1)S(1)} %collective-permute-done.xr, bf16[256,384]{1,0:T(8,128)(2,1)S(1)} %get-tuple-element.37.dkeep, bf16[256,384]{1,0:T(8,128)(2,1)S(1)} %collective-permute-done.8.dxr, ...), custom_call_target="tpu_custom_call" | custom-call | flops 1 | bytes 1 | tf_op jit(solution)/shard_map/own_pass/pallas_call | solution.py:264
  53.2 0.4 collective-permute-done.14.se
  53.7 1.6 %key_pass.5 = (bf16[2,256,128]{2,1,0:T(8,128)(2,1)S(1)}, bf16[2,256,128]{2,1,0:T(8,128)(2,1)S(1)}) custom-call(bf16[3,256,384]{2,1,0:T(8,128)(2,1)S(1)} %copy-done, bf16[3,256,384]{2,1,0:T(8,128)(2,1)S(1)} %collective-permute-done.xr, bf16[3,256,384]{2,1,0:T(8,128)(2,1)S(1)} %collective-permute-done.2.e0, ...), custom_call_target="tpu_custom_call" | custom-call | flops 1 | bytes 1 | tf_op jit(solution)/shard_map/key_pass/pallas_call | solution.py:321
  55.3 0.6 collective-permute-start.18
  55.9 1.4 %key_pass.4 = (bf16[2,256,128]{2,1,0:T(8,128)(2,1)S(1)}, bf16[2,256,128]{2,1,0:T(8,128)(2,1)S(1)}) custom-call(bf16[3,256,384]{2,1,0:T(8,128)(2,1)S(1)} %copy-done, bf16[3,256,384]{2,1,0:T(8,128)(2,1)S(1)} %collective-permute-done.xr, bf16[3,256,384]{2,1,0:T(8,128)(2,1)S(1)} %collective-permute-done.2.e0, ...), custom_call_target="tpu_custom_call" | custom-call | flops 1 | bytes 1 | tf_op jit(solution)/shard_map/key_pass/pallas_call | solution.py:321
  57.2 1.6 %collective-permute-start.17 = (bf16[2,256,128]{2,1,0:T(8,128)(2,1)S(1)}, bf16[2,256,128]{2,1,0:T(8,128)(2,1)S(1)}, u32[]{:S(2)}, u32[]{:S(2)}) collective-permute-start(bf16[2,256,128]{2,1,0:T(8,128)(2,1)S(1)} %get-tuple-element.51), channel_id=1, source_target_pairs={{0,4},{4,0},{8,12},{12,8},{16,20},{20,16},{24,28},{28,24},{1,5},{5... | collective-permute-start | bytes 393224 | tf_op jit(solution)/shard_map/ppermute | solution.py:372
  58.8 1.4 %key_pass.3 = (bf16[2,256,128]{2,1,0:T(8,128)(2,1)S(1)}, bf16[2,256,128]{2,1,0:T(8,128)(2,1)S(1)}) custom-call(bf16[3,256,384]{2,1,0:T(8,128)(2,1)S(1)} %copy-done, bf16[3,256,384]{2,1,0:T(8,128)(2,1)S(1)} %collective-permute-done.xr, bf16[3,256,384]{2,1,0:T(8,128)(2,1)S(1)} %collective-permute-done.2.e0, ...), custom_call_target="tpu_custom_call" | custom-call | flops 1 | bytes 1 | tf_op jit(solution)/shard_map/key_pass/pallas_call | solution.py:321
  60.1 0.6 collective-permute-start.16
  60.7 0.9 %collective-permute-done.18.refs_5_ = bf16[2,256,128]{2,1,0:T(8,128)(2,1)S(1)} collective-permute-done((bf16[2,256,128]{2,1,0:T(8,128)(2,1)S(1)}, bf16[2,256,128]{2,1,0:T(8,128)(2,1)S(1)}, u32[]{:S(2)}, u32[]{:S(2)}) %collective-permute-start.18) | collective-permute-done | bytes 131104 | tf_op jit(solution)/shard_map/ppermute | solution.py:372
  61.7 2.8 %collective-permute-done.17.refs_4_ = bf16[2,256,128]{2,1,0:T(8,128)(2,1)S(1)} collective-permute-done((bf16[2,256,128]{2,1,0:T(8,128)(2,1)S(1)}, bf16[2,256,128]{2,1,0:T(8,128)(2,1)S(1)}, u32[]{:S(2)}, u32[]{:S(2)}) %collective-permute-start.17) | collective-permute-done | bytes 131104 | tf_op jit(solution)/shard_map/ppermute | solution.py:372
  64.5 2.0 %collective-permute-done.16.refs_3_ = bf16[2,256,128]{2,1,0:T(8,128)(2,1)S(1)} collective-permute-done((bf16[2,256,128]{2,1,0:T(8,128)(2,1)S(1)}, bf16[2,256,128]{2,1,0:T(8,128)(2,1)S(1)}, u32[]{:S(2)}, u32[]{:S(2)}) %collective-permute-start.16) | collective-permute-done | bytes 131104 | tf_op jit(solution)/shard_map/ppermute | solution.py:372
  66.5 1.2 %unpack.1 = (bf16[256,768]{1,0:T(8,128)(2,1)}, bf16[256,768]{1,0:T(8,128)(2,1)}, bf16[256,768]{1,0:T(8,128)(2,1)}) custom-call(bf16[256,384]{1,0:T(8,128)(2,1)S(1)} %get-tuple-element.39.q_keep, bf16[256,384]{1,0:T(8,128)(2,1)S(1)} %collective-permute-done.11.q_got, bf16[2,256,128]{2,1,0:T(8,128)(2,1)S(1)} %get-tuple-element.46.refs_0_, ...), custom_call_target="tpu_custom_call" | custom-call | flops 1 | bytes 1 | tf_op jit(solution)/shard_map/unpack/pallas_call | solution.py:351
  (20 shorter events, 0.3 us)
Async XLA Ops:
  0.6 8.7 %collective-permute-start.4 = (bf16[256,1536]{1,0:T(8,128)(2,1)}, bf16[256,1536]{1,0:T(8,128)(2,1)S(1)}, u32[]{:S(2)}, u32[]{:S(2)}) collective-permute-start(bf16[256,1536]{1,0:T(8,128)(2,1)} %og.1), channel_id=1, source_target_pairs={{0,1},{1,0},{2,3},{3,2},{4,5},{5,4},{6,7},{7,6},{8,9},{9,8},{10,11... | collective-permute-start | bytes 2359304 | tf_op jit(solution)/shard_map/ppermute | solution.py:369
  1.1 20.9 %collective-permute-start.1 = (bf16[256,1536]{1,0:T(8,128)(2,1)}, bf16[256,1536]{1,0:T(8,128)(2,1)S(1)}, u32[]{:S(2)}, u32[]{:S(2)}) collective-permute-start(bf16[256,1536]{1,0:T(8,128)(2,1)} %og.1), channel_id=1, source_target_pairs={{0,2},{1,3},{2,0},{3,1},{4,6},{5,7},{6,4},{7,5},{8,10},{9,11},{10,... | collective-permute-start | bytes 2359304 | tf_op jit(solution)/shard_map/ppermute | solution.py:369
  6.2 15.7 %collective-permute-start.2 = (bf16[3,256,384]{2,1,0:T(8,128)(2,1)}, bf16[3,256,384]{2,1,0:T(8,128)(2,1)S(1)}, u32[]{:S(2)}, u32[]{:S(2)}) collective-permute-start(bf16[3,256,384]{2,1,0:T(8,128)(2,1)} %get-tuple-element.28.keep), channel_id=1, source_target_pairs={{0,8},{1,9},{2,10},{3,11},{4,12},{5,13},{6,14},{7,15},{8,0},{9,1},... | collective-permute-start | bytes 1769480 | tf_op jit(solution)/shard_map/ppermute | solution.py:386
  7.8 14.0 %collective-permute-start.3 = (bf16[3,256,384]{2,1,0:T(8,128)(2,1)}, bf16[3,256,384]{2,1,0:T(8,128)(2,1)S(1)}, u32[]{:S(2)}, u32[]{:S(2)}) collective-permute-start(bf16[3,256,384]{2,1,0:T(8,128)(2,1)} %get-tuple-element.28.keep), channel_id=1, source_target_pairs={{0,1},{1,0},{2,3},{3,2},{4,5},{5,4},{6,7},{7,6},{8,16},{9,17},{10,... | collective-permute-start | bytes 1769480 | tf_op jit(solution)/shard_map/ppermute | solution.py:386
  7.8 16.0 %collective-permute-start = (bf16[3,256,384]{2,1,0:T(8,128)(2,1)}, bf16[3,256,384]{2,1,0:T(8,128)(2,1)S(1)}, u32[]{:S(2)}, u32[]{:S(2)}) collective-permute-start(bf16[3,256,384]{2,1,0:T(8,128)(2,1)} %get-tuple-element.29), channel_id=1, source_target_pairs={{0,4},{4,0},{8,12},{12,8},{16,20},{20,16},{24,28},{28,24},{1,5},{5... | collective-permute-start | bytes 1769480 | tf_op jit(solution)/shard_map/ppermute | solution.py:372
  9.3 1.1 %copy-start.1 = (bf16[256,1536]{1,0:T(8,128)(2,1)S(1)}, bf16[256,1536]{1,0:T(8,128)(2,1)}, u32[]{:S(2)}) copy-start(bf16[256,1536]{1,0:T(8,128)(2,1)} %og.1) | copy-start | bytes 2359300
  22.1 4.8 %collective-permute-start.7 = (bf16[256,1536]{1,0:T(8,128)(2,1)S(1)}, bf16[256,1536]{1,0:T(8,128)(2,1)S(1)}, u32[]{:S(2)}, u32[]{:S(2)}) collective-permute-start(bf16[256,1536]{1,0:T(8,128)(2,1)S(1)} %collective-permute-done.1.piece), channel_id=1, source_target_pairs={{0,1},{1,0},{2,3},{3,2},{4,5},{5,4},{6,7},{7,6},{8,9},{9,8},{10,11... | collective-permute-start | bytes 2359304 | tf_op jit(solution)/shard_map/ppermute | solution.py:369
  23.8 16.5 %collective-permute-start.5 = (bf16[3,256,384]{2,1,0:T(8,128)(2,1)S(1)}, bf16[3,256,384]{2,1,0:T(8,128)(2,1)S(1)}, u32[]{:S(2)}, u32[]{:S(2)}) collective-permute-start(bf16[3,256,384]{2,1,0:T(8,128)(2,1)S(1)} %collective-permute-done.xr), channel_id=1, source_target_pairs={{0,8},{1,9},{2,10},{3,11},{4,12},{5,13},{6,14},{7,15},{8,0},{9,1},... | collective-permute-start | bytes 1769480 | tf_op jit(solution)/shard_map/ppermute | solution.py:386
  26.0 14.2 %collective-permute-start.6 = (bf16[3,256,384]{2,1,0:T(8,128)(2,1)S(1)}, bf16[3,256,384]{2,1,0:T(8,128)(2,1)S(1)}, u32[]{:S(2)}, u32[]{:S(2)}) collective-permute-start(bf16[3,256,384]{2,1,0:T(8,128)(2,1)S(1)} %collective-permute-done.xr), channel_id=1, source_target_pairs={{0,1},{1,0},{2,3},{3,2},{4,5},{5,4},{6,7},{7,6},{8,16},{9,17},{10,... | collective-permute-start | bytes 1769480 | tf_op jit(solution)/shard_map/ppermute | solution.py:386
  26.8 13.4 %copy-start = (bf16[3,256,384]{2,1,0:T(8,128)(2,1)S(1)}, bf16[3,256,384]{2,1,0:T(8,128)(2,1)}, u32[]{:S(2)}) copy-start(bf16[3,256,384]{2,1,0:T(8,128)(2,1)} %get-tuple-element.28.keep) | copy-start | bytes 1769476
  27.7 12.6 %collective-permute-start.8 = (bf16[256,384]{1,0:T(8,128)(2,1)S(1)}, bf16[256,384]{1,0:T(8,128)(2,1)S(1)}, u32[]{:S(2)}, u32[]{:S(2)}) collective-permute-start(bf16[256,384]{1,0:T(8,128)(2,1)S(1)} %get-tuple-element.38), channel_id=1, source_target_pairs={{0,4},{4,0},{8,12},{12,8},{16,20},{20,16},{24,28},{28,24},{1,5},{5... | collective-permute-start | bytes 589832 | tf_op jit(solution)/shard_map/ppermute | solution.py:372
  29.3 20.4 %collective-permute-start.10 = (bf16[256,384]{1,0:T(8,128)(2,1)S(1)}, bf16[256,384]{1,0:T(8,128)(2,1)S(1)}, u32[]{:S(2)}, u32[]{:S(2)}) collective-permute-start(bf16[256,384]{1,0:T(8,128)(2,1)S(1)} %get-tuple-element.37.dkeep), channel_id=1, source_target_pairs={{0,1},{1,0},{2,3},{3,2},{4,5},{5,4},{6,7},{7,6},{8,16},{9,17},{10,... | collective-permute-start | bytes 589832 | tf_op jit(solution)/shard_map/ppermute | solution.py:386
  29.5 20.2 %collective-permute-start.9 = (bf16[256,384]{1,0:T(8,128)(2,1)S(1)}, bf16[256,384]{1,0:T(8,128)(2,1)S(1)}, u32[]{:S(2)}, u32[]{:S(2)}) collective-permute-start(bf16[256,384]{1,0:T(8,128)(2,1)S(1)} %get-tuple-element.37.dkeep), channel_id=1, source_target_pairs={{0,8},{1,9},{2,10},{3,11},{4,12},{5,13},{6,14},{7,15},{8,0},{9,1},... | collective-permute-start | bytes 589832 | tf_op jit(solution)/shard_map/ppermute | solution.py:386
  46.1 7.2 %collective-permute-start.11 = (bf16[256,384]{1,0:T(8,128)(2,1)S(1)}, bf16[256,384]{1,0:T(8,128)(2,1)S(1)}, u32[]{:S(2)}, u32[]{:S(2)}) collective-permute-start(bf16[256,384]{1,0:T(8,128)(2,1)S(1)} %get-tuple-element.42), channel_id=1, source_target_pairs={{0,4},{4,0},{8,12},{12,8},{16,20},{20,16},{24,28},{28,24},{1,5},{5... | collective-permute-start | bytes 589832 | tf_op jit(solution)/shard_map/ppermute | solution.py:372
  47.6 6.0 %collective-permute-start.12 = (bf16[256,384]{1,0:T(8,128)(2,1)S(1)}, bf16[256,384]{1,0:T(8,128)(2,1)S(1)}, u32[]{:S(2)}, u32[]{:S(2)}) collective-permute-start(bf16[256,384]{1,0:T(8,128)(2,1)S(1)} %collective-permute-done.8.dxr), channel_id=1, source_target_pairs={{0,8},{1,9},{2,10},{3,11},{4,12},{5,13},{6,14},{7,15},{8,0},{9,1},... | collective-permute-start | bytes 589832 | tf_op jit(solution)/shard_map/ppermute | solution.py:386
  49.7 4.0 %collective-permute-start.13 = (bf16[256,384]{1,0:T(8,128)(2,1)S(1)}, bf16[256,384]{1,0:T(8,128)(2,1)S(1)}, u32[]{:S(2)}, u32[]{:S(2)}) collective-permute-start(bf16[256,384]{1,0:T(8,128)(2,1)S(1)} %collective-permute-done.8.dxr), channel_id=1, source_target_pairs={{0,1},{1,0},{2,3},{3,2},{4,5},{5,4},{6,7},{7,6},{8,16},{9,17},{10,... | collective-permute-start | bytes 589832 | tf_op jit(solution)/shard_map/ppermute | solution.py:386
  49.7 4.0 %collective-permute-start.14 = (f32[8,512]{1,0:T(8,128)S(1)}, f32[8,512]{1,0:T(8,128)S(1)}, u32[]{:S(2)}, u32[]{:S(2)}) collective-permute-start(f32[8,512]{1,0:T(8,128)S(1)} %get-tuple-element.41.stats), channel_id=1, source_target_pairs={{0,8},{1,9},{2,10},{3,11},{4,12},{5,13},{6,14},{7,15},{8,0},{9,1},... | collective-permute-start | bytes 49160 | tf_op jit(solution)/shard_map/ppermute | solution.py:386
  50.9 2.7 %collective-permute-start.15 = (f32[8,512]{1,0:T(8,128)S(1)}, f32[8,512]{1,0:T(8,128)S(1)}, u32[]{:S(2)}, u32[]{:S(2)}) collective-permute-start(f32[8,512]{1,0:T(8,128)S(1)} %get-tuple-element.41.stats), channel_id=1, source_target_pairs={{0,1},{1,0},{2,3},{3,2},{4,5},{5,4},{6,7},{7,6},{8,16},{9,17},{10,... | collective-permute-start | bytes 49160 | tf_op jit(solution)/shard_map/ppermute | solution.py:386
  55.3 6.4 %collective-permute-start.18 = (bf16[2,256,128]{2,1,0:T(8,128)(2,1)S(1)}, bf16[2,256,128]{2,1,0:T(8,128)(2,1)S(1)}, u32[]{:S(2)}, u32[]{:S(2)}) collective-permute-start(bf16[2,256,128]{2,1,0:T(8,128)(2,1)S(1)} %get-tuple-element.52), channel_id=1, source_target_pairs={{0,4},{4,0},{8,12},{12,8},{16,20},{20,16},{24,28},{28,24},{1,5},{5... | collective-permute-start | bytes 393224 | tf_op jit(solution)/shard_map/ppermute | solution.py:372
  57.2 7.3 %collective-permute-start.17 = (bf16[2,256,128]{2,1,0:T(8,128)(2,1)S(1)}, bf16[2,256,128]{2,1,0:T(8,128)(2,1)S(1)}, u32[]{:S(2)}, u32[]{:S(2)}) collective-permute-start(bf16[2,256,128]{2,1,0:T(8,128)(2,1)S(1)} %get-tuple-element.51), channel_id=1, source_target_pairs={{0,4},{4,0},{8,12},{12,8},{16,20},{20,16},{24,28},{28,24},{1,5},{5... | collective-permute-start | bytes 393224 | tf_op jit(solution)/shard_map/ppermute | solution.py:372
  60.1 6.3 %collective-permute-start.16 = (bf16[2,256,128]{2,1,0:T(8,128)(2,1)S(1)}, bf16[2,256,128]{2,1,0:T(8,128)(2,1)S(1)}, u32[]{:S(2)}, u32[]{:S(2)}) collective-permute-start(bf16[2,256,128]{2,1,0:T(8,128)(2,1)S(1)} %get-tuple-element.50), channel_id=1, source_target_pairs={{0,4},{4,0},{8,12},{12,8},{16,20},{20,16},{24,28},{28,24},{1,5},{5... | collective-permute-start | bytes 393224 | tf_op jit(solution)/shard_map/ppermute | solution.py:372

commit v5 on v4

v5 whole, which is shorter than its diff:
```python
import functools
import math

import jax
import jax.numpy as jnp
from jax import lax
from jax.experimental import pallas as pl
from jax.experimental.pallas import tpu as pltpu
from jax.sharding import PartitionSpec as P

HD = 128
BF16 = jnp.bfloat16
F32 = jnp.float32
BIG = 1e30
ANY = pl.BlockSpec(memory_space=pl.ANY)
VM = pl.BlockSpec(memory_space=pltpu.VMEM)
HBM = pl.BlockSpec(memory_space=pltpu.HBM)


def params(mib=40):
    return pltpu.CompilerParams(vmem_limit_bytes=mib << 20)


def nt(a, b):
    return lax.dot_general(a, b, (((1,), (1,)), ((), ())), preferred_element_type=F32)


def nn(a, b):
    return lax.dot_general(a, b, (((1,), (0,)), ((), ())), preferred_element_type=F32)


def cost(flops=1):
    return pl.CostEstimate(flops=int(flops), bytes_accessed=1, transcendentals=0)


def pack_kernel(q, k, v, keep, send_kv, send_q, sem):
    half = q.shape[1] // 2
    x = lax.rem(lax.axis_index("ctx"), 2)
    mine = pl.ds(pl.multiple_of(x * half, half), half)
    theirs = pl.ds(pl.multiple_of((1 - x) * half, half), half)
    pairs = (
        (k.at[:, theirs], send_kv.at[0]),
        (v.at[:, theirs], send_kv.at[1]),
        (k.at[:, mine], keep.at[0]),
        (v.at[:, mine], keep.at[1]),
        (q.at[:, mine], keep.at[2]),
        (q.at[:, theirs], send_q.at[0]),
    )
    copies = [pltpu.make_async_copy(a, b, sem.at[i]) for i, (a, b) in enumerate(pairs)]
    for copy in copies:
        copy.start()
    for copy in copies:
        copy.wait()


def pack(q, k, v):
    rows, cols = q.shape
    three, two, one = (jax.ShapeDtypeStruct((n, rows, cols // 2), BF16) for n in (3, 2, 1))
    return pl.pallas_call(
        pack_kernel,
        out_shape=(three, two, one),
        in_specs=[ANY] * 3,
        out_specs=(VM,) * 3,
        scratch_shapes=[pltpu.SemaphoreType.DMA((6,))],
        compiler_params=params(60),
        cost_estimate=cost(),
        name="pack",
    )(q, k, v)


def join_kernel(mine, theirs, out):
    out[0] = mine[...]
    out[1] = theirs[...]


def join(mine, theirs):
    return pl.pallas_call(
        join_kernel,
        out_shape=jax.ShapeDtypeStruct((2, *mine.shape), BF16),
        in_specs=[VM] * 2,
        out_specs=VM,
        compiler_params=params(16),
        cost_estimate=cost(),
        name="join",
    )(mine, theirs)


def first_kernel(og, near, w, acc, wy, wf, wbuf, sem):
    width = og.shape[1]
    me = lax.axis_index("mp")
    copies = []
    for flip, target in enumerate((wbuf.at[0], wbuf.at[1], wy, wf)):
        first = pl.multiple_of(jnp.bitwise_xor(me, flip) * width, width)
        copies.append(pltpu.make_async_copy(w.at[:, pl.ds(first, width)], target, sem.at[flip]))
    for copy in copies:
        copy.start()
    copies[0].wait()
    acc[...] = nt(og[...], wbuf[0])
    copies[1].wait()
    acc[...] += nt(near[...], wbuf[1])
    copies[2].wait()
    copies[3].wait()


def first_piece(og, near, w):
    rows, width = og.shape
    heads = w.shape[0]
    part = jax.ShapeDtypeStruct((heads, width), BF16)
    return pl.pallas_call(
        first_kernel,
        out_shape=(jax.ShapeDtypeStruct((rows, heads), F32), part, part),
        in_specs=[VM, VM, ANY],
        out_specs=(VM, VM, VM),
        scratch_shapes=[pltpu.VMEM((2, heads, width), BF16), pltpu.SemaphoreType.DMA((4,))],
        compiler_params=params(46),
        cost_estimate=cost(),
        name="head_grad_first",
    )(og, near, w)


def next_kernel(acc, piece, w, out):
    out[...] = acc[...] + nt(piece[...], w[...])


def last_kernel(acc, piece, w, keep, send):
    total = acc[...] + nt(piece[...], w[...])
    half = total.shape[1] // 2
    x = lax.rem(lax.axis_index("ctx"), 2)
    low = total[:, :half].astype(BF16)
    high = total[:, half:].astype(BF16)

    @pl.when(x == 0)
    def _():
        keep[...] = low
        send[...] = high

    @pl.when(x != 0)
    def _():
        keep[...] = high
        send[...] = low


def grad_piece(acc, piece, w, last):
    rows, heads = acc.shape
    half = jax.ShapeDtypeStruct((rows, heads // 2), BF16)
    return pl.pallas_call(
        last_kernel if last else next_kernel,
        out_shape=(half, half) if last else jax.ShapeDtypeStruct((rows, heads), F32),
        in_specs=[VM] * 3,
        out_specs=(VM, VM) if last else VM,
        compiler_params=params(30),
        cost_estimate=cost(),
        name="head_grad",
    )(acc, piece, w)


def place():
    position = lax.axis_index("ctx")
    block = position // 2
    low_ok = block > 0
    high_ok = block < lax.axis_size("ctx") // 2 - 1
    odd = lax.rem(block, 2) == 1
    even_ok = jnp.logical_or(jnp.logical_and(odd, low_ok), jnp.logical_and(jnp.logical_not(odd), high_ok))
    odd_ok = jnp.logical_or(jnp.logical_and(odd, high_ok), jnp.logical_and(jnp.logical_not(odd), low_ok))
    turned = lax.rem(position + block, 2) == 1
    return even_ok, odd_ok, turned


def off(ok):
    return jnp.where(ok, 0.0, BIG).astype(F32)


def query_kernel(scale, own, has_marks, *refs):
    refs = list(refs)
    q, d, keep, xr, e, o, e_other, o_other = refs[:8]
    q = q.at[q.shape[0] - 1]
    before = refs[8] if has_marks else None
    out, stats, fifth = refs[-3:]
    rows = q.shape[0]
    heads = q.shape[1] // HD
    even_ok, odd_ok, turned = place()
    from_even = turned if own else jnp.logical_not(turned)

    @pl.when(from_even)
    def _():
        fifth[...] = e_other[0:2]

    @pl.when(jnp.logical_not(from_even))
    def _():
        fifth[...] = o_other[0:2]

    c = scale * math.log2(math.e)
    even_off, odd_off = off(even_ok), off(odd_ok)
    lane = lax.broadcasted_iota(jnp.int32, (rows, HD), 1)
    runs = (
        (keep, None),
        (xr, None),
        (e, even_off),
        (o, odd_off),
        (fifth, jnp.where(from_even, even_off, odd_off)),
    )
    mark = jnp.zeros((rows, HD), F32)
    for head in range(heads):
        cols = slice(head * HD, (head + 1) * HD)
        query = q[:, cols]
        grad = d[:, cols]
        scores = [nt(query, ref[0, :, cols]) for ref, _ in runs]
        top = None
        for s, (_, gone) in zip(scores, runs):
            m = jnp.max(s, -1, keepdims=True)
            m = m if gone is None else m - gone
            top = m if top is None else jnp.maximum(top, m)
        top = top * c
        weights = [
            jnp.exp2(s * c - (top if gone is None else top + gone))
            for s, (_, gone) in zip(scores, runs)
        ]
        total = jnp.sum(sum(weights), -1, keepdims=True)
        grads = [nt(grad, ref[1, :, cols]) for ref, _ in runs]
        inverse = 1.0 / total
        delta = jnp.sum(sum(w * g for w, g in zip(weights, grads)), -1, keepdims=True) * inverse
        result = sum(
            nn((w * (g - delta)).astype(BF16), ref[0, :, cols])
            for w, g, (ref, _) in zip(weights, grads, runs)
        )
        out[:, cols] = (result * (inverse * scale)).astype(BF16)
        mark = jnp.where(lane == 2 * head, top + jnp.log2(total), mark)
        mark = jnp.where(lane == 2 * head + 1, delta, mark)
    marks = jnp.transpose(mark)[: stats.shape[0], :]
    if has_marks:
        stats[:, :rows] = before[...]
        stats[:, rows:] = marks
    else:
        stats[...] = marks


def query_pass(own, q, d, keep, xr, e, o, e_other, o_other, before=None):
    rows, cols = d.shape
    operands = [q, d, keep, xr, e, o, e_other, o_other]
    if before is not None:
        operands.append(before)
    return pl.pallas_call(
        functools.partial(query_kernel, HD ** -0.5, own, before is not None),
        out_shape=(
            jax.ShapeDtypeStruct((rows, cols), BF16),
            jax.ShapeDtypeStruct((8, rows if before is None else 2 * rows), F32),
        ),
        in_specs=[VM] * len(operands),
        out_specs=(VM, VM),
        scratch_shapes=[pltpu.VMEM((2, rows, cols), BF16)],
        compiler_params=params(30),
        cost_estimate=cost(6e9),
        name="query_pass",
    )(*operands)


def key_step(scale, key, value, steps):
    c = scale * math.log2(math.e)
    key_sum = None
    value_sum = None
    for query, grad, total, delta in steps:
        weight = jnp.exp2(nt(key, query) * c - total)
        change = weight * (nt(value, grad) - delta)
        v = nn(weight.astype(BF16), grad)
        k = nn(change.astype(BF16), query)
        value_sum = v if value_sum is None else value_sum + v
        key_sum = k if key_sum is None else key_sum + k
    return key_sum, value_sum


def own_kernel(scale, keep, xkv, xq, dkeep, dxr, stats, sums):
    rows = keep.shape[1]
    heads = keep.shape[2] // HD
    for mine, keys in enumerate((keep, xkv)):
        for head in range(heads):
            cols = slice(head * HD, (head + 1) * HD)
            steps = []
            for i, (q, d) in enumerate(((keep.at[2], dkeep), (xq.at[0], dxr))):
                span = slice(i * rows, (i + 1) * rows)
                steps.append((
                    q[:, cols],
                    d[:, cols],
                    stats[2 * head : 2 * head + 1, span],
                    stats[2 * head + 1 : 2 * head + 2, span],
                ))
            k, v = key_step(scale, keys[0, :, cols], keys[1, :, cols], steps)
            sums[mine, 0, :, cols] = k
            sums[mine, 1, :, cols] = v


def own_pass(*operands):
    _, rows, cols = operands[0].shape
    return pl.pallas_call(
        functools.partial(own_kernel, HD ** -0.5),
        out_shape=jax.ShapeDtypeStruct((2, 2, rows, cols), F32),
        in_specs=[VM] * 6,
        out_specs=VM,
        compiler_params=params(30),
        cost_estimate=cost(),
        name="own_pass",
    )(*operands)


def key_kernel(scale, own, heads, kv, e0, o0, e1, o1, de, do, se, so, sums, out, fifth_q, fifth_d):
    rows = kv.shape[1]
    even_ok, odd_ok, turned = place()
    from_even = turned if own else jnp.logical_not(turned)
    even_q = (e0.at[e0.shape[0] - 1], e1.at[e1.shape[0] - 1])
    odd_q = (o0.at[o0.shape[0] - 1], o1.at[o1.shape[0] - 1])
    same, other = (0, 1) if own else (1, 0)
    wanted = slice(heads[0] * HD, (heads[-1] + 1) * HD)

    @pl.when(from_even)
    def _():
        fifth_q[...] = even_q[other][:, wanted]
        fifth_d[...] = de[other, :, wanted]

    @pl.when(jnp.logical_not(from_even))
    def _():
        fifth_q[...] = odd_q[other][:, wanted]
        fifth_d[...] = do[other, :, wanted]

    row = lax.broadcasted_iota(jnp.int32, se.shape, 0)
    nothing = jnp.where(lax.rem(row, 2) == 0, jnp.float32(BIG), jnp.float32(0.0))
    even = jnp.where(even_ok, se[...], nothing)
    odd = jnp.where(odd_ok, so[...], nothing)
    span = slice(same * rows, (same + 1) * rows)
    across = slice(other * rows, (other + 1) * rows)
    fifth = jnp.where(from_even, even[:, across], odd[:, across])
    for i, head in enumerate(heads):
        cols = slice(head * HD, (head + 1) * HD)
        to = slice(i * HD, (i + 1) * HD)
        a, b = 2 * head, 2 * head + 1
        steps = (
            (even_q[same][:, cols], de[same, :, cols], even[a : a + 1, span], even[b : b + 1, span]),
            (odd_q[same][:, cols], do[same, :, cols], odd[a : a + 1, span], odd[b : b + 1, span]),
            (fifth_q[:, to], fifth_d[:, to], fifth[a : a + 1], fifth[b : b + 1]),
        )
        k, v = key_step(scale, kv[0, :, cols], kv[1, :, cols], steps)
        out[0, :, to] = ((k + sums[same, 0, :, cols]) * scale).astype(BF16)
        out[1, :, to] = (v + sums[same, 1, :, cols]).astype(BF16)


def key_pass(own, heads, kv, *operands):
    _, rows, _ = kv.shape
    wide = HD * len(heads)
    return pl.pallas_call(
        functools.partial(key_kernel, HD ** -0.5, own, heads),
        out_shape=jax.ShapeDtypeStruct((2, rows, wide), BF16),
        in_specs=[VM] * (1 + len(operands)),
        out_specs=VM,
        scratch_shapes=[pltpu.VMEM((rows, wide), BF16)] * 2,
        compiler_params=params(30),
        cost_estimate=cost(),
        name="key_pass",
    )(kv, *operands)


def unpack_kernel(q_keep, q_got, kv_keep, *refs):
    got, (dq, dk, dv) = refs[:-3], refs[-3:]
    half = q_keep.shape[1]
    x = lax.rem(lax.axis_index("ctx"), 2)
    mine = pl.multiple_of(x * half, half)
    theirs = pl.multiple_of((1 - x) * half, half)
    dq[:, pl.ds(mine, half)] = q_keep[...]
    dq[:, pl.ds(theirs, half)] = q_got[...]
    for i, out in enumerate((dk, dv)):
        out[:, pl.ds(mine, half)] = kv_keep[i]
        first = 0
        for piece in got:
            width = piece.shape[2]
            out[:, pl.ds(theirs + first, width)] = piece[i]
            first += width


def unpack(q_keep, q_got, kv_keep, *got):
    rows, half = q_keep.shape
    whole = jax.ShapeDtypeStruct((rows, 2 * half), BF16)
    return pl.pallas_call(
        unpack_kernel,
        out_shape=(whole,) * 3,
        in_specs=[VM] * (3 + len(got)),
        out_specs=(VM,) * 3,
        compiler_params=params(16),
        cost_estimate=cost(),
        name="unpack",
    )(q_keep, q_got, kv_keep, *got)


def body(queries, keys, values, out_grad, out_weight):
    length = lax.axis_size("ctx")
    lanes = lax.axis_size("mp")
    blocks = length // 2
    width = out_grad.shape[1]

    def over_mp(array, flip):
        return lax.ppermute(array, "mp", [(i, i ^ flip) for i in range(lanes)])

    def over_x(array):
        return lax.ppermute(array, "ctx", [(i, i ^ 1) for i in range(length)])

    def over_z(array, first):
        pairs = []
        for position in range(length):
            block = position // 2
            other = ((block - first) ^ 1) + first
            for lane in range(lanes):
                source = position * lanes + lane
                if block >= first and other < blocks:
                    target = (2 * other + position % 2) * lanes + lane
                else:
                    target = position * lanes + (lane ^ 1)
                pairs.append((source, target))
        return lax.ppermute(array, ("ctx", "mp"), pairs)

    y = over_mp(out_grad, 2)
    near = over_mp(out_grad, 1)
    keep, send_kv, send_q = pack(queries, keys, values)
    xkv = over_x(send_kv)
    e0, o0 = over_z(keep, 0), over_z(keep, 1)
    xq = over_x(send_q)
    acc, wy, wf = first_piece(out_grad, near, out_weight)
    e1, o1 = over_z(xkv, 0), over_z(xkv, 1)
    qe1, qo1 = over_z(xq, 0), over_z(xq, 1)
    y, e0, o0, xkv, xq, acc = lax.optimization_barrier((y, e0, o0, xkv, xq, acc))
    far = over_mp(y, 1)
    acc = grad_piece(acc, y, wy, False)
    dkeep, dsend = grad_piece(acc, far, wf, True)
    dxr = over_x(dsend)

    both_d = join(dkeep, dxr)
    de, do = over_z(both_d, 0), over_z(both_d, 1)
    dq_keep, stats = query_pass(True, keep, dkeep, keep, xkv, e0, o0, e1, o1)
    stats, qe1, qo1 = lax.optimization_barrier((stats, qe1, qo1))
    dq_send, stats = query_pass(False, xq, dxr, keep, xkv, e1, o1, e0, o0, stats)
    se, so = over_z(stats, 0), over_z(stats, 1)
    dq_got = over_x(dq_send)
    sums = own_pass(keep, xkv, xq, dkeep, dxr, stats)
    sums, dq_got = lax.optimization_barrier((sums, dq_got))
    heads = dkeep.shape[1] // HD
    got = [
        over_x(key_pass(False, (head,), xkv, e0, o0, qe1, qo1, de, do, se, so, sums))
        for head in range(heads)
    ]
    kv_keep = key_pass(True, tuple(range(heads)), keep, e0, o0, qe1, qo1, de, do, se, so, sums)
    return tuple(unpack(dq_keep, dq_got, kv_keep, *got))


def solution(mesh):
    placed = (P("ctx", "mp"), P("ctx", "mp"), P("ctx", "mp"), P("ctx", "mp"), P("mp", None))
    return jax.shard_map(
        body,
        mesh=mesh,
        in_specs=placed,
        out_specs=(P("ctx", "mp"), P("ctx", "mp"), P("ctx", "mp")),
        check_vma=False,
    )
```

time: 67.8 us -> 65.4 us (0.965)
  waiting for transfers between devices: 24.6 us -> 21.1 us
  starting transfers between devices: 19.7 us -> 20.5 us
    ppermute x10, waiting for transfers between devices: 17 us -> 6.35 us  [over_z(): return lax.ppermute(array, ('ctx', 'mp'), pairs)]
    ppermute x6 -> x7, waiting for transfers between devices: 7.43 us -> 14.8 us  [over_x(): return lax.ppermute(array, 'ctx', [(i, i ^ 1) for i in range(length)])]
    ppermute x6 -> x7, starting transfers between devices: 7.35 us -> 8.87 us  [over_x(): return lax.ppermute(array, 'ctx', [(i, i ^ 1) for i in range(length)])]
    ppermute x10, starting transfers between devices: 9.21 us -> 8.48 us  [over_z(): return lax.ppermute(array, ('ctx', 'mp'), pairs)]
    pallas_call x6 -> x9, Pallas kernels: 13.7 us -> 13.9 us  [the longest x2 5.96 us: query_pass(): pl.pallas_call(functools.partial(query_kernel, HD ** (-0.5), own, before...]
  transfers between devices with their start and end apart: 19 -> 20, of which waited for: 8 -> 6; matrix products, arithmetic and copies ran while one was open for 0% -> 0% of each run, Pallas kernels for 28% -> 30%
where the time goes in v5:
time: 65.4 us; the launch traced here: 65.3 us
  Pallas kernels  21.7 us (33%)
  waiting for transfers between devices  21.1 us (32%)
  starting transfers between devices  20.5 us (31%)
  local copies, waits for them, and re-layouts  1.14 us (2%)
  between operations  0.78 us (1%)
    ppermute x7, waiting for transfers between devices, over_x(): return lax.ppermute(array, 'ctx', [(i, i ^ 1) for i in range(length)])  14.8 us
    ppermute x7, starting transfers between devices, over_x(): return lax.ppermute(array, 'ctx', [(i, i ^ 1) for i in range(length)])  8.87 us
    ppermute x10, starting transfers between devices, over_z(): return lax.ppermute(array, ('ctx', 'mp'), pairs)  8.48 us
    ppermute x10, waiting for transfers between devices, over_z(): return lax.ppermute(array, ('ctx', 'mp'), pairs)  6.35 us
    pallas_call x2, Pallas kernels, query_pass(): pl.pallas_call(functools.partial(query_kernel, HD ** (-0.5), own, before...  5.96 us
    pallas_call x4, Pallas kernels, key_pass(): pl.pallas_call(functools.partial(key_kernel, HD ** (-0.5), own, heads), o...  4.41 us
    pallas_call x1, Pallas kernels, first_piece(): pl.pallas_call(first_kernel, out_shape=(jax.ShapeDtypeStruct((rows, heads...  3.82 us
    ppermute x3, starting transfers between devices, over_mp(): return lax.ppermute(array, 'mp', [(i, i ^ flip) for i in range(lanes)])  3.18 us
  transfers between devices with their start and end apart: 20, of which 6 were waited for; matrix products, arithmetic and copies ran while one was open for 0% of the time, Pallas kernels for 30%

profile of v5, /device:TPU:0, one launch (start us, length us, event | category | flops | bytes accessed | tf_op | source)
XLA Modules:
  0.0 65.3 jit_solution(14443276627406151688)
XLA Ops:
  1.1 2.6 %collective-permute-start = (bf16[256,1536]{1,0:T(8,128)(2,1)}, bf16[256,1536]{1,0:T(8,128)(2,1)S(1)}, u32[]{:S(2)}, u32[]{:S(2)}) collective-permute-start(bf16[256,1536]{1,0:T(8,128)(2,1)} %og.1), channel_id=1, source_target_pairs={{0,2},{1,3},{2,0},{3,1},{4,6},{5,7},{6,4},{7,5},{8,10},{9,11},{10,... | collective-permute-start | bytes 2359304 | tf_op jit(solution)/shard_map/ppermute | solution.py:397
  3.7 2.4 %pack.1 = (bf16[3,256,384]{2,1,0:T(8,128)(2,1)}, bf16[2,256,384]{2,1,0:T(8,128)(2,1)}, bf16[1,256,384]{2,1,0:T(8,128)(2,1)}) custom-call(bf16[256,768]{1,0:T(8,128)(2,1)} %q.1, bf16[256,768]{1,0:T(8,128)(2,1)} %k.1, bf16[256,768]{1,0:T(8,128)(2,1)} %v.1), custom_call_target="tpu_custom_call" | custom-call | flops 1 | bytes 1 | tf_op jit(solution)/shard_map/pack/pallas_call | solution.py:59
  6.1 1.6 %collective-permute-start.1 = (bf16[3,256,384]{2,1,0:T(8,128)(2,1)}, bf16[3,256,384]{2,1,0:T(8,128)(2,1)S(1)}, u32[]{:S(2)}, u32[]{:S(2)}) collective-permute-start(bf16[3,256,384]{2,1,0:T(8,128)(2,1)} %get-tuple-element.26.refs_0_.refs_2_.keep.kv), channel_id=1, source_target_pairs={{0,8},{1,9},{2,10},{3,11},{4,12},{5,13},{6,14},{7,15},{8,0},{9,1},... | collective-permute-start | bytes 1769480 | tf_op jit(solution)/shard_map/ppermute | solution.py:414
  7.8 1.5 %collective-permute-start.3 = (bf16[2,256,384]{2,1,0:T(8,128)(2,1)}, bf16[2,256,384]{2,1,0:T(8,128)(2,1)S(1)}, u32[]{:S(2)}, u32[]{:S(2)}) collective-permute-start(bf16[2,256,384]{2,1,0:T(8,128)(2,1)} %get-tuple-element.27), channel_id=1, source_target_pairs={{0,4},{4,0},{8,12},{12,8},{16,20},{20,16},{24,28},{28,24},{1,5},{5... | collective-permute-start | bytes 1179656 | tf_op jit(solution)/shard_map/ppermute | solution.py:400
  9.3 0.5 collective-permute-start.4
  9.8 1.1 %copy-done.1 = bf16[256,1536]{1,0:T(8,128)(2,1)S(1)} copy-done((bf16[256,1536]{1,0:T(8,128)(2,1)S(1)}, bf16[256,1536]{1,0:T(8,128)(2,1)}, u32[]{:S(2)}) %copy-start.1) | copy-done | bytes 786456
  10.9 3.8 %head_grad_first.1 = (f32[256,768]{1,0:T(8,128)S(1)}, bf16[768,1536]{1,0:T(8,128)(2,1)S(1)}, bf16[768,1536]{1,0:T(8,128)(2,1)S(1)}) custom-call(bf16[256,1536]{1,0:T(8,128)(2,1)S(1)} %copy-done.1, bf16[256,1536]{1,0:T(8,128)(2,1)S(1)} %collective-permute-done.5.near, bf16[768,6144]{1,0:T(8,128)(2,1)} %w.1), custom_call_target="tpu_custom_call" | custom-call | flops 1 | bytes 1 | tf_op jit(solution)/shard_map/head_grad_first/pallas_call | solution.py:109
  14.8 9.0 %collective-permute-done.4.refs_0_.xq = bf16[1,256,384]{2,1,0:T(8,128)(2,1)S(1)} collective-permute-done((bf16[1,256,384]{2,1,0:T(8,128)(2,1)}, bf16[1,256,384]{2,1,0:T(8,128)(2,1)S(1)}, u32[]{:S(2)}, u32[]{:S(2)}) %collective-permute-start.4) | collective-permute-done | bytes 196640 | tf_op jit(solution)/shard_map/ppermute | solution.py:400
  23.8 2.3 %collective-permute-start.7 = (bf16[2,256,384]{2,1,0:T(8,128)(2,1)S(1)}, bf16[2,256,384]{2,1,0:T(8,128)(2,1)S(1)}, u32[]{:S(2)}, u32[]{:S(2)}) collective-permute-start(bf16[2,256,384]{2,1,0:T(8,128)(2,1)S(1)} %collective-permute-done.3.refs_3_.xkv.kv), channel_id=1, source_target_pairs={{0,8},{1,9},{2,10},{3,11},{4,12},{5,13},{6,14},{7,15},{8,0},{9,1},... | collective-permute-start | bytes 1179656 | tf_op jit(solution)/shard_map/ppermute | solution.py:414
  26.3 1.2 %collective-permute-start.10 = (bf16[1,256,384]{2,1,0:T(8,128)(2,1)S(1)}, bf16[1,256,384]{2,1,0:T(8,128)(2,1)S(1)}, u32[]{:S(2)}, u32[]{:S(2)}) collective-permute-start(bf16[1,256,384]{2,1,0:T(8,128)(2,1)S(1)} %collective-permute-done.4.refs_0_.xq), channel_id=1, source_target_pairs={{0,8},{1,9},{2,10},{3,11},{4,12},{5,13},{6,14},{7,15},{8,0},{9,1},... | collective-permute-start | bytes 589832 | tf_op jit(solution)/shard_map/ppermute | solution.py:414
  27.5 0.8 %head_grad.2.acc = f32[256,768]{1,0:T(8,128)S(1)} custom-call(f32[256,768]{1,0:T(8,128)S(1)} %get-tuple-element.30.acc, bf16[256,1536]{1,0:T(8,128)(2,1)S(1)} %collective-permute-done.piece, bf16[768,1536]{1,0:T(8,128)(2,1)S(1)} %get-tuple-element.32.w), custom_call_target="tpu_custom_call" | custom-call | flops 1 | bytes 1 | tf_op jit(solution)/shard_map/head_grad/pallas_call | solution.py:146
  28.3 0.9 %head_grad.3 = (bf16[256,384]{1,0:T(8,128)(2,1)S(1)}, bf16[256,384]{1,0:T(8,128)(2,1)S(1)}) custom-call(f32[256,768]{1,0:T(8,128)S(1)} %head_grad.2.acc, bf16[256,1536]{1,0:T(8,128)(2,1)S(1)} %collective-permute-done.6.piece, bf16[768,1536]{1,0:T(8,128)(2,1)S(1)} %get-tuple-element.33.w), custom_call_target="tpu_custom_call" | custom-call | flops 1 | bytes 1 | tf_op jit(solution)/shard_map/head_grad/pallas_call | solution.py:146
  29.2 1.6 %collective-permute-start.9 = (bf16[256,384]{1,0:T(8,128)(2,1)S(1)}, bf16[256,384]{1,0:T(8,128)(2,1)S(1)}, u32[]{:S(2)}, u32[]{:S(2)}) collective-permute-start(bf16[256,384]{1,0:T(8,128)(2,1)S(1)} %get-tuple-element.40), channel_id=1, source_target_pairs={{0,4},{4,0},{8,12},{12,8},{16,20},{20,16},{24,28},{28,24},{1,5},{5... | collective-permute-start | bytes 589832 | tf_op jit(solution)/shard_map/ppermute | solution.py:400
  30.8 5.4 %collective-permute-done.7.refs_6_.refs_4_ = bf16[2,256,384]{2,1,0:T(8,128)(2,1)S(1)} collective-permute-done((bf16[2,256,384]{2,1,0:T(8,128)(2,1)S(1)}, bf16[2,256,384]{2,1,0:T(8,128)(2,1)S(1)}, u32[]{:S(2)}, u32[]{:S(2)}) %collective-permute-start.7) | collective-permute-done | bytes 393248 | tf_op jit(solution)/shard_map/ppermute | solution.py:414
  36.1 3.0 %query_pass.2 = (bf16[256,384]{1,0:T(8,128)(2,1)S(1)}, f32[8,256]{1,0:T(8,128)S(1)}) custom-call(bf16[3,256,384]{2,1,0:T(8,128)(2,1)S(1)} %copy-done, bf16[256,384]{1,0:T(8,128)(2,1)S(1)} %get-tuple-element.34.refs_1_.dkeep.mine, bf16[3,256,384]{2,1,0:T(8,128)(2,1)S(1)} %copy-done, bf16[2,256,384]{2,1,0:T(8,128)(2,1)S(1)} %collective-permute-done.3.refs_3_.xkv.kv, ...), custom_call_target="tpu_custom_call" | custom-call | flops 6000000000 | bytes 1 | tf_op jit(solution)/shard_map/query_pass/pallas_call | solution.py:242
  39.1 1.0 %collective-permute-done.10.e1 = bf16[1,256,384]{2,1,0:T(8,128)(2,1)S(1)} collective-permute-done((bf16[1,256,384]{2,1,0:T(8,128)(2,1)S(1)}, bf16[1,256,384]{2,1,0:T(8,128)(2,1)S(1)}, u32[]{:S(2)}, u32[]{:S(2)}) %collective-permute-start.10) | collective-permute-done | bytes 196640 | tf_op jit(solution)/shard_map/ppermute | solution.py:414
  40.1 1.8 %collective-permute-start.13 = (bf16[2,256,384]{2,1,0:T(8,128)(2,1)S(1)}, bf16[2,256,384]{2,1,0:T(8,128)(2,1)S(1)}, u32[]{:S(2)}, u32[]{:S(2)}) collective-permute-start(bf16[2,256,384]{2,1,0:T(8,128)(2,1)S(1)} %join.1), channel_id=1, source_target_pairs={{0,8},{1,9},{2,10},{3,11},{4,12},{5,13},{6,14},{7,15},{8,0},{9,1},... | collective-permute-start | bytes 1179656 | tf_op jit(solution)/shard_map/ppermute | solution.py:414
  41.9 3.0 %query_pass.3 = (bf16[256,384]{1,0:T(8,128)(2,1)S(1)}, f32[8,512]{1,0:T(8,128)S(1)}) custom-call(bf16[1,256,384]{2,1,0:T(8,128)(2,1)S(1)} %collective-permute-done.4.refs_0_.xq, bf16[256,384]{1,0:T(8,128)(2,1)S(1)} %collective-permute-done.9.refs_1_.dxr.theirs, bf16[3,256,384]{2,1,0:T(8,128)(2,1)S(1)} %copy-done, ...), custom_call_target="tpu_custom_call" | custom-call | flops 6000000000 | bytes 1 | tf_op jit(solution)/shard_map/query_pass/pallas_call | solution.py:242
  44.9 1.6 %collective-permute-start.12 = (bf16[256,384]{1,0:T(8,128)(2,1)S(1)}, bf16[256,384]{1,0:T(8,128)(2,1)S(1)}, u32[]{:S(2)}, u32[]{:S(2)}) collective-permute-start(bf16[256,384]{1,0:T(8,128)(2,1)S(1)} %get-tuple-element.44), channel_id=1, source_target_pairs={{0,4},{4,0},{8,12},{12,8},{16,20},{20,16},{24,28},{28,24},{1,5},{5... | collective-permute-start | bytes 589832 | tf_op jit(solution)/shard_map/ppermute | solution.py:400
  46.5 1.3 %collective-permute-start.15 = (f32[8,512]{1,0:T(8,128)S(1)}, f32[8,512]{1,0:T(8,128)S(1)}, u32[]{:S(2)}, u32[]{:S(2)}) collective-permute-start(f32[8,512]{1,0:T(8,128)S(1)} %get-tuple-element.43.stats), channel_id=1, source_target_pairs={{0,8},{1,9},{2,10},{3,11},{4,12},{5,13},{6,14},{7,15},{8,0},{9,1},... | collective-permute-start | bytes 49160 | tf_op jit(solution)/shard_map/ppermute | solution.py:414
  47.8 2.3 %own_pass.1.sums = f32[2,2,256,384]{3,2,1,0:T(8,128)S(1)} custom-call(bf16[3,256,384]{2,1,0:T(8,128)(2,1)S(1)} %copy-done, bf16[2,256,384]{2,1,0:T(8,128)(2,1)S(1)} %collective-permute-done.3.refs_3_.xkv.kv, bf16[1,256,384]{2,1,0:T(8,128)(2,1)S(1)} %collective-permute-done.4.refs_0_.xq, bf16[256,384]{1,0:T(8,128)(2,1)S(1)} %get-tuple-element.34.refs_1_.dkeep.mine, ...), custom_call_target="tpu_custom_call" | custom-call | flops 1 | bytes 1 | tf_op jit(solution)/shard_map/own_pass/pallas_call | solution.py:293
  50.1 2.2 %collective-permute-done.12.q_got = bf16[256,384]{1,0:T(8,128)(2,1)S(1)} collective-permute-done((bf16[256,384]{1,0:T(8,128)(2,1)S(1)}, bf16[256,384]{1,0:T(8,128)(2,1)S(1)}, u32[]{:S(2)}, u32[]{:S(2)}) %collective-permute-start.12) | collective-permute-done | bytes 196640 | tf_op jit(solution)/shard_map/ppermute | solution.py:400
  52.3 1.0 %key_pass.7 = bf16[2,256,128]{2,1,0:T(8,128)(2,1)S(1)} custom-call(bf16[2,256,384]{2,1,0:T(8,128)(2,1)S(1)} %collective-permute-done.3.refs_3_.xkv.kv, bf16[3,256,384]{2,1,0:T(8,128)(2,1)S(1)} %collective-permute-done.1.refs_4_.refs_6_.e0, bf16[3,256,384]{2,1,0:T(8,128)(2,1)S(1)} %collective-permute-done.2.refs_5_.refs_7_.o0, ...), custom_call_target="tpu_custom_call" | custom-call | flops 1 | bytes 1 | tf_op jit(solution)/shard_map/key_pass/pallas_call | solution.py:347
  53.3 1.6 %collective-permute-start.19 = (bf16[2,256,128]{2,1,0:T(8,128)(2,1)S(1)}, bf16[2,256,128]{2,1,0:T(8,128)(2,1)S(1)}, u32[]{:S(2)}, u32[]{:S(2)}) collective-permute-start(bf16[2,256,128]{2,1,0:T(8,128)(2,1)S(1)} %key_pass.7), channel_id=1, source_target_pairs={{0,4},{4,0},{8,12},{12,8},{16,20},{20,16},{24,28},{28,24},{1,5},{5... | collective-permute-start | bytes 393224 | tf_op jit(solution)/shard_map/ppermute | solution.py:400
  54.9 0.8 %key_pass.6 = bf16[2,256,128]{2,1,0:T(8,128)(2,1)S(1)} custom-call(bf16[2,256,384]{2,1,0:T(8,128)(2,1)S(1)} %collective-permute-done.3.refs_3_.xkv.kv, bf16[3,256,384]{2,1,0:T(8,128)(2,1)S(1)} %collective-permute-done.1.refs_4_.refs_6_.e0, bf16[3,256,384]{2,1,0:T(8,128)(2,1)S(1)} %collective-permute-done.2.refs_5_.refs_7_.o0, ...), custom_call_target="tpu_custom_call" | custom-call | flops 1 | bytes 1 | tf_op jit(solution)/shard_map/key_pass/pallas_call | solution.py:347
  55.6 0.6 collective-permute-start.18
  56.2 0.8 %key_pass.5 = bf16[2,256,128]{2,1,0:T(8,128)(2,1)S(1)} custom-call(bf16[2,256,384]{2,1,0:T(8,128)(2,1)S(1)} %collective-permute-done.3.refs_3_.xkv.kv, bf16[3,256,384]{2,1,0:T(8,128)(2,1)S(1)} %collective-permute-done.1.refs_4_.refs_6_.e0, bf16[3,256,384]{2,1,0:T(8,128)(2,1)S(1)} %collective-permute-done.2.refs_5_.refs_7_.o0, ...), custom_call_target="tpu_custom_call" | custom-call | flops 1 | bytes 1 | tf_op jit(solution)/shard_map/key_pass/pallas_call | solution.py:347
  57.0 1.6 %collective-permute-start.17 = (bf16[2,256,128]{2,1,0:T(8,128)(2,1)S(1)}, bf16[2,256,128]{2,1,0:T(8,128)(2,1)S(1)}, u32[]{:S(2)}, u32[]{:S(2)}) collective-permute-start(bf16[2,256,128]{2,1,0:T(8,128)(2,1)S(1)} %key_pass.5), channel_id=1, source_target_pairs={{0,4},{4,0},{8,12},{12,8},{16,20},{20,16},{24,28},{28,24},{1,5},{5... | collective-permute-start | bytes 393224 | tf_op jit(solution)/shard_map/ppermute | solution.py:400
  58.6 1.9 %key_pass.4.kv_keep = bf16[2,256,384]{2,1,0:T(8,128)(2,1)S(1)} custom-call(bf16[3,256,384]{2,1,0:T(8,128)(2,1)S(1)} %copy-done, bf16[3,256,384]{2,1,0:T(8,128)(2,1)S(1)} %collective-permute-done.1.refs_4_.refs_6_.e0, bf16[3,256,384]{2,1,0:T(8,128)(2,1)S(1)} %collective-permute-done.2.refs_5_.refs_7_.o0, bf16[1,256,384]{2,1,0:T(8,128)(2,1)S(1)} %collective-permute-done.10.e1, ...), custom_call_target="tpu_custom_call" | custom-call | flops 1 | bytes 1 | tf_op jit(solution)/shard_map/key_pass/pallas_call | solution.py:347
  60.5 1.6 %collective-permute-done.18.refs_1_ = bf16[2,256,128]{2,1,0:T(8,128)(2,1)S(1)} collective-permute-done((bf16[2,256,128]{2,1,0:T(8,128)(2,1)S(1)}, bf16[2,256,128]{2,1,0:T(8,128)(2,1)S(1)}, u32[]{:S(2)}, u32[]{:S(2)}) %collective-permute-start.18) | collective-permute-done | bytes 131104 | tf_op jit(solution)/shard_map/ppermute | solution.py:400
  62.1 2.0 %collective-permute-done.17.refs_0_ = bf16[2,256,128]{2,1,0:T(8,128)(2,1)S(1)} collective-permute-done((bf16[2,256,128]{2,1,0:T(8,128)(2,1)S(1)}, bf16[2,256,128]{2,1,0:T(8,128)(2,1)S(1)}, u32[]{:S(2)}, u32[]{:S(2)}) %collective-permute-start.17) | collective-permute-done | bytes 131104 | tf_op jit(solution)/shard_map/ppermute | solution.py:400
  64.1 1.1 %unpack.1 = (bf16[256,768]{1,0:T(8,128)(2,1)}, bf16[256,768]{1,0:T(8,128)(2,1)}, bf16[256,768]{1,0:T(8,128)(2,1)}) custom-call(bf16[256,384]{1,0:T(8,128)(2,1)S(1)} %get-tuple-element.38.q_keep, bf16[256,384]{1,0:T(8,128)(2,1)S(1)} %collective-permute-done.12.q_got, bf16[2,256,384]{2,1,0:T(8,128)(2,1)S(1)} %key_pass.4.kv_keep, ...), custom_call_target="tpu_custom_call" | custom-call | flops 1 | bytes 1 | tf_op jit(solution)/shard_map/unpack/pallas_call | solution.py:379
  (25 shorter events, 0.8 us)
Async XLA Ops:
  0.6 8.6 %collective-permute-start.5 = (bf16[256,1536]{1,0:T(8,128)(2,1)}, bf16[256,1536]{1,0:T(8,128)(2,1)S(1)}, u32[]{:S(2)}, u32[]{:S(2)}) collective-permute-start(bf16[256,1536]{1,0:T(8,128)(2,1)} %og.1), channel_id=1, source_target_pairs={{0,1},{1,0},{2,3},{3,2},{4,5},{5,4},{6,7},{7,6},{8,9},{9,8},{10,11... | collective-permute-start | bytes 2359304 | tf_op jit(solution)/shard_map/ppermute | solution.py:397
  1.1 22.6 %collective-permute-start = (bf16[256,1536]{1,0:T(8,128)(2,1)}, bf16[256,1536]{1,0:T(8,128)(2,1)S(1)}, u32[]{:S(2)}, u32[]{:S(2)}) collective-permute-start(bf16[256,1536]{1,0:T(8,128)(2,1)} %og.1), channel_id=1, source_target_pairs={{0,2},{1,3},{2,0},{3,1},{4,6},{5,7},{6,4},{7,5},{8,10},{9,11},{10,... | collective-permute-start | bytes 2359304 | tf_op jit(solution)/shard_map/ppermute | solution.py:397
  6.1 17.6 %collective-permute-start.1 = (bf16[3,256,384]{2,1,0:T(8,128)(2,1)}, bf16[3,256,384]{2,1,0:T(8,128)(2,1)S(1)}, u32[]{:S(2)}, u32[]{:S(2)}) collective-permute-start(bf16[3,256,384]{2,1,0:T(8,128)(2,1)} %get-tuple-element.26.refs_0_.refs_2_.keep.kv), channel_id=1, source_target_pairs={{0,8},{1,9},{2,10},{3,11},{4,12},{5,13},{6,14},{7,15},{8,0},{9,1},... | collective-permute-start | bytes 1769480 | tf_op jit(solution)/shard_map/ppermute | solution.py:414
  7.8 16.0 %collective-permute-start.2 = (bf16[3,256,384]{2,1,0:T(8,128)(2,1)}, bf16[3,256,384]{2,1,0:T(8,128)(2,1)S(1)}, u32[]{:S(2)}, u32[]{:S(2)}) collective-permute-start(bf16[3,256,384]{2,1,0:T(8,128)(2,1)} %get-tuple-element.26.refs_0_.refs_2_.keep.kv), channel_id=1, source_target_pairs={{0,1},{1,0},{2,3},{3,2},{4,5},{5,4},{6,7},{7,6},{8,16},{9,17},{10,... | collective-permute-start | bytes 1769480 | tf_op jit(solution)/shard_map/ppermute | solution.py:414
  7.8 16.0 %collective-permute-start.3 = (bf16[2,256,384]{2,1,0:T(8,128)(2,1)}, bf16[2,256,384]{2,1,0:T(8,128)(2,1)S(1)}, u32[]{:S(2)}, u32[]{:S(2)}) collective-permute-start(bf16[2,256,384]{2,1,0:T(8,128)(2,1)} %get-tuple-element.27), channel_id=1, source_target_pairs={{0,4},{4,0},{8,12},{12,8},{16,20},{20,16},{24,28},{28,24},{1,5},{5... | collective-permute-start | bytes 1179656 | tf_op jit(solution)/shard_map/ppermute | solution.py:400
  9.3 14.5 %collective-permute-start.4 = (bf16[1,256,384]{2,1,0:T(8,128)(2,1)}, bf16[1,256,384]{2,1,0:T(8,128)(2,1)S(1)}, u32[]{:S(2)}, u32[]{:S(2)}) collective-permute-start(bf16[1,256,384]{2,1,0:T(8,128)(2,1)} %get-tuple-element.28), channel_id=1, source_target_pairs={{0,4},{4,0},{8,12},{12,8},{16,20},{20,16},{24,28},{28,24},{1,5},{5... | collective-permute-start | bytes 589832 | tf_op jit(solution)/shard_map/ppermute | solution.py:400
  9.8 1.1 %copy-start.1 = (bf16[256,1536]{1,0:T(8,128)(2,1)S(1)}, bf16[256,1536]{1,0:T(8,128)(2,1)}, u32[]{:S(2)}) copy-start(bf16[256,1536]{1,0:T(8,128)(2,1)} %og.1) | copy-start | bytes 2359300
  23.8 4.6 %collective-permute-start.6 = (bf16[256,1536]{1,0:T(8,128)(2,1)S(1)}, bf16[256,1536]{1,0:T(8,128)(2,1)S(1)}, u32[]{:S(2)}, u32[]{:S(2)}) collective-permute-start(bf16[256,1536]{1,0:T(8,128)(2,1)S(1)} %collective-permute-done.piece), channel_id=1, source_target_pairs={{0,1},{1,0},{2,3},{3,2},{4,5},{5,4},{6,7},{7,6},{8,9},{9,8},{10,11... | collective-permute-start | bytes 2359304 | tf_op jit(solution)/shard_map/ppermute | solution.py:397
  23.8 12.3 %collective-permute-start.7 = (bf16[2,256,384]{2,1,0:T(8,128)(2,1)S(1)}, bf16[2,256,384]{2,1,0:T(8,128)(2,1)S(1)}, u32[]{:S(2)}, u32[]{:S(2)}) collective-permute-start(bf16[2,256,384]{2,1,0:T(8,128)(2,1)S(1)} %collective-permute-done.3.refs_3_.xkv.kv), channel_id=1, source_target_pairs={{0,8},{1,9},{2,10},{3,11},{4,12},{5,13},{6,14},{7,15},{8,0},{9,1},... | collective-permute-start | bytes 1179656 | tf_op jit(solution)/shard_map/ppermute | solution.py:414
  26.1 10.0 %collective-permute-start.8 = (bf16[2,256,384]{2,1,0:T(8,128)(2,1)S(1)}, bf16[2,256,384]{2,1,0:T(8,128)(2,1)S(1)}, u32[]{:S(2)}, u32[]{:S(2)}) collective-permute-start(bf16[2,256,384]{2,1,0:T(8,128)(2,1)S(1)} %collective-permute-done.3.refs_3_.xkv.kv), channel_id=1, source_target_pairs={{0,1},{1,0},{2,3},{3,2},{4,5},{5,4},{6,7},{7,6},{8,16},{9,17},{10,... | collective-permute-start | bytes 1179656 | tf_op jit(solution)/shard_map/ppermute | solution.py:414
  26.3 13.8 %collective-permute-start.10 = (bf16[1,256,384]{2,1,0:T(8,128)(2,1)S(1)}, bf16[1,256,384]{2,1,0:T(8,128)(2,1)S(1)}, u32[]{:S(2)}, u32[]{:S(2)}) collective-permute-start(bf16[1,256,384]{2,1,0:T(8,128)(2,1)S(1)} %collective-permute-done.4.refs_0_.xq), channel_id=1, source_target_pairs={{0,8},{1,9},{2,10},{3,11},{4,12},{5,13},{6,14},{7,15},{8,0},{9,1},... | collective-permute-start | bytes 589832 | tf_op jit(solution)/shard_map/ppermute | solution.py:414
  27.5 12.6 %collective-permute-start.11 = (bf16[1,256,384]{2,1,0:T(8,128)(2,1)S(1)}, bf16[1,256,384]{2,1,0:T(8,128)(2,1)S(1)}, u32[]{:S(2)}, u32[]{:S(2)}) collective-permute-start(bf16[1,256,384]{2,1,0:T(8,128)(2,1)S(1)} %collective-permute-done.4.refs_0_.xq), channel_id=1, source_target_pairs={{0,1},{1,0},{2,3},{3,2},{4,5},{5,4},{6,7},{7,6},{8,16},{9,17},{10,... | collective-permute-start | bytes 589832 | tf_op jit(solution)/shard_map/ppermute | solution.py:414
  28.3 7.8 %copy-start = (bf16[3,256,384]{2,1,0:T(8,128)(2,1)S(1)}, bf16[3,256,384]{2,1,0:T(8,128)(2,1)}, u32[]{:S(2)}) copy-start(bf16[3,256,384]{2,1,0:T(8,128)(2,1)} %get-tuple-element.26.refs_0_.refs_2_.keep.kv) | copy-start | bytes 1769476
  29.2 10.9 %collective-permute-start.9 = (bf16[256,384]{1,0:T(8,128)(2,1)S(1)}, bf16[256,384]{1,0:T(8,128)(2,1)S(1)}, u32[]{:S(2)}, u32[]{:S(2)}) collective-permute-start(bf16[256,384]{1,0:T(8,128)(2,1)S(1)} %get-tuple-element.40), channel_id=1, source_target_pairs={{0,4},{4,0},{8,12},{12,8},{16,20},{20,16},{24,28},{28,24},{1,5},{5... | collective-permute-start | bytes 589832 | tf_op jit(solution)/shard_map/ppermute | solution.py:400
  40.1 12.2 %collective-permute-start.13 = (bf16[2,256,384]{2,1,0:T(8,128)(2,1)S(1)}, bf16[2,256,384]{2,1,0:T(8,128)(2,1)S(1)}, u32[]{:S(2)}, u32[]{:S(2)}) collective-permute-start(bf16[2,256,384]{2,1,0:T(8,128)(2,1)S(1)} %join.1), channel_id=1, source_target_pairs={{0,8},{1,9},{2,10},{3,11},{4,12},{5,13},{6,14},{7,15},{8,0},{9,1},... | collective-permute-start | bytes 1179656 | tf_op jit(solution)/shard_map/ppermute | solution.py:414
  41.9 10.4 %collective-permute-start.14 = (bf16[2,256,384]{2,1,0:T(8,128)(2,1)S(1)}, bf16[2,256,384]{2,1,0:T(8,128)(2,1)S(1)}, u32[]{:S(2)}, u32[]{:S(2)}) collective-permute-start(bf16[2,256,384]{2,1,0:T(8,128)(2,1)S(1)} %join.1), channel_id=1, source_target_pairs={{0,1},{1,0},{2,3},{3,2},{4,5},{5,4},{6,7},{7,6},{8,16},{9,17},{10,... | collective-permute-start | bytes 1179656 | tf_op jit(solution)/shard_map/ppermute | solution.py:414
  44.9 7.4 %collective-permute-start.12 = (bf16[256,384]{1,0:T(8,128)(2,1)S(1)}, bf16[256,384]{1,0:T(8,128)(2,1)S(1)}, u32[]{:S(2)}, u32[]{:S(2)}) collective-permute-start(bf16[256,384]{1,0:T(8,128)(2,1)S(1)} %get-tuple-element.44), channel_id=1, source_target_pairs={{0,4},{4,0},{8,12},{12,8},{16,20},{20,16},{24,28},{28,24},{1,5},{5... | collective-permute-start | bytes 589832 | tf_op jit(solution)/shard_map/ppermute | solution.py:400
  46.5 5.8 %collective-permute-start.15 = (f32[8,512]{1,0:T(8,128)S(1)}, f32[8,512]{1,0:T(8,128)S(1)}, u32[]{:S(2)}, u32[]{:S(2)}) collective-permute-start(f32[8,512]{1,0:T(8,128)S(1)} %get-tuple-element.43.stats), channel_id=1, source_target_pairs={{0,8},{1,9},{2,10},{3,11},{4,12},{5,13},{6,14},{7,15},{8,0},{9,1},... | collective-permute-start | bytes 49160 | tf_op jit(solution)/shard_map/ppermute | solution.py:414
  47.8 4.5 %collective-permute-start.16 = (f32[8,512]{1,0:T(8,128)S(1)}, f32[8,512]{1,0:T(8,128)S(1)}, u32[]{:S(2)}, u32[]{:S(2)}) collective-permute-start(f32[8,512]{1,0:T(8,128)S(1)} %get-tuple-element.43.stats), channel_id=1, source_target_pairs={{0,1},{1,0},{2,3},{3,2},{4,5},{5,4},{6,7},{7,6},{8,16},{9,17},{10,... | collective-permute-start | bytes 49160 | tf_op jit(solution)/shard_map/ppermute | solution.py:414
  53.3 7.2 %collective-permute-start.19 = (bf16[2,256,128]{2,1,0:T(8,128)(2,1)S(1)}, bf16[2,256,128]{2,1,0:T(8,128)(2,1)S(1)}, u32[]{:S(2)}, u32[]{:S(2)}) collective-permute-start(bf16[2,256,128]{2,1,0:T(8,128)(2,1)S(1)} %key_pass.7), channel_id=1, source_target_pairs={{0,4},{4,0},{8,12},{12,8},{16,20},{20,16},{24,28},{28,24},{1,5},{5... | collective-permute-start | bytes 393224 | tf_op jit(solution)/shard_map/ppermute | solution.py:400
  55.6 6.5 %collective-permute-start.18 = (bf16[2,256,128]{2,1,0:T(8,128)(2,1)S(1)}, bf16[2,256,128]{2,1,0:T(8,128)(2,1)S(1)}, u32[]{:S(2)}, u32[]{:S(2)}) collective-permute-start(bf16[2,256,128]{2,1,0:T(8,128)(2,1)S(1)} %key_pass.6), channel_id=1, source_target_pairs={{0,4},{4,0},{8,12},{12,8},{16,20},{20,16},{24,28},{28,24},{1,5},{5... | collective-permute-start | bytes 393224 | tf_op jit(solution)/shard_map/ppermute | solution.py:400
  57.0 7.1 %collective-permute-start.17 = (bf16[2,256,128]{2,1,0:T(8,128)(2,1)S(1)}, bf16[2,256,128]{2,1,0:T(8,128)(2,1)S(1)}, u32[]{:S(2)}, u32[]{:S(2)}) collective-permute-start(bf16[2,256,128]{2,1,0:T(8,128)(2,1)S(1)} %key_pass.5), channel_id=1, source_target_pairs={{0,4},{4,0},{8,12},{12,8},{16,20},{20,16},{24,28},{28,24},{1,5},{5... | collective-permute-start | bytes 393224 | tf_op jit(solution)/shard_map/ppermute | solution.py:400

commit v6 on v5

--- a/solution.py
+++ b/solution.py
@@ -249,7 +249,7 @@
         out_specs=(VM, VM),
         scratch_shapes=[pltpu.VMEM((2, rows, cols), BF16)],
         compiler_params=params(30),
-        cost_estimate=cost(6e9),
+        cost_estimate=cost(6e9 if own else 1),
         name="query_pass",
     )(*operands)
 
@@ -418,11 +418,13 @@
     keep, send_kv, send_q = pack(queries, keys, values)
     xkv = over_x(send_kv)
     e0, o0 = over_z(keep, 0), over_z(keep, 1)
+    xkv, send_q = lax.optimization_barrier((xkv, send_q))
     xq = over_x(send_q)
     acc, wy, wf = first_piece(out_grad, near, out_weight)
     e1, o1 = over_z(xkv, 0), over_z(xkv, 1)
+    y, e0, o0, xq, acc = lax.optimization_barrier((y, e0, o0, xq, acc))
+    xq, e1, o1 = lax.optimization_barrier((xq, e1, o1))
     qe1, qo1 = over_z(xq, 0), over_z(xq, 1)
-    y, e0, o0, xkv, xq, acc = lax.optimization_barrier((y, e0, o0, xkv, xq, acc))
     far = over_mp(y, 1)
     acc = grad_piece(acc, y, wy, False)
     dkeep, dsend = grad_piece(acc, far, wf, True)
@@ -431,8 +433,8 @@
     both_d = join(dkeep, dxr)
     de, do = over_z(both_d, 0), over_z(both_d, 1)
     dq_keep, stats = query_pass(True, keep, dkeep, keep, xkv, e0, o0, e1, o1)
+    dq_send, stats = query_pass(False, xq, dxr, keep, xkv, e1, o1, e0, o0, stats)
     stats, qe1, qo1 = lax.optimization_barrier((stats, qe1, qo1))
-    dq_send, stats = query_pass(False, xq, dxr, keep, xkv, e1, o1, e0, o0, stats)
     se, so = over_z(stats, 0), over_z(stats, 1)
     dq_got = over_x(dq_send)
     sums = own_pass(keep, xkv, xq, dkeep, dxr, stats)

time: 65.4 us -> 67.1 us (1.026)
  starting transfers between devices: 20.5 us -> 22.3 us
    ppermute x10, starting transfers between devices: 8.48 us -> 9.96 us  [over_z(): return lax.ppermute(array, ('ctx', 'mp'), pairs)]
  transfers between devices with their start and end apart: 20 -> 20, of which waited for: 6 -> 5; matrix products, arithmetic and copies ran while one was open for 0% -> 0% of each run, Pallas kernels for 30% -> 29%
where the time goes in v6:
time: 67.1 us; the launch traced here: 66.9 us
  starting transfers between devices  22.3 us (33%)
  Pallas kernels  21.7 us (32%)
  waiting for transfers between devices  20.9 us (31%)
  local copies, waits for them, and re-layouts  1.14 us (2%)
  between operations  0.79 us (1%)
    ppermute x7, waiting for transfers between devices, over_x(): return lax.ppermute(array, 'ctx', [(i, i ^ 1) for i in range(length)])  14.2 us
    ppermute x10, starting transfers between devices, over_z(): return lax.ppermute(array, ('ctx', 'mp'), pairs)  9.96 us
    ppermute x7, starting transfers between devices, over_x(): return lax.ppermute(array, 'ctx', [(i, i ^ 1) for i in range(length)])  9.19 us
    ppermute x10, waiting for transfers between devices, over_z(): return lax.ppermute(array, ('ctx', 'mp'), pairs)  6.73 us
    pallas_call x2, Pallas kernels, query_pass(): pl.pallas_call(functools.partial(query_kernel, HD ** (-0.5), own, before...  5.96 us
    pallas_call x4, Pallas kernels, key_pass(): pl.pallas_call(functools.partial(key_kernel, HD ** (-0.5), own, heads), o...  4.4 us
    pallas_call x1, Pallas kernels, first_piece(): pl.pallas_call(first_kernel, out_shape=(jax.ShapeDtypeStruct((rows, heads...  3.82 us
    ppermute x3, starting transfers between devices, over_mp(): return lax.ppermute(array, 'mp', [(i, i ^ flip) for i in range(lanes)])  3.18 us
  transfers between devices with their start and end apart: 20, of which 5 were waited for; matrix products, arithmetic and copies ran while one was open for 0% of the time, Pallas kernels for 29%

profile of v6, /device:TPU:0, one launch (start us, length us, event | category | flops | bytes accessed | tf_op | source)
XLA Modules:
  0.0 66.9 jit_solution(2552681956345220794)
XLA Ops:
  0.6 0.5 collective-permute-start.5
  1.1 2.6 %collective-permute-start = (bf16[256,1536]{1,0:T(8,128)(2,1)}, bf16[256,1536]{1,0:T(8,128)(2,1)S(1)}, u32[]{:S(2)}, u32[]{:S(2)}) collective-permute-start(bf16[256,1536]{1,0:T(8,128)(2,1)} %og.1), channel_id=1, source_target_pairs={{0,2},{1,3},{2,0},{3,1},{4,6},{5,7},{6,4},{7,5},{8,10},{9,11},{10,... | collective-permute-start | bytes 2359304 | tf_op jit(solution)/shard_map/ppermute | solution.py:397
  3.7 2.4 %pack.1 = (bf16[3,256,384]{2,1,0:T(8,128)(2,1)}, bf16[2,256,384]{2,1,0:T(8,128)(2,1)}, bf16[1,256,384]{2,1,0:T(8,128)(2,1)}) custom-call(bf16[256,768]{1,0:T(8,128)(2,1)} %q.1, bf16[256,768]{1,0:T(8,128)(2,1)} %k.1, bf16[256,768]{1,0:T(8,128)(2,1)} %v.1), custom_call_target="tpu_custom_call" | custom-call | flops 1 | bytes 1 | tf_op jit(solution)/shard_map/pack/pallas_call | solution.py:59
  6.1 1.6 %collective-permute-start.3 = (bf16[2,256,384]{2,1,0:T(8,128)(2,1)}, bf16[2,256,384]{2,1,0:T(8,128)(2,1)S(1)}, u32[]{:S(2)}, u32[]{:S(2)}) collective-permute-start(bf16[2,256,384]{2,1,0:T(8,128)(2,1)} %get-tuple-element.31), channel_id=1, source_target_pairs={{0,4},{4,0},{8,12},{12,8},{16,20},{20,16},{24,28},{28,24},{1,5},{5... | collective-permute-start | bytes 1179656 | tf_op jit(solution)/shard_map/ppermute | solution.py:400
  7.7 1.6 %collective-permute-start.1 = (bf16[3,256,384]{2,1,0:T(8,128)(2,1)}, bf16[3,256,384]{2,1,0:T(8,128)(2,1)S(1)}, u32[]{:S(2)}, u32[]{:S(2)}) collective-permute-start(bf16[3,256,384]{2,1,0:T(8,128)(2,1)} %get-tuple-element.30.refs_0_.refs_2_.keep.kv), channel_id=1, source_target_pairs={{0,8},{1,9},{2,10},{3,11},{4,12},{5,13},{6,14},{7,15},{8,0},{9,1},... | collective-permute-start | bytes 1769480 | tf_op jit(solution)/shard_map/ppermute | solution.py:414
  9.3 8.3 %collective-permute-done.3.refs_3_.xkv.kv = bf16[2,256,384]{2,1,0:T(8,128)(2,1)S(1)} collective-permute-done((bf16[2,256,384]{2,1,0:T(8,128)(2,1)}, bf16[2,256,384]{2,1,0:T(8,128)(2,1)S(1)}, u32[]{:S(2)}, u32[]{:S(2)}) %collective-permute-start.3) | collective-permute-done | bytes 393248 | tf_op jit(solution)/shard_map/ppermute | solution.py:400
  17.6 1.5 %collective-permute-start.4 = (bf16[1,256,384]{2,1,0:T(8,128)(2,1)}, bf16[1,256,384]{2,1,0:T(8,128)(2,1)S(1)}, u32[]{:S(2)}, u32[]{:S(2)}) collective-permute-start(bf16[1,256,384]{2,1,0:T(8,128)(2,1)} %get-tuple-element.33), channel_id=1, source_target_pairs={{0,4},{4,0},{8,12},{12,8},{16,20},{20,16},{24,28},{28,24},{1,5},{5... | collective-permute-start | bytes 589832 | tf_op jit(solution)/shard_map/ppermute | solution.py:400
  19.1 1.1 %copy-done.1 = bf16[256,1536]{1,0:T(8,128)(2,1)S(1)} copy-done((bf16[256,1536]{1,0:T(8,128)(2,1)S(1)}, bf16[256,1536]{1,0:T(8,128)(2,1)}, u32[]{:S(2)}) %copy-start.1) | copy-done | bytes 786456
  20.2 3.8 %head_grad_first.1 = (f32[256,768]{1,0:T(8,128)S(1)}, bf16[768,1536]{1,0:T(8,128)(2,1)S(1)}, bf16[768,1536]{1,0:T(8,128)(2,1)S(1)}) custom-call(bf16[256,1536]{1,0:T(8,128)(2,1)S(1)} %copy-done.1, bf16[256,1536]{1,0:T(8,128)(2,1)S(1)} %collective-permute-done.5.near, bf16[768,6144]{1,0:T(8,128)(2,1)} %w.1), custom_call_target="tpu_custom_call" | custom-call | flops 1 | bytes 1 | tf_op jit(solution)/shard_map/head_grad_first/pallas_call | solution.py:109
  24.2 1.7 %collective-permute-start.7 = (bf16[2,256,384]{2,1,0:T(8,128)(2,1)S(1)}, bf16[2,256,384]{2,1,0:T(8,128)(2,1)S(1)}, u32[]{:S(2)}, u32[]{:S(2)}) collective-permute-start(bf16[2,256,384]{2,1,0:T(8,128)(2,1)S(1)} %collective-permute-done.3.refs_3_.xkv.kv), channel_id=1, source_target_pairs={{0,8},{1,9},{2,10},{3,11},{4,12},{5,13},{6,14},{7,15},{8,0},{9,1},... | collective-permute-start | bytes 1179656 | tf_op jit(solution)/shard_map/ppermute | solution.py:414
  26.0 0.8 %head_grad.2.acc = f32[256,768]{1,0:T(8,128)S(1)} custom-call(f32[256,768]{1,0:T(8,128)S(1)} %get-tuple-element.35.acc, bf16[256,1536]{1,0:T(8,128)(2,1)S(1)} %collective-permute-done.piece, bf16[768,1536]{1,0:T(8,128)(2,1)S(1)} %get-tuple-element.37.w), custom_call_target="tpu_custom_call" | custom-call | flops 1 | bytes 1 | tf_op jit(solution)/shard_map/head_grad/pallas_call | solution.py:146
  26.9 0.9 %head_grad.3 = (bf16[256,384]{1,0:T(8,128)(2,1)S(1)}, bf16[256,384]{1,0:T(8,128)(2,1)S(1)}) custom-call(f32[256,768]{1,0:T(8,128)S(1)} %head_grad.2.acc, bf16[256,1536]{1,0:T(8,128)(2,1)S(1)} %collective-permute-done.6.piece, bf16[768,1536]{1,0:T(8,128)(2,1)S(1)} %get-tuple-element.38.w), custom_call_target="tpu_custom_call" | custom-call | flops 1 | bytes 1 | tf_op jit(solution)/shard_map/head_grad/pallas_call | solution.py:146
  27.7 1.3 %collective-permute-start.9 = (bf16[256,384]{1,0:T(8,128)(2,1)S(1)}, bf16[256,384]{1,0:T(8,128)(2,1)S(1)}, u32[]{:S(2)}, u32[]{:S(2)}) collective-permute-start(bf16[256,384]{1,0:T(8,128)(2,1)S(1)} %get-tuple-element.48), channel_id=1, source_target_pairs={{0,4},{4,0},{8,12},{12,8},{16,20},{20,16},{24,28},{28,24},{1,5},{5... | collective-permute-start | bytes 589832 | tf_op jit(solution)/shard_map/ppermute | solution.py:400
  29.0 6.7 %collective-permute-done.7.refs_6_.refs_4_ = bf16[2,256,384]{2,1,0:T(8,128)(2,1)S(1)} collective-permute-done((bf16[2,256,384]{2,1,0:T(8,128)(2,1)S(1)}, bf16[2,256,384]{2,1,0:T(8,128)(2,1)S(1)}, u32[]{:S(2)}, u32[]{:S(2)}) %collective-permute-start.7) | collective-permute-done | bytes 393248 | tf_op jit(solution)/shard_map/ppermute | solution.py:414
  35.7 2.7 %collective-permute-start.10 = (bf16[1,256,384]{2,1,0:T(8,128)(2,1)S(1)}, bf16[1,256,384]{2,1,0:T(8,128)(2,1)S(1)}, u32[]{:S(2)}, u32[]{:S(2)}) collective-permute-start(bf16[1,256,384]{2,1,0:T(8,128)(2,1)S(1)} %collective-permute-done.4.refs_0_.xq), channel_id=1, source_target_pairs={{0,8},{1,9},{2,10},{3,11},{4,12},{5,13},{6,14},{7,15},{8,0},{9,1},... | collective-permute-start | bytes 589832 | tf_op jit(solution)/shard_map/ppermute | solution.py:414
  38.5 2.1 %collective-permute-start.13 = (bf16[2,256,384]{2,1,0:T(8,128)(2,1)S(1)}, bf16[2,256,384]{2,1,0:T(8,128)(2,1)S(1)}, u32[]{:S(2)}, u32[]{:S(2)}) collective-permute-start(bf16[2,256,384]{2,1,0:T(8,128)(2,1)S(1)} %join.1), channel_id=1, source_target_pairs={{0,8},{1,9},{2,10},{3,11},{4,12},{5,13},{6,14},{7,15},{8,0},{9,1},... | collective-permute-start | bytes 1179656 | tf_op jit(solution)/shard_map/ppermute | solution.py:414
  40.6 3.0 %query_pass.2 = (bf16[256,384]{1,0:T(8,128)(2,1)S(1)}, f32[8,256]{1,0:T(8,128)S(1)}) custom-call(bf16[3,256,384]{2,1,0:T(8,128)(2,1)S(1)} %copy-done, bf16[256,384]{1,0:T(8,128)(2,1)S(1)} %get-tuple-element.39.refs_1_.dkeep.mine, bf16[3,256,384]{2,1,0:T(8,128)(2,1)S(1)} %copy-done, bf16[2,256,384]{2,1,0:T(8,128)(2,1)S(1)} %collective-permute-done.3.refs_3_.xkv.kv, ...), custom_call_target="tpu_custom_call" | custom-call | flops 6000000000 | bytes 1 | tf_op jit(solution)/shard_map/query_pass/pallas_call | solution.py:242
  43.5 3.0 %query_pass.3 = (bf16[256,384]{1,0:T(8,128)(2,1)S(1)}, f32[8,512]{1,0:T(8,128)S(1)}) custom-call(bf16[1,256,384]{2,1,0:T(8,128)(2,1)S(1)} %collective-permute-done.4.refs_0_.xq, bf16[256,384]{1,0:T(8,128)(2,1)S(1)} %collective-permute-done.9.refs_1_.dxr.theirs, bf16[3,256,384]{2,1,0:T(8,128)(2,1)S(1)} %copy-done, ...), custom_call_target="tpu_custom_call" | custom-call | flops 1 | bytes 1 | tf_op jit(solution)/shard_map/query_pass/pallas_call | solution.py:242
  46.5 1.4 %collective-permute-start.12 = (bf16[256,384]{1,0:T(8,128)(2,1)S(1)}, bf16[256,384]{1,0:T(8,128)(2,1)S(1)}, u32[]{:S(2)}, u32[]{:S(2)}) collective-permute-start(bf16[256,384]{1,0:T(8,128)(2,1)S(1)} %get-tuple-element.52), channel_id=1, source_target_pairs={{0,4},{4,0},{8,12},{12,8},{16,20},{20,16},{24,28},{28,24},{1,5},{5... | collective-permute-start | bytes 589832 | tf_op jit(solution)/shard_map/ppermute | solution.py:400
  47.9 1.7 %collective-permute-start.15 = (f32[8,512]{1,0:T(8,128)S(1)}, f32[8,512]{1,0:T(8,128)S(1)}, u32[]{:S(2)}, u32[]{:S(2)}) collective-permute-start(f32[8,512]{1,0:T(8,128)S(1)} %get-tuple-element.51.stats), channel_id=1, source_target_pairs={{0,8},{1,9},{2,10},{3,11},{4,12},{5,13},{6,14},{7,15},{8,0},{9,1},... | collective-permute-start | bytes 49160 | tf_op jit(solution)/shard_map/ppermute | solution.py:414
  49.6 2.3 %own_pass.1.sums = f32[2,2,256,384]{3,2,1,0:T(8,128)S(1)} custom-call(bf16[3,256,384]{2,1,0:T(8,128)(2,1)S(1)} %copy-done, bf16[2,256,384]{2,1,0:T(8,128)(2,1)S(1)} %collective-permute-done.3.refs_3_.xkv.kv, bf16[1,256,384]{2,1,0:T(8,128)(2,1)S(1)} %collective-permute-done.4.refs_0_.xq, bf16[256,384]{1,0:T(8,128)(2,1)S(1)} %get-tuple-element.39.refs_1_.dkeep.mine, ...), custom_call_target="tpu_custom_call" | custom-call | flops 1 | bytes 1 | tf_op jit(solution)/shard_map/own_pass/pallas_call | solution.py:293
  51.9 2.0 %collective-permute-done.12.q_got = bf16[256,384]{1,0:T(8,128)(2,1)S(1)} collective-permute-done((bf16[256,384]{1,0:T(8,128)(2,1)S(1)}, bf16[256,384]{1,0:T(8,128)(2,1)S(1)}, u32[]{:S(2)}, u32[]{:S(2)}) %collective-permute-start.12) | collective-permute-done | bytes 196640 | tf_op jit(solution)/shard_map/ppermute | solution.py:400
  53.9 1.0 %key_pass.7 = bf16[2,256,128]{2,1,0:T(8,128)(2,1)S(1)} custom-call(bf16[2,256,384]{2,1,0:T(8,128)(2,1)S(1)} %collective-permute-done.3.refs_3_.xkv.kv, bf16[3,256,384]{2,1,0:T(8,128)(2,1)S(1)} %collective-permute-done.1.refs_4_.refs_6_.e0, bf16[3,256,384]{2,1,0:T(8,128)(2,1)S(1)} %collective-permute-done.2.refs_5_.refs_7_.o0, ...), custom_call_target="tpu_custom_call" | custom-call | flops 1 | bytes 1 | tf_op jit(solution)/shard_map/key_pass/pallas_call | solution.py:347
  54.9 1.4 %collective-permute-start.19 = (bf16[2,256,128]{2,1,0:T(8,128)(2,1)S(1)}, bf16[2,256,128]{2,1,0:T(8,128)(2,1)S(1)}, u32[]{:S(2)}, u32[]{:S(2)}) collective-permute-start(bf16[2,256,128]{2,1,0:T(8,128)(2,1)S(1)} %key_pass.7), channel_id=1, source_target_pairs={{0,4},{4,0},{8,12},{12,8},{16,20},{20,16},{24,28},{28,24},{1,5},{5... | collective-permute-start | bytes 393224 | tf_op jit(solution)/shard_map/ppermute | solution.py:400
  56.3 0.8 %key_pass.6 = bf16[2,256,128]{2,1,0:T(8,128)(2,1)S(1)} custom-call(bf16[2,256,384]{2,1,0:T(8,128)(2,1)S(1)} %collective-permute-done.3.refs_3_.xkv.kv, bf16[3,256,384]{2,1,0:T(8,128)(2,1)S(1)} %collective-permute-done.1.refs_4_.refs_6_.e0, bf16[3,256,384]{2,1,0:T(8,128)(2,1)S(1)} %collective-permute-done.2.refs_5_.refs_7_.o0, ...), custom_call_target="tpu_custom_call" | custom-call | flops 1 | bytes 1 | tf_op jit(solution)/shard_map/key_pass/pallas_call | solution.py:347
  57.0 0.8 %collective-permute-start.18 = (bf16[2,256,128]{2,1,0:T(8,128)(2,1)S(1)}, bf16[2,256,128]{2,1,0:T(8,128)(2,1)S(1)}, u32[]{:S(2)}, u32[]{:S(2)}) collective-permute-start(bf16[2,256,128]{2,1,0:T(8,128)(2,1)S(1)} %key_pass.6), channel_id=1, source_target_pairs={{0,4},{4,0},{8,12},{12,8},{16,20},{20,16},{24,28},{28,24},{1,5},{5... | collective-permute-start | bytes 393224 | tf_op jit(solution)/shard_map/ppermute | solution.py:400
  57.8 0.8 %key_pass.5 = bf16[2,256,128]{2,1,0:T(8,128)(2,1)S(1)} custom-call(bf16[2,256,384]{2,1,0:T(8,128)(2,1)S(1)} %collective-permute-done.3.refs_3_.xkv.kv, bf16[3,256,384]{2,1,0:T(8,128)(2,1)S(1)} %collective-permute-done.1.refs_4_.refs_6_.e0, bf16[3,256,384]{2,1,0:T(8,128)(2,1)S(1)} %collective-permute-done.2.refs_5_.refs_7_.o0, ...), custom_call_target="tpu_custom_call" | custom-call | flops 1 | bytes 1 | tf_op jit(solution)/shard_map/key_pass/pallas_call | solution.py:347
  58.6 1.4 %collective-permute-start.17 = (bf16[2,256,128]{2,1,0:T(8,128)(2,1)S(1)}, bf16[2,256,128]{2,1,0:T(8,128)(2,1)S(1)}, u32[]{:S(2)}, u32[]{:S(2)}) collective-permute-start(bf16[2,256,128]{2,1,0:T(8,128)(2,1)S(1)} %key_pass.5), channel_id=1, source_target_pairs={{0,4},{4,0},{8,12},{12,8},{16,20},{20,16},{24,28},{28,24},{1,5},{5... | collective-permute-start | bytes 393224 | tf_op jit(solution)/shard_map/ppermute | solution.py:400
  59.9 1.9 %key_pass.4.kv_keep = bf16[2,256,384]{2,1,0:T(8,128)(2,1)S(1)} custom-call(bf16[3,256,384]{2,1,0:T(8,128)(2,1)S(1)} %copy-done, bf16[3,256,384]{2,1,0:T(8,128)(2,1)S(1)} %collective-permute-done.1.refs_4_.refs_6_.e0, bf16[3,256,384]{2,1,0:T(8,128)(2,1)S(1)} %collective-permute-done.2.refs_5_.refs_7_.o0, bf16[1,256,384]{2,1,0:T(8,128)(2,1)S(1)} %collective-permute-done.10.e1, ...), custom_call_target="tpu_custom_call" | custom-call | flops 1 | bytes 1 | tf_op jit(solution)/shard_map/key_pass/pallas_call | solution.py:347
  61.9 2.1 %collective-permute-done.18.refs_1_ = bf16[2,256,128]{2,1,0:T(8,128)(2,1)S(1)} collective-permute-done((bf16[2,256,128]{2,1,0:T(8,128)(2,1)S(1)}, bf16[2,256,128]{2,1,0:T(8,128)(2,1)S(1)}, u32[]{:S(2)}, u32[]{:S(2)}) %collective-permute-start.18) | collective-permute-done | bytes 131104 | tf_op jit(solution)/shard_map/ppermute | solution.py:400
  64.0 1.8 %collective-permute-done.17.refs_0_ = bf16[2,256,128]{2,1,0:T(8,128)(2,1)S(1)} collective-permute-done((bf16[2,256,128]{2,1,0:T(8,128)(2,1)S(1)}, bf16[2,256,128]{2,1,0:T(8,128)(2,1)S(1)}, u32[]{:S(2)}, u32[]{:S(2)}) %collective-permute-start.17) | collective-permute-done | bytes 131104 | tf_op jit(solution)/shard_map/ppermute | solution.py:400
  65.7 1.1 %unpack.1 = (bf16[256,768]{1,0:T(8,128)(2,1)}, bf16[256,768]{1,0:T(8,128)(2,1)}, bf16[256,768]{1,0:T(8,128)(2,1)}) custom-call(bf16[256,384]{1,0:T(8,128)(2,1)S(1)} %get-tuple-element.46.q_keep, bf16[256,384]{1,0:T(8,128)(2,1)S(1)} %collective-permute-done.12.q_got, bf16[2,256,384]{2,1,0:T(8,128)(2,1)S(1)} %key_pass.4.kv_keep, ...), custom_call_target="tpu_custom_call" | custom-call | flops 1 | bytes 1 | tf_op jit(solution)/shard_map/unpack/pallas_call | solution.py:379
  (25 shorter events, 0.3 us)
Async XLA Ops:
  0.6 18.5 %collective-permute-start.5 = (bf16[256,1536]{1,0:T(8,128)(2,1)}, bf16[256,1536]{1,0:T(8,128)(2,1)S(1)}, u32[]{:S(2)}, u32[]{:S(2)}) collective-permute-start(bf16[256,1536]{1,0:T(8,128)(2,1)} %og.1), channel_id=1, source_target_pairs={{0,1},{1,0},{2,3},{3,2},{4,5},{5,4},{6,7},{7,6},{8,9},{9,8},{10,11... | collective-permute-start | bytes 2359304 | tf_op jit(solution)/shard_map/ppermute | solution.py:397
  1.1 22.9 %collective-permute-start = (bf16[256,1536]{1,0:T(8,128)(2,1)}, bf16[256,1536]{1,0:T(8,128)(2,1)S(1)}, u32[]{:S(2)}, u32[]{:S(2)}) collective-permute-start(bf16[256,1536]{1,0:T(8,128)(2,1)} %og.1), channel_id=1, source_target_pairs={{0,2},{1,3},{2,0},{3,1},{4,6},{5,7},{6,4},{7,5},{8,10},{9,11},{10,... | collective-permute-start | bytes 2359304 | tf_op jit(solution)/shard_map/ppermute | solution.py:397
  6.1 11.5 %collective-permute-start.3 = (bf16[2,256,384]{2,1,0:T(8,128)(2,1)}, bf16[2,256,384]{2,1,0:T(8,128)(2,1)S(1)}, u32[]{:S(2)}, u32[]{:S(2)}) collective-permute-start(bf16[2,256,384]{2,1,0:T(8,128)(2,1)} %get-tuple-element.31), channel_id=1, source_target_pairs={{0,4},{4,0},{8,12},{12,8},{16,20},{20,16},{24,28},{28,24},{1,5},{5... | collective-permute-start | bytes 1179656 | tf_op jit(solution)/shard_map/ppermute | solution.py:400
  7.7 16.4 %collective-permute-start.1 = (bf16[3,256,384]{2,1,0:T(8,128)(2,1)}, bf16[3,256,384]{2,1,0:T(8,128)(2,1)S(1)}, u32[]{:S(2)}, u32[]{:S(2)}) collective-permute-start(bf16[3,256,384]{2,1,0:T(8,128)(2,1)} %get-tuple-element.30.refs_0_.refs_2_.keep.kv), channel_id=1, source_target_pairs={{0,8},{1,9},{2,10},{3,11},{4,12},{5,13},{6,14},{7,15},{8,0},{9,1},... | collective-permute-start | bytes 1769480 | tf_op jit(solution)/shard_map/ppermute | solution.py:414
  9.3 14.8 %collective-permute-start.2 = (bf16[3,256,384]{2,1,0:T(8,128)(2,1)}, bf16[3,256,384]{2,1,0:T(8,128)(2,1)S(1)}, u32[]{:S(2)}, u32[]{:S(2)}) collective-permute-start(bf16[3,256,384]{2,1,0:T(8,128)(2,1)} %get-tuple-element.30.refs_0_.refs_2_.keep.kv), channel_id=1, source_target_pairs={{0,1},{1,0},{2,3},{3,2},{4,5},{5,4},{6,7},{7,6},{8,16},{9,17},{10,... | collective-permute-start | bytes 1769480 | tf_op jit(solution)/shard_map/ppermute | solution.py:414
  17.6 6.5 %collective-permute-start.4 = (bf16[1,256,384]{2,1,0:T(8,128)(2,1)}, bf16[1,256,384]{2,1,0:T(8,128)(2,1)S(1)}, u32[]{:S(2)}, u32[]{:S(2)}) collective-permute-start(bf16[1,256,384]{2,1,0:T(8,128)(2,1)} %get-tuple-element.33), channel_id=1, source_target_pairs={{0,4},{4,0},{8,12},{12,8},{16,20},{20,16},{24,28},{28,24},{1,5},{5... | collective-permute-start | bytes 589832 | tf_op jit(solution)/shard_map/ppermute | solution.py:400
  19.1 1.1 %copy-start.1 = (bf16[256,1536]{1,0:T(8,128)(2,1)S(1)}, bf16[256,1536]{1,0:T(8,128)(2,1)}, u32[]{:S(2)}) copy-start(bf16[256,1536]{1,0:T(8,128)(2,1)} %og.1) | copy-start | bytes 2359300
  24.1 2.7 %collective-permute-start.6 = (bf16[256,1536]{1,0:T(8,128)(2,1)S(1)}, bf16[256,1536]{1,0:T(8,128)(2,1)S(1)}, u32[]{:S(2)}, u32[]{:S(2)}) collective-permute-start(bf16[256,1536]{1,0:T(8,128)(2,1)S(1)} %collective-permute-done.piece), channel_id=1, source_target_pairs={{0,1},{1,0},{2,3},{3,2},{4,5},{5,4},{6,7},{7,6},{8,9},{9,8},{10,11... | collective-permute-start | bytes 2359304 | tf_op jit(solution)/shard_map/ppermute | solution.py:397
  24.2 11.5 %collective-permute-start.7 = (bf16[2,256,384]{2,1,0:T(8,128)(2,1)S(1)}, bf16[2,256,384]{2,1,0:T(8,128)(2,1)S(1)}, u32[]{:S(2)}, u32[]{:S(2)}) collective-permute-start(bf16[2,256,384]{2,1,0:T(8,128)(2,1)S(1)} %collective-permute-done.3.refs_3_.xkv.kv), channel_id=1, source_target_pairs={{0,8},{1,9},{2,10},{3,11},{4,12},{5,13},{6,14},{7,15},{8,0},{9,1},... | collective-permute-start | bytes 1179656 | tf_op jit(solution)/shard_map/ppermute | solution.py:414
  25.9 9.8 %collective-permute-start.8 = (bf16[2,256,384]{2,1,0:T(8,128)(2,1)S(1)}, bf16[2,256,384]{2,1,0:T(8,128)(2,1)S(1)}, u32[]{:S(2)}, u32[]{:S(2)}) collective-permute-start(bf16[2,256,384]{2,1,0:T(8,128)(2,1)S(1)} %collective-permute-done.3.refs_3_.xkv.kv), channel_id=1, source_target_pairs={{0,1},{1,0},{2,3},{3,2},{4,5},{5,4},{6,7},{7,6},{8,16},{9,17},{10,... | collective-permute-start | bytes 1179656 | tf_op jit(solution)/shard_map/ppermute | solution.py:414
  26.8 13.7 %copy-start = (bf16[3,256,384]{2,1,0:T(8,128)(2,1)S(1)}, bf16[3,256,384]{2,1,0:T(8,128)(2,1)}, u32[]{:S(2)}) copy-start(bf16[3,256,384]{2,1,0:T(8,128)(2,1)} %get-tuple-element.30.refs_0_.refs_2_.keep.kv) | copy-start | bytes 1769476
  27.7 10.7 %collective-permute-start.9 = (bf16[256,384]{1,0:T(8,128)(2,1)S(1)}, bf16[256,384]{1,0:T(8,128)(2,1)S(1)}, u32[]{:S(2)}, u32[]{:S(2)}) collective-permute-start(bf16[256,384]{1,0:T(8,128)(2,1)S(1)} %get-tuple-element.48), channel_id=1, source_target_pairs={{0,4},{4,0},{8,12},{12,8},{16,20},{20,16},{24,28},{28,24},{1,5},{5... | collective-permute-start | bytes 589832 | tf_op jit(solution)/shard_map/ppermute | solution.py:400
  35.7 12.2 %collective-permute-start.10 = (bf16[1,256,384]{2,1,0:T(8,128)(2,1)S(1)}, bf16[1,256,384]{2,1,0:T(8,128)(2,1)S(1)}, u32[]{:S(2)}, u32[]{:S(2)}) collective-permute-start(bf16[1,256,384]{2,1,0:T(8,128)(2,1)S(1)} %collective-permute-done.4.refs_0_.xq), channel_id=1, source_target_pairs={{0,8},{1,9},{2,10},{3,11},{4,12},{5,13},{6,14},{7,15},{8,0},{9,1},... | collective-permute-start | bytes 589832 | tf_op jit(solution)/shard_map/ppermute | solution.py:414
  38.4 9.5 %collective-permute-start.11 = (bf16[1,256,384]{2,1,0:T(8,128)(2,1)S(1)}, bf16[1,256,384]{2,1,0:T(8,128)(2,1)S(1)}, u32[]{:S(2)}, u32[]{:S(2)}) collective-permute-start(bf16[1,256,384]{2,1,0:T(8,128)(2,1)S(1)} %collective-permute-done.4.refs_0_.xq), channel_id=1, source_target_pairs={{0,1},{1,0},{2,3},{3,2},{4,5},{5,4},{6,7},{7,6},{8,16},{9,17},{10,... | collective-permute-start | bytes 589832 | tf_op jit(solution)/shard_map/ppermute | solution.py:414
  38.5 15.5 %collective-permute-start.13 = (bf16[2,256,384]{2,1,0:T(8,128)(2,1)S(1)}, bf16[2,256,384]{2,1,0:T(8,128)(2,1)S(1)}, u32[]{:S(2)}, u32[]{:S(2)}) collective-permute-start(bf16[2,256,384]{2,1,0:T(8,128)(2,1)S(1)} %join.1), channel_id=1, source_target_pairs={{0,8},{1,9},{2,10},{3,11},{4,12},{5,13},{6,14},{7,15},{8,0},{9,1},... | collective-permute-start | bytes 1179656 | tf_op jit(solution)/shard_map/ppermute | solution.py:414
  40.5 13.4 %collective-permute-start.14 = (bf16[2,256,384]{2,1,0:T(8,128)(2,1)S(1)}, bf16[2,256,384]{2,1,0:T(8,128)(2,1)S(1)}, u32[]{:S(2)}, u32[]{:S(2)}) collective-permute-start(bf16[2,256,384]{2,1,0:T(8,128)(2,1)S(1)} %join.1), channel_id=1, source_target_pairs={{0,1},{1,0},{2,3},{3,2},{4,5},{5,4},{6,7},{7,6},{8,16},{9,17},{10,... | collective-permute-start | bytes 1179656 | tf_op jit(solution)/shard_map/ppermute | solution.py:414
  46.5 7.4 %collective-permute-start.12 = (bf16[256,384]{1,0:T(8,128)(2,1)S(1)}, bf16[256,384]{1,0:T(8,128)(2,1)S(1)}, u32[]{:S(2)}, u32[]{:S(2)}) collective-permute-start(bf16[256,384]{1,0:T(8,128)(2,1)S(1)} %get-tuple-element.52), channel_id=1, source_target_pairs={{0,4},{4,0},{8,12},{12,8},{16,20},{20,16},{24,28},{28,24},{1,5},{5... | collective-permute-start | bytes 589832 | tf_op jit(solution)/shard_map/ppermute | solution.py:400
  47.9 6.0 %collective-permute-start.15 = (f32[8,512]{1,0:T(8,128)S(1)}, f32[8,512]{1,0:T(8,128)S(1)}, u32[]{:S(2)}, u32[]{:S(2)}) collective-permute-start(f32[8,512]{1,0:T(8,128)S(1)} %get-tuple-element.51.stats), channel_id=1, source_target_pairs={{0,8},{1,9},{2,10},{3,11},{4,12},{5,13},{6,14},{7,15},{8,0},{9,1},... | collective-permute-start | bytes 49160 | tf_op jit(solution)/shard_map/ppermute | solution.py:414
  49.6 4.3 %collective-permute-start.16 = (f32[8,512]{1,0:T(8,128)S(1)}, f32[8,512]{1,0:T(8,128)S(1)}, u32[]{:S(2)}, u32[]{:S(2)}) collective-permute-start(f32[8,512]{1,0:T(8,128)S(1)} %get-tuple-element.51.stats), channel_id=1, source_target_pairs={{0,1},{1,0},{2,3},{3,2},{4,5},{5,4},{6,7},{7,6},{8,16},{9,17},{10,... | collective-permute-start | bytes 49160 | tf_op jit(solution)/shard_map/ppermute | solution.py:414
  54.9 7.0 %collective-permute-start.19 = (bf16[2,256,128]{2,1,0:T(8,128)(2,1)S(1)}, bf16[2,256,128]{2,1,0:T(8,128)(2,1)S(1)}, u32[]{:S(2)}, u32[]{:S(2)}) collective-permute-start(bf16[2,256,128]{2,1,0:T(8,128)(2,1)S(1)} %key_pass.7), channel_id=1, source_target_pairs={{0,4},{4,0},{8,12},{12,8},{16,20},{20,16},{24,28},{28,24},{1,5},{5... | collective-permute-start | bytes 393224 | tf_op jit(solution)/shard_map/ppermute | solution.py:400
  57.0 6.9 %collective-permute-start.18 = (bf16[2,256,128]{2,1,0:T(8,128)(2,1)S(1)}, bf16[2,256,128]{2,1,0:T(8,128)(2,1)S(1)}, u32[]{:S(2)}, u32[]{:S(2)}) collective-permute-start(bf16[2,256,128]{2,1,0:T(8,128)(2,1)S(1)} %key_pass.6), channel_id=1, source_target_pairs={{0,4},{4,0},{8,12},{12,8},{16,20},{20,16},{24,28},{28,24},{1,5},{5... | collective-permute-start | bytes 393224 | tf_op jit(solution)/shard_map/ppermute | solution.py:400
  58.6 7.1 %collective-permute-start.17 = (bf16[2,256,128]{2,1,0:T(8,128)(2,1)S(1)}, bf16[2,256,128]{2,1,0:T(8,128)(2,1)S(1)}, u32[]{:S(2)}, u32[]{:S(2)}) collective-permute-start(bf16[2,256,128]{2,1,0:T(8,128)(2,1)S(1)} %key_pass.5), channel_id=1, source_target_pairs={{0,4},{4,0},{8,12},{12,8},{16,20},{20,16},{24,28},{28,24},{1,5},{5... | collective-permute-start | bytes 393224 | tf_op jit(solution)/shard_map/ppermute | solution.py:400

commit v7 on v6

--- a/solution.py
+++ b/solution.py
@@ -33,18 +33,18 @@
     return pl.CostEstimate(flops=int(flops), bytes_accessed=1, transcendentals=0)
 
 
-def pack_kernel(q, k, v, keep, send_kv, send_q, sem):
+def pack_kernel(q, k, v, keep, send, sem):
     half = q.shape[1] // 2
     x = lax.rem(lax.axis_index("ctx"), 2)
     mine = pl.ds(pl.multiple_of(x * half, half), half)
     theirs = pl.ds(pl.multiple_of((1 - x) * half, half), half)
     pairs = (
-        (k.at[:, theirs], send_kv.at[0]),
-        (v.at[:, theirs], send_kv.at[1]),
+        (k.at[:, theirs], send.at[0]),
+        (v.at[:, theirs], send.at[1]),
         (k.at[:, mine], keep.at[0]),
         (v.at[:, mine], keep.at[1]),
         (q.at[:, mine], keep.at[2]),
-        (q.at[:, theirs], send_q.at[0]),
+        (q.at[:, theirs], send.at[2]),
     )
     copies = [pltpu.make_async_copy(a, b, sem.at[i]) for i, (a, b) in enumerate(pairs)]
     for copy in copies:
@@ -55,12 +55,12 @@
 
 def pack(q, k, v):
     rows, cols = q.shape
-    three, two, one = (jax.ShapeDtypeStruct((n, rows, cols // 2), BF16) for n in (3, 2, 1))
+    part = jax.ShapeDtypeStruct((3, rows, cols // 2), BF16)
     return pl.pallas_call(
         pack_kernel,
-        out_shape=(three, two, one),
+        out_shape=(part, part),
         in_specs=[ANY] * 3,
-        out_specs=(VM,) * 3,
+        out_specs=(VM,) * 2,
         scratch_shapes=[pltpu.SemaphoreType.DMA((6,))],
         compiler_params=params(60),
         cost_estimate=cost(),
@@ -152,6 +152,23 @@
         cost_estimate=cost(),
         name="head_grad",
     )(acc, piece, w)
+
+
+def after_kernel(value, other, out):
+    del value, other, out
+
+
+def after(value, other):
+    return pl.pallas_call(
+        after_kernel,
+        out_shape=jax.ShapeDtypeStruct(value.shape, value.dtype),
+        in_specs=[ANY, ANY],
+        out_specs=ANY,
+        input_output_aliases={0: 0},
+        compiler_params=params(16),
+        cost_estimate=cost(1e8),
+        name="after",
+    )(value, other)
 
 
 def place():
@@ -268,14 +285,14 @@
     return key_sum, value_sum
 
 
-def own_kernel(scale, keep, xkv, xq, dkeep, dxr, stats, sums):
+def own_kernel(scale, keep, xr, dkeep, dxr, stats, sums):
     rows = keep.shape[1]
     heads = keep.shape[2] // HD
-    for mine, keys in enumerate((keep, xkv)):
+    for mine, keys in enumerate((keep, xr)):
         for head in range(heads):
             cols = slice(head * HD, (head + 1) * HD)
             steps = []
-            for i, (q, d) in enumerate(((keep.at[2], dkeep), (xq.at[0], dxr))):
+            for i, (q, d) in enumerate(((keep.at[2], dkeep), (xr.at[2], dxr))):
                 span = slice(i * rows, (i + 1) * rows)
                 steps.append((
                     q[:, cols],
@@ -293,7 +310,7 @@
     return pl.pallas_call(
         functools.partial(own_kernel, HD ** -0.5),
         out_shape=jax.ShapeDtypeStruct((2, 2, rows, cols), F32),
-        in_specs=[VM] * 6,
+        in_specs=[VM] * 5,
         out_specs=VM,
         compiler_params=params(30),
         cost_estimate=cost(),
@@ -415,16 +432,13 @@
 
     y = over_mp(out_grad, 2)
     near = over_mp(out_grad, 1)
-    keep, send_kv, send_q = pack(queries, keys, values)
-    xkv = over_x(send_kv)
+    keep, send = pack(queries, keys, values)
+    xr = over_x(send)
     e0, o0 = over_z(keep, 0), over_z(keep, 1)
-    xkv, send_q = lax.optimization_barrier((xkv, send_q))
-    xq = over_x(send_q)
     acc, wy, wf = first_piece(out_grad, near, out_weight)
-    e1, o1 = over_z(xkv, 0), over_z(xkv, 1)
-    y, e0, o0, xq, acc = lax.optimization_barrier((y, e0, o0, xq, acc))
-    xq, e1, o1 = lax.optimization_barrier((xq, e1, o1))
-    qe1, qo1 = over_z(xq, 0), over_z(xq, 1)
+    e1, o1 = over_z(xr, 0), over_z(xr, 1)
+    acc = after(acc, xr)
+    y, e0, o0, acc = lax.optimization_barrier((y, e0, o0, acc))
     far = over_mp(y, 1)
     acc = grad_piece(acc, y, wy, False)
     dkeep, dsend = grad_piece(acc, far, wf, True)
@@ -432,19 +446,18 @@
 
     both_d = join(dkeep, dxr)
     de, do = over_z(both_d, 0), over_z(both_d, 1)
-    dq_keep, stats = query_pass(True, keep, dkeep, keep, xkv, e0, o0, e1, o1)
-    dq_send, stats = query_pass(False, xq, dxr, keep, xkv, e1, o1, e0, o0, stats)
-    stats, qe1, qo1 = lax.optimization_barrier((stats, qe1, qo1))
+    dq_keep, stats = query_pass(True, keep, dkeep, keep, xr, e0, o0, e1, o1)
+    dq_send, stats = query_pass(False, xr, dxr, keep, xr, e1, o1, e0, o0, stats)
     se, so = over_z(stats, 0), over_z(stats, 1)
     dq_got = over_x(dq_send)
-    sums = own_pass(keep, xkv, xq, dkeep, dxr, stats)
+    sums = own_pass(keep, xr, dkeep, dxr, stats)
     sums, dq_got = lax.optimization_barrier((sums, dq_got))
     heads = dkeep.shape[1] // HD
     got = [
-        over_x(key_pass(False, (head,), xkv, e0, o0, qe1, qo1, de, do, se, so, sums))
+        over_x(key_pass(False, (head,), xr, e0, o0, e1, o1, de, do, se, so, sums))
         for head in range(heads)
     ]
-    kv_keep = key_pass(True, tuple(range(heads)), keep, e0, o0, qe1, qo1, de, do, se, so, sums)
+    kv_keep = key_pass(True, tuple(range(heads)), keep, e0, o0, e1, o1, de, do, se, so, sums)
     return tuple(unpack(dq_keep, dq_got, kv_keep, *got))
 
 

time: 67.1 us -> 65.3 us (0.973)
  starting transfers between devices: 22.3 us -> 16.8 us
  waiting for transfers between devices: 20.9 us -> 24.9 us
    ppermute x7 -> x6, waiting for transfers between devices: 14.2 us -> 20.1 us  [over_x(): return lax.ppermute(array, 'ctx', [(i, i ^ 1) for i in range(length)])]
    ppermute x7 -> x6, starting transfers between devices: 9.19 us -> 5.48 us  [over_x(): return lax.ppermute(array, 'ctx', [(i, i ^ 1) for i in range(length)])]
    ppermute x10 -> x8, waiting for transfers between devices: 6.73 us -> 4.79 us  [over_z(): return lax.ppermute(array, ('ctx', 'mp'), pairs)]
    ppermute x10 -> x8, starting transfers between devices: 9.96 us -> 8.17 us  [over_z(): return lax.ppermute(array, ('ctx', 'mp'), pairs)]
    pallas_call x1 -> x2, Pallas kernels: 2.39 us -> 2.42 us  [the longest x1 2.42 us: pack(): pl.pallas_call(pack_kernel, out_shape=(part, part), in_specs=[ANY] * 3, o...]
  transfers between devices with their start and end apart: 20 -> 17, of which waited for: 5 -> 8; matrix products, arithmetic and copies ran while one was open for 0% -> 0% of each run, Pallas kernels for 29% -> 30%
where the time goes in v7:
time: 65.3 us; the launch traced here: 65.2 us
  waiting for transfers between devices  24.9 us (38%)
  Pallas kernels  21.6 us (33%)
  starting transfers between devices  16.8 us (26%)
  local copies, waits for them, and re-layouts  1.14 us (2%)
  between operations  0.76 us (1%)
    ppermute x6, waiting for transfers between devices, over_x(): return lax.ppermute(array, 'ctx', [(i, i ^ 1) for i in range(length)])  20.1 us
    ppermute x8, starting transfers between devices, over_z(): return lax.ppermute(array, ('ctx', 'mp'), pairs)  8.17 us
    pallas_call x2, Pallas kernels, query_pass(): pl.pallas_call(functools.partial(query_kernel, HD ** (-0.5), own, before...  5.98 us
    ppermute x6, starting transfers between devices, over_x(): return lax.ppermute(array, 'ctx', [(i, i ^ 1) for i in range(length)])  5.48 us
    ppermute x8, waiting for transfers between devices, over_z(): return lax.ppermute(array, ('ctx', 'mp'), pairs)  4.79 us
    pallas_call x4, Pallas kernels, key_pass(): pl.pallas_call(functools.partial(key_kernel, HD ** (-0.5), own, heads), o...  4.27 us
    pallas_call x1, Pallas kernels, first_piece(): pl.pallas_call(first_kernel, out_shape=(jax.ShapeDtypeStruct((rows, heads...  3.82 us
    ppermute x3, starting transfers between devices, over_mp(): return lax.ppermute(array, 'mp', [(i, i ^ flip) for i in range(lanes)])  3.12 us
  transfers between devices with their start and end apart: 17, of which 8 were waited for; matrix products, arithmetic and copies ran while one was open for 0% of the time, Pallas kernels for 30%

profile of v7, /device:TPU:0, one launch (start us, length us, event | category | flops | bytes accessed | tf_op | source)
XLA Modules:
  0.0 65.2 jit_solution(17812558714164550156)
XLA Ops:
  0.6 0.5 collective-permute-start.3
  1.1 2.6 %collective-permute-start = (bf16[256,1536]{1,0:T(8,128)(2,1)}, bf16[256,1536]{1,0:T(8,128)(2,1)S(1)}, u32[]{:S(2)}, u32[]{:S(2)}) collective-permute-start(bf16[256,1536]{1,0:T(8,128)(2,1)} %og.1), channel_id=1, source_target_pairs={{0,2},{1,3},{2,0},{3,1},{4,6},{5,7},{6,4},{7,5},{8,10},{9,11},{10,... | collective-permute-start | bytes 2359304 | tf_op jit(solution)/shard_map/ppermute | solution.py:414
  3.7 2.4 %pack.1 = (bf16[3,256,384]{2,1,0:T(8,128)(2,1)}, bf16[3,256,384]{2,1,0:T(8,128)(2,1)}) custom-call(bf16[256,768]{1,0:T(8,128)(2,1)} %q.1, bf16[256,768]{1,0:T(8,128)(2,1)} %k.1, bf16[256,768]{1,0:T(8,128)(2,1)} %v.1), custom_call_target="tpu_custom_call" | custom-call | flops 1 | bytes 1 | tf_op jit(solution)/shard_map/pack/pallas_call | solution.py:59
  6.2 1.6 %collective-permute-start.4 = (bf16[3,256,384]{2,1,0:T(8,128)(2,1)}, bf16[3,256,384]{2,1,0:T(8,128)(2,1)S(1)}, u32[]{:S(2)}, u32[]{:S(2)}) collective-permute-start(bf16[3,256,384]{2,1,0:T(8,128)(2,1)} %get-tuple-element.22), channel_id=1, source_target_pairs={{0,4},{4,0},{8,12},{12,8},{16,20},{20,16},{24,28},{28,24},{1,5},{5... | collective-permute-start | bytes 1769480 | tf_op jit(solution)/shard_map/ppermute | solution.py:417
  7.7 1.6 %collective-permute-start.1 = (bf16[3,256,384]{2,1,0:T(8,128)(2,1)}, bf16[3,256,384]{2,1,0:T(8,128)(2,1)S(1)}, u32[]{:S(2)}, u32[]{:S(2)}) collective-permute-start(bf16[3,256,384]{2,1,0:T(8,128)(2,1)} %get-tuple-element.20.refs_0_.refs_2_.keep.kv), channel_id=1, source_target_pairs={{0,8},{1,9},{2,10},{3,11},{4,12},{5,13},{6,14},{7,15},{8,0},{9,1},... | collective-permute-start | bytes 1769480 | tf_op jit(solution)/shard_map/ppermute | solution.py:431
  9.3 1.1 %copy-done.1 = bf16[256,1536]{1,0:T(8,128)(2,1)S(1)} copy-done((bf16[256,1536]{1,0:T(8,128)(2,1)S(1)}, bf16[256,1536]{1,0:T(8,128)(2,1)}, u32[]{:S(2)}) %copy-start.1) | copy-done | bytes 786456
  10.4 3.8 %head_grad_first.1 = (f32[256,768]{1,0:T(8,128)S(1)}, bf16[768,1536]{1,0:T(8,128)(2,1)S(1)}, bf16[768,1536]{1,0:T(8,128)(2,1)S(1)}) custom-call(bf16[256,1536]{1,0:T(8,128)(2,1)S(1)} %copy-done.1, bf16[256,1536]{1,0:T(8,128)(2,1)S(1)} %collective-permute-done.3.near, bf16[768,6144]{1,0:T(8,128)(2,1)} %w.1), custom_call_target="tpu_custom_call" | custom-call | flops 1 | bytes 1 | tf_op jit(solution)/shard_map/head_grad_first/pallas_call | solution.py:109
  14.3 7.6 %collective-permute-done.4.other.refs_3_.refs_0_.xr.kv = bf16[3,256,384]{2,1,0:T(8,128)(2,1)S(1)} collective-permute-done((bf16[3,256,384]{2,1,0:T(8,128)(2,1)}, bf16[3,256,384]{2,1,0:T(8,128)(2,1)S(1)}, u32[]{:S(2)}, u32[]{:S(2)}) %collective-permute-start.4) | collective-permute-done | bytes 589856 | tf_op jit(solution)/shard_map/ppermute | solution.py:417
  21.8 1.2 %collective-permute-done.1.refs_4_.refs_6_.e0 = bf16[3,256,384]{2,1,0:T(8,128)(2,1)S(1)} collective-permute-done((bf16[3,256,384]{2,1,0:T(8,128)(2,1)}, bf16[3,256,384]{2,1,0:T(8,128)(2,1)S(1)}, u32[]{:S(2)}, u32[]{:S(2)}) %collective-permute-start.1) | collective-permute-done | bytes 589856 | tf_op jit(solution)/shard_map/ppermute | solution.py:431
  23.1 2.7 %collective-permute-start.6 = (bf16[3,256,384]{2,1,0:T(8,128)(2,1)S(1)}, bf16[3,256,384]{2,1,0:T(8,128)(2,1)S(1)}, u32[]{:S(2)}, u32[]{:S(2)}) collective-permute-start(bf16[3,256,384]{2,1,0:T(8,128)(2,1)S(1)} %collective-permute-done.4.other.refs_3_.refs_0_.xr.kv), channel_id=1, source_target_pairs={{0,8},{1,9},{2,10},{3,11},{4,12},{5,13},{6,14},{7,15},{8,0},{9,1},... | collective-permute-start | bytes 1769480 | tf_op jit(solution)/shard_map/ppermute | solution.py:431
  26.0 0.8 %head_grad.2.acc = f32[256,768]{1,0:T(8,128)S(1)} custom-call(f32[256,768]{1,0:T(8,128)S(1)} %after.1.acc, bf16[256,1536]{1,0:T(8,128)(2,1)S(1)} %collective-permute-done.piece, bf16[768,1536]{1,0:T(8,128)(2,1)S(1)} %get-tuple-element.25.w), custom_call_target="tpu_custom_call" | custom-call | flops 1 | bytes 1 | tf_op jit(solution)/shard_map/head_grad/pallas_call | solution.py:146
  26.9 0.9 %head_grad.3 = (bf16[256,384]{1,0:T(8,128)(2,1)S(1)}, bf16[256,384]{1,0:T(8,128)(2,1)S(1)}) custom-call(f32[256,768]{1,0:T(8,128)S(1)} %head_grad.2.acc, bf16[256,1536]{1,0:T(8,128)(2,1)S(1)} %collective-permute-done.5.piece, bf16[768,1536]{1,0:T(8,128)(2,1)S(1)} %get-tuple-element.26.w), custom_call_target="tpu_custom_call" | custom-call | flops 1 | bytes 1 | tf_op jit(solution)/shard_map/head_grad/pallas_call | solution.py:146
  27.7 0.6 collective-permute-start.8
  28.3 6.6 %collective-permute-done.8.refs_1_.dxr.theirs = bf16[256,384]{1,0:T(8,128)(2,1)S(1)} collective-permute-done((bf16[256,384]{1,0:T(8,128)(2,1)S(1)}, bf16[256,384]{1,0:T(8,128)(2,1)S(1)}, u32[]{:S(2)}, u32[]{:S(2)}) %collective-permute-start.8) | collective-permute-done | bytes 196640 | tf_op jit(solution)/shard_map/ppermute | solution.py:417
  34.9 1.5 %collective-permute-start.10 = (bf16[2,256,384]{2,1,0:T(8,128)(2,1)S(1)}, bf16[2,256,384]{2,1,0:T(8,128)(2,1)S(1)}, u32[]{:S(2)}, u32[]{:S(2)}) collective-permute-start(bf16[2,256,384]{2,1,0:T(8,128)(2,1)S(1)} %join.1), channel_id=1, source_target_pairs={{0,8},{1,9},{2,10},{3,11},{4,12},{5,13},{6,14},{7,15},{8,0},{9,1},... | collective-permute-start | bytes 1179656 | tf_op jit(solution)/shard_map/ppermute | solution.py:431
  36.4 3.6 %collective-permute-done.6.refs_6_.refs_4_.e1 = bf16[3,256,384]{2,1,0:T(8,128)(2,1)S(1)} collective-permute-done((bf16[3,256,384]{2,1,0:T(8,128)(2,1)S(1)}, bf16[3,256,384]{2,1,0:T(8,128)(2,1)S(1)}, u32[]{:S(2)}, u32[]{:S(2)}) %collective-permute-start.6) | collective-permute-done | bytes 589856 | tf_op jit(solution)/shard_map/ppermute | solution.py:431
  40.0 3.0 %query_pass.2 = (bf16[256,384]{1,0:T(8,128)(2,1)S(1)}, f32[8,256]{1,0:T(8,128)S(1)}) custom-call(bf16[3,256,384]{2,1,0:T(8,128)(2,1)S(1)} %copy-done, bf16[256,384]{1,0:T(8,128)(2,1)S(1)} %get-tuple-element.27.refs_1_.dkeep.mine, bf16[3,256,384]{2,1,0:T(8,128)(2,1)S(1)} %copy-done, ...), custom_call_target="tpu_custom_call" | custom-call | flops 6000000000 | bytes 1 | tf_op jit(solution)/shard_map/query_pass/pallas_call | solution.py:259
  43.0 3.0 %query_pass.3 = (bf16[256,384]{1,0:T(8,128)(2,1)S(1)}, f32[8,512]{1,0:T(8,128)S(1)}) custom-call(bf16[3,256,384]{2,1,0:T(8,128)(2,1)S(1)} %collective-permute-done.4.other.refs_3_.refs_0_.xr.kv, bf16[256,384]{1,0:T(8,128)(2,1)S(1)} %collective-permute-done.8.refs_1_.dxr.theirs, bf16[3,256,384]{2,1,0:T(8,128)(2,1)S(1)} %copy-done, ...), custom_call_target="tpu_custom_call" | custom-call | flops 1 | bytes 1 | tf_op jit(solution)/shard_map/query_pass/pallas_call | solution.py:259
  46.0 0.6 collective-permute-start.9
  46.6 2.1 %collective-permute-start.12 = (f32[8,512]{1,0:T(8,128)S(1)}, f32[8,512]{1,0:T(8,128)S(1)}, u32[]{:S(2)}, u32[]{:S(2)}) collective-permute-start(f32[8,512]{1,0:T(8,128)S(1)} %get-tuple-element.33.stats), channel_id=1, source_target_pairs={{0,8},{1,9},{2,10},{3,11},{4,12},{5,13},{6,14},{7,15},{8,0},{9,1},... | collective-permute-start | bytes 49160 | tf_op jit(solution)/shard_map/ppermute | solution.py:431
  48.7 2.3 %own_pass.1.sums = f32[2,2,256,384]{3,2,1,0:T(8,128)S(1)} custom-call(bf16[3,256,384]{2,1,0:T(8,128)(2,1)S(1)} %copy-done, bf16[3,256,384]{2,1,0:T(8,128)(2,1)S(1)} %collective-permute-done.4.other.refs_3_.refs_0_.xr.kv, bf16[256,384]{1,0:T(8,128)(2,1)S(1)} %get-tuple-element.27.refs_1_.dkeep.mine, ...), custom_call_target="tpu_custom_call" | custom-call | flops 1 | bytes 1 | tf_op jit(solution)/shard_map/own_pass/pallas_call | solution.py:310
  51.0 1.6 %collective-permute-done.9.q_got = bf16[256,384]{1,0:T(8,128)(2,1)S(1)} collective-permute-done((bf16[256,384]{1,0:T(8,128)(2,1)S(1)}, bf16[256,384]{1,0:T(8,128)(2,1)S(1)}, u32[]{:S(2)}, u32[]{:S(2)}) %collective-permute-start.9) | collective-permute-done | bytes 196640 | tf_op jit(solution)/shard_map/ppermute | solution.py:417
  52.6 0.8 %key_pass.7 = bf16[2,256,128]{2,1,0:T(8,128)(2,1)S(1)} custom-call(bf16[3,256,384]{2,1,0:T(8,128)(2,1)S(1)} %collective-permute-done.4.other.refs_3_.refs_0_.xr.kv, bf16[3,256,384]{2,1,0:T(8,128)(2,1)S(1)} %collective-permute-done.1.refs_4_.refs_6_.e0, bf16[3,256,384]{2,1,0:T(8,128)(2,1)S(1)} %collective-permute-done.2.refs_5_.refs_7_.o0, ...), custom_call_target="tpu_custom_call" | custom-call | flops 1 | bytes 1 | tf_op jit(solution)/shard_map/key_pass/pallas_call | solution.py:364
  53.4 0.6 collective-permute-start.16
  54.0 0.8 %key_pass.6 = bf16[2,256,128]{2,1,0:T(8,128)(2,1)S(1)} custom-call(bf16[3,256,384]{2,1,0:T(8,128)(2,1)S(1)} %collective-permute-done.4.other.refs_3_.refs_0_.xr.kv, bf16[3,256,384]{2,1,0:T(8,128)(2,1)S(1)} %collective-permute-done.1.refs_4_.refs_6_.e0, bf16[3,256,384]{2,1,0:T(8,128)(2,1)S(1)} %collective-permute-done.2.refs_5_.refs_7_.o0, ...), custom_call_target="tpu_custom_call" | custom-call | flops 1 | bytes 1 | tf_op jit(solution)/shard_map/key_pass/pallas_call | solution.py:364
  54.8 1.6 %collective-permute-start.15 = (bf16[2,256,128]{2,1,0:T(8,128)(2,1)S(1)}, bf16[2,256,128]{2,1,0:T(8,128)(2,1)S(1)}, u32[]{:S(2)}, u32[]{:S(2)}) collective-permute-start(bf16[2,256,128]{2,1,0:T(8,128)(2,1)S(1)} %key_pass.6), channel_id=1, source_target_pairs={{0,4},{4,0},{8,12},{12,8},{16,20},{20,16},{24,28},{28,24},{1,5},{5... | collective-permute-start | bytes 393224 | tf_op jit(solution)/shard_map/ppermute | solution.py:417
  56.4 0.8 %key_pass.5 = bf16[2,256,128]{2,1,0:T(8,128)(2,1)S(1)} custom-call(bf16[3,256,384]{2,1,0:T(8,128)(2,1)S(1)} %collective-permute-done.4.other.refs_3_.refs_0_.xr.kv, bf16[3,256,384]{2,1,0:T(8,128)(2,1)S(1)} %collective-permute-done.1.refs_4_.refs_6_.e0, bf16[3,256,384]{2,1,0:T(8,128)(2,1)S(1)} %collective-permute-done.2.refs_5_.refs_7_.o0, ...), custom_call_target="tpu_custom_call" | custom-call | flops 1 | bytes 1 | tf_op jit(solution)/shard_map/key_pass/pallas_call | solution.py:364
  57.1 0.6 collective-permute-start.14
  57.7 1.9 %key_pass.4.kv_keep = bf16[2,256,384]{2,1,0:T(8,128)(2,1)S(1)} custom-call(bf16[3,256,384]{2,1,0:T(8,128)(2,1)S(1)} %copy-done, bf16[3,256,384]{2,1,0:T(8,128)(2,1)S(1)} %collective-permute-done.1.refs_4_.refs_6_.e0, bf16[3,256,384]{2,1,0:T(8,128)(2,1)S(1)} %collective-permute-done.2.refs_5_.refs_7_.o0, ...), custom_call_target="tpu_custom_call" | custom-call | flops 1 | bytes 1 | tf_op jit(solution)/shard_map/key_pass/pallas_call | solution.py:364
  59.9 2.7 %collective-permute-done.15.refs_1_ = bf16[2,256,128]{2,1,0:T(8,128)(2,1)S(1)} collective-permute-done((bf16[2,256,128]{2,1,0:T(8,128)(2,1)S(1)}, bf16[2,256,128]{2,1,0:T(8,128)(2,1)S(1)}, u32[]{:S(2)}, u32[]{:S(2)}) %collective-permute-start.15) | collective-permute-done | bytes 131104 | tf_op jit(solution)/shard_map/ppermute | solution.py:417
  62.6 1.4 %collective-permute-done.14.refs_0_ = bf16[2,256,128]{2,1,0:T(8,128)(2,1)S(1)} collective-permute-done((bf16[2,256,128]{2,1,0:T(8,128)(2,1)S(1)}, bf16[2,256,128]{2,1,0:T(8,128)(2,1)S(1)}, u32[]{:S(2)}, u32[]{:S(2)}) %collective-permute-start.14) | collective-permute-done | bytes 131104 | tf_op jit(solution)/shard_map/ppermute | solution.py:417
  64.0 1.2 %unpack.1 = (bf16[256,768]{1,0:T(8,128)(2,1)}, bf16[256,768]{1,0:T(8,128)(2,1)}, bf16[256,768]{1,0:T(8,128)(2,1)}) custom-call(bf16[256,384]{1,0:T(8,128)(2,1)S(1)} %get-tuple-element.30.q_keep, bf16[256,384]{1,0:T(8,128)(2,1)S(1)} %collective-permute-done.9.q_got, bf16[2,256,384]{2,1,0:T(8,128)(2,1)S(1)} %key_pass.4.kv_keep, ...), custom_call_target="tpu_custom_call" | custom-call | flops 1 | bytes 1 | tf_op jit(solution)/shard_map/unpack/pallas_call | solution.py:396
  (20 shorter events, 0.5 us)
Async XLA Ops:
  0.6 8.7 %collective-permute-start.3 = (bf16[256,1536]{1,0:T(8,128)(2,1)}, bf16[256,1536]{1,0:T(8,128)(2,1)S(1)}, u32[]{:S(2)}, u32[]{:S(2)}) collective-permute-start(bf16[256,1536]{1,0:T(8,128)(2,1)} %og.1), channel_id=1, source_target_pairs={{0,1},{1,0},{2,3},{3,2},{4,5},{5,4},{6,7},{7,6},{8,9},{9,8},{10,11... | collective-permute-start | bytes 2359304 | tf_op jit(solution)/shard_map/ppermute | solution.py:414
  1.1 21.9 %collective-permute-start = (bf16[256,1536]{1,0:T(8,128)(2,1)}, bf16[256,1536]{1,0:T(8,128)(2,1)S(1)}, u32[]{:S(2)}, u32[]{:S(2)}) collective-permute-start(bf16[256,1536]{1,0:T(8,128)(2,1)} %og.1), channel_id=1, source_target_pairs={{0,2},{1,3},{2,0},{3,1},{4,6},{5,7},{6,4},{7,5},{8,10},{9,11},{10,... | collective-permute-start | bytes 2359304 | tf_op jit(solution)/shard_map/ppermute | solution.py:414
  6.2 15.7 %collective-permute-start.4 = (bf16[3,256,384]{2,1,0:T(8,128)(2,1)}, bf16[3,256,384]{2,1,0:T(8,128)(2,1)S(1)}, u32[]{:S(2)}, u32[]{:S(2)}) collective-permute-start(bf16[3,256,384]{2,1,0:T(8,128)(2,1)} %get-tuple-element.22), channel_id=1, source_target_pairs={{0,4},{4,0},{8,12},{12,8},{16,20},{20,16},{24,28},{28,24},{1,5},{5... | collective-permute-start | bytes 1769480 | tf_op jit(solution)/shard_map/ppermute | solution.py:417
  7.7 15.3 %collective-permute-start.1 = (bf16[3,256,384]{2,1,0:T(8,128)(2,1)}, bf16[3,256,384]{2,1,0:T(8,128)(2,1)S(1)}, u32[]{:S(2)}, u32[]{:S(2)}) collective-permute-start(bf16[3,256,384]{2,1,0:T(8,128)(2,1)} %get-tuple-element.20.refs_0_.refs_2_.keep.kv), channel_id=1, source_target_pairs={{0,8},{1,9},{2,10},{3,11},{4,12},{5,13},{6,14},{7,15},{8,0},{9,1},... | collective-permute-start | bytes 1769480 | tf_op jit(solution)/shard_map/ppermute | solution.py:431
  9.3 13.8 %collective-permute-start.2 = (bf16[3,256,384]{2,1,0:T(8,128)(2,1)}, bf16[3,256,384]{2,1,0:T(8,128)(2,1)S(1)}, u32[]{:S(2)}, u32[]{:S(2)}) collective-permute-start(bf16[3,256,384]{2,1,0:T(8,128)(2,1)} %get-tuple-element.20.refs_0_.refs_2_.keep.kv), channel_id=1, source_target_pairs={{0,1},{1,0},{2,3},{3,2},{4,5},{5,4},{6,7},{7,6},{8,16},{9,17},{10,... | collective-permute-start | bytes 1769480 | tf_op jit(solution)/shard_map/ppermute | solution.py:431
  9.3 1.1 %copy-start.1 = (bf16[256,1536]{1,0:T(8,128)(2,1)S(1)}, bf16[256,1536]{1,0:T(8,128)(2,1)}, u32[]{:S(2)}) copy-start(bf16[256,1536]{1,0:T(8,128)(2,1)} %og.1) | copy-start | bytes 2359300
  23.1 3.8 %collective-permute-start.5 = (bf16[256,1536]{1,0:T(8,128)(2,1)S(1)}, bf16[256,1536]{1,0:T(8,128)(2,1)S(1)}, u32[]{:S(2)}, u32[]{:S(2)}) collective-permute-start(bf16[256,1536]{1,0:T(8,128)(2,1)S(1)} %collective-permute-done.piece), channel_id=1, source_target_pairs={{0,1},{1,0},{2,3},{3,2},{4,5},{5,4},{6,7},{7,6},{8,9},{9,8},{10,11... | collective-permute-start | bytes 2359304 | tf_op jit(solution)/shard_map/ppermute | solution.py:414
  23.1 16.9 %collective-permute-start.6 = (bf16[3,256,384]{2,1,0:T(8,128)(2,1)S(1)}, bf16[3,256,384]{2,1,0:T(8,128)(2,1)S(1)}, u32[]{:S(2)}, u32[]{:S(2)}) collective-permute-start(bf16[3,256,384]{2,1,0:T(8,128)(2,1)S(1)} %collective-permute-done.4.other.refs_3_.refs_0_.xr.kv), channel_id=1, source_target_pairs={{0,8},{1,9},{2,10},{3,11},{4,12},{5,13},{6,14},{7,15},{8,0},{9,1},... | collective-permute-start | bytes 1769480 | tf_op jit(solution)/shard_map/ppermute | solution.py:431
  25.8 14.2 %collective-permute-start.7 = (bf16[3,256,384]{2,1,0:T(8,128)(2,1)S(1)}, bf16[3,256,384]{2,1,0:T(8,128)(2,1)S(1)}, u32[]{:S(2)}, u32[]{:S(2)}) collective-permute-start(bf16[3,256,384]{2,1,0:T(8,128)(2,1)S(1)} %collective-permute-done.4.other.refs_3_.refs_0_.xr.kv), channel_id=1, source_target_pairs={{0,1},{1,0},{2,3},{3,2},{4,5},{5,4},{6,7},{7,6},{8,16},{9,17},{10,... | collective-permute-start | bytes 1769480 | tf_op jit(solution)/shard_map/ppermute | solution.py:431
  26.9 13.1 %copy-start = (bf16[3,256,384]{2,1,0:T(8,128)(2,1)S(1)}, bf16[3,256,384]{2,1,0:T(8,128)(2,1)}, u32[]{:S(2)}) copy-start(bf16[3,256,384]{2,1,0:T(8,128)(2,1)} %get-tuple-element.20.refs_0_.refs_2_.keep.kv) | copy-start | bytes 1769476
  27.7 7.1 %collective-permute-start.8 = (bf16[256,384]{1,0:T(8,128)(2,1)S(1)}, bf16[256,384]{1,0:T(8,128)(2,1)S(1)}, u32[]{:S(2)}, u32[]{:S(2)}) collective-permute-start(bf16[256,384]{1,0:T(8,128)(2,1)S(1)} %get-tuple-element.31), channel_id=1, source_target_pairs={{0,4},{4,0},{8,12},{12,8},{16,20},{20,16},{24,28},{28,24},{1,5},{5... | collective-permute-start | bytes 589832 | tf_op jit(solution)/shard_map/ppermute | solution.py:417
  34.9 17.7 %collective-permute-start.10 = (bf16[2,256,384]{2,1,0:T(8,128)(2,1)S(1)}, bf16[2,256,384]{2,1,0:T(8,128)(2,1)S(1)}, u32[]{:S(2)}, u32[]{:S(2)}) collective-permute-start(bf16[2,256,384]{2,1,0:T(8,128)(2,1)S(1)} %join.1), channel_id=1, source_target_pairs={{0,8},{1,9},{2,10},{3,11},{4,12},{5,13},{6,14},{7,15},{8,0},{9,1},... | collective-permute-start | bytes 1179656 | tf_op jit(solution)/shard_map/ppermute | solution.py:431
  36.4 16.2 %collective-permute-start.11 = (bf16[2,256,384]{2,1,0:T(8,128)(2,1)S(1)}, bf16[2,256,384]{2,1,0:T(8,128)(2,1)S(1)}, u32[]{:S(2)}, u32[]{:S(2)}) collective-permute-start(bf16[2,256,384]{2,1,0:T(8,128)(2,1)S(1)} %join.1), channel_id=1, source_target_pairs={{0,1},{1,0},{2,3},{3,2},{4,5},{5,4},{6,7},{7,6},{8,16},{9,17},{10,... | collective-permute-start | bytes 1179656 | tf_op jit(solution)/shard_map/ppermute | solution.py:431
  46.0 6.6 %collective-permute-start.9 = (bf16[256,384]{1,0:T(8,128)(2,1)S(1)}, bf16[256,384]{1,0:T(8,128)(2,1)S(1)}, u32[]{:S(2)}, u32[]{:S(2)}) collective-permute-start(bf16[256,384]{1,0:T(8,128)(2,1)S(1)} %get-tuple-element.34), channel_id=1, source_target_pairs={{0,4},{4,0},{8,12},{12,8},{16,20},{20,16},{24,28},{28,24},{1,5},{5... | collective-permute-start | bytes 589832 | tf_op jit(solution)/shard_map/ppermute | solution.py:417
  46.6 6.0 %collective-permute-start.12 = (f32[8,512]{1,0:T(8,128)S(1)}, f32[8,512]{1,0:T(8,128)S(1)}, u32[]{:S(2)}, u32[]{:S(2)}) collective-permute-start(f32[8,512]{1,0:T(8,128)S(1)} %get-tuple-element.33.stats), channel_id=1, source_target_pairs={{0,8},{1,9},{2,10},{3,11},{4,12},{5,13},{6,14},{7,15},{8,0},{9,1},... | collective-permute-start | bytes 49160 | tf_op jit(solution)/shard_map/ppermute | solution.py:431
  48.7 3.9 %collective-permute-start.13 = (f32[8,512]{1,0:T(8,128)S(1)}, f32[8,512]{1,0:T(8,128)S(1)}, u32[]{:S(2)}, u32[]{:S(2)}) collective-permute-start(f32[8,512]{1,0:T(8,128)S(1)} %get-tuple-element.33.stats), channel_id=1, source_target_pairs={{0,1},{1,0},{2,3},{3,2},{4,5},{5,4},{6,7},{7,6},{8,16},{9,17},{10,... | collective-permute-start | bytes 49160 | tf_op jit(solution)/shard_map/ppermute | solution.py:431
  53.4 6.4 %collective-permute-start.16 = (bf16[2,256,128]{2,1,0:T(8,128)(2,1)S(1)}, bf16[2,256,128]{2,1,0:T(8,128)(2,1)S(1)}, u32[]{:S(2)}, u32[]{:S(2)}) collective-permute-start(bf16[2,256,128]{2,1,0:T(8,128)(2,1)S(1)} %key_pass.7), channel_id=1, source_target_pairs={{0,4},{4,0},{8,12},{12,8},{16,20},{20,16},{24,28},{28,24},{1,5},{5... | collective-permute-start | bytes 393224 | tf_op jit(solution)/shard_map/ppermute | solution.py:417
  54.8 7.8 %collective-permute-start.15 = (bf16[2,256,128]{2,1,0:T(8,128)(2,1)S(1)}, bf16[2,256,128]{2,1,0:T(8,128)(2,1)S(1)}, u32[]{:S(2)}, u32[]{:S(2)}) collective-permute-start(bf16[2,256,128]{2,1,0:T(8,128)(2,1)S(1)} %key_pass.6), channel_id=1, source_target_pairs={{0,4},{4,0},{8,12},{12,8},{16,20},{20,16},{24,28},{28,24},{1,5},{5... | collective-permute-start | bytes 393224 | tf_op jit(solution)/shard_map/ppermute | solution.py:417
  57.1 6.8 %collective-permute-start.14 = (bf16[2,256,128]{2,1,0:T(8,128)(2,1)S(1)}, bf16[2,256,128]{2,1,0:T(8,128)(2,1)S(1)}, u32[]{:S(2)}, u32[]{:S(2)}) collective-permute-start(bf16[2,256,128]{2,1,0:T(8,128)(2,1)S(1)} %key_pass.5), channel_id=1, source_target_pairs={{0,4},{4,0},{8,12},{12,8},{16,20},{20,16},{24,28},{28,24},{1,5},{5... | collective-permute-start | bytes 393224 | tf_op jit(solution)/shard_map/ppermute | solution.py:417

commit v8 on v7

--- a/solution.py
+++ b/solution.py
@@ -154,21 +154,17 @@
     )(acc, piece, w)
 
 
-def after_kernel(value, other, out):
-    del value, other, out
-
-
-def after(value, other):
-    return pl.pallas_call(
-        after_kernel,
+def after(value, *others, flops):
+    return pl.pallas_call(
+        lambda *refs: None,
         out_shape=jax.ShapeDtypeStruct(value.shape, value.dtype),
-        in_specs=[ANY, ANY],
+        in_specs=[ANY] * (1 + len(others)),
         out_specs=ANY,
         input_output_aliases={0: 0},
         compiler_params=params(16),
-        cost_estimate=cost(1e8),
+        cost_estimate=cost(flops),
         name="after",
-    )(value, other)
+    )(value, *others)
 
 
 def place():
@@ -437,10 +433,11 @@
     e0, o0 = over_z(keep, 0), over_z(keep, 1)
     acc, wy, wf = first_piece(out_grad, near, out_weight)
     e1, o1 = over_z(xr, 0), over_z(xr, 1)
-    acc = after(acc, xr)
-    y, e0, o0, acc = lax.optimization_barrier((y, e0, o0, acc))
+    acc = after(acc, xr, flops=1e8)
+    y, acc = lax.optimization_barrier((y, acc))
     far = over_mp(y, 1)
     acc = grad_piece(acc, y, wy, False)
+    acc = after(acc, e0, o0, flops=3e9)
     dkeep, dsend = grad_piece(acc, far, wf, True)
     dxr = over_x(dsend)
 
@@ -451,12 +448,12 @@
     se, so = over_z(stats, 0), over_z(stats, 1)
     dq_got = over_x(dq_send)
     sums = own_pass(keep, xr, dkeep, dxr, stats)
-    sums, dq_got = lax.optimization_barrier((sums, dq_got))
     heads = dkeep.shape[1] // HD
-    got = [
-        over_x(key_pass(False, (head,), xr, e0, o0, e1, o1, de, do, se, so, sums))
-        for head in range(heads)
-    ]
+    got = []
+    for head in range(heads):
+        if head == 1:
+            sums, dq_got = lax.optimization_barrier((sums, dq_got))
+        got.append(over_x(key_pass(False, (head,), xr, e0, o0, e1, o1, de, do, se, so, sums)))
     kv_keep = key_pass(True, tuple(range(heads)), keep, e0, o0, e1, o1, de, do, se, so, sums)
     return tuple(unpack(dq_keep, dq_got, kv_keep, *got))
 

time: 65.3 us -> 64.8 us (level)
  waiting for transfers between devices: 24.9 us -> 20.7 us
  starting transfers between devices: 16.8 us -> 20.4 us
    ppermute x6, starting transfers between devices: 5.48 us -> 8.27 us  [over_x(): return lax.ppermute(array, 'ctx', [(i, i ^ 1) for i in range(length)])]
    ppermute x8, waiting for transfers between devices: 4.79 us -> 2.52 us  [over_z(): return lax.ppermute(array, ('ctx', 'mp'), pairs)]
    ppermute x6, waiting for transfers between devices: 20.1 us -> 17.9 us  [over_x(): return lax.ppermute(array, 'ctx', [(i, i ^ 1) for i in range(length)])]
    ppermute x8, starting transfers between devices: 8.17 us -> 8.99 us  [over_z(): return lax.ppermute(array, ('ctx', 'mp'), pairs)]
  transfers between devices with their start and end apart: 17 -> 17, of which waited for: 8 -> 6; matrix products, arithmetic and copies ran while one was open for 0% -> 0% of each run, Pallas kernels for 30% -> 30%
where the time goes in v8:
time: 64.8 us; the launch traced here: 64.6 us
  Pallas kernels  21.6 us (33%)
  waiting for transfers between devices  20.7 us (32%)
  starting transfers between devices  20.4 us (31%)
  local copies, waits for them, and re-layouts  1.14 us (2%)
  between operations  0.81 us (1%)
    ppermute x6, waiting for transfers between devices, over_x(): return lax.ppermute(array, 'ctx', [(i, i ^ 1) for i in range(length)])  17.9 us
    ppermute x8, starting transfers between devices, over_z(): return lax.ppermute(array, ('ctx', 'mp'), pairs)  8.99 us
    ppermute x6, starting transfers between devices, over_x(): return lax.ppermute(array, 'ctx', [(i, i ^ 1) for i in range(length)])  8.27 us
    pallas_call x2, Pallas kernels, query_pass(): pl.pallas_call(functools.partial(query_kernel, HD ** (-0.5), own, before...  5.98 us
    pallas_call x4, Pallas kernels, key_pass(): pl.pallas_call(functools.partial(key_kernel, HD ** (-0.5), own, heads), o...  4.27 us
    pallas_call x1, Pallas kernels, first_piece(): pl.pallas_call(first_kernel, out_shape=(jax.ShapeDtypeStruct((rows, heads...  3.82 us
    ppermute x3, starting transfers between devices, over_mp(): return lax.ppermute(array, 'mp', [(i, i ^ flip) for i in range(lanes)])  3.12 us
    ppermute x8, waiting for transfers between devices, over_z(): return lax.ppermute(array, ('ctx', 'mp'), pairs)  2.52 us
  transfers between devices with their start and end apart: 17, of which 6 were waited for; matrix products, arithmetic and copies ran while one was open for 0% of the time, Pallas kernels for 30%

profile of v8, /device:TPU:0, one launch (start us, length us, event | category | flops | bytes accessed | tf_op | source)
XLA Modules:
  0.0 64.6 jit_solution(4192126856539313771)
XLA Ops:
  0.6 0.5 collective-permute-start.1
  1.1 2.6 %collective-permute-start = (bf16[256,1536]{1,0:T(8,128)(2,1)}, bf16[256,1536]{1,0:T(8,128)(2,1)S(1)}, u32[]{:S(2)}, u32[]{:S(2)}) collective-permute-start(bf16[256,1536]{1,0:T(8,128)(2,1)} %og.1), channel_id=1, source_target_pairs={{0,2},{1,3},{2,0},{3,1},{4,6},{5,7},{6,4},{7,5},{8,10},{9,11},{10,... | collective-permute-start | bytes 2359304 | tf_op jit(solution)/shard_map/ppermute | solution.py:410
  3.7 2.4 %pack.1 = (bf16[3,256,384]{2,1,0:T(8,128)(2,1)}, bf16[3,256,384]{2,1,0:T(8,128)(2,1)}) custom-call(bf16[256,768]{1,0:T(8,128)(2,1)} %q.1, bf16[256,768]{1,0:T(8,128)(2,1)} %k.1, bf16[256,768]{1,0:T(8,128)(2,1)} %v.1), custom_call_target="tpu_custom_call" | custom-call | flops 1 | bytes 1 | tf_op jit(solution)/shard_map/pack/pallas_call | solution.py:59
  6.2 1.6 %collective-permute-start.2 = (bf16[3,256,384]{2,1,0:T(8,128)(2,1)}, bf16[3,256,384]{2,1,0:T(8,128)(2,1)S(1)}, u32[]{:S(2)}, u32[]{:S(2)}) collective-permute-start(bf16[3,256,384]{2,1,0:T(8,128)(2,1)} %get-tuple-element.20), channel_id=1, source_target_pairs={{0,4},{4,0},{8,12},{12,8},{16,20},{20,16},{24,28},{28,24},{1,5},{5... | collective-permute-start | bytes 1769480 | tf_op jit(solution)/shard_map/ppermute | solution.py:413
  7.7 1.6 %collective-permute-start.3 = (bf16[3,256,384]{2,1,0:T(8,128)(2,1)}, bf16[3,256,384]{2,1,0:T(8,128)(2,1)S(1)}, u32[]{:S(2)}, u32[]{:S(2)}) collective-permute-start(bf16[3,256,384]{2,1,0:T(8,128)(2,1)} %get-tuple-element.18.refs_0_.refs_2_.keep.kv), channel_id=1, source_target_pairs={{0,8},{1,9},{2,10},{3,11},{4,12},{5,13},{6,14},{7,15},{8,0},{9,1},... | collective-permute-start | bytes 1769480 | tf_op jit(solution)/shard_map/ppermute | solution.py:427
  9.3 1.1 %copy-done.1 = bf16[256,1536]{1,0:T(8,128)(2,1)S(1)} copy-done((bf16[256,1536]{1,0:T(8,128)(2,1)S(1)}, bf16[256,1536]{1,0:T(8,128)(2,1)}, u32[]{:S(2)}) %copy-start.1) | copy-done | bytes 786456
  10.4 3.8 %head_grad_first.1 = (f32[256,768]{1,0:T(8,128)S(1)}, bf16[768,1536]{1,0:T(8,128)(2,1)S(1)}, bf16[768,1536]{1,0:T(8,128)(2,1)S(1)}) custom-call(bf16[256,1536]{1,0:T(8,128)(2,1)S(1)} %copy-done.1, bf16[256,1536]{1,0:T(8,128)(2,1)S(1)} %collective-permute-done.1.near, bf16[768,6144]{1,0:T(8,128)(2,1)} %w.1), custom_call_target="tpu_custom_call" | custom-call | flops 1 | bytes 1 | tf_op jit(solution)/shard_map/head_grad_first/pallas_call | solution.py:109
  14.3 7.6 %collective-permute-done.2.refs_1_.refs_3_.refs_0_.xr.kv = bf16[3,256,384]{2,1,0:T(8,128)(2,1)S(1)} collective-permute-done((bf16[3,256,384]{2,1,0:T(8,128)(2,1)}, bf16[3,256,384]{2,1,0:T(8,128)(2,1)S(1)}, u32[]{:S(2)}, u32[]{:S(2)}) %collective-permute-start.2) | collective-permute-done | bytes 589856 | tf_op jit(solution)/shard_map/ppermute | solution.py:413
  21.8 0.2 collective-permute-done.piece
  22.1 1.8 %collective-permute-start.6 = (bf16[3,256,384]{2,1,0:T(8,128)(2,1)S(1)}, bf16[3,256,384]{2,1,0:T(8,128)(2,1)S(1)}, u32[]{:S(2)}, u32[]{:S(2)}) collective-permute-start(bf16[3,256,384]{2,1,0:T(8,128)(2,1)S(1)} %collective-permute-done.2.refs_1_.refs_3_.refs_0_.xr.kv), channel_id=1, source_target_pairs={{0,8},{1,9},{2,10},{3,11},{4,12},{5,13},{6,14},{7,15},{8,0},{9,1},... | collective-permute-start | bytes 1769480 | tf_op jit(solution)/shard_map/ppermute | solution.py:427
  23.9 0.2 collective-permute-start.7
  24.1 0.8 %head_grad.2.refs_0_ = f32[256,768]{1,0:T(8,128)S(1)} custom-call(f32[256,768]{1,0:T(8,128)S(1)} %after.2.acc, bf16[256,1536]{1,0:T(8,128)(2,1)S(1)} %collective-permute-done.piece, bf16[768,1536]{1,0:T(8,128)(2,1)S(1)} %get-tuple-element.23.w), custom_call_target="tpu_custom_call" | custom-call | flops 1 | bytes 1 | tf_op jit(solution)/shard_map/head_grad/pallas_call | solution.py:146
  25.0 0.9 %head_grad.3 = (bf16[256,384]{1,0:T(8,128)(2,1)S(1)}, bf16[256,384]{1,0:T(8,128)(2,1)S(1)}) custom-call(f32[256,768]{1,0:T(8,128)S(1)} %after.3.acc, bf16[256,1536]{1,0:T(8,128)(2,1)S(1)} %collective-permute-done.5.piece, bf16[768,1536]{1,0:T(8,128)(2,1)S(1)} %get-tuple-element.24.w), custom_call_target="tpu_custom_call" | custom-call | flops 1 | bytes 1 | tf_op jit(solution)/shard_map/head_grad/pallas_call | solution.py:146
  25.9 1.6 %collective-permute-start.8 = (bf16[256,384]{1,0:T(8,128)(2,1)S(1)}, bf16[256,384]{1,0:T(8,128)(2,1)S(1)}, u32[]{:S(2)}, u32[]{:S(2)}) collective-permute-start(bf16[256,384]{1,0:T(8,128)(2,1)S(1)} %get-tuple-element.27), channel_id=1, source_target_pairs={{0,4},{4,0},{8,12},{12,8},{16,20},{20,16},{24,28},{28,24},{1,5},{5... | collective-permute-start | bytes 589832 | tf_op jit(solution)/shard_map/ppermute | solution.py:413
  27.4 5.6 %collective-permute-done.8.refs_1_.dxr.theirs = bf16[256,384]{1,0:T(8,128)(2,1)S(1)} collective-permute-done((bf16[256,384]{1,0:T(8,128)(2,1)S(1)}, bf16[256,384]{1,0:T(8,128)(2,1)S(1)}, u32[]{:S(2)}, u32[]{:S(2)}) %collective-permute-start.8) | collective-permute-done | bytes 196640 | tf_op jit(solution)/shard_map/ppermute | solution.py:413
  33.0 2.7 %collective-permute-start.10 = (bf16[2,256,384]{2,1,0:T(8,128)(2,1)S(1)}, bf16[2,256,384]{2,1,0:T(8,128)(2,1)S(1)}, u32[]{:S(2)}, u32[]{:S(2)}) collective-permute-start(bf16[2,256,384]{2,1,0:T(8,128)(2,1)S(1)} %join.1), channel_id=1, source_target_pairs={{0,8},{1,9},{2,10},{3,11},{4,12},{5,13},{6,14},{7,15},{8,0},{9,1},... | collective-permute-start | bytes 1179656 | tf_op jit(solution)/shard_map/ppermute | solution.py:427
  35.7 2.5 %collective-permute-done.6.refs_6_.refs_4_.e1 = bf16[3,256,384]{2,1,0:T(8,128)(2,1)S(1)} collective-permute-done((bf16[3,256,384]{2,1,0:T(8,128)(2,1)S(1)}, bf16[3,256,384]{2,1,0:T(8,128)(2,1)S(1)}, u32[]{:S(2)}, u32[]{:S(2)}) %collective-permute-start.6) | collective-permute-done | bytes 589856 | tf_op jit(solution)/shard_map/ppermute | solution.py:427
  38.2 3.0 %query_pass.2 = (bf16[256,384]{1,0:T(8,128)(2,1)S(1)}, f32[8,256]{1,0:T(8,128)S(1)}) custom-call(bf16[3,256,384]{2,1,0:T(8,128)(2,1)S(1)} %copy-done, bf16[256,384]{1,0:T(8,128)(2,1)S(1)} %get-tuple-element.25.refs_1_.dkeep.mine, bf16[3,256,384]{2,1,0:T(8,128)(2,1)S(1)} %copy-done, ...), custom_call_target="tpu_custom_call" | custom-call | flops 6000000000 | bytes 1 | tf_op jit(solution)/shard_map/query_pass/pallas_call | solution.py:255
  41.2 3.0 %query_pass.3 = (bf16[256,384]{1,0:T(8,128)(2,1)S(1)}, f32[8,512]{1,0:T(8,128)S(1)}) custom-call(bf16[3,256,384]{2,1,0:T(8,128)(2,1)S(1)} %collective-permute-done.2.refs_1_.refs_3_.refs_0_.xr.kv, bf16[256,384]{1,0:T(8,128)(2,1)S(1)} %collective-permute-done.8.refs_1_.dxr.theirs, bf16[3,256,384]{2,1,0:T(8,128)(2,1)S(1)} %copy-done, ...), custom_call_target="tpu_custom_call" | custom-call | flops 1 | bytes 1 | tf_op jit(solution)/shard_map/query_pass/pallas_call | solution.py:255
  44.2 1.8 %collective-permute-start.9 = (bf16[256,384]{1,0:T(8,128)(2,1)S(1)}, bf16[256,384]{1,0:T(8,128)(2,1)S(1)}, u32[]{:S(2)}, u32[]{:S(2)}) collective-permute-start(bf16[256,384]{1,0:T(8,128)(2,1)S(1)} %get-tuple-element.30), channel_id=1, source_target_pairs={{0,4},{4,0},{8,12},{12,8},{16,20},{20,16},{24,28},{28,24},{1,5},{5... | collective-permute-start | bytes 589832 | tf_op jit(solution)/shard_map/ppermute | solution.py:413
  46.0 2.7 %collective-permute-start.12 = (f32[8,512]{1,0:T(8,128)S(1)}, f32[8,512]{1,0:T(8,128)S(1)}, u32[]{:S(2)}, u32[]{:S(2)}) collective-permute-start(f32[8,512]{1,0:T(8,128)S(1)} %get-tuple-element.29.stats), channel_id=1, source_target_pairs={{0,8},{1,9},{2,10},{3,11},{4,12},{5,13},{6,14},{7,15},{8,0},{9,1},... | collective-permute-start | bytes 49160 | tf_op jit(solution)/shard_map/ppermute | solution.py:427
  48.7 2.3 %own_pass.1.sums = f32[2,2,256,384]{3,2,1,0:T(8,128)S(1)} custom-call(bf16[3,256,384]{2,1,0:T(8,128)(2,1)S(1)} %copy-done, bf16[3,256,384]{2,1,0:T(8,128)(2,1)S(1)} %collective-permute-done.2.refs_1_.refs_3_.refs_0_.xr.kv, bf16[256,384]{1,0:T(8,128)(2,1)S(1)} %get-tuple-element.25.refs_1_.dkeep.mine, ...), custom_call_target="tpu_custom_call" | custom-call | flops 1 | bytes 1 | tf_op jit(solution)/shard_map/own_pass/pallas_call | solution.py:306
  51.0 0.8 %key_pass.7 = bf16[2,256,128]{2,1,0:T(8,128)(2,1)S(1)} custom-call(bf16[3,256,384]{2,1,0:T(8,128)(2,1)S(1)} %collective-permute-done.2.refs_1_.refs_3_.refs_0_.xr.kv, bf16[3,256,384]{2,1,0:T(8,128)(2,1)S(1)} %collective-permute-done.3.refs_1_.refs_4_.refs_6_.e0, bf16[3,256,384]{2,1,0:T(8,128)(2,1)S(1)} %collective-permute-done.4.refs_2_.refs_5_.refs_7_.o0, ...), custom_call_target="tpu_custom_call" | custom-call | flops 1 | bytes 1 | tf_op jit(solution)/shard_map/key_pass/pallas_call | solution.py:360
  51.8 1.2 %collective-permute-start.16 = (bf16[2,256,128]{2,1,0:T(8,128)(2,1)S(1)}, bf16[2,256,128]{2,1,0:T(8,128)(2,1)S(1)}, u32[]{:S(2)}, u32[]{:S(2)}) collective-permute-start(bf16[2,256,128]{2,1,0:T(8,128)(2,1)S(1)} %key_pass.7), channel_id=1, source_target_pairs={{0,4},{4,0},{8,12},{12,8},{16,20},{20,16},{24,28},{28,24},{1,5},{5... | collective-permute-start | bytes 393224 | tf_op jit(solution)/shard_map/ppermute | solution.py:413
  53.0 0.8 %key_pass.6 = bf16[2,256,128]{2,1,0:T(8,128)(2,1)S(1)} custom-call(bf16[3,256,384]{2,1,0:T(8,128)(2,1)S(1)} %collective-permute-done.2.refs_1_.refs_3_.refs_0_.xr.kv, bf16[3,256,384]{2,1,0:T(8,128)(2,1)S(1)} %collective-permute-done.3.refs_1_.refs_4_.refs_6_.e0, bf16[3,256,384]{2,1,0:T(8,128)(2,1)S(1)} %collective-permute-done.4.refs_2_.refs_5_.refs_7_.o0, ...), custom_call_target="tpu_custom_call" | custom-call | flops 1 | bytes 1 | tf_op jit(solution)/shard_map/key_pass/pallas_call | solution.py:360
  53.8 1.0 %collective-permute-start.15 = (bf16[2,256,128]{2,1,0:T(8,128)(2,1)S(1)}, bf16[2,256,128]{2,1,0:T(8,128)(2,1)S(1)}, u32[]{:S(2)}, u32[]{:S(2)}) collective-permute-start(bf16[2,256,128]{2,1,0:T(8,128)(2,1)S(1)} %key_pass.6), channel_id=1, source_target_pairs={{0,4},{4,0},{8,12},{12,8},{16,20},{20,16},{24,28},{28,24},{1,5},{5... | collective-permute-start | bytes 393224 | tf_op jit(solution)/shard_map/ppermute | solution.py:413
  54.8 0.8 %key_pass.5 = bf16[2,256,128]{2,1,0:T(8,128)(2,1)S(1)} custom-call(bf16[3,256,384]{2,1,0:T(8,128)(2,1)S(1)} %collective-permute-done.2.refs_1_.refs_3_.refs_0_.xr.kv, bf16[3,256,384]{2,1,0:T(8,128)(2,1)S(1)} %collective-permute-done.3.refs_1_.refs_4_.refs_6_.e0, bf16[3,256,384]{2,1,0:T(8,128)(2,1)S(1)} %collective-permute-done.4.refs_2_.refs_5_.refs_7_.o0, ...), custom_call_target="tpu_custom_call" | custom-call | flops 1 | bytes 1 | tf_op jit(solution)/shard_map/key_pass/pallas_call | solution.py:360
  55.6 1.2 %collective-permute-start.14 = (bf16[2,256,128]{2,1,0:T(8,128)(2,1)S(1)}, bf16[2,256,128]{2,1,0:T(8,128)(2,1)S(1)}, u32[]{:S(2)}, u32[]{:S(2)}) collective-permute-start(bf16[2,256,128]{2,1,0:T(8,128)(2,1)S(1)} %key_pass.5), channel_id=1, source_target_pairs={{0,4},{4,0},{8,12},{12,8},{16,20},{20,16},{24,28},{28,24},{1,5},{5... | collective-permute-start | bytes 393224 | tf_op jit(solution)/shard_map/ppermute | solution.py:413
  56.7 1.9 %key_pass.4.kv_keep = bf16[2,256,384]{2,1,0:T(8,128)(2,1)S(1)} custom-call(bf16[3,256,384]{2,1,0:T(8,128)(2,1)S(1)} %copy-done, bf16[3,256,384]{2,1,0:T(8,128)(2,1)S(1)} %collective-permute-done.3.refs_1_.refs_4_.refs_6_.e0, bf16[3,256,384]{2,1,0:T(8,128)(2,1)S(1)} %collective-permute-done.4.refs_2_.refs_5_.refs_7_.o0, ...), custom_call_target="tpu_custom_call" | custom-call | flops 1 | bytes 1 | tf_op jit(solution)/shard_map/key_pass/pallas_call | solution.py:360
  58.7 2.3 %collective-permute-done.15.refs_1_ = bf16[2,256,128]{2,1,0:T(8,128)(2,1)S(1)} collective-permute-done((bf16[2,256,128]{2,1,0:T(8,128)(2,1)S(1)}, bf16[2,256,128]{2,1,0:T(8,128)(2,1)S(1)}, u32[]{:S(2)}, u32[]{:S(2)}) %collective-permute-start.15) | collective-permute-done | bytes 131104 | tf_op jit(solution)/shard_map/ppermute | solution.py:413
  61.0 2.4 %collective-permute-done.14.refs_0_ = bf16[2,256,128]{2,1,0:T(8,128)(2,1)S(1)} collective-permute-done((bf16[2,256,128]{2,1,0:T(8,128)(2,1)S(1)}, bf16[2,256,128]{2,1,0:T(8,128)(2,1)S(1)}, u32[]{:S(2)}, u32[]{:S(2)}) %collective-permute-start.14) | collective-permute-done | bytes 131104 | tf_op jit(solution)/shard_map/ppermute | solution.py:413
  63.4 1.2 %unpack.1 = (bf16[256,768]{1,0:T(8,128)(2,1)}, bf16[256,768]{1,0:T(8,128)(2,1)}, bf16[256,768]{1,0:T(8,128)(2,1)}) custom-call(bf16[256,384]{1,0:T(8,128)(2,1)S(1)} %get-tuple-element.26.q_keep, bf16[256,384]{1,0:T(8,128)(2,1)S(1)} %collective-permute-done.9.q_got, bf16[2,256,384]{2,1,0:T(8,128)(2,1)S(1)} %key_pass.4.kv_keep, ...), custom_call_target="tpu_custom_call" | custom-call | flops 1 | bytes 1 | tf_op jit(solution)/shard_map/unpack/pallas_call | solution.py:392
  (21 shorter events, 0.1 us)
Async XLA Ops:
  0.6 8.7 %collective-permute-start.1 = (bf16[256,1536]{1,0:T(8,128)(2,1)}, bf16[256,1536]{1,0:T(8,128)(2,1)S(1)}, u32[]{:S(2)}, u32[]{:S(2)}) collective-permute-start(bf16[256,1536]{1,0:T(8,128)(2,1)} %og.1), channel_id=1, source_target_pairs={{0,1},{1,0},{2,3},{3,2},{4,5},{5,4},{6,7},{7,6},{8,9},{9,8},{10,11... | collective-permute-start | bytes 2359304 | tf_op jit(solution)/shard_map/ppermute | solution.py:410
  1.1 20.9 %collective-permute-start = (bf16[256,1536]{1,0:T(8,128)(2,1)}, bf16[256,1536]{1,0:T(8,128)(2,1)S(1)}, u32[]{:S(2)}, u32[]{:S(2)}) collective-permute-start(bf16[256,1536]{1,0:T(8,128)(2,1)} %og.1), channel_id=1, source_target_pairs={{0,2},{1,3},{2,0},{3,1},{4,6},{5,7},{6,4},{7,5},{8,10},{9,11},{10,... | collective-permute-start | bytes 2359304 | tf_op jit(solution)/shard_map/ppermute | solution.py:410
  6.2 15.7 %collective-permute-start.2 = (bf16[3,256,384]{2,1,0:T(8,128)(2,1)}, bf16[3,256,384]{2,1,0:T(8,128)(2,1)S(1)}, u32[]{:S(2)}, u32[]{:S(2)}) collective-permute-start(bf16[3,256,384]{2,1,0:T(8,128)(2,1)} %get-tuple-element.20), channel_id=1, source_target_pairs={{0,4},{4,0},{8,12},{12,8},{16,20},{20,16},{24,28},{28,24},{1,5},{5... | collective-permute-start | bytes 1769480 | tf_op jit(solution)/shard_map/ppermute | solution.py:413
  7.7 17.2 %collective-permute-start.3 = (bf16[3,256,384]{2,1,0:T(8,128)(2,1)}, bf16[3,256,384]{2,1,0:T(8,128)(2,1)S(1)}, u32[]{:S(2)}, u32[]{:S(2)}) collective-permute-start(bf16[3,256,384]{2,1,0:T(8,128)(2,1)} %get-tuple-element.18.refs_0_.refs_2_.keep.kv), channel_id=1, source_target_pairs={{0,8},{1,9},{2,10},{3,11},{4,12},{5,13},{6,14},{7,15},{8,0},{9,1},... | collective-permute-start | bytes 1769480 | tf_op jit(solution)/shard_map/ppermute | solution.py:427
  9.3 15.7 %collective-permute-start.4 = (bf16[3,256,384]{2,1,0:T(8,128)(2,1)}, bf16[3,256,384]{2,1,0:T(8,128)(2,1)S(1)}, u32[]{:S(2)}, u32[]{:S(2)}) collective-permute-start(bf16[3,256,384]{2,1,0:T(8,128)(2,1)} %get-tuple-element.18.refs_0_.refs_2_.keep.kv), channel_id=1, source_target_pairs={{0,1},{1,0},{2,3},{3,2},{4,5},{5,4},{6,7},{7,6},{8,16},{9,17},{10,... | collective-permute-start | bytes 1769480 | tf_op jit(solution)/shard_map/ppermute | solution.py:427
  9.3 1.1 %copy-start.1 = (bf16[256,1536]{1,0:T(8,128)(2,1)S(1)}, bf16[256,1536]{1,0:T(8,128)(2,1)}, u32[]{:S(2)}) copy-start(bf16[256,1536]{1,0:T(8,128)(2,1)} %og.1) | copy-start | bytes 2359300
  22.1 2.9 %collective-permute-start.5 = (bf16[256,1536]{1,0:T(8,128)(2,1)S(1)}, bf16[256,1536]{1,0:T(8,128)(2,1)S(1)}, u32[]{:S(2)}, u32[]{:S(2)}) collective-permute-start(bf16[256,1536]{1,0:T(8,128)(2,1)S(1)} %collective-permute-done.piece), channel_id=1, source_target_pairs={{0,1},{1,0},{2,3},{3,2},{4,5},{5,4},{6,7},{7,6},{8,9},{9,8},{10,11... | collective-permute-start | bytes 2359304 | tf_op jit(solution)/shard_map/ppermute | solution.py:410
  22.1 16.1 %collective-permute-start.6 = (bf16[3,256,384]{2,1,0:T(8,128)(2,1)S(1)}, bf16[3,256,384]{2,1,0:T(8,128)(2,1)S(1)}, u32[]{:S(2)}, u32[]{:S(2)}) collective-permute-start(bf16[3,256,384]{2,1,0:T(8,128)(2,1)S(1)} %collective-permute-done.2.refs_1_.refs_3_.refs_0_.xr.kv), channel_id=1, source_target_pairs={{0,8},{1,9},{2,10},{3,11},{4,12},{5,13},{6,14},{7,15},{8,0},{9,1},... | collective-permute-start | bytes 1769480 | tf_op jit(solution)/shard_map/ppermute | solution.py:427
  23.9 14.3 %collective-permute-start.7 = (bf16[3,256,384]{2,1,0:T(8,128)(2,1)S(1)}, bf16[3,256,384]{2,1,0:T(8,128)(2,1)S(1)}, u32[]{:S(2)}, u32[]{:S(2)}) collective-permute-start(bf16[3,256,384]{2,1,0:T(8,128)(2,1)S(1)} %collective-permute-done.2.refs_1_.refs_3_.refs_0_.xr.kv), channel_id=1, source_target_pairs={{0,1},{1,0},{2,3},{3,2},{4,5},{5,4},{6,7},{7,6},{8,16},{9,17},{10,... | collective-permute-start | bytes 1769480 | tf_op jit(solution)/shard_map/ppermute | solution.py:427
  25.0 13.2 %copy-start = (bf16[3,256,384]{2,1,0:T(8,128)(2,1)S(1)}, bf16[3,256,384]{2,1,0:T(8,128)(2,1)}, u32[]{:S(2)}) copy-start(bf16[3,256,384]{2,1,0:T(8,128)(2,1)} %get-tuple-element.18.refs_0_.refs_2_.keep.kv) | copy-start | bytes 1769476
  25.9 7.2 %collective-permute-start.8 = (bf16[256,384]{1,0:T(8,128)(2,1)S(1)}, bf16[256,384]{1,0:T(8,128)(2,1)S(1)}, u32[]{:S(2)}, u32[]{:S(2)}) collective-permute-start(bf16[256,384]{1,0:T(8,128)(2,1)S(1)} %get-tuple-element.27), channel_id=1, source_target_pairs={{0,4},{4,0},{8,12},{12,8},{16,20},{20,16},{24,28},{28,24},{1,5},{5... | collective-permute-start | bytes 589832 | tf_op jit(solution)/shard_map/ppermute | solution.py:413
  33.0 18.0 %collective-permute-start.10 = (bf16[2,256,384]{2,1,0:T(8,128)(2,1)S(1)}, bf16[2,256,384]{2,1,0:T(8,128)(2,1)S(1)}, u32[]{:S(2)}, u32[]{:S(2)}) collective-permute-start(bf16[2,256,384]{2,1,0:T(8,128)(2,1)S(1)} %join.1), channel_id=1, source_target_pairs={{0,8},{1,9},{2,10},{3,11},{4,12},{5,13},{6,14},{7,15},{8,0},{9,1},... | collective-permute-start | bytes 1179656 | tf_op jit(solution)/shard_map/ppermute | solution.py:427
  35.7 15.3 %collective-permute-start.11 = (bf16[2,256,384]{2,1,0:T(8,128)(2,1)S(1)}, bf16[2,256,384]{2,1,0:T(8,128)(2,1)S(1)}, u32[]{:S(2)}, u32[]{:S(2)}) collective-permute-start(bf16[2,256,384]{2,1,0:T(8,128)(2,1)S(1)} %join.1), channel_id=1, source_target_pairs={{0,1},{1,0},{2,3},{3,2},{4,5},{5,4},{6,7},{7,6},{8,16},{9,17},{10,... | collective-permute-start | bytes 1179656 | tf_op jit(solution)/shard_map/ppermute | solution.py:427
  44.2 6.8 %collective-permute-start.9 = (bf16[256,384]{1,0:T(8,128)(2,1)S(1)}, bf16[256,384]{1,0:T(8,128)(2,1)S(1)}, u32[]{:S(2)}, u32[]{:S(2)}) collective-permute-start(bf16[256,384]{1,0:T(8,128)(2,1)S(1)} %get-tuple-element.30), channel_id=1, source_target_pairs={{0,4},{4,0},{8,12},{12,8},{16,20},{20,16},{24,28},{28,24},{1,5},{5... | collective-permute-start | bytes 589832 | tf_op jit(solution)/shard_map/ppermute | solution.py:413
  46.0 5.0 %collective-permute-start.12 = (f32[8,512]{1,0:T(8,128)S(1)}, f32[8,512]{1,0:T(8,128)S(1)}, u32[]{:S(2)}, u32[]{:S(2)}) collective-permute-start(f32[8,512]{1,0:T(8,128)S(1)} %get-tuple-element.29.stats), channel_id=1, source_target_pairs={{0,8},{1,9},{2,10},{3,11},{4,12},{5,13},{6,14},{7,15},{8,0},{9,1},... | collective-permute-start | bytes 49160 | tf_op jit(solution)/shard_map/ppermute | solution.py:427
  48.7 2.3 %collective-permute-start.13 = (f32[8,512]{1,0:T(8,128)S(1)}, f32[8,512]{1,0:T(8,128)S(1)}, u32[]{:S(2)}, u32[]{:S(2)}) collective-permute-start(f32[8,512]{1,0:T(8,128)S(1)} %get-tuple-element.29.stats), channel_id=1, source_target_pairs={{0,1},{1,0},{2,3},{3,2},{4,5},{5,4},{6,7},{7,6},{8,16},{9,17},{10,... | collective-permute-start | bytes 49160 | tf_op jit(solution)/shard_map/ppermute | solution.py:427
  51.8 6.8 %collective-permute-start.16 = (bf16[2,256,128]{2,1,0:T(8,128)(2,1)S(1)}, bf16[2,256,128]{2,1,0:T(8,128)(2,1)S(1)}, u32[]{:S(2)}, u32[]{:S(2)}) collective-permute-start(bf16[2,256,128]{2,1,0:T(8,128)(2,1)S(1)} %key_pass.7), channel_id=1, source_target_pairs={{0,4},{4,0},{8,12},{12,8},{16,20},{20,16},{24,28},{28,24},{1,5},{5... | collective-permute-start | bytes 393224 | tf_op jit(solution)/shard_map/ppermute | solution.py:413
  53.8 7.2 %collective-permute-start.15 = (bf16[2,256,128]{2,1,0:T(8,128)(2,1)S(1)}, bf16[2,256,128]{2,1,0:T(8,128)(2,1)S(1)}, u32[]{:S(2)}, u32[]{:S(2)}) collective-permute-start(bf16[2,256,128]{2,1,0:T(8,128)(2,1)S(1)} %key_pass.6), channel_id=1, source_target_pairs={{0,4},{4,0},{8,12},{12,8},{16,20},{20,16},{24,28},{28,24},{1,5},{5... | collective-permute-start | bytes 393224 | tf_op jit(solution)/shard_map/ppermute | solution.py:413
  55.6 7.9 %collective-permute-start.14 = (bf16[2,256,128]{2,1,0:T(8,128)(2,1)S(1)}, bf16[2,256,128]{2,1,0:T(8,128)(2,1)S(1)}, u32[]{:S(2)}, u32[]{:S(2)}) collective-permute-start(bf16[2,256,128]{2,1,0:T(8,128)(2,1)S(1)} %key_pass.5), channel_id=1, source_target_pairs={{0,4},{4,0},{8,12},{12,8},{16,20},{20,16},{24,28},{28,24},{1,5},{5... | collective-permute-start | bytes 393224 | tf_op jit(solution)/shard_map/ppermute | solution.py:413

commit v9 on v8

--- a/solution.py
+++ b/solution.py
@@ -33,18 +33,18 @@
     return pl.CostEstimate(flops=int(flops), bytes_accessed=1, transcendentals=0)
 
 
-def pack_kernel(q, k, v, keep, send, sem):
+def pack_kernel(q, k, v, keep, send_kv, send_q, sem):
     half = q.shape[1] // 2
     x = lax.rem(lax.axis_index("ctx"), 2)
     mine = pl.ds(pl.multiple_of(x * half, half), half)
     theirs = pl.ds(pl.multiple_of((1 - x) * half, half), half)
     pairs = (
-        (k.at[:, theirs], send.at[0]),
-        (v.at[:, theirs], send.at[1]),
+        (k.at[:, theirs], send_kv.at[0]),
+        (v.at[:, theirs], send_kv.at[1]),
         (k.at[:, mine], keep.at[0]),
         (v.at[:, mine], keep.at[1]),
         (q.at[:, mine], keep.at[2]),
-        (q.at[:, theirs], send.at[2]),
+        (q.at[:, theirs], send_q),
     )
     copies = [pltpu.make_async_copy(a, b, sem.at[i]) for i, (a, b) in enumerate(pairs)]
     for copy in copies:
@@ -55,12 +55,13 @@
 
 def pack(q, k, v):
     rows, cols = q.shape
-    part = jax.ShapeDtypeStruct((3, rows, cols // 2), BF16)
+    three, two = (jax.ShapeDtypeStruct((n, rows, cols // 2), BF16) for n in (3, 2))
+    one = jax.ShapeDtypeStruct((rows, cols // 2), BF16)
     return pl.pallas_call(
         pack_kernel,
-        out_shape=(part, part),
+        out_shape=(three, two, one),
         in_specs=[ANY] * 3,
-        out_specs=(VM,) * 2,
+        out_specs=(VM,) * 3,
         scratch_shapes=[pltpu.SemaphoreType.DMA((6,))],
         compiler_params=params(60),
         cost_estimate=cost(),
@@ -68,21 +69,21 @@
     )(q, k, v)
 
 
-def join_kernel(mine, theirs, out):
-    out[0] = mine[...]
-    out[1] = theirs[...]
-
-
-def join(mine, theirs):
+def join_kernel(first, second, out):
+    out[0] = first[...]
+    out[1] = second[...]
+
+
+def join(first, second):
     return pl.pallas_call(
         join_kernel,
-        out_shape=jax.ShapeDtypeStruct((2, *mine.shape), BF16),
+        out_shape=jax.ShapeDtypeStruct((2, *first.shape), BF16),
         in_specs=[VM] * 2,
         out_specs=VM,
         compiler_params=params(16),
         cost_estimate=cost(),
         name="join",
-    )(mine, theirs)
+    )(first, second)
 
 
 def first_kernel(og, near, w, acc, wy, wf, wbuf, sem):
@@ -186,7 +187,7 @@
 def query_kernel(scale, own, has_marks, *refs):
     refs = list(refs)
     q, d, keep, xr, e, o, e_other, o_other = refs[:8]
-    q = q.at[q.shape[0] - 1]
+    q = q if len(q.shape) == 2 else q.at[2]
     before = refs[8] if has_marks else None
     out, stats, fifth = refs[-3:]
     rows = q.shape[0]
@@ -281,14 +282,14 @@
     return key_sum, value_sum
 
 
-def own_kernel(scale, keep, xr, dkeep, dxr, stats, sums):
+def own_kernel(scale, keep, xkv, xq, dkeep, dxr, stats, sums):
     rows = keep.shape[1]
     heads = keep.shape[2] // HD
-    for mine, keys in enumerate((keep, xr)):
+    for mine, keys in enumerate((keep, xkv)):
         for head in range(heads):
             cols = slice(head * HD, (head + 1) * HD)
             steps = []
-            for i, (q, d) in enumerate(((keep.at[2], dkeep), (xr.at[2], dxr))):
+            for i, (q, d) in enumerate(((keep.at[2], dkeep), (xq, dxr))):
                 span = slice(i * rows, (i + 1) * rows)
                 steps.append((
                     q[:, cols],
@@ -306,7 +307,7 @@
     return pl.pallas_call(
         functools.partial(own_kernel, HD ** -0.5),
         out_shape=jax.ShapeDtypeStruct((2, 2, rows, cols), F32),
-        in_specs=[VM] * 5,
+        in_specs=[VM] * 6,
         out_specs=VM,
         compiler_params=params(30),
         cost_estimate=cost(),
@@ -314,24 +315,24 @@
     )(*operands)
 
 
-def key_kernel(scale, own, heads, kv, e0, o0, e1, o1, de, do, se, so, sums, out, fifth_q, fifth_d):
+def key_kernel(scale, own, heads, kv, e0, o0, mixed_e, mixed_o, de1, do1, se, so, sums, out, fifth_q, fifth_d):
     rows = kv.shape[1]
     even_ok, odd_ok, turned = place()
     from_even = turned if own else jnp.logical_not(turned)
-    even_q = (e0.at[e0.shape[0] - 1], e1.at[e1.shape[0] - 1])
-    odd_q = (o0.at[o0.shape[0] - 1], o1.at[o1.shape[0] - 1])
+    even_q, odd_q = (e0.at[2], mixed_e.at[0]), (o0.at[2], mixed_o.at[0])
+    even_d, odd_d = (mixed_e.at[1], de1), (mixed_o.at[1], do1)
     same, other = (0, 1) if own else (1, 0)
     wanted = slice(heads[0] * HD, (heads[-1] + 1) * HD)
 
     @pl.when(from_even)
     def _():
         fifth_q[...] = even_q[other][:, wanted]
-        fifth_d[...] = de[other, :, wanted]
+        fifth_d[...] = even_d[other][:, wanted]
 
     @pl.when(jnp.logical_not(from_even))
     def _():
         fifth_q[...] = odd_q[other][:, wanted]
-        fifth_d[...] = do[other, :, wanted]
+        fifth_d[...] = odd_d[other][:, wanted]
 
     row = lax.broadcasted_iota(jnp.int32, se.shape, 0)
     nothing = jnp.where(lax.rem(row, 2) == 0, jnp.float32(BIG), jnp.float32(0.0))
@@ -345,8 +346,8 @@
         to = slice(i * HD, (i + 1) * HD)
         a, b = 2 * head, 2 * head + 1
         steps = (
-            (even_q[same][:, cols], de[same, :, cols], even[a : a + 1, span], even[b : b + 1, span]),
-            (odd_q[same][:, cols], do[same, :, cols], odd[a : a + 1, span], odd[b : b + 1, span]),
+            (even_q[same][:, cols], even_d[same][:, cols], even[a : a + 1, span], even[b : b + 1, span]),
+            (odd_q[same][:, cols], odd_d[same][:, cols], odd[a : a + 1, span], odd[b : b + 1, span]),
             (fifth_q[:, to], fifth_d[:, to], fifth[a : a + 1], fifth[b : b + 1]),
         )
         k, v = key_step(scale, kv[0, :, cols], kv[1, :, cols], steps)
@@ -364,7 +365,7 @@
         out_specs=VM,
         scratch_shapes=[pltpu.VMEM((rows, wide), BF16)] * 2,
         compiler_params=params(30),
-        cost_estimate=cost(),
+        cost_estimate=cost(1e9),
         name="key_pass",
     )(kv, *operands)
 
@@ -428,33 +429,38 @@
 
     y = over_mp(out_grad, 2)
     near = over_mp(out_grad, 1)
-    keep, send = pack(queries, keys, values)
-    xr = over_x(send)
+    keep, send_kv, send_q = pack(queries, keys, values)
+    xkv, xq = over_x(send_kv), over_x(send_q)
     e0, o0 = over_z(keep, 0), over_z(keep, 1)
     acc, wy, wf = first_piece(out_grad, near, out_weight)
-    e1, o1 = over_z(xr, 0), over_z(xr, 1)
-    acc = after(acc, xr, flops=1e8)
+    e1, o1 = over_z(xkv, 0), over_z(xkv, 1)
+    acc = after(acc, xkv, flops=1e8)
     y, acc = lax.optimization_barrier((y, acc))
     far = over_mp(y, 1)
     acc = grad_piece(acc, y, wy, False)
     acc = after(acc, e0, o0, flops=3e9)
     dkeep, dsend = grad_piece(acc, far, wf, True)
-    dxr = over_x(dsend)
-
-    both_d = join(dkeep, dxr)
-    de, do = over_z(both_d, 0), over_z(both_d, 1)
-    dq_keep, stats = query_pass(True, keep, dkeep, keep, xr, e0, o0, e1, o1)
-    dq_send, stats = query_pass(False, xr, dxr, keep, xr, e1, o1, e0, o0, stats)
+    dxr = after(over_x(dsend), flops=6e9)
+
+    late_q, e1, o1 = lax.optimization_barrier((xq, e1, o1))
+    mixed = join(late_q, dkeep)
+    mixed_e, mixed_o = over_z(mixed, 0), over_z(mixed, 1)
+    de1, do1 = over_z(dxr, 0), over_z(dxr, 1)
+    dq_keep, stats = query_pass(True, keep, dkeep, keep, xkv, e0, o0, e1, o1)
+    dq_send, stats = query_pass(False, xq, dxr, keep, xkv, e1, o1, e0, o0, stats)
+    stats, mixed_e, mixed_o = lax.optimization_barrier((stats, mixed_e, mixed_o))
     se, so = over_z(stats, 0), over_z(stats, 1)
     dq_got = over_x(dq_send)
-    sums = own_pass(keep, xr, dkeep, dxr, stats)
+    sums = own_pass(keep, xkv, xq, dkeep, dxr, stats)
+    sums = after(sums, de1, do1, flops=3e9)
     heads = dkeep.shape[1] // HD
+    theirs = (e0, o0, mixed_e, mixed_o, de1, do1, se, so)
     got = []
     for head in range(heads):
         if head == 1:
             sums, dq_got = lax.optimization_barrier((sums, dq_got))
-        got.append(over_x(key_pass(False, (head,), xr, e0, o0, e1, o1, de, do, se, so, sums)))
-    kv_keep = key_pass(True, tuple(range(heads)), keep, e0, o0, e1, o1, de, do, se, so, sums)
+        got.append(over_x(key_pass(False, (head,), xkv, *theirs, sums)))
+    kv_keep = key_pass(True, tuple(range(heads)), keep, *theirs, sums)
     return tuple(unpack(dq_keep, dq_got, kv_keep, *got))
 
 

time: 64.8 us -> 67.2 us (1.037)
  waiting for transfers between devices: 20.7 us -> 22.2 us
  starting transfers between devices: 20.4 us -> 21.2 us
    ppermute x6 -> x7, waiting for transfers between devices: 17.9 us -> 10.4 us  [over_x(): return lax.ppermute(array, 'ctx', [(i, i ^ 1) for i in range(length)])]
    ppermute x8 -> x10, waiting for transfers between devices: 2.52 us -> 7.27 us  [over_z(): return lax.ppermute(array, ('ctx', 'mp'), pairs)]
    ppermute x3, waiting for transfers between devices: 0.25 us -> 4.49 us  [over_mp(): return lax.ppermute(array, 'mp', [(i, i ^ flip) for i in range(lanes)])]
    ppermute x8 -> x10, starting transfers between devices: 8.99 us -> 10.8 us  [over_z(): return lax.ppermute(array, ('ctx', 'mp'), pairs)]
    ppermute x6 -> x7, starting transfers between devices: 8.27 us -> 7.26 us  [over_x(): return lax.ppermute(array, 'ctx', [(i, i ^ 1) for i in range(length)])]
  transfers between devices with their start and end apart: 17 -> 20, of which waited for: 6 -> 9; matrix products, arithmetic and copies ran while one was open for 0% -> 0% of each run, Pallas kernels for 30% -> 29%
where the time goes in v9:
time: 67.2 us; the launch traced here: 67 us
  waiting for transfers between devices  22.2 us (33%)
  Pallas kernels  21.7 us (32%)
  starting transfers between devices  21.2 us (32%)
  local copies, waits for them, and re-layouts  1.14 us (2%)
  between operations  0.8 us (1%)
    ppermute x10, starting transfers between devices, over_z(): return lax.ppermute(array, ('ctx', 'mp'), pairs)  10.8 us
    ppermute x7, waiting for transfers between devices, over_x(): return lax.ppermute(array, 'ctx', [(i, i ^ 1) for i in range(length)])  10.4 us
    ppermute x10, waiting for transfers between devices, over_z(): return lax.ppermute(array, ('ctx', 'mp'), pairs)  7.27 us
    ppermute x7, starting transfers between devices, over_x(): return lax.ppermute(array, 'ctx', [(i, i ^ 1) for i in range(length)])  7.26 us
    pallas_call x2, Pallas kernels, query_pass(): pl.pallas_call(functools.partial(query_kernel, HD ** (-0.5), own, before...  5.96 us
    ppermute x3, waiting for transfers between devices, over_mp(): return lax.ppermute(array, 'mp', [(i, i ^ flip) for i in range(lanes)])  4.49 us
    pallas_call x4, Pallas kernels, key_pass(): pl.pallas_call(functools.partial(key_kernel, HD ** (-0.5), own, heads), o...  4.37 us
    pallas_call x1, Pallas kernels, first_piece(): pl.pallas_call(first_kernel, out_shape=(jax.ShapeDtypeStruct((rows, heads...  3.85 us
  transfers between devices with their start and end apart: 20, of which 9 were waited for; matrix products, arithmetic and copies ran while one was open for 0% of the time, Pallas kernels for 29%

profile of v9, /device:TPU:0, one launch (start us, length us, event | category | flops | bytes accessed | tf_op | source)
XLA Modules:
  0.0 67.0 jit_solution(6507020368415517575)
XLA Ops:
  1.1 2.6 %collective-permute-start = (bf16[256,1536]{1,0:T(8,128)(2,1)}, bf16[256,1536]{1,0:T(8,128)(2,1)S(1)}, u32[]{:S(2)}, u32[]{:S(2)}) collective-permute-start(bf16[256,1536]{1,0:T(8,128)(2,1)} %og.1), channel_id=1, source_target_pairs={{0,2},{1,3},{2,0},{3,1},{4,6},{5,7},{6,4},{7,5},{8,10},{9,11},{10,... | collective-permute-start | bytes 2359304 | tf_op jit(solution)/shard_map/ppermute | solution.py:411
  3.7 2.4 %pack.1 = (bf16[3,256,384]{2,1,0:T(8,128)(2,1)}, bf16[2,256,384]{2,1,0:T(8,128)(2,1)}, bf16[256,384]{1,0:T(8,128)(2,1)}) custom-call(bf16[256,768]{1,0:T(8,128)(2,1)} %q.1, bf16[256,768]{1,0:T(8,128)(2,1)} %k.1, bf16[256,768]{1,0:T(8,128)(2,1)} %v.1), custom_call_target="tpu_custom_call" | custom-call | flops 1 | bytes 1 | tf_op jit(solution)/shard_map/pack/pallas_call | solution.py:60
  6.1 1.6 %collective-permute-start.2 = (bf16[2,256,384]{2,1,0:T(8,128)(2,1)}, bf16[2,256,384]{2,1,0:T(8,128)(2,1)S(1)}, u32[]{:S(2)}, u32[]{:S(2)}) collective-permute-start(bf16[2,256,384]{2,1,0:T(8,128)(2,1)} %get-tuple-element.27), channel_id=1, source_target_pairs={{0,4},{4,0},{8,12},{12,8},{16,20},{20,16},{24,28},{28,24},{1,5},{5... | collective-permute-start | bytes 1179656 | tf_op jit(solution)/shard_map/ppermute | solution.py:414
  7.7 1.6 %collective-permute-start.3 = (bf16[3,256,384]{2,1,0:T(8,128)(2,1)}, bf16[3,256,384]{2,1,0:T(8,128)(2,1)S(1)}, u32[]{:S(2)}, u32[]{:S(2)}) collective-permute-start(bf16[3,256,384]{2,1,0:T(8,128)(2,1)} %get-tuple-element.25.refs_0_.refs_2_.keep.kv), channel_id=1, source_target_pairs={{0,8},{1,9},{2,10},{3,11},{4,12},{5,13},{6,14},{7,15},{8,0},{9,1},... | collective-permute-start | bytes 1769480 | tf_op jit(solution)/shard_map/ppermute | solution.py:428
  9.3 1.1 %copy-done.1 = bf16[256,1536]{1,0:T(8,128)(2,1)S(1)} copy-done((bf16[256,1536]{1,0:T(8,128)(2,1)S(1)}, bf16[256,1536]{1,0:T(8,128)(2,1)}, u32[]{:S(2)}) %copy-start.1) | copy-done | bytes 786456
  10.4 3.8 %head_grad_first.1 = (f32[256,768]{1,0:T(8,128)S(1)}, bf16[768,1536]{1,0:T(8,128)(2,1)S(1)}, bf16[768,1536]{1,0:T(8,128)(2,1)S(1)}) custom-call(bf16[256,1536]{1,0:T(8,128)(2,1)S(1)} %copy-done.1, bf16[256,1536]{1,0:T(8,128)(2,1)S(1)} %collective-permute-done.1.near, bf16[768,6144]{1,0:T(8,128)(2,1)} %w.1), custom_call_target="tpu_custom_call" | custom-call | flops 1 | bytes 1 | tf_op jit(solution)/shard_map/head_grad_first/pallas_call | solution.py:110
  14.3 3.3 %collective-permute-done.2.refs_1_.refs_3_.xkv.kv = bf16[2,256,384]{2,1,0:T(8,128)(2,1)S(1)} collective-permute-done((bf16[2,256,384]{2,1,0:T(8,128)(2,1)}, bf16[2,256,384]{2,1,0:T(8,128)(2,1)S(1)}, u32[]{:S(2)}, u32[]{:S(2)}) %collective-permute-start.2) | collective-permute-done | bytes 393248 | tf_op jit(solution)/shard_map/ppermute | solution.py:414
  17.6 4.5 %collective-permute-done.piece = bf16[256,1536]{1,0:T(8,128)(2,1)S(1)} collective-permute-done((bf16[256,1536]{1,0:T(8,128)(2,1)}, bf16[256,1536]{1,0:T(8,128)(2,1)S(1)}, u32[]{:S(2)}, u32[]{:S(2)}) %collective-permute-start) | collective-permute-done | bytes 786464 | tf_op jit(solution)/shard_map/ppermute | solution.py:411
  22.1 1.7 %collective-permute-start.6 = (bf16[256,384]{1,0:T(8,128)(2,1)S(1)}, bf16[256,384]{1,0:T(8,128)(2,1)S(1)}, u32[]{:S(2)}, u32[]{:S(2)}) collective-permute-start(bf16[256,384]{1,0:T(8,128)(2,1)S(1)} %copy-done.2), channel_id=1, source_target_pairs={{0,4},{4,0},{8,12},{12,8},{16,20},{20,16},{24,28},{28,24},{1,5},{5... | collective-permute-start | bytes 589832 | tf_op jit(solution)/shard_map/ppermute | solution.py:414
  23.8 1.6 %collective-permute-start.7 = (bf16[2,256,384]{2,1,0:T(8,128)(2,1)S(1)}, bf16[2,256,384]{2,1,0:T(8,128)(2,1)S(1)}, u32[]{:S(2)}, u32[]{:S(2)}) collective-permute-start(bf16[2,256,384]{2,1,0:T(8,128)(2,1)S(1)} %collective-permute-done.2.refs_1_.refs_3_.xkv.kv), channel_id=1, source_target_pairs={{0,8},{1,9},{2,10},{3,11},{4,12},{5,13},{6,14},{7,15},{8,0},{9,1},... | collective-permute-start | bytes 1179656 | tf_op jit(solution)/shard_map/ppermute | solution.py:428
  25.4 0.8 %head_grad.2.refs_0_ = f32[256,768]{1,0:T(8,128)S(1)} custom-call(f32[256,768]{1,0:T(8,128)S(1)} %after.4.acc, bf16[256,1536]{1,0:T(8,128)(2,1)S(1)} %collective-permute-done.piece, bf16[768,1536]{1,0:T(8,128)(2,1)S(1)} %get-tuple-element.30.w), custom_call_target="tpu_custom_call" | custom-call | flops 1 | bytes 1 | tf_op jit(solution)/shard_map/head_grad/pallas_call | solution.py:147
  26.3 0.9 %head_grad.3 = (bf16[256,384]{1,0:T(8,128)(2,1)S(1)}, bf16[256,384]{1,0:T(8,128)(2,1)S(1)}) custom-call(f32[256,768]{1,0:T(8,128)S(1)} %after.5.acc, bf16[256,1536]{1,0:T(8,128)(2,1)S(1)} %collective-permute-done.5.piece, bf16[768,1536]{1,0:T(8,128)(2,1)S(1)} %get-tuple-element.31.w), custom_call_target="tpu_custom_call" | custom-call | flops 1 | bytes 1 | tf_op jit(solution)/shard_map/head_grad/pallas_call | solution.py:147
  27.2 0.6 collective-permute-start.9
  27.8 1.6 %collective-permute-done.6.refs_0_.first.xq = bf16[256,384]{1,0:T(8,128)(2,1)S(1)} collective-permute-done((bf16[256,384]{1,0:T(8,128)(2,1)S(1)}, bf16[256,384]{1,0:T(8,128)(2,1)S(1)}, u32[]{:S(2)}, u32[]{:S(2)}) %collective-permute-start.6) | collective-permute-done | bytes 196640 | tf_op jit(solution)/shard_map/ppermute | solution.py:414
  29.4 5.7 %collective-permute-done.7.refs_6_.refs_4_ = bf16[2,256,384]{2,1,0:T(8,128)(2,1)S(1)} collective-permute-done((bf16[2,256,384]{2,1,0:T(8,128)(2,1)S(1)}, bf16[2,256,384]{2,1,0:T(8,128)(2,1)S(1)}, u32[]{:S(2)}, u32[]{:S(2)}) %collective-permute-start.7) | collective-permute-done | bytes 393248 | tf_op jit(solution)/shard_map/ppermute | solution.py:428
  35.1 3.7 %collective-permute-start.10 = (bf16[2,256,384]{2,1,0:T(8,128)(2,1)S(1)}, bf16[2,256,384]{2,1,0:T(8,128)(2,1)S(1)}, u32[]{:S(2)}, u32[]{:S(2)}) collective-permute-start(bf16[2,256,384]{2,1,0:T(8,128)(2,1)S(1)} %join.1), channel_id=1, source_target_pairs={{0,8},{1,9},{2,10},{3,11},{4,12},{5,13},{6,14},{7,15},{8,0},{9,1},... | collective-permute-start | bytes 1179656 | tf_op jit(solution)/shard_map/ppermute | solution.py:428
  38.8 1.8 %collective-permute-start.12 = (bf16[256,384]{1,0:T(8,128)(2,1)S(1)}, bf16[256,384]{1,0:T(8,128)(2,1)S(1)}, u32[]{:S(2)}, u32[]{:S(2)}) collective-permute-start(bf16[256,384]{1,0:T(8,128)(2,1)S(1)} %after.6.refs_1_.dxr), channel_id=1, source_target_pairs={{0,8},{1,9},{2,10},{3,11},{4,12},{5,13},{6,14},{7,15},{8,0},{9,1},... | collective-permute-start | bytes 589832 | tf_op jit(solution)/shard_map/ppermute | solution.py:428
  40.6 3.0 %query_pass.2 = (bf16[256,384]{1,0:T(8,128)(2,1)S(1)}, f32[8,256]{1,0:T(8,128)S(1)}) custom-call(bf16[3,256,384]{2,1,0:T(8,128)(2,1)S(1)} %copy-done, bf16[256,384]{1,0:T(8,128)(2,1)S(1)} %get-tuple-element.32.refs_1_.second.dkeep, bf16[3,256,384]{2,1,0:T(8,128)(2,1)S(1)} %copy-done, bf16[2,256,384]{2,1,0:T(8,128)(2,1)S(1)} %collective-permute-done.2.refs_1_.refs_3_.xkv.kv, ...), custom_call_target="tpu_custom_call" | custom-call | flops 6000000000 | bytes 1 | tf_op jit(solution)/shard_map/query_pass/pallas_call | solution.py:256
  43.6 3.0 %query_pass.3 = (bf16[256,384]{1,0:T(8,128)(2,1)S(1)}, f32[8,512]{1,0:T(8,128)S(1)}) custom-call(bf16[256,384]{1,0:T(8,128)(2,1)S(1)} %collective-permute-done.6.refs_0_.first.xq, bf16[256,384]{1,0:T(8,128)(2,1)S(1)} %after.6.refs_1_.dxr, bf16[3,256,384]{2,1,0:T(8,128)(2,1)S(1)} %copy-done, ...), custom_call_target="tpu_custom_call" | custom-call | flops 1 | bytes 1 | tf_op jit(solution)/shard_map/query_pass/pallas_call | solution.py:256
  46.6 0.6 collective-permute-start.14
  47.2 1.6 %collective-permute-done.10.mixed_e = bf16[2,256,384]{2,1,0:T(8,128)(2,1)S(1)} collective-permute-done((bf16[2,256,384]{2,1,0:T(8,128)(2,1)S(1)}, bf16[2,256,384]{2,1,0:T(8,128)(2,1)S(1)}, u32[]{:S(2)}, u32[]{:S(2)}) %collective-permute-start.10) | collective-permute-done | bytes 393248 | tf_op jit(solution)/shard_map/ppermute | solution.py:428
  48.8 2.1 %collective-permute-start.15 = (f32[8,512]{1,0:T(8,128)S(1)}, f32[8,512]{1,0:T(8,128)S(1)}, u32[]{:S(2)}, u32[]{:S(2)}) collective-permute-start(f32[8,512]{1,0:T(8,128)S(1)} %get-tuple-element.41.stats), channel_id=1, source_target_pairs={{0,8},{1,9},{2,10},{3,11},{4,12},{5,13},{6,14},{7,15},{8,0},{9,1},... | collective-permute-start | bytes 49160 | tf_op jit(solution)/shard_map/ppermute | solution.py:428
  50.9 2.3 %own_pass.1.refs_0_ = f32[2,2,256,384]{3,2,1,0:T(8,128)S(1)} custom-call(bf16[3,256,384]{2,1,0:T(8,128)(2,1)S(1)} %copy-done, bf16[2,256,384]{2,1,0:T(8,128)(2,1)S(1)} %collective-permute-done.2.refs_1_.refs_3_.xkv.kv, bf16[256,384]{1,0:T(8,128)(2,1)S(1)} %collective-permute-done.6.refs_0_.first.xq, ...), custom_call_target="tpu_custom_call" | custom-call | flops 1 | bytes 1 | tf_op jit(solution)/shard_map/own_pass/pallas_call | solution.py:307
  53.2 0.7 %collective-permute-done.14.q_got = bf16[256,384]{1,0:T(8,128)(2,1)S(1)} collective-permute-done((bf16[256,384]{1,0:T(8,128)(2,1)S(1)}, bf16[256,384]{1,0:T(8,128)(2,1)S(1)}, u32[]{:S(2)}, u32[]{:S(2)}) %collective-permute-start.14) | collective-permute-done | bytes 196640 | tf_op jit(solution)/shard_map/ppermute | solution.py:414
  54.0 0.9 %key_pass.7 = bf16[2,256,128]{2,1,0:T(8,128)(2,1)S(1)} custom-call(bf16[2,256,384]{2,1,0:T(8,128)(2,1)S(1)} %collective-permute-done.2.refs_1_.refs_3_.xkv.kv, bf16[3,256,384]{2,1,0:T(8,128)(2,1)S(1)} %collective-permute-done.3.refs_1_.refs_4_.refs_6_.e0, bf16[3,256,384]{2,1,0:T(8,128)(2,1)S(1)} %collective-permute-done.4.refs_2_.refs_5_.refs_7_.o0, ...), custom_call_target="tpu_custom_call" | custom-call | flops 1000000000 | bytes 1 | tf_op jit(solution)/shard_map/key_pass/pallas_call | solution.py:361
  55.5 0.8 %key_pass.6 = bf16[2,256,128]{2,1,0:T(8,128)(2,1)S(1)} custom-call(bf16[2,256,384]{2,1,0:T(8,128)(2,1)S(1)} %collective-permute-done.2.refs_1_.refs_3_.xkv.kv, bf16[3,256,384]{2,1,0:T(8,128)(2,1)S(1)} %collective-permute-done.3.refs_1_.refs_4_.refs_6_.e0, bf16[3,256,384]{2,1,0:T(8,128)(2,1)S(1)} %collective-permute-done.4.refs_2_.refs_5_.refs_7_.o0, ...), custom_call_target="tpu_custom_call" | custom-call | flops 1000000000 | bytes 1 | tf_op jit(solution)/shard_map/key_pass/pallas_call | solution.py:361
  56.3 1.6 %collective-permute-start.18 = (bf16[2,256,128]{2,1,0:T(8,128)(2,1)S(1)}, bf16[2,256,128]{2,1,0:T(8,128)(2,1)S(1)}, u32[]{:S(2)}, u32[]{:S(2)}) collective-permute-start(bf16[2,256,128]{2,1,0:T(8,128)(2,1)S(1)} %key_pass.6), channel_id=1, source_target_pairs={{0,4},{4,0},{8,12},{12,8},{16,20},{20,16},{24,28},{28,24},{1,5},{5... | collective-permute-start | bytes 393224 | tf_op jit(solution)/shard_map/ppermute | solution.py:414
  57.9 0.8 %key_pass.5 = bf16[2,256,128]{2,1,0:T(8,128)(2,1)S(1)} custom-call(bf16[2,256,384]{2,1,0:T(8,128)(2,1)S(1)} %collective-permute-done.2.refs_1_.refs_3_.xkv.kv, bf16[3,256,384]{2,1,0:T(8,128)(2,1)S(1)} %collective-permute-done.3.refs_1_.refs_4_.refs_6_.e0, bf16[3,256,384]{2,1,0:T(8,128)(2,1)S(1)} %collective-permute-done.4.refs_2_.refs_5_.refs_7_.o0, ...), custom_call_target="tpu_custom_call" | custom-call | flops 1000000000 | bytes 1 | tf_op jit(solution)/shard_map/key_pass/pallas_call | solution.py:361
  59.2 1.9 %key_pass.4.kv_keep = bf16[2,256,384]{2,1,0:T(8,128)(2,1)S(1)} custom-call(bf16[3,256,384]{2,1,0:T(8,128)(2,1)S(1)} %copy-done, bf16[3,256,384]{2,1,0:T(8,128)(2,1)S(1)} %collective-permute-done.3.refs_1_.refs_4_.refs_6_.e0, bf16[3,256,384]{2,1,0:T(8,128)(2,1)S(1)} %collective-permute-done.4.refs_2_.refs_5_.refs_7_.o0, ...), custom_call_target="tpu_custom_call" | custom-call | flops 1000000000 | bytes 1 | tf_op jit(solution)/shard_map/key_pass/pallas_call | solution.py:361
  61.4 2.8 %collective-permute-done.18.refs_1_ = bf16[2,256,128]{2,1,0:T(8,128)(2,1)S(1)} collective-permute-done((bf16[2,256,128]{2,1,0:T(8,128)(2,1)S(1)}, bf16[2,256,128]{2,1,0:T(8,128)(2,1)S(1)}, u32[]{:S(2)}, u32[]{:S(2)}) %collective-permute-start.18) | collective-permute-done | bytes 131104 | tf_op jit(solution)/shard_map/ppermute | solution.py:414
  64.2 1.7 %collective-permute-done.17.refs_0_ = bf16[2,256,128]{2,1,0:T(8,128)(2,1)S(1)} collective-permute-done((bf16[2,256,128]{2,1,0:T(8,128)(2,1)S(1)}, bf16[2,256,128]{2,1,0:T(8,128)(2,1)S(1)}, u32[]{:S(2)}, u32[]{:S(2)}) %collective-permute-start.17) | collective-permute-done | bytes 131104 | tf_op jit(solution)/shard_map/ppermute | solution.py:414
  65.8 1.1 %unpack.1 = (bf16[256,768]{1,0:T(8,128)(2,1)}, bf16[256,768]{1,0:T(8,128)(2,1)}, bf16[256,768]{1,0:T(8,128)(2,1)}) custom-call(bf16[256,384]{1,0:T(8,128)(2,1)S(1)} %get-tuple-element.36.q_keep, bf16[256,384]{1,0:T(8,128)(2,1)S(1)} %collective-permute-done.14.q_got, bf16[2,256,384]{2,1,0:T(8,128)(2,1)S(1)} %key_pass.4.kv_keep, ...), custom_call_target="tpu_custom_call" | custom-call | flops 1 | bytes 1 | tf_op jit(solution)/shard_map/unpack/pallas_call | solution.py:393
  (31 shorter events, 2.1 us)
Async XLA Ops:
  0.6 8.6 %collective-permute-start.1 = (bf16[256,1536]{1,0:T(8,128)(2,1)}, bf16[256,1536]{1,0:T(8,128)(2,1)S(1)}, u32[]{:S(2)}, u32[]{:S(2)}) collective-permute-start(bf16[256,1536]{1,0:T(8,128)(2,1)} %og.1), channel_id=1, source_target_pairs={{0,1},{1,0},{2,3},{3,2},{4,5},{5,4},{6,7},{7,6},{8,9},{9,8},{10,11... | collective-permute-start | bytes 2359304 | tf_op jit(solution)/shard_map/ppermute | solution.py:411
  1.1 20.9 %collective-permute-start = (bf16[256,1536]{1,0:T(8,128)(2,1)}, bf16[256,1536]{1,0:T(8,128)(2,1)S(1)}, u32[]{:S(2)}, u32[]{:S(2)}) collective-permute-start(bf16[256,1536]{1,0:T(8,128)(2,1)} %og.1), channel_id=1, source_target_pairs={{0,2},{1,3},{2,0},{3,1},{4,6},{5,7},{6,4},{7,5},{8,10},{9,11},{10,... | collective-permute-start | bytes 2359304 | tf_op jit(solution)/shard_map/ppermute | solution.py:411
  6.1 11.5 %collective-permute-start.2 = (bf16[2,256,384]{2,1,0:T(8,128)(2,1)}, bf16[2,256,384]{2,1,0:T(8,128)(2,1)S(1)}, u32[]{:S(2)}, u32[]{:S(2)}) collective-permute-start(bf16[2,256,384]{2,1,0:T(8,128)(2,1)} %get-tuple-element.27), channel_id=1, source_target_pairs={{0,4},{4,0},{8,12},{12,8},{16,20},{20,16},{24,28},{28,24},{1,5},{5... | collective-permute-start | bytes 1179656 | tf_op jit(solution)/shard_map/ppermute | solution.py:414
  7.7 18.5 %collective-permute-start.3 = (bf16[3,256,384]{2,1,0:T(8,128)(2,1)}, bf16[3,256,384]{2,1,0:T(8,128)(2,1)S(1)}, u32[]{:S(2)}, u32[]{:S(2)}) collective-permute-start(bf16[3,256,384]{2,1,0:T(8,128)(2,1)} %get-tuple-element.25.refs_0_.refs_2_.keep.kv), channel_id=1, source_target_pairs={{0,8},{1,9},{2,10},{3,11},{4,12},{5,13},{6,14},{7,15},{8,0},{9,1},... | collective-permute-start | bytes 1769480 | tf_op jit(solution)/shard_map/ppermute | solution.py:428
  9.3 17.0 %collective-permute-start.4 = (bf16[3,256,384]{2,1,0:T(8,128)(2,1)}, bf16[3,256,384]{2,1,0:T(8,128)(2,1)S(1)}, u32[]{:S(2)}, u32[]{:S(2)}) collective-permute-start(bf16[3,256,384]{2,1,0:T(8,128)(2,1)} %get-tuple-element.25.refs_0_.refs_2_.keep.kv), channel_id=1, source_target_pairs={{0,1},{1,0},{2,3},{3,2},{4,5},{5,4},{6,7},{7,6},{8,16},{9,17},{10,... | collective-permute-start | bytes 1769480 | tf_op jit(solution)/shard_map/ppermute | solution.py:428
  9.3 1.1 %copy-start.1 = (bf16[256,1536]{1,0:T(8,128)(2,1)S(1)}, bf16[256,1536]{1,0:T(8,128)(2,1)}, u32[]{:S(2)}) copy-start(bf16[256,1536]{1,0:T(8,128)(2,1)} %og.1) | copy-start | bytes 2359300
  10.4 11.7 %copy-start.2 = (bf16[256,384]{1,0:T(8,128)(2,1)S(1)}, bf16[256,384]{1,0:T(8,128)(2,1)}, u32[]{:S(2)}) copy-start(bf16[256,384]{1,0:T(8,128)(2,1)} %get-tuple-element.33) | copy-start | bytes 589828
  22.1 4.2 %collective-permute-start.5 = (bf16[256,1536]{1,0:T(8,128)(2,1)S(1)}, bf16[256,1536]{1,0:T(8,128)(2,1)S(1)}, u32[]{:S(2)}, u32[]{:S(2)}) collective-permute-start(bf16[256,1536]{1,0:T(8,128)(2,1)S(1)} %collective-permute-done.piece), channel_id=1, source_target_pairs={{0,1},{1,0},{2,3},{3,2},{4,5},{5,4},{6,7},{7,6},{8,9},{9,8},{10,11... | collective-permute-start | bytes 2359304 | tf_op jit(solution)/shard_map/ppermute | solution.py:411
  22.1 7.3 %collective-permute-start.6 = (bf16[256,384]{1,0:T(8,128)(2,1)S(1)}, bf16[256,384]{1,0:T(8,128)(2,1)S(1)}, u32[]{:S(2)}, u32[]{:S(2)}) collective-permute-start(bf16[256,384]{1,0:T(8,128)(2,1)S(1)} %copy-done.2), channel_id=1, source_target_pairs={{0,4},{4,0},{8,12},{12,8},{16,20},{20,16},{24,28},{28,24},{1,5},{5... | collective-permute-start | bytes 589832 | tf_op jit(solution)/shard_map/ppermute | solution.py:414
  23.8 11.2 %collective-permute-start.7 = (bf16[2,256,384]{2,1,0:T(8,128)(2,1)S(1)}, bf16[2,256,384]{2,1,0:T(8,128)(2,1)S(1)}, u32[]{:S(2)}, u32[]{:S(2)}) collective-permute-start(bf16[2,256,384]{2,1,0:T(8,128)(2,1)S(1)} %collective-permute-done.2.refs_1_.refs_3_.xkv.kv), channel_id=1, source_target_pairs={{0,8},{1,9},{2,10},{3,11},{4,12},{5,13},{6,14},{7,15},{8,0},{9,1},... | collective-permute-start | bytes 1179656 | tf_op jit(solution)/shard_map/ppermute | solution.py:428
  26.2 8.9 %collective-permute-start.8 = (bf16[2,256,384]{2,1,0:T(8,128)(2,1)S(1)}, bf16[2,256,384]{2,1,0:T(8,128)(2,1)S(1)}, u32[]{:S(2)}, u32[]{:S(2)}) collective-permute-start(bf16[2,256,384]{2,1,0:T(8,128)(2,1)S(1)} %collective-permute-done.2.refs_1_.refs_3_.xkv.kv), channel_id=1, source_target_pairs={{0,1},{1,0},{2,3},{3,2},{4,5},{5,4},{6,7},{7,6},{8,16},{9,17},{10,... | collective-permute-start | bytes 1179656 | tf_op jit(solution)/shard_map/ppermute | solution.py:428
  27.2 11.6 %collective-permute-start.9 = (bf16[256,384]{1,0:T(8,128)(2,1)S(1)}, bf16[256,384]{1,0:T(8,128)(2,1)S(1)}, u32[]{:S(2)}, u32[]{:S(2)}) collective-permute-start(bf16[256,384]{1,0:T(8,128)(2,1)S(1)} %get-tuple-element.37), channel_id=1, source_target_pairs={{0,4},{4,0},{8,12},{12,8},{16,20},{20,16},{24,28},{28,24},{1,5},{5... | collective-permute-start | bytes 589832 | tf_op jit(solution)/shard_map/ppermute | solution.py:414
  35.1 5.5 %copy-start = (bf16[3,256,384]{2,1,0:T(8,128)(2,1)S(1)}, bf16[3,256,384]{2,1,0:T(8,128)(2,1)}, u32[]{:S(2)}) copy-start(bf16[3,256,384]{2,1,0:T(8,128)(2,1)} %get-tuple-element.25.refs_0_.refs_2_.keep.kv) | copy-start | bytes 1769476
  35.1 13.7 %collective-permute-start.10 = (bf16[2,256,384]{2,1,0:T(8,128)(2,1)S(1)}, bf16[2,256,384]{2,1,0:T(8,128)(2,1)S(1)}, u32[]{:S(2)}, u32[]{:S(2)}) collective-permute-start(bf16[2,256,384]{2,1,0:T(8,128)(2,1)S(1)} %join.1), channel_id=1, source_target_pairs={{0,8},{1,9},{2,10},{3,11},{4,12},{5,13},{6,14},{7,15},{8,0},{9,1},... | collective-permute-start | bytes 1179656 | tf_op jit(solution)/shard_map/ppermute | solution.py:428
  38.8 10.0 %collective-permute-start.11 = (bf16[2,256,384]{2,1,0:T(8,128)(2,1)S(1)}, bf16[2,256,384]{2,1,0:T(8,128)(2,1)S(1)}, u32[]{:S(2)}, u32[]{:S(2)}) collective-permute-start(bf16[2,256,384]{2,1,0:T(8,128)(2,1)S(1)} %join.1), channel_id=1, source_target_pairs={{0,1},{1,0},{2,3},{3,2},{4,5},{5,4},{6,7},{7,6},{8,16},{9,17},{10,... | collective-permute-start | bytes 1179656 | tf_op jit(solution)/shard_map/ppermute | solution.py:428
  38.8 14.4 %collective-permute-start.12 = (bf16[256,384]{1,0:T(8,128)(2,1)S(1)}, bf16[256,384]{1,0:T(8,128)(2,1)S(1)}, u32[]{:S(2)}, u32[]{:S(2)}) collective-permute-start(bf16[256,384]{1,0:T(8,128)(2,1)S(1)} %after.6.refs_1_.dxr), channel_id=1, source_target_pairs={{0,8},{1,9},{2,10},{3,11},{4,12},{5,13},{6,14},{7,15},{8,0},{9,1},... | collective-permute-start | bytes 589832 | tf_op jit(solution)/shard_map/ppermute | solution.py:428
  40.6 12.6 %collective-permute-start.13 = (bf16[256,384]{1,0:T(8,128)(2,1)S(1)}, bf16[256,384]{1,0:T(8,128)(2,1)S(1)}, u32[]{:S(2)}, u32[]{:S(2)}) collective-permute-start(bf16[256,384]{1,0:T(8,128)(2,1)S(1)} %after.6.refs_1_.dxr), channel_id=1, source_target_pairs={{0,1},{1,0},{2,3},{3,2},{4,5},{5,4},{6,7},{7,6},{8,16},{9,17},{10,... | collective-permute-start | bytes 589832 | tf_op jit(solution)/shard_map/ppermute | solution.py:428
  46.6 7.4 %collective-permute-start.14 = (bf16[256,384]{1,0:T(8,128)(2,1)S(1)}, bf16[256,384]{1,0:T(8,128)(2,1)S(1)}, u32[]{:S(2)}, u32[]{:S(2)}) collective-permute-start(bf16[256,384]{1,0:T(8,128)(2,1)S(1)} %get-tuple-element.42), channel_id=1, source_target_pairs={{0,4},{4,0},{8,12},{12,8},{16,20},{20,16},{24,28},{28,24},{1,5},{5... | collective-permute-start | bytes 589832 | tf_op jit(solution)/shard_map/ppermute | solution.py:414
  48.8 5.2 %collective-permute-start.15 = (f32[8,512]{1,0:T(8,128)S(1)}, f32[8,512]{1,0:T(8,128)S(1)}, u32[]{:S(2)}, u32[]{:S(2)}) collective-permute-start(f32[8,512]{1,0:T(8,128)S(1)} %get-tuple-element.41.stats), channel_id=1, source_target_pairs={{0,8},{1,9},{2,10},{3,11},{4,12},{5,13},{6,14},{7,15},{8,0},{9,1},... | collective-permute-start | bytes 49160 | tf_op jit(solution)/shard_map/ppermute | solution.py:428
  50.9 3.1 %collective-permute-start.16 = (f32[8,512]{1,0:T(8,128)S(1)}, f32[8,512]{1,0:T(8,128)S(1)}, u32[]{:S(2)}, u32[]{:S(2)}) collective-permute-start(f32[8,512]{1,0:T(8,128)S(1)} %get-tuple-element.41.stats), channel_id=1, source_target_pairs={{0,1},{1,0},{2,3},{3,2},{4,5},{5,4},{6,7},{7,6},{8,16},{9,17},{10,... | collective-permute-start | bytes 49160 | tf_op jit(solution)/shard_map/ppermute | solution.py:428
  54.9 6.4 %collective-permute-start.19 = (bf16[2,256,128]{2,1,0:T(8,128)(2,1)S(1)}, bf16[2,256,128]{2,1,0:T(8,128)(2,1)S(1)}, u32[]{:S(2)}, u32[]{:S(2)}) collective-permute-start(bf16[2,256,128]{2,1,0:T(8,128)(2,1)S(1)} %key_pass.7), channel_id=1, source_target_pairs={{0,4},{4,0},{8,12},{12,8},{16,20},{20,16},{24,28},{28,24},{1,5},{5... | collective-permute-start | bytes 393224 | tf_op jit(solution)/shard_map/ppermute | solution.py:414
  56.3 7.9 %collective-permute-start.18 = (bf16[2,256,128]{2,1,0:T(8,128)(2,1)S(1)}, bf16[2,256,128]{2,1,0:T(8,128)(2,1)S(1)}, u32[]{:S(2)}, u32[]{:S(2)}) collective-permute-start(bf16[2,256,128]{2,1,0:T(8,128)(2,1)S(1)} %key_pass.6), channel_id=1, source_target_pairs={{0,4},{4,0},{8,12},{12,8},{16,20},{20,16},{24,28},{28,24},{1,5},{5... | collective-permute-start | bytes 393224 | tf_op jit(solution)/shard_map/ppermute | solution.py:414
  58.6 7.2 %collective-permute-start.17 = (bf16[2,256,128]{2,1,0:T(8,128)(2,1)S(1)}, bf16[2,256,128]{2,1,0:T(8,128)(2,1)S(1)}, u32[]{:S(2)}, u32[]{:S(2)}) collective-permute-start(bf16[2,256,128]{2,1,0:T(8,128)(2,1)S(1)} %key_pass.5), channel_id=1, source_target_pairs={{0,4},{4,0},{8,12},{12,8},{16,20},{20,16},{24,28},{28,24},{1,5},{5... | collective-permute-start | bytes 393224 | tf_op jit(solution)/shard_map/ppermute | solution.py:414

commit v10 on v9

--- a/solution.py
+++ b/solution.py
@@ -69,21 +69,21 @@
     )(q, k, v)
 
 
-def join_kernel(first, second, out):
-    out[0] = first[...]
-    out[1] = second[...]
-
-
-def join(first, second):
+def join_kernel(*refs):
+    for i, ref in enumerate(refs[:-1]):
+        refs[-1][i] = ref[...]
+
+
+def join(*pieces):
     return pl.pallas_call(
         join_kernel,
-        out_shape=jax.ShapeDtypeStruct((2, *first.shape), BF16),
-        in_specs=[VM] * 2,
+        out_shape=jax.ShapeDtypeStruct((len(pieces), *pieces[0].shape), BF16),
+        in_specs=[VM] * len(pieces),
         out_specs=VM,
         compiler_params=params(16),
         cost_estimate=cost(),
         name="join",
-    )(first, second)
+    )(*pieces)
 
 
 def first_kernel(og, near, w, acc, wy, wf, wbuf, sem):
@@ -242,8 +242,8 @@
         mark = jnp.where(lane == 2 * head + 1, delta, mark)
     marks = jnp.transpose(mark)[: stats.shape[0], :]
     if has_marks:
-        stats[:, :rows] = before[...]
-        stats[:, rows:] = marks
+        stats[:, :rows] = marks
+        stats[:, rows:] = before[...]
     else:
         stats[...] = marks
 
@@ -282,31 +282,30 @@
     return key_sum, value_sum
 
 
-def own_kernel(scale, keep, xkv, xq, dkeep, dxr, stats, sums):
+def own_kernel(scale, keys, keep, xq, dkeep, dxr, stats, sums):
     rows = keep.shape[1]
     heads = keep.shape[2] // HD
-    for mine, keys in enumerate((keep, xkv)):
-        for head in range(heads):
-            cols = slice(head * HD, (head + 1) * HD)
-            steps = []
-            for i, (q, d) in enumerate(((keep.at[2], dkeep), (xq, dxr))):
-                span = slice(i * rows, (i + 1) * rows)
-                steps.append((
-                    q[:, cols],
-                    d[:, cols],
-                    stats[2 * head : 2 * head + 1, span],
-                    stats[2 * head + 1 : 2 * head + 2, span],
-                ))
-            k, v = key_step(scale, keys[0, :, cols], keys[1, :, cols], steps)
-            sums[mine, 0, :, cols] = k
-            sums[mine, 1, :, cols] = v
+    for head in range(heads):
+        cols = slice(head * HD, (head + 1) * HD)
+        steps = []
+        for i, (q, d) in enumerate(((keep.at[2], dkeep), (xq, dxr))):
+            span = slice(i * rows, (i + 1) * rows)
+            steps.append((
+                q[:, cols],
+                d[:, cols],
+                stats[2 * head : 2 * head + 1, span],
+                stats[2 * head + 1 : 2 * head + 2, span],
+            ))
+        k, v = key_step(scale, keys[0, :, cols], keys[1, :, cols], steps)
+        sums[0, :, cols] = k
+        sums[1, :, cols] = v
 
 
 def own_pass(*operands):
     _, rows, cols = operands[0].shape
     return pl.pallas_call(
         functools.partial(own_kernel, HD ** -0.5),
-        out_shape=jax.ShapeDtypeStruct((2, 2, rows, cols), F32),
+        out_shape=jax.ShapeDtypeStruct((2, rows, cols), F32),
         in_specs=[VM] * 6,
         out_specs=VM,
         compiler_params=params(30),
@@ -315,12 +314,12 @@
     )(*operands)
 
 
-def key_kernel(scale, own, heads, kv, e0, o0, mixed_e, mixed_o, de1, do1, se, so, sums, out, fifth_q, fifth_d):
+def key_kernel(scale, own, heads, kv, e0, o0, late_e, late_o, se, so, sums, out, fifth_q, fifth_d):
     rows = kv.shape[1]
     even_ok, odd_ok, turned = place()
     from_even = turned if own else jnp.logical_not(turned)
-    even_q, odd_q = (e0.at[2], mixed_e.at[0]), (o0.at[2], mixed_o.at[0])
-    even_d, odd_d = (mixed_e.at[1], de1), (mixed_o.at[1], do1)
+    even_q, odd_q = (e0.at[2], late_e.at[0]), (o0.at[2], late_o.at[0])
+    even_d, odd_d = (late_e.at[1], late_e.at[2]), (late_o.at[1], late_o.at[2])
     same, other = (0, 1) if own else (1, 0)
     wanted = slice(heads[0] * HD, (heads[-1] + 1) * HD)
 
@@ -351,8 +350,8 @@
             (fifth_q[:, to], fifth_d[:, to], fifth[a : a + 1], fifth[b : b + 1]),
         )
         k, v = key_step(scale, kv[0, :, cols], kv[1, :, cols], steps)
-        out[0, :, to] = ((k + sums[same, 0, :, cols]) * scale).astype(BF16)
-        out[1, :, to] = (v + sums[same, 1, :, cols]).astype(BF16)
+        out[0, :, to] = ((k + sums[0, :, cols]) * scale).astype(BF16)
+        out[1, :, to] = (v + sums[1, :, cols]).astype(BF16)
 
 
 def key_pass(own, heads, kv, *operands):
@@ -434,7 +433,7 @@
     e0, o0 = over_z(keep, 0), over_z(keep, 1)
     acc, wy, wf = first_piece(out_grad, near, out_weight)
     e1, o1 = over_z(xkv, 0), over_z(xkv, 1)
-    acc = after(acc, xkv, flops=1e8)
+    acc = after(acc, xkv, xq, flops=1e8)
     y, acc = lax.optimization_barrier((y, acc))
     far = over_mp(y, 1)
     acc = grad_piece(acc, y, wy, False)
@@ -442,25 +441,24 @@
     dkeep, dsend = grad_piece(acc, far, wf, True)
     dxr = after(over_x(dsend), flops=6e9)
 
-    late_q, e1, o1 = lax.optimization_barrier((xq, e1, o1))
-    mixed = join(late_q, dkeep)
-    mixed_e, mixed_o = over_z(mixed, 0), over_z(mixed, 1)
-    de1, do1 = over_z(dxr, 0), over_z(dxr, 1)
-    dq_keep, stats = query_pass(True, keep, dkeep, keep, xkv, e0, o0, e1, o1)
-    dq_send, stats = query_pass(False, xq, dxr, keep, xkv, e1, o1, e0, o0, stats)
-    stats, mixed_e, mixed_o = lax.optimization_barrier((stats, mixed_e, mixed_o))
+    xq, e1, o1 = lax.optimization_barrier((xq, e1, o1))
+    late = join(xq, dkeep, dxr)
+    late_e, late_o = over_z(late, 0), over_z(late, 1)
+    dq_send, marks = query_pass(False, xq, dxr, keep, xkv, e1, o1, e0, o0)
+    dq_keep, stats = query_pass(True, keep, dkeep, keep, xkv, e0, o0, e1, o1, marks)
+    dq_got = after(over_x(dq_send), flops=6e9)
     se, so = over_z(stats, 0), over_z(stats, 1)
-    dq_got = over_x(dq_send)
-    sums = own_pass(keep, xkv, xq, dkeep, dxr, stats)
-    sums = after(sums, de1, do1, flops=3e9)
+    sums = own_pass(xkv, keep, xq, dkeep, dxr, stats)
+    sums = after(sums, late_e, late_o, flops=3e9)
+    own_sums = own_pass(keep, keep, xq, dkeep, dxr, stats)
     heads = dkeep.shape[1] // HD
-    theirs = (e0, o0, mixed_e, mixed_o, de1, do1, se, so)
+    theirs = (e0, o0, late_e, late_o, se, so)
     got = []
     for head in range(heads):
         if head == 1:
             sums, dq_got = lax.optimization_barrier((sums, dq_got))
         got.append(over_x(key_pass(False, (head,), xkv, *theirs, sums)))
-    kv_keep = key_pass(True, tuple(range(heads)), keep, *theirs, sums)
+    kv_keep = key_pass(True, tuple(range(heads)), keep, *theirs, own_sums)
     return tuple(unpack(dq_keep, dq_got, kv_keep, *got))
 
 

time: 67.2 us -> 63 us (0.938)
  waiting for transfers between devices: 22.2 us -> 18.4 us
    ppermute x3, waiting for transfers between devices: 4.49 us -> 0.28 us  [over_mp(): return lax.ppermute(array, 'mp', [(i, i ^ flip) for i in range(lanes)])]
    ppermute x10 -> x8, starting transfers between devices: 10.8 us -> 8.64 us  [over_z(): return lax.ppermute(array, ('ctx', 'mp'), pairs)]
    ppermute x10 -> x8, waiting for transfers between devices: 7.27 us -> 9.01 us  [over_z(): return lax.ppermute(array, ('ctx', 'mp'), pairs)]
    ppermute x7, starting transfers between devices: 7.26 us -> 8.94 us  [over_x(): return lax.ppermute(array, 'ctx', [(i, i ^ 1) for i in range(length)])]
    ppermute x7, waiting for transfers between devices: 10.4 us -> 9.08 us  [over_x(): return lax.ppermute(array, 'ctx', [(i, i ^ 1) for i in range(length)])]
    pallas_call x1 -> x2, Pallas kernels: 2.28 us -> 2.44 us  [own_pass(): pl.pallas_call(functools.partial(own_kernel, HD ** (-0.5)), out_shape=jax...]
  transfers between devices with their start and end apart: 20 -> 18, of which waited for: 9 -> 7; matrix products, arithmetic and copies ran while one was open for 0% -> 0% of each run, Pallas kernels for 29% -> 32%
where the time goes in v10:
time: 63 us; the launch traced here: 62.8 us
  Pallas kernels  21.8 us (35%)
  starting transfers between devices  20.7 us (33%)
  waiting for transfers between devices  18.4 us (29%)
  local copies, waits for them, and re-layouts  1.14 us (2%)
  between operations  0.8 us (1%)
    ppermute x7, waiting for transfers between devices, over_x(): return lax.ppermute(array, 'ctx', [(i, i ^ 1) for i in range(length)])  9.08 us
    ppermute x8, waiting for transfers between devices, over_z(): return lax.ppermute(array, ('ctx', 'mp'), pairs)  9.01 us
    ppermute x7, starting transfers between devices, over_x(): return lax.ppermute(array, 'ctx', [(i, i ^ 1) for i in range(length)])  8.94 us
    ppermute x8, starting transfers between devices, over_z(): return lax.ppermute(array, ('ctx', 'mp'), pairs)  8.64 us
    pallas_call x2, Pallas kernels, query_pass(): pl.pallas_call(functools.partial(query_kernel, HD ** (-0.5), own, before...  5.94 us
    pallas_call x4, Pallas kernels, key_pass(): pl.pallas_call(functools.partial(key_kernel, HD ** (-0.5), own, heads), o...  4.39 us
    pallas_call x1, Pallas kernels, first_piece(): pl.pallas_call(first_kernel, out_shape=(jax.ShapeDtypeStruct((rows, heads...  3.82 us
    ppermute x3, starting transfers between devices, over_mp(): return lax.ppermute(array, 'mp', [(i, i ^ flip) for i in range(lanes)])  3.12 us
  transfers between devices with their start and end apart: 18, of which 7 were waited for; matrix products, arithmetic and copies ran while one was open for 0% of the time, Pallas kernels for 32%

profile of v10, /device:TPU:0, one launch (start us, length us, event | category | flops | bytes accessed | tf_op | source)
XLA Modules:
  0.0 62.8 jit_solution(595027518087038672)
XLA Ops:
  0.6 0.5 collective-permute-start.1
  1.1 2.6 %collective-permute-start = (bf16[256,1536]{1,0:T(8,128)(2,1)}, bf16[256,1536]{1,0:T(8,128)(2,1)S(1)}, u32[]{:S(2)}, u32[]{:S(2)}) collective-permute-start(bf16[256,1536]{1,0:T(8,128)(2,1)} %og.1), channel_id=1, source_target_pairs={{0,2},{1,3},{2,0},{3,1},{4,6},{5,7},{6,4},{7,5},{8,10},{9,11},{10,... | collective-permute-start | bytes 2359304 | tf_op jit(solution)/shard_map/ppermute | solution.py:410
  3.7 2.4 %pack.1 = (bf16[3,256,384]{2,1,0:T(8,128)(2,1)}, bf16[2,256,384]{2,1,0:T(8,128)(2,1)}, bf16[256,384]{1,0:T(8,128)(2,1)}) custom-call(bf16[256,768]{1,0:T(8,128)(2,1)} %q.1, bf16[256,768]{1,0:T(8,128)(2,1)} %k.1, bf16[256,768]{1,0:T(8,128)(2,1)} %v.1), custom_call_target="tpu_custom_call" | custom-call | flops 1 | bytes 1 | tf_op jit(solution)/shard_map/pack/pallas_call | solution.py:60
  6.1 1.6 %collective-permute-start.2 = (bf16[2,256,384]{2,1,0:T(8,128)(2,1)}, bf16[2,256,384]{2,1,0:T(8,128)(2,1)S(1)}, u32[]{:S(2)}, u32[]{:S(2)}) collective-permute-start(bf16[2,256,384]{2,1,0:T(8,128)(2,1)} %get-tuple-element.24), channel_id=1, source_target_pairs={{0,4},{4,0},{8,12},{12,8},{16,20},{20,16},{24,28},{28,24},{1,5},{5... | collective-permute-start | bytes 1179656 | tf_op jit(solution)/shard_map/ppermute | solution.py:413
  7.7 0.5 collective-permute-start.3
  8.2 1.6 %collective-permute-start.4 = (bf16[3,256,384]{2,1,0:T(8,128)(2,1)}, bf16[3,256,384]{2,1,0:T(8,128)(2,1)S(1)}, u32[]{:S(2)}, u32[]{:S(2)}) collective-permute-start(bf16[3,256,384]{2,1,0:T(8,128)(2,1)} %get-tuple-element.22.refs_2_.refs_0_.keep.keys.kv), channel_id=1, source_target_pairs={{0,8},{1,9},{2,10},{3,11},{4,12},{5,13},{6,14},{7,15},{8,0},{9,1},... | collective-permute-start | bytes 1769480 | tf_op jit(solution)/shard_map/ppermute | solution.py:427
  9.8 1.1 %copy-done.1 = bf16[256,1536]{1,0:T(8,128)(2,1)S(1)} copy-done((bf16[256,1536]{1,0:T(8,128)(2,1)S(1)}, bf16[256,1536]{1,0:T(8,128)(2,1)}, u32[]{:S(2)}) %copy-start.1) | copy-done | bytes 786456
  10.9 3.8 %head_grad_first.1 = (f32[256,768]{1,0:T(8,128)S(1)}, bf16[768,1536]{1,0:T(8,128)(2,1)S(1)}, bf16[768,1536]{1,0:T(8,128)(2,1)S(1)}) custom-call(bf16[256,1536]{1,0:T(8,128)(2,1)S(1)} %copy-done.1, bf16[256,1536]{1,0:T(8,128)(2,1)S(1)} %collective-permute-done.1.near, bf16[768,6144]{1,0:T(8,128)(2,1)} %w.1), custom_call_target="tpu_custom_call" | custom-call | flops 1 | bytes 1 | tf_op jit(solution)/shard_map/head_grad_first/pallas_call | solution.py:110
  14.8 7.0 %collective-permute-done.3.refs_2_.refs_0_.xq = bf16[256,384]{1,0:T(8,128)(2,1)S(1)} collective-permute-done((bf16[256,384]{1,0:T(8,128)(2,1)}, bf16[256,384]{1,0:T(8,128)(2,1)S(1)}, u32[]{:S(2)}, u32[]{:S(2)}) %collective-permute-start.3) | collective-permute-done | bytes 196640 | tf_op jit(solution)/shard_map/ppermute | solution.py:413
  22.1 1.8 %collective-permute-start.7 = (bf16[2,256,384]{2,1,0:T(8,128)(2,1)S(1)}, bf16[2,256,384]{2,1,0:T(8,128)(2,1)S(1)}, u32[]{:S(2)}, u32[]{:S(2)}) collective-permute-start(bf16[2,256,384]{2,1,0:T(8,128)(2,1)S(1)} %collective-permute-done.2.refs_1_.refs_3_.keys.kv), channel_id=1, source_target_pairs={{0,8},{1,9},{2,10},{3,11},{4,12},{5,13},{6,14},{7,15},{8,0},{9,1},... | collective-permute-start | bytes 1179656 | tf_op jit(solution)/shard_map/ppermute | solution.py:427
  24.1 0.8 %head_grad.2.refs_0_ = f32[256,768]{1,0:T(8,128)S(1)} custom-call(f32[256,768]{1,0:T(8,128)S(1)} %after.5.acc, bf16[256,1536]{1,0:T(8,128)(2,1)S(1)} %collective-permute-done.piece, bf16[768,1536]{1,0:T(8,128)(2,1)S(1)} %get-tuple-element.28.w), custom_call_target="tpu_custom_call" | custom-call | flops 1 | bytes 1 | tf_op jit(solution)/shard_map/head_grad/pallas_call | solution.py:147
  25.0 0.9 %head_grad.3 = (bf16[256,384]{1,0:T(8,128)(2,1)S(1)}, bf16[256,384]{1,0:T(8,128)(2,1)S(1)}) custom-call(f32[256,768]{1,0:T(8,128)S(1)} %after.6.acc, bf16[256,1536]{1,0:T(8,128)(2,1)S(1)} %collective-permute-done.6.piece, bf16[768,1536]{1,0:T(8,128)(2,1)S(1)} %get-tuple-element.29.w), custom_call_target="tpu_custom_call" | custom-call | flops 1 | bytes 1 | tf_op jit(solution)/shard_map/head_grad/pallas_call | solution.py:147
  25.9 1.5 %collective-permute-start.9 = (bf16[256,384]{1,0:T(8,128)(2,1)S(1)}, bf16[256,384]{1,0:T(8,128)(2,1)S(1)}, u32[]{:S(2)}, u32[]{:S(2)}) collective-permute-start(bf16[256,384]{1,0:T(8,128)(2,1)S(1)} %get-tuple-element.34), channel_id=1, source_target_pairs={{0,4},{4,0},{8,12},{12,8},{16,20},{20,16},{24,28},{28,24},{1,5},{5... | collective-permute-start | bytes 589832 | tf_op jit(solution)/shard_map/ppermute | solution.py:413
  27.4 6.3 %collective-permute-done.7.refs_4_.refs_6_ = bf16[2,256,384]{2,1,0:T(8,128)(2,1)S(1)} collective-permute-done((bf16[2,256,384]{2,1,0:T(8,128)(2,1)S(1)}, bf16[2,256,384]{2,1,0:T(8,128)(2,1)S(1)}, u32[]{:S(2)}, u32[]{:S(2)}) %collective-permute-start.7) | collective-permute-done | bytes 393248 | tf_op jit(solution)/shard_map/ppermute | solution.py:427
  33.8 2.9 %collective-permute-start.10 = (bf16[3,256,384]{2,1,0:T(8,128)(2,1)S(1)}, bf16[3,256,384]{2,1,0:T(8,128)(2,1)S(1)}, u32[]{:S(2)}, u32[]{:S(2)}) collective-permute-start(bf16[3,256,384]{2,1,0:T(8,128)(2,1)S(1)} %join.1), channel_id=1, source_target_pairs={{0,8},{1,9},{2,10},{3,11},{4,12},{5,13},{6,14},{7,15},{8,0},{9,1},... | collective-permute-start | bytes 1769480 | tf_op jit(solution)/shard_map/ppermute | solution.py:427
  36.7 3.0 %query_pass.2 = (bf16[256,384]{1,0:T(8,128)(2,1)S(1)}, f32[8,256]{1,0:T(8,128)S(1)}) custom-call(bf16[256,384]{1,0:T(8,128)(2,1)S(1)} %collective-permute-done.3.refs_2_.refs_0_.xq, bf16[256,384]{1,0:T(8,128)(2,1)S(1)} %after.7.refs_1_.dxr.refs_2_, bf16[3,256,384]{2,1,0:T(8,128)(2,1)S(1)} %copy-done, ...), custom_call_target="tpu_custom_call" | custom-call | flops 1 | bytes 1 | tf_op jit(solution)/shard_map/query_pass/pallas_call | solution.py:256
  39.7 1.6 %collective-permute-start.12 = (bf16[256,384]{1,0:T(8,128)(2,1)S(1)}, bf16[256,384]{1,0:T(8,128)(2,1)S(1)}, u32[]{:S(2)}, u32[]{:S(2)}) collective-permute-start(bf16[256,384]{1,0:T(8,128)(2,1)S(1)} %get-tuple-element.38), channel_id=1, source_target_pairs={{0,4},{4,0},{8,12},{12,8},{16,20},{20,16},{24,28},{28,24},{1,5},{5... | collective-permute-start | bytes 589832 | tf_op jit(solution)/shard_map/ppermute | solution.py:413
  41.2 3.0 %query_pass.3 = (bf16[256,384]{1,0:T(8,128)(2,1)S(1)}, f32[8,512]{1,0:T(8,128)S(1)}) custom-call(bf16[3,256,384]{2,1,0:T(8,128)(2,1)S(1)} %copy-done, bf16[256,384]{1,0:T(8,128)(2,1)S(1)} %get-tuple-element.30.refs_1_.dkeep, bf16[3,256,384]{2,1,0:T(8,128)(2,1)S(1)} %copy-done, bf16[2,256,384]{2,1,0:T(8,128)(2,1)S(1)} %collective-permute-done.2.refs_1_.refs_3_.keys.kv, ...), custom_call_target="tpu_custom_call" | custom-call | flops 6000000000 | bytes 1 | tf_op jit(solution)/shard_map/query_pass/pallas_call | solution.py:256
  44.2 2.1 %collective-permute-start.13 = (f32[8,512]{1,0:T(8,128)S(1)}, f32[8,512]{1,0:T(8,128)S(1)}, u32[]{:S(2)}, u32[]{:S(2)}) collective-permute-start(f32[8,512]{1,0:T(8,128)S(1)} %get-tuple-element.37.stats), channel_id=1, source_target_pairs={{0,8},{1,9},{2,10},{3,11},{4,12},{5,13},{6,14},{7,15},{8,0},{9,1},... | collective-permute-start | bytes 49160 | tf_op jit(solution)/shard_map/ppermute | solution.py:427
  46.3 1.2 %own_pass.2.refs_0_ = f32[2,256,384]{2,1,0:T(8,128)S(1)} custom-call(bf16[2,256,384]{2,1,0:T(8,128)(2,1)S(1)} %collective-permute-done.2.refs_1_.refs_3_.keys.kv, bf16[3,256,384]{2,1,0:T(8,128)(2,1)S(1)} %copy-done, bf16[256,384]{1,0:T(8,128)(2,1)S(1)} %collective-permute-done.3.refs_2_.refs_0_.xq, bf16[256,384]{1,0:T(8,128)(2,1)S(1)} %get-tuple-element.30.refs_1_.dkeep, ...), custom_call_target="tpu_custom_call" | custom-call | flops 1 | bytes 1 | tf_op jit(solution)/shard_map/own_pass/pallas_call | solution.py:306
  47.5 2.5 %collective-permute-done.10.refs_1_.late_e = bf16[3,256,384]{2,1,0:T(8,128)(2,1)S(1)} collective-permute-done((bf16[3,256,384]{2,1,0:T(8,128)(2,1)S(1)}, bf16[3,256,384]{2,1,0:T(8,128)(2,1)S(1)}, u32[]{:S(2)}, u32[]{:S(2)}) %collective-permute-start.10) | collective-permute-done | bytes 589856 | tf_op jit(solution)/shard_map/ppermute | solution.py:427
  50.3 0.8 %key_pass.7 = bf16[2,256,128]{2,1,0:T(8,128)(2,1)S(1)} custom-call(bf16[2,256,384]{2,1,0:T(8,128)(2,1)S(1)} %collective-permute-done.2.refs_1_.refs_3_.keys.kv, bf16[3,256,384]{2,1,0:T(8,128)(2,1)S(1)} %collective-permute-done.4.refs_1_.refs_6_.refs_4_.e0, bf16[3,256,384]{2,1,0:T(8,128)(2,1)S(1)} %collective-permute-done.5.refs_2_.refs_7_.refs_5_.o0, ...), custom_call_target="tpu_custom_call" | custom-call | flops 1000000000 | bytes 1 | tf_op jit(solution)/shard_map/key_pass/pallas_call | solution.py:360
  51.0 1.6 %collective-permute-start.17 = (bf16[2,256,128]{2,1,0:T(8,128)(2,1)S(1)}, bf16[2,256,128]{2,1,0:T(8,128)(2,1)S(1)}, u32[]{:S(2)}, u32[]{:S(2)}) collective-permute-start(bf16[2,256,128]{2,1,0:T(8,128)(2,1)S(1)} %key_pass.7), channel_id=1, source_target_pairs={{0,4},{4,0},{8,12},{12,8},{16,20},{20,16},{24,28},{28,24},{1,5},{5... | collective-permute-start | bytes 393224 | tf_op jit(solution)/shard_map/ppermute | solution.py:413
  52.6 0.8 %key_pass.6 = bf16[2,256,128]{2,1,0:T(8,128)(2,1)S(1)} custom-call(bf16[2,256,384]{2,1,0:T(8,128)(2,1)S(1)} %collective-permute-done.2.refs_1_.refs_3_.keys.kv, bf16[3,256,384]{2,1,0:T(8,128)(2,1)S(1)} %collective-permute-done.4.refs_1_.refs_6_.refs_4_.e0, bf16[3,256,384]{2,1,0:T(8,128)(2,1)S(1)} %collective-permute-done.5.refs_2_.refs_7_.refs_5_.o0, ...), custom_call_target="tpu_custom_call" | custom-call | flops 1000000000 | bytes 1 | tf_op jit(solution)/shard_map/key_pass/pallas_call | solution.py:360
  53.3 0.6 collective-permute-start.16
  53.9 0.9 %key_pass.5 = bf16[2,256,128]{2,1,0:T(8,128)(2,1)S(1)} custom-call(bf16[2,256,384]{2,1,0:T(8,128)(2,1)S(1)} %collective-permute-done.2.refs_1_.refs_3_.keys.kv, bf16[3,256,384]{2,1,0:T(8,128)(2,1)S(1)} %collective-permute-done.4.refs_1_.refs_6_.refs_4_.e0, bf16[3,256,384]{2,1,0:T(8,128)(2,1)S(1)} %collective-permute-done.5.refs_2_.refs_7_.refs_5_.o0, ...), custom_call_target="tpu_custom_call" | custom-call | flops 1000000000 | bytes 1 | tf_op jit(solution)/shard_map/key_pass/pallas_call | solution.py:360
  54.9 1.6 %collective-permute-start.15 = (bf16[2,256,128]{2,1,0:T(8,128)(2,1)S(1)}, bf16[2,256,128]{2,1,0:T(8,128)(2,1)S(1)}, u32[]{:S(2)}, u32[]{:S(2)}) collective-permute-start(bf16[2,256,128]{2,1,0:T(8,128)(2,1)S(1)} %key_pass.5), channel_id=1, source_target_pairs={{0,4},{4,0},{8,12},{12,8},{16,20},{20,16},{24,28},{28,24},{1,5},{5... | collective-permute-start | bytes 393224 | tf_op jit(solution)/shard_map/ppermute | solution.py:413
  56.5 1.2 %own_pass.3.sums = f32[2,256,384]{2,1,0:T(8,128)S(1)} custom-call(bf16[3,256,384]{2,1,0:T(8,128)(2,1)S(1)} %copy-done, bf16[3,256,384]{2,1,0:T(8,128)(2,1)S(1)} %copy-done, bf16[256,384]{1,0:T(8,128)(2,1)S(1)} %collective-permute-done.3.refs_2_.refs_0_.xq, bf16[256,384]{1,0:T(8,128)(2,1)S(1)} %get-tuple-element.30.refs_1_.dkeep, ...), custom_call_target="tpu_custom_call" | custom-call | flops 1 | bytes 1 | tf_op jit(solution)/shard_map/own_pass/pallas_call | solution.py:306
  57.7 1.9 %key_pass.4.kv_keep = bf16[2,256,384]{2,1,0:T(8,128)(2,1)S(1)} custom-call(bf16[3,256,384]{2,1,0:T(8,128)(2,1)S(1)} %copy-done, bf16[3,256,384]{2,1,0:T(8,128)(2,1)S(1)} %collective-permute-done.4.refs_1_.refs_6_.refs_4_.e0, bf16[3,256,384]{2,1,0:T(8,128)(2,1)S(1)} %collective-permute-done.5.refs_2_.refs_7_.refs_5_.o0, ...), custom_call_target="tpu_custom_call" | custom-call | flops 1000000000 | bytes 1 | tf_op jit(solution)/shard_map/key_pass/pallas_call | solution.py:360
  59.6 0.4 collective-permute-done.16.refs_1_
  60.0 1.6 %collective-permute-done.15.refs_0_ = bf16[2,256,128]{2,1,0:T(8,128)(2,1)S(1)} collective-permute-done((bf16[2,256,128]{2,1,0:T(8,128)(2,1)S(1)}, bf16[2,256,128]{2,1,0:T(8,128)(2,1)S(1)}, u32[]{:S(2)}, u32[]{:S(2)}) %collective-permute-start.15) | collective-permute-done | bytes 131104 | tf_op jit(solution)/shard_map/ppermute | solution.py:413
  61.7 1.2 %unpack.1 = (bf16[256,768]{1,0:T(8,128)(2,1)}, bf16[256,768]{1,0:T(8,128)(2,1)}, bf16[256,768]{1,0:T(8,128)(2,1)}) custom-call(bf16[256,384]{1,0:T(8,128)(2,1)S(1)} %get-tuple-element.36.q_keep, bf16[256,384]{1,0:T(8,128)(2,1)S(1)} %after.9.q_got, bf16[2,256,384]{2,1,0:T(8,128)(2,1)S(1)} %key_pass.4.kv_keep, ...), custom_call_target="tpu_custom_call" | custom-call | flops 1 | bytes 1 | tf_op jit(solution)/shard_map/unpack/pallas_call | solution.py:392
  (27 shorter events, 0.8 us)
Async XLA Ops:
  0.6 9.2 %collective-permute-start.1 = (bf16[256,1536]{1,0:T(8,128)(2,1)}, bf16[256,1536]{1,0:T(8,128)(2,1)S(1)}, u32[]{:S(2)}, u32[]{:S(2)}) collective-permute-start(bf16[256,1536]{1,0:T(8,128)(2,1)} %og.1), channel_id=1, source_target_pairs={{0,1},{1,0},{2,3},{3,2},{4,5},{5,4},{6,7},{7,6},{8,9},{9,8},{10,11... | collective-permute-start | bytes 2359304 | tf_op jit(solution)/shard_map/ppermute | solution.py:410
  1.1 20.9 %collective-permute-start = (bf16[256,1536]{1,0:T(8,128)(2,1)}, bf16[256,1536]{1,0:T(8,128)(2,1)S(1)}, u32[]{:S(2)}, u32[]{:S(2)}) collective-permute-start(bf16[256,1536]{1,0:T(8,128)(2,1)} %og.1), channel_id=1, source_target_pairs={{0,2},{1,3},{2,0},{3,1},{4,6},{5,7},{6,4},{7,5},{8,10},{9,11},{10,... | collective-permute-start | bytes 2359304 | tf_op jit(solution)/shard_map/ppermute | solution.py:410
  6.1 15.7 %collective-permute-start.2 = (bf16[2,256,384]{2,1,0:T(8,128)(2,1)}, bf16[2,256,384]{2,1,0:T(8,128)(2,1)S(1)}, u32[]{:S(2)}, u32[]{:S(2)}) collective-permute-start(bf16[2,256,384]{2,1,0:T(8,128)(2,1)} %get-tuple-element.24), channel_id=1, source_target_pairs={{0,4},{4,0},{8,12},{12,8},{16,20},{20,16},{24,28},{28,24},{1,5},{5... | collective-permute-start | bytes 1179656 | tf_op jit(solution)/shard_map/ppermute | solution.py:413
  7.7 14.1 %collective-permute-start.3 = (bf16[256,384]{1,0:T(8,128)(2,1)}, bf16[256,384]{1,0:T(8,128)(2,1)S(1)}, u32[]{:S(2)}, u32[]{:S(2)}) collective-permute-start(bf16[256,384]{1,0:T(8,128)(2,1)} %get-tuple-element.25), channel_id=1, source_target_pairs={{0,4},{4,0},{8,12},{12,8},{16,20},{20,16},{24,28},{28,24},{1,5},{5... | collective-permute-start | bytes 589832 | tf_op jit(solution)/shard_map/ppermute | solution.py:413
  8.2 16.7 %collective-permute-start.4 = (bf16[3,256,384]{2,1,0:T(8,128)(2,1)}, bf16[3,256,384]{2,1,0:T(8,128)(2,1)S(1)}, u32[]{:S(2)}, u32[]{:S(2)}) collective-permute-start(bf16[3,256,384]{2,1,0:T(8,128)(2,1)} %get-tuple-element.22.refs_2_.refs_0_.keep.keys.kv), channel_id=1, source_target_pairs={{0,8},{1,9},{2,10},{3,11},{4,12},{5,13},{6,14},{7,15},{8,0},{9,1},... | collective-permute-start | bytes 1769480 | tf_op jit(solution)/shard_map/ppermute | solution.py:427
  9.8 15.1 %collective-permute-start.5 = (bf16[3,256,384]{2,1,0:T(8,128)(2,1)}, bf16[3,256,384]{2,1,0:T(8,128)(2,1)S(1)}, u32[]{:S(2)}, u32[]{:S(2)}) collective-permute-start(bf16[3,256,384]{2,1,0:T(8,128)(2,1)} %get-tuple-element.22.refs_2_.refs_0_.keep.keys.kv), channel_id=1, source_target_pairs={{0,1},{1,0},{2,3},{3,2},{4,5},{5,4},{6,7},{7,6},{8,16},{9,17},{10,... | collective-permute-start | bytes 1769480 | tf_op jit(solution)/shard_map/ppermute | solution.py:427
  9.8 1.1 %copy-start.1 = (bf16[256,1536]{1,0:T(8,128)(2,1)S(1)}, bf16[256,1536]{1,0:T(8,128)(2,1)}, u32[]{:S(2)}) copy-start(bf16[256,1536]{1,0:T(8,128)(2,1)} %og.1) | copy-start | bytes 2359300
  22.1 2.9 %collective-permute-start.6 = (bf16[256,1536]{1,0:T(8,128)(2,1)S(1)}, bf16[256,1536]{1,0:T(8,128)(2,1)S(1)}, u32[]{:S(2)}, u32[]{:S(2)}) collective-permute-start(bf16[256,1536]{1,0:T(8,128)(2,1)S(1)} %collective-permute-done.piece), channel_id=1, source_target_pairs={{0,1},{1,0},{2,3},{3,2},{4,5},{5,4},{6,7},{7,6},{8,9},{9,8},{10,11... | collective-permute-start | bytes 2359304 | tf_op jit(solution)/shard_map/ppermute | solution.py:410
  22.1 11.6 %collective-permute-start.7 = (bf16[2,256,384]{2,1,0:T(8,128)(2,1)S(1)}, bf16[2,256,384]{2,1,0:T(8,128)(2,1)S(1)}, u32[]{:S(2)}, u32[]{:S(2)}) collective-permute-start(bf16[2,256,384]{2,1,0:T(8,128)(2,1)S(1)} %collective-permute-done.2.refs_1_.refs_3_.keys.kv), channel_id=1, source_target_pairs={{0,8},{1,9},{2,10},{3,11},{4,12},{5,13},{6,14},{7,15},{8,0},{9,1},... | collective-permute-start | bytes 1179656 | tf_op jit(solution)/shard_map/ppermute | solution.py:427
  23.9 9.8 %collective-permute-start.8 = (bf16[2,256,384]{2,1,0:T(8,128)(2,1)S(1)}, bf16[2,256,384]{2,1,0:T(8,128)(2,1)S(1)}, u32[]{:S(2)}, u32[]{:S(2)}) collective-permute-start(bf16[2,256,384]{2,1,0:T(8,128)(2,1)S(1)} %collective-permute-done.2.refs_1_.refs_3_.keys.kv), channel_id=1, source_target_pairs={{0,1},{1,0},{2,3},{3,2},{4,5},{5,4},{6,7},{7,6},{8,16},{9,17},{10,... | collective-permute-start | bytes 1179656 | tf_op jit(solution)/shard_map/ppermute | solution.py:427
  25.8 10.9 %copy-start = (bf16[3,256,384]{2,1,0:T(8,128)(2,1)S(1)}, bf16[3,256,384]{2,1,0:T(8,128)(2,1)}, u32[]{:S(2)}) copy-start(bf16[3,256,384]{2,1,0:T(8,128)(2,1)} %get-tuple-element.22.refs_2_.refs_0_.keep.keys.kv) | copy-start | bytes 1769476
  25.9 7.8 %collective-permute-start.9 = (bf16[256,384]{1,0:T(8,128)(2,1)S(1)}, bf16[256,384]{1,0:T(8,128)(2,1)S(1)}, u32[]{:S(2)}, u32[]{:S(2)}) collective-permute-start(bf16[256,384]{1,0:T(8,128)(2,1)S(1)} %get-tuple-element.34), channel_id=1, source_target_pairs={{0,4},{4,0},{8,12},{12,8},{16,20},{20,16},{24,28},{28,24},{1,5},{5... | collective-permute-start | bytes 589832 | tf_op jit(solution)/shard_map/ppermute | solution.py:413
  33.8 16.3 %collective-permute-start.10 = (bf16[3,256,384]{2,1,0:T(8,128)(2,1)S(1)}, bf16[3,256,384]{2,1,0:T(8,128)(2,1)S(1)}, u32[]{:S(2)}, u32[]{:S(2)}) collective-permute-start(bf16[3,256,384]{2,1,0:T(8,128)(2,1)S(1)} %join.1), channel_id=1, source_target_pairs={{0,8},{1,9},{2,10},{3,11},{4,12},{5,13},{6,14},{7,15},{8,0},{9,1},... | collective-permute-start | bytes 1769480 | tf_op jit(solution)/shard_map/ppermute | solution.py:427
  36.7 13.4 %collective-permute-start.11 = (bf16[3,256,384]{2,1,0:T(8,128)(2,1)S(1)}, bf16[3,256,384]{2,1,0:T(8,128)(2,1)S(1)}, u32[]{:S(2)}, u32[]{:S(2)}) collective-permute-start(bf16[3,256,384]{2,1,0:T(8,128)(2,1)S(1)} %join.1), channel_id=1, source_target_pairs={{0,1},{1,0},{2,3},{3,2},{4,5},{5,4},{6,7},{7,6},{8,16},{9,17},{10,... | collective-permute-start | bytes 1769480 | tf_op jit(solution)/shard_map/ppermute | solution.py:427
  39.7 7.9 %collective-permute-start.12 = (bf16[256,384]{1,0:T(8,128)(2,1)S(1)}, bf16[256,384]{1,0:T(8,128)(2,1)S(1)}, u32[]{:S(2)}, u32[]{:S(2)}) collective-permute-start(bf16[256,384]{1,0:T(8,128)(2,1)S(1)} %get-tuple-element.38), channel_id=1, source_target_pairs={{0,4},{4,0},{8,12},{12,8},{16,20},{20,16},{24,28},{28,24},{1,5},{5... | collective-permute-start | bytes 589832 | tf_op jit(solution)/shard_map/ppermute | solution.py:413
  44.2 6.0 %collective-permute-start.13 = (f32[8,512]{1,0:T(8,128)S(1)}, f32[8,512]{1,0:T(8,128)S(1)}, u32[]{:S(2)}, u32[]{:S(2)}) collective-permute-start(f32[8,512]{1,0:T(8,128)S(1)} %get-tuple-element.37.stats), channel_id=1, source_target_pairs={{0,8},{1,9},{2,10},{3,11},{4,12},{5,13},{6,14},{7,15},{8,0},{9,1},... | collective-permute-start | bytes 49160 | tf_op jit(solution)/shard_map/ppermute | solution.py:427
  46.3 4.0 %collective-permute-start.14 = (f32[8,512]{1,0:T(8,128)S(1)}, f32[8,512]{1,0:T(8,128)S(1)}, u32[]{:S(2)}, u32[]{:S(2)}) collective-permute-start(f32[8,512]{1,0:T(8,128)S(1)} %get-tuple-element.37.stats), channel_id=1, source_target_pairs={{0,1},{1,0},{2,3},{3,2},{4,5},{5,4},{6,7},{7,6},{8,16},{9,17},{10,... | collective-permute-start | bytes 49160 | tf_op jit(solution)/shard_map/ppermute | solution.py:427
  51.0 8.6 %collective-permute-start.17 = (bf16[2,256,128]{2,1,0:T(8,128)(2,1)S(1)}, bf16[2,256,128]{2,1,0:T(8,128)(2,1)S(1)}, u32[]{:S(2)}, u32[]{:S(2)}) collective-permute-start(bf16[2,256,128]{2,1,0:T(8,128)(2,1)S(1)} %key_pass.7), channel_id=1, source_target_pairs={{0,4},{4,0},{8,12},{12,8},{16,20},{20,16},{24,28},{28,24},{1,5},{5... | collective-permute-start | bytes 393224 | tf_op jit(solution)/shard_map/ppermute | solution.py:413
  53.3 6.7 %collective-permute-start.16 = (bf16[2,256,128]{2,1,0:T(8,128)(2,1)S(1)}, bf16[2,256,128]{2,1,0:T(8,128)(2,1)S(1)}, u32[]{:S(2)}, u32[]{:S(2)}) collective-permute-start(bf16[2,256,128]{2,1,0:T(8,128)(2,1)S(1)} %key_pass.6), channel_id=1, source_target_pairs={{0,4},{4,0},{8,12},{12,8},{16,20},{20,16},{24,28},{28,24},{1,5},{5... | collective-permute-start | bytes 393224 | tf_op jit(solution)/shard_map/ppermute | solution.py:413
  54.9 6.8 %collective-permute-start.15 = (bf16[2,256,128]{2,1,0:T(8,128)(2,1)S(1)}, bf16[2,256,128]{2,1,0:T(8,128)(2,1)S(1)}, u32[]{:S(2)}, u32[]{:S(2)}) collective-permute-start(bf16[2,256,128]{2,1,0:T(8,128)(2,1)S(1)} %key_pass.5), channel_id=1, source_target_pairs={{0,4},{4,0},{8,12},{12,8},{16,20},{20,16},{24,28},{28,24},{1,5},{5... | collective-permute-start | bytes 393224 | tf_op jit(solution)/shard_map/ppermute | solution.py:413

commit v11 on v10

--- a/solution.py
+++ b/solution.py
@@ -237,7 +237,7 @@
             nn((w * (g - delta)).astype(BF16), ref[0, :, cols])
             for w, g, (ref, _) in zip(weights, grads, runs)
         )
-        out[:, cols] = (result * (inverse * scale)).astype(BF16)
+        out[0, :, cols] = (result * (inverse * scale)).astype(BF16)
         mark = jnp.where(lane == 2 * head, top + jnp.log2(total), mark)
         mark = jnp.where(lane == 2 * head + 1, delta, mark)
     marks = jnp.transpose(mark)[: stats.shape[0], :]
@@ -256,7 +256,7 @@
     return pl.pallas_call(
         functools.partial(query_kernel, HD ** -0.5, own, before is not None),
         out_shape=(
-            jax.ShapeDtypeStruct((rows, cols), BF16),
+            jax.ShapeDtypeStruct((1, rows, cols), BF16),
             jax.ShapeDtypeStruct((8, rows if before is None else 2 * rows), F32),
         ),
         in_specs=[VM] * len(operands),
@@ -369,35 +369,40 @@
     )(kv, *operands)
 
 
-def unpack_kernel(q_keep, q_got, kv_keep, *refs):
-    got, (dq, dk, dv) = refs[:-3], refs[-3:]
-    half = q_keep.shape[1]
+def unpack_kernel(n_out, kept, *refs):
+    got, outs, sem = refs[: -1 - n_out], refs[-1 - n_out : -1], refs[-1]
+    half = kept.shape[2]
     x = lax.rem(lax.axis_index("ctx"), 2)
     mine = pl.multiple_of(x * half, half)
     theirs = pl.multiple_of((1 - x) * half, half)
-    dq[:, pl.ds(mine, half)] = q_keep[...]
-    dq[:, pl.ds(theirs, half)] = q_got[...]
-    for i, out in enumerate((dk, dv)):
-        out[:, pl.ds(mine, half)] = kv_keep[i]
+    copies = []
+    for i, out in enumerate(outs):
+        pairs = [(kept.at[i], out.at[:, pl.ds(mine, half)])]
         first = 0
         for piece in got:
             width = piece.shape[2]
-            out[:, pl.ds(theirs + first, width)] = piece[i]
+            pairs.append((piece.at[i], out.at[:, pl.ds(theirs + first, width)]))
             first += width
-
-
-def unpack(q_keep, q_got, kv_keep, *got):
-    rows, half = q_keep.shape
-    whole = jax.ShapeDtypeStruct((rows, 2 * half), BF16)
-    return pl.pallas_call(
-        unpack_kernel,
-        out_shape=(whole,) * 3,
-        in_specs=[VM] * (3 + len(got)),
-        out_specs=(VM,) * 3,
+        for a, b in pairs:
+            copies.append(pltpu.make_async_copy(a, b, sem.at[len(copies)]))
+    for copy in copies:
+        copy.start()
+    for copy in copies:
+        copy.wait()
+
+
+def unpack(kept, *got):
+    n, rows, half = kept.shape
+    return pl.pallas_call(
+        functools.partial(unpack_kernel, n),
+        out_shape=(jax.ShapeDtypeStruct((rows, 2 * half), BF16),) * n,
+        in_specs=[VM] * (1 + len(got)),
+        out_specs=(ANY,) * n,
+        scratch_shapes=[pltpu.SemaphoreType.DMA((n * (1 + len(got)),))],
         compiler_params=params(16),
         cost_estimate=cost(),
         name="unpack",
-    )(q_keep, q_got, kv_keep, *got)
+    )(kept, *got)
 
 
 def body(queries, keys, values, out_grad, out_weight):
@@ -456,10 +461,11 @@
     got = []
     for head in range(heads):
         if head == 1:
-            sums, dq_got = lax.optimization_barrier((sums, dq_got))
+            dq, = unpack(dq_keep, dq_got)
+            sums, dq = lax.optimization_barrier((sums, dq))
         got.append(over_x(key_pass(False, (head,), xkv, *theirs, sums)))
     kv_keep = key_pass(True, tuple(range(heads)), keep, *theirs, own_sums)
-    return tuple(unpack(dq_keep, dq_got, kv_keep, *got))
+    return (dq, *unpack(kv_keep, *got))
 
 
 def solution(mesh):

time: 63 us -> 63 us (level)
  waiting for transfers between devices: 18.4 us -> 17.6 us
    ppermute x8, waiting for transfers between devices: 9.01 us -> 8.23 us  [over_z(): return lax.ppermute(array, ('ctx', 'mp'), pairs)]
    pallas_call x1 -> x2, Pallas kernels: 1.16 us -> 1.71 us  [unpack(): pl.pallas_call(functools.partial(unpack_kernel, n), out_shape=(jax.ShapeD...]
  transfers between devices with their start and end apart: 18 -> 18, of which waited for: 7 -> 7; matrix products, arithmetic and copies ran while one was open for 0% -> 0% of each run, Pallas kernels for 32% -> 33%
where the time goes in v11:
time: 63 us; the launch traced here: 62.8 us
  Pallas kernels  22.4 us (36%)
  starting transfers between devices  20.7 us (33%)
  waiting for transfers between devices  17.6 us (28%)
  local copies, waits for them, and re-layouts  1.14 us (2%)
  between operations  0.97 us (2%)
    ppermute x7, waiting for transfers between devices, over_x(): return lax.ppermute(array, 'ctx', [(i, i ^ 1) for i in range(length)])  9.08 us
    ppermute x7, starting transfers between devices, over_x(): return lax.ppermute(array, 'ctx', [(i, i ^ 1) for i in range(length)])  8.94 us
    ppermute x8, starting transfers between devices, over_z(): return lax.ppermute(array, ('ctx', 'mp'), pairs)  8.64 us
    ppermute x8, waiting for transfers between devices, over_z(): return lax.ppermute(array, ('ctx', 'mp'), pairs)  8.23 us
    pallas_call x2, Pallas kernels, query_pass(): pl.pallas_call(functools.partial(query_kernel, HD ** (-0.5), own, before...  5.94 us
    pallas_call x4, Pallas kernels, key_pass(): pl.pallas_call(functools.partial(key_kernel, HD ** (-0.5), own, heads), o...  4.39 us
    pallas_call x1, Pallas kernels, first_piece(): pl.pallas_call(first_kernel, out_shape=(jax.ShapeDtypeStruct((rows, heads...  3.82 us
    ppermute x3, starting transfers between devices, over_mp(): return lax.ppermute(array, 'mp', [(i, i ^ flip) for i in range(lanes)])  3.12 us
  transfers between devices with their start and end apart: 18, of which 7 were waited for; matrix products, arithmetic and copies ran while one was open for 0% of the time, Pallas kernels for 33%

profile of v11, /device:TPU:0, one launch (start us, length us, event | category | flops | bytes accessed | tf_op | source)
XLA Modules:
  0.0 62.8 jit_solution(778854769926165535)
XLA Ops:
  0.6 0.5 collective-permute-start.5
  1.1 2.6 %collective-permute-start.4 = (bf16[256,1536]{1,0:T(8,128)(2,1)}, bf16[256,1536]{1,0:T(8,128)(2,1)S(1)}, u32[]{:S(2)}, u32[]{:S(2)}) collective-permute-start(bf16[256,1536]{1,0:T(8,128)(2,1)} %og.1), channel_id=1, source_target_pairs={{0,2},{1,3},{2,0},{3,1},{4,6},{5,7},{6,4},{7,5},{8,10},{9,11},{10,... | collective-permute-start | bytes 2359304 | tf_op jit(solution)/shard_map/ppermute | solution.py:415
  3.7 2.4 %pack.1 = (bf16[3,256,384]{2,1,0:T(8,128)(2,1)}, bf16[2,256,384]{2,1,0:T(8,128)(2,1)}, bf16[256,384]{1,0:T(8,128)(2,1)}) custom-call(bf16[256,768]{1,0:T(8,128)(2,1)} %q.1, bf16[256,768]{1,0:T(8,128)(2,1)} %k.1, bf16[256,768]{1,0:T(8,128)(2,1)} %v.1), custom_call_target="tpu_custom_call" | custom-call | flops 1 | bytes 1 | tf_op jit(solution)/shard_map/pack/pallas_call | solution.py:60
  6.1 1.6 %collective-permute-start = (bf16[2,256,384]{2,1,0:T(8,128)(2,1)}, bf16[2,256,384]{2,1,0:T(8,128)(2,1)S(1)}, u32[]{:S(2)}, u32[]{:S(2)}) collective-permute-start(bf16[2,256,384]{2,1,0:T(8,128)(2,1)} %get-tuple-element.24), channel_id=1, source_target_pairs={{0,4},{4,0},{8,12},{12,8},{16,20},{20,16},{24,28},{28,24},{1,5},{5... | collective-permute-start | bytes 1179656 | tf_op jit(solution)/shard_map/ppermute | solution.py:418
  7.7 0.5 collective-permute-start.1
  8.2 1.6 %collective-permute-start.6 = (bf16[3,256,384]{2,1,0:T(8,128)(2,1)}, bf16[3,256,384]{2,1,0:T(8,128)(2,1)S(1)}, u32[]{:S(2)}, u32[]{:S(2)}) collective-permute-start(bf16[3,256,384]{2,1,0:T(8,128)(2,1)} %get-tuple-element.25.refs_2_.refs_0_.keep.keys.kv), channel_id=1, source_target_pairs={{0,8},{1,9},{2,10},{3,11},{4,12},{5,13},{6,14},{7,15},{8,0},{9,1},... | collective-permute-start | bytes 1769480 | tf_op jit(solution)/shard_map/ppermute | solution.py:432
  9.8 1.1 %copy-done.1 = bf16[256,1536]{1,0:T(8,128)(2,1)S(1)} copy-done((bf16[256,1536]{1,0:T(8,128)(2,1)S(1)}, bf16[256,1536]{1,0:T(8,128)(2,1)}, u32[]{:S(2)}) %copy-start.1) | copy-done | bytes 786456
  10.9 3.8 %head_grad_first.1 = (f32[256,768]{1,0:T(8,128)S(1)}, bf16[768,1536]{1,0:T(8,128)(2,1)S(1)}, bf16[768,1536]{1,0:T(8,128)(2,1)S(1)}) custom-call(bf16[256,1536]{1,0:T(8,128)(2,1)S(1)} %copy-done.1, bf16[256,1536]{1,0:T(8,128)(2,1)S(1)} %collective-permute-done.5.near, bf16[768,6144]{1,0:T(8,128)(2,1)} %w.1), custom_call_target="tpu_custom_call" | custom-call | flops 1 | bytes 1 | tf_op jit(solution)/shard_map/head_grad_first/pallas_call | solution.py:110
  14.8 7.0 %collective-permute-done.1.refs_2_.refs_0_.xq = bf16[256,384]{1,0:T(8,128)(2,1)S(1)} collective-permute-done((bf16[256,384]{1,0:T(8,128)(2,1)}, bf16[256,384]{1,0:T(8,128)(2,1)S(1)}, u32[]{:S(2)}, u32[]{:S(2)}) %collective-permute-start.1) | collective-permute-done | bytes 196640 | tf_op jit(solution)/shard_map/ppermute | solution.py:418
  22.1 1.8 %collective-permute-start.2 = (bf16[2,256,384]{2,1,0:T(8,128)(2,1)S(1)}, bf16[2,256,384]{2,1,0:T(8,128)(2,1)S(1)}, u32[]{:S(2)}, u32[]{:S(2)}) collective-permute-start(bf16[2,256,384]{2,1,0:T(8,128)(2,1)S(1)} %collective-permute-done.refs_1_.refs_3_.keys.kv), channel_id=1, source_target_pairs={{0,8},{1,9},{2,10},{3,11},{4,12},{5,13},{6,14},{7,15},{8,0},{9,1},... | collective-permute-start | bytes 1179656 | tf_op jit(solution)/shard_map/ppermute | solution.py:432
  24.1 0.8 %head_grad.2.refs_0_ = f32[256,768]{1,0:T(8,128)S(1)} custom-call(f32[256,768]{1,0:T(8,128)S(1)} %after.5.acc, bf16[256,1536]{1,0:T(8,128)(2,1)S(1)} %collective-permute-done.4.piece, bf16[768,1536]{1,0:T(8,128)(2,1)S(1)} %get-tuple-element.31.w), custom_call_target="tpu_custom_call" | custom-call | flops 1 | bytes 1 | tf_op jit(solution)/shard_map/head_grad/pallas_call | solution.py:147
  25.0 0.9 %head_grad.3 = (bf16[256,384]{1,0:T(8,128)(2,1)S(1)}, bf16[256,384]{1,0:T(8,128)(2,1)S(1)}) custom-call(f32[256,768]{1,0:T(8,128)S(1)} %after.6.acc, bf16[256,1536]{1,0:T(8,128)(2,1)S(1)} %collective-permute-done.8.piece, bf16[768,1536]{1,0:T(8,128)(2,1)S(1)} %get-tuple-element.32.w), custom_call_target="tpu_custom_call" | custom-call | flops 1 | bytes 1 | tf_op jit(solution)/shard_map/head_grad/pallas_call | solution.py:147
  25.9 1.5 %collective-permute-start.9 = (bf16[256,384]{1,0:T(8,128)(2,1)S(1)}, bf16[256,384]{1,0:T(8,128)(2,1)S(1)}, u32[]{:S(2)}, u32[]{:S(2)}) collective-permute-start(bf16[256,384]{1,0:T(8,128)(2,1)S(1)} %get-tuple-element.34), channel_id=1, source_target_pairs={{0,4},{4,0},{8,12},{12,8},{16,20},{20,16},{24,28},{28,24},{1,5},{5... | collective-permute-start | bytes 589832 | tf_op jit(solution)/shard_map/ppermute | solution.py:418
  27.4 6.3 %collective-permute-done.2.refs_4_.refs_6_ = bf16[2,256,384]{2,1,0:T(8,128)(2,1)S(1)} collective-permute-done((bf16[2,256,384]{2,1,0:T(8,128)(2,1)S(1)}, bf16[2,256,384]{2,1,0:T(8,128)(2,1)S(1)}, u32[]{:S(2)}, u32[]{:S(2)}) %collective-permute-start.2) | collective-permute-done | bytes 393248 | tf_op jit(solution)/shard_map/ppermute | solution.py:432
  33.8 2.9 %collective-permute-start.10 = (bf16[3,256,384]{2,1,0:T(8,128)(2,1)S(1)}, bf16[3,256,384]{2,1,0:T(8,128)(2,1)S(1)}, u32[]{:S(2)}, u32[]{:S(2)}) collective-permute-start(bf16[3,256,384]{2,1,0:T(8,128)(2,1)S(1)} %join.1), channel_id=1, source_target_pairs={{0,8},{1,9},{2,10},{3,11},{4,12},{5,13},{6,14},{7,15},{8,0},{9,1},... | collective-permute-start | bytes 1769480 | tf_op jit(solution)/shard_map/ppermute | solution.py:432
  36.7 3.0 %query_pass.2 = (bf16[1,256,384]{2,1,0:T(8,128)(2,1)S(1)}, f32[8,256]{1,0:T(8,128)S(1)}) custom-call(bf16[256,384]{1,0:T(8,128)(2,1)S(1)} %collective-permute-done.1.refs_2_.refs_0_.xq, bf16[256,384]{1,0:T(8,128)(2,1)S(1)} %after.7.refs_1_.dxr.refs_2_, bf16[3,256,384]{2,1,0:T(8,128)(2,1)S(1)} %copy-done, ...), custom_call_target="tpu_custom_call" | custom-call | flops 1 | bytes 1 | tf_op jit(solution)/shard_map/query_pass/pallas_call | solution.py:256
  39.7 1.6 %collective-permute-start.12 = (bf16[1,256,384]{2,1,0:T(8,128)(2,1)S(1)}, bf16[1,256,384]{2,1,0:T(8,128)(2,1)S(1)}, u32[]{:S(2)}, u32[]{:S(2)}) collective-permute-start(bf16[1,256,384]{2,1,0:T(8,128)(2,1)S(1)} %get-tuple-element.40), channel_id=1, source_target_pairs={{0,4},{4,0},{8,12},{12,8},{16,20},{20,16},{24,28},{28,24},{1,5},{5... | collective-permute-start | bytes 589832 | tf_op jit(solution)/shard_map/ppermute | solution.py:418
  41.2 3.0 %query_pass.3 = (bf16[1,256,384]{2,1,0:T(8,128)(2,1)S(1)}, f32[8,512]{1,0:T(8,128)S(1)}) custom-call(bf16[3,256,384]{2,1,0:T(8,128)(2,1)S(1)} %copy-done, bf16[256,384]{1,0:T(8,128)(2,1)S(1)} %get-tuple-element.33.refs_1_.dkeep, bf16[3,256,384]{2,1,0:T(8,128)(2,1)S(1)} %copy-done, bf16[2,256,384]{2,1,0:T(8,128)(2,1)S(1)} %collective-permute-done.refs_1_.refs_3_.keys.kv, ...), custom_call_target="tpu_custom_call" | custom-call | flops 6000000000 | bytes 1 | tf_op jit(solution)/shard_map/query_pass/pallas_call | solution.py:256
  44.2 2.1 %collective-permute-start.13 = (f32[8,512]{1,0:T(8,128)S(1)}, f32[8,512]{1,0:T(8,128)S(1)}, u32[]{:S(2)}, u32[]{:S(2)}) collective-permute-start(f32[8,512]{1,0:T(8,128)S(1)} %get-tuple-element.38.stats), channel_id=1, source_target_pairs={{0,8},{1,9},{2,10},{3,11},{4,12},{5,13},{6,14},{7,15},{8,0},{9,1},... | collective-permute-start | bytes 49160 | tf_op jit(solution)/shard_map/ppermute | solution.py:432
  46.3 1.2 %own_pass.2.refs_0_ = f32[2,256,384]{2,1,0:T(8,128)S(1)} custom-call(bf16[2,256,384]{2,1,0:T(8,128)(2,1)S(1)} %collective-permute-done.refs_1_.refs_3_.keys.kv, bf16[3,256,384]{2,1,0:T(8,128)(2,1)S(1)} %copy-done, bf16[256,384]{1,0:T(8,128)(2,1)S(1)} %collective-permute-done.1.refs_2_.refs_0_.xq, bf16[256,384]{1,0:T(8,128)(2,1)S(1)} %get-tuple-element.33.refs_1_.dkeep, ...), custom_call_target="tpu_custom_call" | custom-call | flops 1 | bytes 1 | tf_op jit(solution)/shard_map/own_pass/pallas_call | solution.py:306
  47.5 0.8 %unpack.2 = bf16[256,768]{1,0:T(8,128)(2,1)} custom-call(bf16[1,256,384]{2,1,0:T(8,128)(2,1)S(1)} %get-tuple-element.39.kept, bf16[1,256,384]{2,1,0:T(8,128)(2,1)S(1)} %after.9.refs_0_), custom_call_target="tpu_custom_call" | custom-call | flops 1 | bytes 1 | tf_op jit(solution)/shard_map/unpack/pallas_call | solution.py:396
  48.3 1.8 %collective-permute-done.10.refs_1_.late_e = bf16[3,256,384]{2,1,0:T(8,128)(2,1)S(1)} collective-permute-done((bf16[3,256,384]{2,1,0:T(8,128)(2,1)S(1)}, bf16[3,256,384]{2,1,0:T(8,128)(2,1)S(1)}, u32[]{:S(2)}, u32[]{:S(2)}) %collective-permute-start.10) | collective-permute-done | bytes 589856 | tf_op jit(solution)/shard_map/ppermute | solution.py:432
  50.3 0.8 %key_pass.7 = bf16[2,256,128]{2,1,0:T(8,128)(2,1)S(1)} custom-call(bf16[2,256,384]{2,1,0:T(8,128)(2,1)S(1)} %collective-permute-done.refs_1_.refs_3_.keys.kv, bf16[3,256,384]{2,1,0:T(8,128)(2,1)S(1)} %collective-permute-done.6.refs_1_.refs_6_.refs_4_.e0, bf16[3,256,384]{2,1,0:T(8,128)(2,1)S(1)} %collective-permute-done.7.refs_2_.refs_7_.refs_5_.o0, ...), custom_call_target="tpu_custom_call" | custom-call | flops 1000000000 | bytes 1 | tf_op jit(solution)/shard_map/key_pass/pallas_call | solution.py:360
  51.0 1.6 %collective-permute-start.17 = (bf16[2,256,128]{2,1,0:T(8,128)(2,1)S(1)}, bf16[2,256,128]{2,1,0:T(8,128)(2,1)S(1)}, u32[]{:S(2)}, u32[]{:S(2)}) collective-permute-start(bf16[2,256,128]{2,1,0:T(8,128)(2,1)S(1)} %key_pass.7), channel_id=1, source_target_pairs={{0,4},{4,0},{8,12},{12,8},{16,20},{20,16},{24,28},{28,24},{1,5},{5... | collective-permute-start | bytes 393224 | tf_op jit(solution)/shard_map/ppermute | solution.py:418
  52.6 0.8 %key_pass.6 = bf16[2,256,128]{2,1,0:T(8,128)(2,1)S(1)} custom-call(bf16[2,256,384]{2,1,0:T(8,128)(2,1)S(1)} %collective-permute-done.refs_1_.refs_3_.keys.kv, bf16[3,256,384]{2,1,0:T(8,128)(2,1)S(1)} %collective-permute-done.6.refs_1_.refs_6_.refs_4_.e0, bf16[3,256,384]{2,1,0:T(8,128)(2,1)S(1)} %collective-permute-done.7.refs_2_.refs_7_.refs_5_.o0, ...), custom_call_target="tpu_custom_call" | custom-call | flops 1000000000 | bytes 1 | tf_op jit(solution)/shard_map/key_pass/pallas_call | solution.py:360
  53.3 0.6 collective-permute-start.16
  53.9 0.9 %key_pass.5 = bf16[2,256,128]{2,1,0:T(8,128)(2,1)S(1)} custom-call(bf16[2,256,384]{2,1,0:T(8,128)(2,1)S(1)} %collective-permute-done.refs_1_.refs_3_.keys.kv, bf16[3,256,384]{2,1,0:T(8,128)(2,1)S(1)} %collective-permute-done.6.refs_1_.refs_6_.refs_4_.e0, bf16[3,256,384]{2,1,0:T(8,128)(2,1)S(1)} %collective-permute-done.7.refs_2_.refs_7_.refs_5_.o0, ...), custom_call_target="tpu_custom_call" | custom-call | flops 1000000000 | bytes 1 | tf_op jit(solution)/shard_map/key_pass/pallas_call | solution.py:360
  54.9 1.6 %collective-permute-start.15 = (bf16[2,256,128]{2,1,0:T(8,128)(2,1)S(1)}, bf16[2,256,128]{2,1,0:T(8,128)(2,1)S(1)}, u32[]{:S(2)}, u32[]{:S(2)}) collective-permute-start(bf16[2,256,128]{2,1,0:T(8,128)(2,1)S(1)} %key_pass.5), channel_id=1, source_target_pairs={{0,4},{4,0},{8,12},{12,8},{16,20},{20,16},{24,28},{28,24},{1,5},{5... | collective-permute-start | bytes 393224 | tf_op jit(solution)/shard_map/ppermute | solution.py:418
  56.5 1.2 %own_pass.3.sums = f32[2,256,384]{2,1,0:T(8,128)S(1)} custom-call(bf16[3,256,384]{2,1,0:T(8,128)(2,1)S(1)} %copy-done, bf16[3,256,384]{2,1,0:T(8,128)(2,1)S(1)} %copy-done, bf16[256,384]{1,0:T(8,128)(2,1)S(1)} %collective-permute-done.1.refs_2_.refs_0_.xq, bf16[256,384]{1,0:T(8,128)(2,1)S(1)} %get-tuple-element.33.refs_1_.dkeep, ...), custom_call_target="tpu_custom_call" | custom-call | flops 1 | bytes 1 | tf_op jit(solution)/shard_map/own_pass/pallas_call | solution.py:306
  57.7 1.9 %key_pass.4.kept = bf16[2,256,384]{2,1,0:T(8,128)(2,1)S(1)} custom-call(bf16[3,256,384]{2,1,0:T(8,128)(2,1)S(1)} %copy-done, bf16[3,256,384]{2,1,0:T(8,128)(2,1)S(1)} %collective-permute-done.6.refs_1_.refs_6_.refs_4_.e0, bf16[3,256,384]{2,1,0:T(8,128)(2,1)S(1)} %collective-permute-done.7.refs_2_.refs_7_.refs_5_.o0, ...), custom_call_target="tpu_custom_call" | custom-call | flops 1000000000 | bytes 1 | tf_op jit(solution)/shard_map/key_pass/pallas_call | solution.py:360
  60.0 1.6 %collective-permute-done.15.refs_0_ = bf16[2,256,128]{2,1,0:T(8,128)(2,1)S(1)} collective-permute-done((bf16[2,256,128]{2,1,0:T(8,128)(2,1)S(1)}, bf16[2,256,128]{2,1,0:T(8,128)(2,1)S(1)}, u32[]{:S(2)}, u32[]{:S(2)}) %collective-permute-start.15) | collective-permute-done | bytes 131104 | tf_op jit(solution)/shard_map/ppermute | solution.py:418
  61.7 0.9 %unpack.3 = (bf16[256,768]{1,0:T(8,128)(2,1)}, bf16[256,768]{1,0:T(8,128)(2,1)}) custom-call(bf16[2,256,384]{2,1,0:T(8,128)(2,1)S(1)} %key_pass.4.kept, bf16[2,256,128]{2,1,0:T(8,128)(2,1)S(1)} %collective-permute-done.15.refs_0_, bf16[2,256,128]{2,1,0:T(8,128)(2,1)S(1)} %collective-permute-done.16.refs_1_, ...), custom_call_target="tpu_custom_call" | custom-call | flops 1 | bytes 1 | tf_op jit(solution)/shard_map/unpack/pallas_call | solution.py:396
  (28 shorter events, 1.2 us)
Async XLA Ops:
  0.6 9.2 %collective-permute-start.5 = (bf16[256,1536]{1,0:T(8,128)(2,1)}, bf16[256,1536]{1,0:T(8,128)(2,1)S(1)}, u32[]{:S(2)}, u32[]{:S(2)}) collective-permute-start(bf16[256,1536]{1,0:T(8,128)(2,1)} %og.1), channel_id=1, source_target_pairs={{0,1},{1,0},{2,3},{3,2},{4,5},{5,4},{6,7},{7,6},{8,9},{9,8},{10,11... | collective-permute-start | bytes 2359304 | tf_op jit(solution)/shard_map/ppermute | solution.py:415
  1.1 20.9 %collective-permute-start.4 = (bf16[256,1536]{1,0:T(8,128)(2,1)}, bf16[256,1536]{1,0:T(8,128)(2,1)S(1)}, u32[]{:S(2)}, u32[]{:S(2)}) collective-permute-start(bf16[256,1536]{1,0:T(8,128)(2,1)} %og.1), channel_id=1, source_target_pairs={{0,2},{1,3},{2,0},{3,1},{4,6},{5,7},{6,4},{7,5},{8,10},{9,11},{10,... | collective-permute-start | bytes 2359304 | tf_op jit(solution)/shard_map/ppermute | solution.py:415
  6.1 15.7 %collective-permute-start = (bf16[2,256,384]{2,1,0:T(8,128)(2,1)}, bf16[2,256,384]{2,1,0:T(8,128)(2,1)S(1)}, u32[]{:S(2)}, u32[]{:S(2)}) collective-permute-start(bf16[2,256,384]{2,1,0:T(8,128)(2,1)} %get-tuple-element.24), channel_id=1, source_target_pairs={{0,4},{4,0},{8,12},{12,8},{16,20},{20,16},{24,28},{28,24},{1,5},{5... | collective-permute-start | bytes 1179656 | tf_op jit(solution)/shard_map/ppermute | solution.py:418
  7.7 14.1 %collective-permute-start.1 = (bf16[256,384]{1,0:T(8,128)(2,1)}, bf16[256,384]{1,0:T(8,128)(2,1)S(1)}, u32[]{:S(2)}, u32[]{:S(2)}) collective-permute-start(bf16[256,384]{1,0:T(8,128)(2,1)} %get-tuple-element.26), channel_id=1, source_target_pairs={{0,4},{4,0},{8,12},{12,8},{16,20},{20,16},{24,28},{28,24},{1,5},{5... | collective-permute-start | bytes 589832 | tf_op jit(solution)/shard_map/ppermute | solution.py:418
  8.2 16.7 %collective-permute-start.6 = (bf16[3,256,384]{2,1,0:T(8,128)(2,1)}, bf16[3,256,384]{2,1,0:T(8,128)(2,1)S(1)}, u32[]{:S(2)}, u32[]{:S(2)}) collective-permute-start(bf16[3,256,384]{2,1,0:T(8,128)(2,1)} %get-tuple-element.25.refs_2_.refs_0_.keep.keys.kv), channel_id=1, source_target_pairs={{0,8},{1,9},{2,10},{3,11},{4,12},{5,13},{6,14},{7,15},{8,0},{9,1},... | collective-permute-start | bytes 1769480 | tf_op jit(solution)/shard_map/ppermute | solution.py:432
  9.8 15.1 %collective-permute-start.7 = (bf16[3,256,384]{2,1,0:T(8,128)(2,1)}, bf16[3,256,384]{2,1,0:T(8,128)(2,1)S(1)}, u32[]{:S(2)}, u32[]{:S(2)}) collective-permute-start(bf16[3,256,384]{2,1,0:T(8,128)(2,1)} %get-tuple-element.25.refs_2_.refs_0_.keep.keys.kv), channel_id=1, source_target_pairs={{0,1},{1,0},{2,3},{3,2},{4,5},{5,4},{6,7},{7,6},{8,16},{9,17},{10,... | collective-permute-start | bytes 1769480 | tf_op jit(solution)/shard_map/ppermute | solution.py:432
  9.8 1.1 %copy-start.1 = (bf16[256,1536]{1,0:T(8,128)(2,1)S(1)}, bf16[256,1536]{1,0:T(8,128)(2,1)}, u32[]{:S(2)}) copy-start(bf16[256,1536]{1,0:T(8,128)(2,1)} %og.1) | copy-start | bytes 2359300
  22.1 2.9 %collective-permute-start.8 = (bf16[256,1536]{1,0:T(8,128)(2,1)S(1)}, bf16[256,1536]{1,0:T(8,128)(2,1)S(1)}, u32[]{:S(2)}, u32[]{:S(2)}) collective-permute-start(bf16[256,1536]{1,0:T(8,128)(2,1)S(1)} %collective-permute-done.4.piece), channel_id=1, source_target_pairs={{0,1},{1,0},{2,3},{3,2},{4,5},{5,4},{6,7},{7,6},{8,9},{9,8},{10,11... | collective-permute-start | bytes 2359304 | tf_op jit(solution)/shard_map/ppermute | solution.py:415
  22.1 11.6 %collective-permute-start.2 = (bf16[2,256,384]{2,1,0:T(8,128)(2,1)S(1)}, bf16[2,256,384]{2,1,0:T(8,128)(2,1)S(1)}, u32[]{:S(2)}, u32[]{:S(2)}) collective-permute-start(bf16[2,256,384]{2,1,0:T(8,128)(2,1)S(1)} %collective-permute-done.refs_1_.refs_3_.keys.kv), channel_id=1, source_target_pairs={{0,8},{1,9},{2,10},{3,11},{4,12},{5,13},{6,14},{7,15},{8,0},{9,1},... | collective-permute-start | bytes 1179656 | tf_op jit(solution)/shard_map/ppermute | solution.py:432
  23.9 9.8 %collective-permute-start.3 = (bf16[2,256,384]{2,1,0:T(8,128)(2,1)S(1)}, bf16[2,256,384]{2,1,0:T(8,128)(2,1)S(1)}, u32[]{:S(2)}, u32[]{:S(2)}) collective-permute-start(bf16[2,256,384]{2,1,0:T(8,128)(2,1)S(1)} %collective-permute-done.refs_1_.refs_3_.keys.kv), channel_id=1, source_target_pairs={{0,1},{1,0},{2,3},{3,2},{4,5},{5,4},{6,7},{7,6},{8,16},{9,17},{10,... | collective-permute-start | bytes 1179656 | tf_op jit(solution)/shard_map/ppermute | solution.py:432
  25.8 10.9 %copy-start = (bf16[3,256,384]{2,1,0:T(8,128)(2,1)S(1)}, bf16[3,256,384]{2,1,0:T(8,128)(2,1)}, u32[]{:S(2)}) copy-start(bf16[3,256,384]{2,1,0:T(8,128)(2,1)} %get-tuple-element.25.refs_2_.refs_0_.keep.keys.kv) | copy-start | bytes 1769476
  25.9 7.8 %collective-permute-start.9 = (bf16[256,384]{1,0:T(8,128)(2,1)S(1)}, bf16[256,384]{1,0:T(8,128)(2,1)S(1)}, u32[]{:S(2)}, u32[]{:S(2)}) collective-permute-start(bf16[256,384]{1,0:T(8,128)(2,1)S(1)} %get-tuple-element.34), channel_id=1, source_target_pairs={{0,4},{4,0},{8,12},{12,8},{16,20},{20,16},{24,28},{28,24},{1,5},{5... | collective-permute-start | bytes 589832 | tf_op jit(solution)/shard_map/ppermute | solution.py:418
  33.8 16.3 %collective-permute-start.10 = (bf16[3,256,384]{2,1,0:T(8,128)(2,1)S(1)}, bf16[3,256,384]{2,1,0:T(8,128)(2,1)S(1)}, u32[]{:S(2)}, u32[]{:S(2)}) collective-permute-start(bf16[3,256,384]{2,1,0:T(8,128)(2,1)S(1)} %join.1), channel_id=1, source_target_pairs={{0,8},{1,9},{2,10},{3,11},{4,12},{5,13},{6,14},{7,15},{8,0},{9,1},... | collective-permute-start | bytes 1769480 | tf_op jit(solution)/shard_map/ppermute | solution.py:432
  36.7 13.4 %collective-permute-start.11 = (bf16[3,256,384]{2,1,0:T(8,128)(2,1)S(1)}, bf16[3,256,384]{2,1,0:T(8,128)(2,1)S(1)}, u32[]{:S(2)}, u32[]{:S(2)}) collective-permute-start(bf16[3,256,384]{2,1,0:T(8,128)(2,1)S(1)} %join.1), channel_id=1, source_target_pairs={{0,1},{1,0},{2,3},{3,2},{4,5},{5,4},{6,7},{7,6},{8,16},{9,17},{10,... | collective-permute-start | bytes 1769480 | tf_op jit(solution)/shard_map/ppermute | solution.py:432
  39.7 7.9 %collective-permute-start.12 = (bf16[1,256,384]{2,1,0:T(8,128)(2,1)S(1)}, bf16[1,256,384]{2,1,0:T(8,128)(2,1)S(1)}, u32[]{:S(2)}, u32[]{:S(2)}) collective-permute-start(bf16[1,256,384]{2,1,0:T(8,128)(2,1)S(1)} %get-tuple-element.40), channel_id=1, source_target_pairs={{0,4},{4,0},{8,12},{12,8},{16,20},{20,16},{24,28},{28,24},{1,5},{5... | collective-permute-start | bytes 589832 | tf_op jit(solution)/shard_map/ppermute | solution.py:418
  44.2 6.0 %collective-permute-start.13 = (f32[8,512]{1,0:T(8,128)S(1)}, f32[8,512]{1,0:T(8,128)S(1)}, u32[]{:S(2)}, u32[]{:S(2)}) collective-permute-start(f32[8,512]{1,0:T(8,128)S(1)} %get-tuple-element.38.stats), channel_id=1, source_target_pairs={{0,8},{1,9},{2,10},{3,11},{4,12},{5,13},{6,14},{7,15},{8,0},{9,1},... | collective-permute-start | bytes 49160 | tf_op jit(solution)/shard_map/ppermute | solution.py:432
  46.3 4.0 %collective-permute-start.14 = (f32[8,512]{1,0:T(8,128)S(1)}, f32[8,512]{1,0:T(8,128)S(1)}, u32[]{:S(2)}, u32[]{:S(2)}) collective-permute-start(f32[8,512]{1,0:T(8,128)S(1)} %get-tuple-element.38.stats), channel_id=1, source_target_pairs={{0,1},{1,0},{2,3},{3,2},{4,5},{5,4},{6,7},{7,6},{8,16},{9,17},{10,... | collective-permute-start | bytes 49160 | tf_op jit(solution)/shard_map/ppermute | solution.py:432
  51.0 8.6 %collective-permute-start.17 = (bf16[2,256,128]{2,1,0:T(8,128)(2,1)S(1)}, bf16[2,256,128]{2,1,0:T(8,128)(2,1)S(1)}, u32[]{:S(2)}, u32[]{:S(2)}) collective-permute-start(bf16[2,256,128]{2,1,0:T(8,128)(2,1)S(1)} %key_pass.7), channel_id=1, source_target_pairs={{0,4},{4,0},{8,12},{12,8},{16,20},{20,16},{24,28},{28,24},{1,5},{5... | collective-permute-start | bytes 393224 | tf_op jit(solution)/shard_map/ppermute | solution.py:418
  53.3 6.7 %collective-permute-start.16 = (bf16[2,256,128]{2,1,0:T(8,128)(2,1)S(1)}, bf16[2,256,128]{2,1,0:T(8,128)(2,1)S(1)}, u32[]{:S(2)}, u32[]{:S(2)}) collective-permute-start(bf16[2,256,128]{2,1,0:T(8,128)(2,1)S(1)} %key_pass.6), channel_id=1, source_target_pairs={{0,4},{4,0},{8,12},{12,8},{16,20},{20,16},{24,28},{28,24},{1,5},{5... | collective-permute-start | bytes 393224 | tf_op jit(solution)/shard_map/ppermute | solution.py:418
  54.9 6.8 %collective-permute-start.15 = (bf16[2,256,128]{2,1,0:T(8,128)(2,1)S(1)}, bf16[2,256,128]{2,1,0:T(8,128)(2,1)S(1)}, u32[]{:S(2)}, u32[]{:S(2)}) collective-permute-start(bf16[2,256,128]{2,1,0:T(8,128)(2,1)S(1)} %key_pass.5), channel_id=1, source_target_pairs={{0,4},{4,0},{8,12},{12,8},{16,20},{20,16},{24,28},{28,24},{1,5},{5... | collective-permute-start | bytes 393224 | tf_op jit(solution)/shard_map/ppermute | solution.py:418

commit v12 on v11

--- a/solution.py
+++ b/solution.py
@@ -314,7 +314,7 @@
     )(*operands)
 
 
-def key_kernel(scale, own, heads, kv, e0, o0, late_e, late_o, se, so, sums, out, fifth_q, fifth_d):
+def key_kernel(scale, own, heads, kv, e0, o0, late_e, late_o, so, se, sums, out, fifth_q, fifth_d):
     rows = kv.shape[1]
     even_ok, odd_ok, turned = place()
     from_even = turned if own else jnp.logical_not(turned)
@@ -435,29 +435,29 @@
     near = over_mp(out_grad, 1)
     keep, send_kv, send_q = pack(queries, keys, values)
     xkv, xq = over_x(send_kv), over_x(send_q)
-    e0, o0 = over_z(keep, 0), over_z(keep, 1)
+    o0, e0 = over_z(keep, 1), over_z(keep, 0)
     acc, wy, wf = first_piece(out_grad, near, out_weight)
-    e1, o1 = over_z(xkv, 0), over_z(xkv, 1)
+    o1, e1 = over_z(xkv, 1), over_z(xkv, 0)
     acc = after(acc, xkv, xq, flops=1e8)
     y, acc = lax.optimization_barrier((y, acc))
     far = over_mp(y, 1)
     acc = grad_piece(acc, y, wy, False)
-    acc = after(acc, e0, o0, flops=3e9)
+    acc = after(acc, o0, e0, flops=3e9)
     dkeep, dsend = grad_piece(acc, far, wf, True)
     dxr = after(over_x(dsend), flops=6e9)
 
-    xq, e1, o1 = lax.optimization_barrier((xq, e1, o1))
+    xq, o1, e1 = lax.optimization_barrier((xq, o1, e1))
     late = join(xq, dkeep, dxr)
-    late_e, late_o = over_z(late, 0), over_z(late, 1)
+    late_o, late_e = over_z(late, 1), over_z(late, 0)
     dq_send, marks = query_pass(False, xq, dxr, keep, xkv, e1, o1, e0, o0)
     dq_keep, stats = query_pass(True, keep, dkeep, keep, xkv, e0, o0, e1, o1, marks)
-    dq_got = after(over_x(dq_send), flops=6e9)
-    se, so = over_z(stats, 0), over_z(stats, 1)
+    dq_got = after(over_x(dq_send), flops=1)
+    so, se = over_z(stats, 1), over_z(stats, 0)
     sums = own_pass(xkv, keep, xq, dkeep, dxr, stats)
-    sums = after(sums, late_e, late_o, flops=3e9)
+    sums = after(sums, late_o, late_e, flops=3e9)
     own_sums = own_pass(keep, keep, xq, dkeep, dxr, stats)
     heads = dkeep.shape[1] // HD
-    theirs = (e0, o0, late_e, late_o, se, so)
+    theirs = (e0, o0, late_e, late_o, so, se)
     got = []
     for head in range(heads):
         if head == 1:

time: 63 us -> 63.9 us (1.014)
  starting transfers between devices: 20.7 us -> 22.5 us
  waiting for transfers between devices: 17.6 us -> 16.7 us
    ppermute x8, starting transfers between devices: 8.64 us -> 10.4 us  [over_z(): return lax.ppermute(array, ('ctx', 'mp'), pairs)]
    ppermute x7, waiting for transfers between devices: 9.08 us -> 7.51 us  [over_x(): return lax.ppermute(array, 'ctx', [(i, i ^ 1) for i in range(length)])]
    ppermute x8, waiting for transfers between devices: 8.23 us -> 8.96 us  [over_z(): return lax.ppermute(array, ('ctx', 'mp'), pairs)]
  transfers between devices with their start and end apart: 18 -> 18, of which waited for: 7 -> 7; matrix products, arithmetic and copies ran while one was open for 0% -> 0% of each run, Pallas kernels for 33% -> 32%
where the time goes in v12:
time: 63.9 us; the launch traced here: 63.7 us
  starting transfers between devices  22.5 us (35%)
  Pallas kernels  22.4 us (35%)
  waiting for transfers between devices  16.7 us (26%)
  local copies, waits for them, and re-layouts  1.14 us (2%)
  between operations  0.98 us (2%)
    ppermute x8, starting transfers between devices, over_z(): return lax.ppermute(array, ('ctx', 'mp'), pairs)  10.4 us
    ppermute x8, waiting for transfers between devices, over_z(): return lax.ppermute(array, ('ctx', 'mp'), pairs)  8.96 us
    ppermute x7, starting transfers between devices, over_x(): return lax.ppermute(array, 'ctx', [(i, i ^ 1) for i in range(length)])  8.93 us
    ppermute x7, waiting for transfers between devices, over_x(): return lax.ppermute(array, 'ctx', [(i, i ^ 1) for i in range(length)])  7.51 us
    pallas_call x2, Pallas kernels, query_pass(): pl.pallas_call(functools.partial(query_kernel, HD ** (-0.5), own, before...  5.94 us
    pallas_call x4, Pallas kernels, key_pass(): pl.pallas_call(functools.partial(key_kernel, HD ** (-0.5), own, heads), o...  4.39 us
    pallas_call x1, Pallas kernels, first_piece(): pl.pallas_call(first_kernel, out_shape=(jax.ShapeDtypeStruct((rows, heads...  3.82 us
    ppermute x3, starting transfers between devices, over_mp(): return lax.ppermute(array, 'mp', [(i, i ^ flip) for i in range(lanes)])  3.12 us
  transfers between devices with their start and end apart: 18, of which 7 were waited for; matrix products, arithmetic and copies ran while one was open for 0% of the time, Pallas kernels for 32%

profile of v12, /device:TPU:0, one launch (start us, length us, event | category | flops | bytes accessed | tf_op | source)
XLA Modules:
  0.0 63.7 jit_solution(12954222519198461207)
XLA Ops:
  0.6 0.5 collective-permute-start.5
  1.1 2.6 %collective-permute-start.4 = (bf16[256,1536]{1,0:T(8,128)(2,1)}, bf16[256,1536]{1,0:T(8,128)(2,1)S(1)}, u32[]{:S(2)}, u32[]{:S(2)}) collective-permute-start(bf16[256,1536]{1,0:T(8,128)(2,1)} %og.1), channel_id=1, source_target_pairs={{0,2},{1,3},{2,0},{3,1},{4,6},{5,7},{6,4},{7,5},{8,10},{9,11},{10,... | collective-permute-start | bytes 2359304 | tf_op jit(solution)/shard_map/ppermute | solution.py:415
  3.7 2.4 %pack.1 = (bf16[3,256,384]{2,1,0:T(8,128)(2,1)}, bf16[2,256,384]{2,1,0:T(8,128)(2,1)}, bf16[256,384]{1,0:T(8,128)(2,1)}) custom-call(bf16[256,768]{1,0:T(8,128)(2,1)} %q.1, bf16[256,768]{1,0:T(8,128)(2,1)} %k.1, bf16[256,768]{1,0:T(8,128)(2,1)} %v.1), custom_call_target="tpu_custom_call" | custom-call | flops 1 | bytes 1 | tf_op jit(solution)/shard_map/pack/pallas_call | solution.py:60
  6.1 1.6 %collective-permute-start = (bf16[2,256,384]{2,1,0:T(8,128)(2,1)}, bf16[2,256,384]{2,1,0:T(8,128)(2,1)S(1)}, u32[]{:S(2)}, u32[]{:S(2)}) collective-permute-start(bf16[2,256,384]{2,1,0:T(8,128)(2,1)} %get-tuple-element.24), channel_id=1, source_target_pairs={{0,4},{4,0},{8,12},{12,8},{16,20},{20,16},{24,28},{28,24},{1,5},{5... | collective-permute-start | bytes 1179656 | tf_op jit(solution)/shard_map/ppermute | solution.py:418
  7.7 0.5 collective-permute-start.1
  8.2 3.2 %collective-permute-start.7 = (bf16[3,256,384]{2,1,0:T(8,128)(2,1)}, bf16[3,256,384]{2,1,0:T(8,128)(2,1)S(1)}, u32[]{:S(2)}, u32[]{:S(2)}) collective-permute-start(bf16[3,256,384]{2,1,0:T(8,128)(2,1)} %get-tuple-element.25.refs_2_.refs_0_.keep.keys.kv), channel_id=1, source_target_pairs={{0,8},{1,9},{2,10},{3,11},{4,12},{5,13},{6,14},{7,15},{8,0},{9,1},... | collective-permute-start | bytes 1769480 | tf_op jit(solution)/shard_map/ppermute | solution.py:432
  11.4 1.1 %copy-done.1 = bf16[256,1536]{1,0:T(8,128)(2,1)S(1)} copy-done((bf16[256,1536]{1,0:T(8,128)(2,1)S(1)}, bf16[256,1536]{1,0:T(8,128)(2,1)}, u32[]{:S(2)}) %copy-start.1) | copy-done | bytes 786456
  12.5 3.8 %head_grad_first.1 = (f32[256,768]{1,0:T(8,128)S(1)}, bf16[768,1536]{1,0:T(8,128)(2,1)S(1)}, bf16[768,1536]{1,0:T(8,128)(2,1)S(1)}) custom-call(bf16[256,1536]{1,0:T(8,128)(2,1)S(1)} %copy-done.1, bf16[256,1536]{1,0:T(8,128)(2,1)S(1)} %collective-permute-done.5.near, bf16[768,6144]{1,0:T(8,128)(2,1)} %w.1), custom_call_target="tpu_custom_call" | custom-call | flops 1 | bytes 1 | tf_op jit(solution)/shard_map/head_grad_first/pallas_call | solution.py:110
  16.3 5.5 %collective-permute-done.1.refs_2_.refs_0_.xq = bf16[256,384]{1,0:T(8,128)(2,1)S(1)} collective-permute-done((bf16[256,384]{1,0:T(8,128)(2,1)}, bf16[256,384]{1,0:T(8,128)(2,1)S(1)}, u32[]{:S(2)}, u32[]{:S(2)}) %collective-permute-start.1) | collective-permute-done | bytes 196640 | tf_op jit(solution)/shard_map/ppermute | solution.py:418
  22.6 2.9 %collective-permute-start.3 = (bf16[2,256,384]{2,1,0:T(8,128)(2,1)S(1)}, bf16[2,256,384]{2,1,0:T(8,128)(2,1)S(1)}, u32[]{:S(2)}, u32[]{:S(2)}) collective-permute-start(bf16[2,256,384]{2,1,0:T(8,128)(2,1)S(1)} %collective-permute-done.refs_1_.refs_3_.keys.kv), channel_id=1, source_target_pairs={{0,8},{1,9},{2,10},{3,11},{4,12},{5,13},{6,14},{7,15},{8,0},{9,1},... | collective-permute-start | bytes 1179656 | tf_op jit(solution)/shard_map/ppermute | solution.py:432
  25.5 0.8 %head_grad.2.refs_0_ = f32[256,768]{1,0:T(8,128)S(1)} custom-call(f32[256,768]{1,0:T(8,128)S(1)} %after.5.acc, bf16[256,1536]{1,0:T(8,128)(2,1)S(1)} %collective-permute-done.4.piece, bf16[768,1536]{1,0:T(8,128)(2,1)S(1)} %get-tuple-element.31.w), custom_call_target="tpu_custom_call" | custom-call | flops 1 | bytes 1 | tf_op jit(solution)/shard_map/head_grad/pallas_call | solution.py:147
  26.3 0.8 %head_grad.3 = (bf16[256,384]{1,0:T(8,128)(2,1)S(1)}, bf16[256,384]{1,0:T(8,128)(2,1)S(1)}) custom-call(f32[256,768]{1,0:T(8,128)S(1)} %after.6.acc, bf16[256,1536]{1,0:T(8,128)(2,1)S(1)} %collective-permute-done.8.piece, bf16[768,1536]{1,0:T(8,128)(2,1)S(1)} %get-tuple-element.32.w), custom_call_target="tpu_custom_call" | custom-call | flops 1 | bytes 1 | tf_op jit(solution)/shard_map/head_grad/pallas_call | solution.py:147
  27.2 1.6 %collective-permute-start.9 = (bf16[256,384]{1,0:T(8,128)(2,1)S(1)}, bf16[256,384]{1,0:T(8,128)(2,1)S(1)}, u32[]{:S(2)}, u32[]{:S(2)}) collective-permute-start(bf16[256,384]{1,0:T(8,128)(2,1)S(1)} %get-tuple-element.34), channel_id=1, source_target_pairs={{0,4},{4,0},{8,12},{12,8},{16,20},{20,16},{24,28},{28,24},{1,5},{5... | collective-permute-start | bytes 589832 | tf_op jit(solution)/shard_map/ppermute | solution.py:418
  28.8 6.2 %collective-permute-done.3.refs_4_.refs_6_ = bf16[2,256,384]{2,1,0:T(8,128)(2,1)S(1)} collective-permute-done((bf16[2,256,384]{2,1,0:T(8,128)(2,1)S(1)}, bf16[2,256,384]{2,1,0:T(8,128)(2,1)S(1)}, u32[]{:S(2)}, u32[]{:S(2)}) %collective-permute-start.3) | collective-permute-done | bytes 393248 | tf_op jit(solution)/shard_map/ppermute | solution.py:432
  35.1 2.2 %collective-permute-start.11 = (bf16[3,256,384]{2,1,0:T(8,128)(2,1)S(1)}, bf16[3,256,384]{2,1,0:T(8,128)(2,1)S(1)}, u32[]{:S(2)}, u32[]{:S(2)}) collective-permute-start(bf16[3,256,384]{2,1,0:T(8,128)(2,1)S(1)} %join.1), channel_id=1, source_target_pairs={{0,8},{1,9},{2,10},{3,11},{4,12},{5,13},{6,14},{7,15},{8,0},{9,1},... | collective-permute-start | bytes 1769480 | tf_op jit(solution)/shard_map/ppermute | solution.py:432
  37.3 3.0 %query_pass.2 = (bf16[1,256,384]{2,1,0:T(8,128)(2,1)S(1)}, f32[8,256]{1,0:T(8,128)S(1)}) custom-call(bf16[256,384]{1,0:T(8,128)(2,1)S(1)} %collective-permute-done.1.refs_2_.refs_0_.xq, bf16[256,384]{1,0:T(8,128)(2,1)S(1)} %after.7.refs_1_.dxr.refs_2_, bf16[3,256,384]{2,1,0:T(8,128)(2,1)S(1)} %copy-done, ...), custom_call_target="tpu_custom_call" | custom-call | flops 1 | bytes 1 | tf_op jit(solution)/shard_map/query_pass/pallas_call | solution.py:256
  40.3 1.6 %collective-permute-start.12 = (bf16[1,256,384]{2,1,0:T(8,128)(2,1)S(1)}, bf16[1,256,384]{2,1,0:T(8,128)(2,1)S(1)}, u32[]{:S(2)}, u32[]{:S(2)}) collective-permute-start(bf16[1,256,384]{2,1,0:T(8,128)(2,1)S(1)} %get-tuple-element.40), channel_id=1, source_target_pairs={{0,4},{4,0},{8,12},{12,8},{16,20},{20,16},{24,28},{28,24},{1,5},{5... | collective-permute-start | bytes 589832 | tf_op jit(solution)/shard_map/ppermute | solution.py:418
  41.8 3.0 %query_pass.3 = (bf16[1,256,384]{2,1,0:T(8,128)(2,1)S(1)}, f32[8,512]{1,0:T(8,128)S(1)}) custom-call(bf16[3,256,384]{2,1,0:T(8,128)(2,1)S(1)} %copy-done, bf16[256,384]{1,0:T(8,128)(2,1)S(1)} %get-tuple-element.33.refs_1_.dkeep, bf16[3,256,384]{2,1,0:T(8,128)(2,1)S(1)} %copy-done, bf16[2,256,384]{2,1,0:T(8,128)(2,1)S(1)} %collective-permute-done.refs_1_.refs_3_.keys.kv, ...), custom_call_target="tpu_custom_call" | custom-call | flops 6000000000 | bytes 1 | tf_op jit(solution)/shard_map/query_pass/pallas_call | solution.py:256
  44.9 1.6 %collective-permute-start.14 = (f32[8,512]{1,0:T(8,128)S(1)}, f32[8,512]{1,0:T(8,128)S(1)}, u32[]{:S(2)}, u32[]{:S(2)}) collective-permute-start(f32[8,512]{1,0:T(8,128)S(1)} %get-tuple-element.38.stats), channel_id=1, source_target_pairs={{0,8},{1,9},{2,10},{3,11},{4,12},{5,13},{6,14},{7,15},{8,0},{9,1},... | collective-permute-start | bytes 49160 | tf_op jit(solution)/shard_map/ppermute | solution.py:432
  46.5 1.2 %own_pass.2.refs_0_ = f32[2,256,384]{2,1,0:T(8,128)S(1)} custom-call(bf16[2,256,384]{2,1,0:T(8,128)(2,1)S(1)} %collective-permute-done.refs_1_.refs_3_.keys.kv, bf16[3,256,384]{2,1,0:T(8,128)(2,1)S(1)} %copy-done, bf16[256,384]{1,0:T(8,128)(2,1)S(1)} %collective-permute-done.1.refs_2_.refs_0_.xq, bf16[256,384]{1,0:T(8,128)(2,1)S(1)} %get-tuple-element.33.refs_1_.dkeep, ...), custom_call_target="tpu_custom_call" | custom-call | flops 1 | bytes 1 | tf_op jit(solution)/shard_map/own_pass/pallas_call | solution.py:306
  47.7 0.8 %unpack.2 = bf16[256,768]{1,0:T(8,128)(2,1)} custom-call(bf16[1,256,384]{2,1,0:T(8,128)(2,1)S(1)} %get-tuple-element.39.kept, bf16[1,256,384]{2,1,0:T(8,128)(2,1)S(1)} %after.9.refs_0_), custom_call_target="tpu_custom_call" | custom-call | flops 1 | bytes 1 | tf_op jit(solution)/shard_map/unpack/pallas_call | solution.py:396
  48.5 2.5 %collective-permute-done.11.refs_2_.late_e = bf16[3,256,384]{2,1,0:T(8,128)(2,1)S(1)} collective-permute-done((bf16[3,256,384]{2,1,0:T(8,128)(2,1)S(1)}, bf16[3,256,384]{2,1,0:T(8,128)(2,1)S(1)}, u32[]{:S(2)}, u32[]{:S(2)}) %collective-permute-start.11) | collective-permute-done | bytes 589856 | tf_op jit(solution)/shard_map/ppermute | solution.py:432
  51.2 0.8 %key_pass.7 = bf16[2,256,128]{2,1,0:T(8,128)(2,1)S(1)} custom-call(bf16[2,256,384]{2,1,0:T(8,128)(2,1)S(1)} %collective-permute-done.refs_1_.refs_3_.keys.kv, bf16[3,256,384]{2,1,0:T(8,128)(2,1)S(1)} %collective-permute-done.7.refs_2_.refs_6_.refs_4_.e0, bf16[3,256,384]{2,1,0:T(8,128)(2,1)S(1)} %collective-permute-done.6.refs_1_.refs_7_.refs_5_.o0, ...), custom_call_target="tpu_custom_call" | custom-call | flops 1000000000 | bytes 1 | tf_op jit(solution)/shard_map/key_pass/pallas_call | solution.py:360
  52.0 1.6 %collective-permute-start.17 = (bf16[2,256,128]{2,1,0:T(8,128)(2,1)S(1)}, bf16[2,256,128]{2,1,0:T(8,128)(2,1)S(1)}, u32[]{:S(2)}, u32[]{:S(2)}) collective-permute-start(bf16[2,256,128]{2,1,0:T(8,128)(2,1)S(1)} %key_pass.7), channel_id=1, source_target_pairs={{0,4},{4,0},{8,12},{12,8},{16,20},{20,16},{24,28},{28,24},{1,5},{5... | collective-permute-start | bytes 393224 | tf_op jit(solution)/shard_map/ppermute | solution.py:418
  53.5 0.8 %key_pass.6 = bf16[2,256,128]{2,1,0:T(8,128)(2,1)S(1)} custom-call(bf16[2,256,384]{2,1,0:T(8,128)(2,1)S(1)} %collective-permute-done.refs_1_.refs_3_.keys.kv, bf16[3,256,384]{2,1,0:T(8,128)(2,1)S(1)} %collective-permute-done.7.refs_2_.refs_6_.refs_4_.e0, bf16[3,256,384]{2,1,0:T(8,128)(2,1)S(1)} %collective-permute-done.6.refs_1_.refs_7_.refs_5_.o0, ...), custom_call_target="tpu_custom_call" | custom-call | flops 1000000000 | bytes 1 | tf_op jit(solution)/shard_map/key_pass/pallas_call | solution.py:360
  54.3 0.6 collective-permute-start.16
  54.9 0.9 %key_pass.5 = bf16[2,256,128]{2,1,0:T(8,128)(2,1)S(1)} custom-call(bf16[2,256,384]{2,1,0:T(8,128)(2,1)S(1)} %collective-permute-done.refs_1_.refs_3_.keys.kv, bf16[3,256,384]{2,1,0:T(8,128)(2,1)S(1)} %collective-permute-done.7.refs_2_.refs_6_.refs_4_.e0, bf16[3,256,384]{2,1,0:T(8,128)(2,1)S(1)} %collective-permute-done.6.refs_1_.refs_7_.refs_5_.o0, ...), custom_call_target="tpu_custom_call" | custom-call | flops 1000000000 | bytes 1 | tf_op jit(solution)/shard_map/key_pass/pallas_call | solution.py:360
  55.8 1.6 %collective-permute-start.15 = (bf16[2,256,128]{2,1,0:T(8,128)(2,1)S(1)}, bf16[2,256,128]{2,1,0:T(8,128)(2,1)S(1)}, u32[]{:S(2)}, u32[]{:S(2)}) collective-permute-start(bf16[2,256,128]{2,1,0:T(8,128)(2,1)S(1)} %key_pass.5), channel_id=1, source_target_pairs={{0,4},{4,0},{8,12},{12,8},{16,20},{20,16},{24,28},{28,24},{1,5},{5... | collective-permute-start | bytes 393224 | tf_op jit(solution)/shard_map/ppermute | solution.py:418
  57.4 1.2 %own_pass.3.sums = f32[2,256,384]{2,1,0:T(8,128)S(1)} custom-call(bf16[3,256,384]{2,1,0:T(8,128)(2,1)S(1)} %copy-done, bf16[3,256,384]{2,1,0:T(8,128)(2,1)S(1)} %copy-done, bf16[256,384]{1,0:T(8,128)(2,1)S(1)} %collective-permute-done.1.refs_2_.refs_0_.xq, bf16[256,384]{1,0:T(8,128)(2,1)S(1)} %get-tuple-element.33.refs_1_.dkeep, ...), custom_call_target="tpu_custom_call" | custom-call | flops 1 | bytes 1 | tf_op jit(solution)/shard_map/own_pass/pallas_call | solution.py:306
  58.6 1.9 %key_pass.4.kept = bf16[2,256,384]{2,1,0:T(8,128)(2,1)S(1)} custom-call(bf16[3,256,384]{2,1,0:T(8,128)(2,1)S(1)} %copy-done, bf16[3,256,384]{2,1,0:T(8,128)(2,1)S(1)} %collective-permute-done.7.refs_2_.refs_6_.refs_4_.e0, bf16[3,256,384]{2,1,0:T(8,128)(2,1)S(1)} %collective-permute-done.6.refs_1_.refs_7_.refs_5_.o0, ...), custom_call_target="tpu_custom_call" | custom-call | flops 1000000000 | bytes 1 | tf_op jit(solution)/shard_map/key_pass/pallas_call | solution.py:360
  60.8 1.8 %collective-permute-done.15.refs_0_ = bf16[2,256,128]{2,1,0:T(8,128)(2,1)S(1)} collective-permute-done((bf16[2,256,128]{2,1,0:T(8,128)(2,1)S(1)}, bf16[2,256,128]{2,1,0:T(8,128)(2,1)S(1)}, u32[]{:S(2)}, u32[]{:S(2)}) %collective-permute-start.15) | collective-permute-done | bytes 131104 | tf_op jit(solution)/shard_map/ppermute | solution.py:418
  62.6 0.9 %unpack.3 = (bf16[256,768]{1,0:T(8,128)(2,1)}, bf16[256,768]{1,0:T(8,128)(2,1)}) custom-call(bf16[2,256,384]{2,1,0:T(8,128)(2,1)S(1)} %key_pass.4.kept, bf16[2,256,128]{2,1,0:T(8,128)(2,1)S(1)} %collective-permute-done.15.refs_0_, bf16[2,256,128]{2,1,0:T(8,128)(2,1)S(1)} %collective-permute-done.16.refs_1_, ...), custom_call_target="tpu_custom_call" | custom-call | flops 1 | bytes 1 | tf_op jit(solution)/shard_map/unpack/pallas_call | solution.py:396
  (28 shorter events, 1.4 us)
Async XLA Ops:
  0.6 7.6 %collective-permute-start.5 = (bf16[256,1536]{1,0:T(8,128)(2,1)}, bf16[256,1536]{1,0:T(8,128)(2,1)S(1)}, u32[]{:S(2)}, u32[]{:S(2)}) collective-permute-start(bf16[256,1536]{1,0:T(8,128)(2,1)} %og.1), channel_id=1, source_target_pairs={{0,1},{1,0},{2,3},{3,2},{4,5},{5,4},{6,7},{7,6},{8,9},{9,8},{10,11... | collective-permute-start | bytes 2359304 | tf_op jit(solution)/shard_map/ppermute | solution.py:415
  1.1 20.9 %collective-permute-start.4 = (bf16[256,1536]{1,0:T(8,128)(2,1)}, bf16[256,1536]{1,0:T(8,128)(2,1)S(1)}, u32[]{:S(2)}, u32[]{:S(2)}) collective-permute-start(bf16[256,1536]{1,0:T(8,128)(2,1)} %og.1), channel_id=1, source_target_pairs={{0,2},{1,3},{2,0},{3,1},{4,6},{5,7},{6,4},{7,5},{8,10},{9,11},{10,... | collective-permute-start | bytes 2359304 | tf_op jit(solution)/shard_map/ppermute | solution.py:415
  6.1 15.7 %collective-permute-start = (bf16[2,256,384]{2,1,0:T(8,128)(2,1)}, bf16[2,256,384]{2,1,0:T(8,128)(2,1)S(1)}, u32[]{:S(2)}, u32[]{:S(2)}) collective-permute-start(bf16[2,256,384]{2,1,0:T(8,128)(2,1)} %get-tuple-element.24), channel_id=1, source_target_pairs={{0,4},{4,0},{8,12},{12,8},{16,20},{20,16},{24,28},{28,24},{1,5},{5... | collective-permute-start | bytes 1179656 | tf_op jit(solution)/shard_map/ppermute | solution.py:418
  7.7 14.1 %collective-permute-start.1 = (bf16[256,384]{1,0:T(8,128)(2,1)}, bf16[256,384]{1,0:T(8,128)(2,1)S(1)}, u32[]{:S(2)}, u32[]{:S(2)}) collective-permute-start(bf16[256,384]{1,0:T(8,128)(2,1)} %get-tuple-element.26), channel_id=1, source_target_pairs={{0,4},{4,0},{8,12},{12,8},{16,20},{20,16},{24,28},{28,24},{1,5},{5... | collective-permute-start | bytes 589832 | tf_op jit(solution)/shard_map/ppermute | solution.py:418
  8.2 18.1 %collective-permute-start.6 = (bf16[3,256,384]{2,1,0:T(8,128)(2,1)}, bf16[3,256,384]{2,1,0:T(8,128)(2,1)S(1)}, u32[]{:S(2)}, u32[]{:S(2)}) collective-permute-start(bf16[3,256,384]{2,1,0:T(8,128)(2,1)} %get-tuple-element.25.refs_2_.refs_0_.keep.keys.kv), channel_id=1, source_target_pairs={{0,1},{1,0},{2,3},{3,2},{4,5},{5,4},{6,7},{7,6},{8,16},{9,17},{10,... | collective-permute-start | bytes 1769480 | tf_op jit(solution)/shard_map/ppermute | solution.py:432
  8.2 18.1 %collective-permute-start.7 = (bf16[3,256,384]{2,1,0:T(8,128)(2,1)}, bf16[3,256,384]{2,1,0:T(8,128)(2,1)S(1)}, u32[]{:S(2)}, u32[]{:S(2)}) collective-permute-start(bf16[3,256,384]{2,1,0:T(8,128)(2,1)} %get-tuple-element.25.refs_2_.refs_0_.keep.keys.kv), channel_id=1, source_target_pairs={{0,8},{1,9},{2,10},{3,11},{4,12},{5,13},{6,14},{7,15},{8,0},{9,1},... | collective-permute-start | bytes 1769480 | tf_op jit(solution)/shard_map/ppermute | solution.py:432
  11.4 1.1 %copy-start.1 = (bf16[256,1536]{1,0:T(8,128)(2,1)S(1)}, bf16[256,1536]{1,0:T(8,128)(2,1)}, u32[]{:S(2)}) copy-start(bf16[256,1536]{1,0:T(8,128)(2,1)} %og.1) | copy-start | bytes 2359300
  22.1 4.2 %collective-permute-start.8 = (bf16[256,1536]{1,0:T(8,128)(2,1)S(1)}, bf16[256,1536]{1,0:T(8,128)(2,1)S(1)}, u32[]{:S(2)}, u32[]{:S(2)}) collective-permute-start(bf16[256,1536]{1,0:T(8,128)(2,1)S(1)} %collective-permute-done.4.piece), channel_id=1, source_target_pairs={{0,1},{1,0},{2,3},{3,2},{4,5},{5,4},{6,7},{7,6},{8,9},{9,8},{10,11... | collective-permute-start | bytes 2359304 | tf_op jit(solution)/shard_map/ppermute | solution.py:415
  22.1 6.7 %collective-permute-start.2 = (bf16[2,256,384]{2,1,0:T(8,128)(2,1)S(1)}, bf16[2,256,384]{2,1,0:T(8,128)(2,1)S(1)}, u32[]{:S(2)}, u32[]{:S(2)}) collective-permute-start(bf16[2,256,384]{2,1,0:T(8,128)(2,1)S(1)} %collective-permute-done.refs_1_.refs_3_.keys.kv), channel_id=1, source_target_pairs={{0,1},{1,0},{2,3},{3,2},{4,5},{5,4},{6,7},{7,6},{8,16},{9,17},{10,... | collective-permute-start | bytes 1179656 | tf_op jit(solution)/shard_map/ppermute | solution.py:432
  22.6 12.4 %collective-permute-start.3 = (bf16[2,256,384]{2,1,0:T(8,128)(2,1)S(1)}, bf16[2,256,384]{2,1,0:T(8,128)(2,1)S(1)}, u32[]{:S(2)}, u32[]{:S(2)}) collective-permute-start(bf16[2,256,384]{2,1,0:T(8,128)(2,1)S(1)} %collective-permute-done.refs_1_.refs_3_.keys.kv), channel_id=1, source_target_pairs={{0,8},{1,9},{2,10},{3,11},{4,12},{5,13},{6,14},{7,15},{8,0},{9,1},... | collective-permute-start | bytes 1179656 | tf_op jit(solution)/shard_map/ppermute | solution.py:432
  27.2 10.1 %copy-start = (bf16[3,256,384]{2,1,0:T(8,128)(2,1)S(1)}, bf16[3,256,384]{2,1,0:T(8,128)(2,1)}, u32[]{:S(2)}) copy-start(bf16[3,256,384]{2,1,0:T(8,128)(2,1)} %get-tuple-element.25.refs_2_.refs_0_.keep.keys.kv) | copy-start | bytes 1769476
  27.2 7.8 %collective-permute-start.9 = (bf16[256,384]{1,0:T(8,128)(2,1)S(1)}, bf16[256,384]{1,0:T(8,128)(2,1)S(1)}, u32[]{:S(2)}, u32[]{:S(2)}) collective-permute-start(bf16[256,384]{1,0:T(8,128)(2,1)S(1)} %get-tuple-element.34), channel_id=1, source_target_pairs={{0,4},{4,0},{8,12},{12,8},{16,20},{20,16},{24,28},{28,24},{1,5},{5... | collective-permute-start | bytes 589832 | tf_op jit(solution)/shard_map/ppermute | solution.py:418
  35.0 13.4 %collective-permute-start.10 = (bf16[3,256,384]{2,1,0:T(8,128)(2,1)S(1)}, bf16[3,256,384]{2,1,0:T(8,128)(2,1)S(1)}, u32[]{:S(2)}, u32[]{:S(2)}) collective-permute-start(bf16[3,256,384]{2,1,0:T(8,128)(2,1)S(1)} %join.1), channel_id=1, source_target_pairs={{0,1},{1,0},{2,3},{3,2},{4,5},{5,4},{6,7},{7,6},{8,16},{9,17},{10,... | collective-permute-start | bytes 1769480 | tf_op jit(solution)/shard_map/ppermute | solution.py:432
  35.1 15.9 %collective-permute-start.11 = (bf16[3,256,384]{2,1,0:T(8,128)(2,1)S(1)}, bf16[3,256,384]{2,1,0:T(8,128)(2,1)S(1)}, u32[]{:S(2)}, u32[]{:S(2)}) collective-permute-start(bf16[3,256,384]{2,1,0:T(8,128)(2,1)S(1)} %join.1), channel_id=1, source_target_pairs={{0,8},{1,9},{2,10},{3,11},{4,12},{5,13},{6,14},{7,15},{8,0},{9,1},... | collective-permute-start | bytes 1769480 | tf_op jit(solution)/shard_map/ppermute | solution.py:432
  40.3 7.4 %collective-permute-start.12 = (bf16[1,256,384]{2,1,0:T(8,128)(2,1)S(1)}, bf16[1,256,384]{2,1,0:T(8,128)(2,1)S(1)}, u32[]{:S(2)}, u32[]{:S(2)}) collective-permute-start(bf16[1,256,384]{2,1,0:T(8,128)(2,1)S(1)} %get-tuple-element.40), channel_id=1, source_target_pairs={{0,4},{4,0},{8,12},{12,8},{16,20},{20,16},{24,28},{28,24},{1,5},{5... | collective-permute-start | bytes 589832 | tf_op jit(solution)/shard_map/ppermute | solution.py:418
  44.8 6.2 %collective-permute-start.13 = (f32[8,512]{1,0:T(8,128)S(1)}, f32[8,512]{1,0:T(8,128)S(1)}, u32[]{:S(2)}, u32[]{:S(2)}) collective-permute-start(f32[8,512]{1,0:T(8,128)S(1)} %get-tuple-element.38.stats), channel_id=1, source_target_pairs={{0,1},{1,0},{2,3},{3,2},{4,5},{5,4},{6,7},{7,6},{8,16},{9,17},{10,... | collective-permute-start | bytes 49160 | tf_op jit(solution)/shard_map/ppermute | solution.py:432
  44.9 6.3 %collective-permute-start.14 = (f32[8,512]{1,0:T(8,128)S(1)}, f32[8,512]{1,0:T(8,128)S(1)}, u32[]{:S(2)}, u32[]{:S(2)}) collective-permute-start(f32[8,512]{1,0:T(8,128)S(1)} %get-tuple-element.38.stats), channel_id=1, source_target_pairs={{0,8},{1,9},{2,10},{3,11},{4,12},{5,13},{6,14},{7,15},{8,0},{9,1},... | collective-permute-start | bytes 49160 | tf_op jit(solution)/shard_map/ppermute | solution.py:432
  52.0 8.6 %collective-permute-start.17 = (bf16[2,256,128]{2,1,0:T(8,128)(2,1)S(1)}, bf16[2,256,128]{2,1,0:T(8,128)(2,1)S(1)}, u32[]{:S(2)}, u32[]{:S(2)}) collective-permute-start(bf16[2,256,128]{2,1,0:T(8,128)(2,1)S(1)} %key_pass.7), channel_id=1, source_target_pairs={{0,4},{4,0},{8,12},{12,8},{16,20},{20,16},{24,28},{28,24},{1,5},{5... | collective-permute-start | bytes 393224 | tf_op jit(solution)/shard_map/ppermute | solution.py:418
  54.3 6.5 %collective-permute-start.16 = (bf16[2,256,128]{2,1,0:T(8,128)(2,1)S(1)}, bf16[2,256,128]{2,1,0:T(8,128)(2,1)S(1)}, u32[]{:S(2)}, u32[]{:S(2)}) collective-permute-start(bf16[2,256,128]{2,1,0:T(8,128)(2,1)S(1)} %key_pass.6), channel_id=1, source_target_pairs={{0,4},{4,0},{8,12},{12,8},{16,20},{20,16},{24,28},{28,24},{1,5},{5... | collective-permute-start | bytes 393224 | tf_op jit(solution)/shard_map/ppermute | solution.py:418
  55.8 6.8 %collective-permute-start.15 = (bf16[2,256,128]{2,1,0:T(8,128)(2,1)S(1)}, bf16[2,256,128]{2,1,0:T(8,128)(2,1)S(1)}, u32[]{:S(2)}, u32[]{:S(2)}) collective-permute-start(bf16[2,256,128]{2,1,0:T(8,128)(2,1)S(1)} %key_pass.5), channel_id=1, source_target_pairs={{0,4},{4,0},{8,12},{12,8},{16,20},{20,16},{24,28},{28,24},{1,5},{5... | collective-permute-start | bytes 393224 | tf_op jit(solution)/shard_map/ppermute | solution.py:418

commit v13 on v11

--- a/solution.py
+++ b/solution.py
@@ -69,17 +69,22 @@
     )(q, k, v)
 
 
-def join_kernel(*refs):
-    for i, ref in enumerate(refs[:-1]):
-        refs[-1][i] = ref[...]
-
-
-def join(*pieces):
-    return pl.pallas_call(
-        join_kernel,
-        out_shape=jax.ShapeDtypeStruct((len(pieces), *pieces[0].shape), BF16),
+def join_kernel(pieces, *refs):
+    first = 0
+    for out in refs[pieces:]:
+        width = out.shape[2]
+        for i, ref in enumerate(refs[:pieces]):
+            out[i] = ref[:, first : first + width]
+        first += width
+
+
+def join(widths, *pieces):
+    rows = pieces[0].shape[0]
+    return pl.pallas_call(
+        functools.partial(join_kernel, len(pieces)),
+        out_shape=tuple(jax.ShapeDtypeStruct((len(pieces), rows, w), BF16) for w in widths),
         in_specs=[VM] * len(pieces),
-        out_specs=VM,
+        out_specs=(VM,) * len(widths),
         compiler_params=params(16),
         cost_estimate=cost(),
         name="join",
@@ -263,7 +268,7 @@
         out_specs=(VM, VM),
         scratch_shapes=[pltpu.VMEM((2, rows, cols), BF16)],
         compiler_params=params(30),
-        cost_estimate=cost(6e9 if own else 1),
+        cost_estimate=cost(1e9 if own else 6e9),
         name="query_pass",
     )(*operands)
 
@@ -314,24 +319,35 @@
     )(*operands)
 
 
-def key_kernel(scale, own, heads, kv, e0, o0, late_e, late_o, se, so, sums, out, fifth_q, fifth_d):
+def key_kernel(scale, own, heads, runs, kv, e0, o0, se, so, sums, *refs):
+    late, (out, fifth_q, fifth_d) = refs[:-3], refs[-3:]
     rows = kv.shape[1]
     even_ok, odd_ok, turned = place()
     from_even = turned if own else jnp.logical_not(turned)
-    even_q, odd_q = (e0.at[2], late_e.at[0]), (o0.at[2], late_o.at[0])
-    even_d, odd_d = (late_e.at[1], late_e.at[2]), (late_o.at[1], late_o.at[2])
     same, other = (0, 1) if own else (1, 0)
-    wanted = slice(heads[0] * HD, (heads[-1] + 1) * HD)
+    where = {}
+    for i, run in enumerate(runs):
+        for at, head in enumerate(run):
+            where[head] = (late[2 * i], late[2 * i + 1], slice(at * HD, (at + 1) * HD))
+
+    def theirs(head, odd, half):
+        ref, cols = where[head][odd], where[head][2]
+        whole = slice(head * HD, (head + 1) * HD)
+        first = (o0 if odd else e0)[2, :, whole] if half == 0 else ref[0, :, cols]
+        return first, ref[1 + half, :, cols]
+
+    def fill(odd):
+        for i, head in enumerate(heads):
+            to = slice(i * HD, (i + 1) * HD)
+            fifth_q[:, to], fifth_d[:, to] = theirs(head, odd, other)
 
     @pl.when(from_even)
     def _():
-        fifth_q[...] = even_q[other][:, wanted]
-        fifth_d[...] = even_d[other][:, wanted]
+        fill(0)
 
     @pl.when(jnp.logical_not(from_even))
     def _():
-        fifth_q[...] = odd_q[other][:, wanted]
-        fifth_d[...] = odd_d[other][:, wanted]
+        fill(1)
 
     row = lax.broadcasted_iota(jnp.int32, se.shape, 0)
     nothing = jnp.where(lax.rem(row, 2) == 0, jnp.float32(BIG), jnp.float32(0.0))
@@ -345,8 +361,8 @@
         to = slice(i * HD, (i + 1) * HD)
         a, b = 2 * head, 2 * head + 1
         steps = (
-            (even_q[same][:, cols], even_d[same][:, cols], even[a : a + 1, span], even[b : b + 1, span]),
-            (odd_q[same][:, cols], odd_d[same][:, cols], odd[a : a + 1, span], odd[b : b + 1, span]),
+            (*theirs(head, 0, same), even[a : a + 1, span], even[b : b + 1, span]),
+            (*theirs(head, 1, same), odd[a : a + 1, span], odd[b : b + 1, span]),
             (fifth_q[:, to], fifth_d[:, to], fifth[a : a + 1], fifth[b : b + 1]),
         )
         k, v = key_step(scale, kv[0, :, cols], kv[1, :, cols], steps)
@@ -354,11 +370,11 @@
         out[1, :, to] = (v + sums[1, :, cols]).astype(BF16)
 
 
-def key_pass(own, heads, kv, *operands):
+def key_pass(own, heads, runs, kv, *operands):
     _, rows, _ = kv.shape
     wide = HD * len(heads)
     return pl.pallas_call(
-        functools.partial(key_kernel, HD ** -0.5, own, heads),
+        functools.partial(key_kernel, HD ** -0.5, own, heads, runs),
         out_shape=jax.ShapeDtypeStruct((2, rows, wide), BF16),
         in_specs=[VM] * (1 + len(operands)),
         out_specs=VM,
@@ -447,24 +463,32 @@
     dxr = after(over_x(dsend), flops=6e9)
 
     xq, e1, o1 = lax.optimization_barrier((xq, e1, o1))
-    late = join(xq, dkeep, dxr)
-    late_e, late_o = over_z(late, 0), over_z(late, 1)
+    heads = dkeep.shape[1] // HD
+    runs = ((0,), tuple(range(1, heads))) if heads > 1 else ((0,),)
+    late = [
+        (over_z(piece, 0), over_z(piece, 1))
+        for piece in join(tuple(HD * len(run) for run in runs), xq, dkeep, dxr)
+    ]
     dq_send, marks = query_pass(False, xq, dxr, keep, xkv, e1, o1, e0, o0)
     dq_keep, stats = query_pass(True, keep, dkeep, keep, xkv, e0, o0, e1, o1, marks)
-    dq_got = after(over_x(dq_send), flops=6e9)
+    dq_got = after(over_x(dq_send), flops=4e9)
+    stats, first_e, first_o = lax.optimization_barrier((stats, *late[0]))
+    late[0] = (first_e, first_o)
     se, so = over_z(stats, 0), over_z(stats, 1)
     sums = own_pass(xkv, keep, xq, dkeep, dxr, stats)
-    sums = after(sums, late_e, late_o, flops=3e9)
     own_sums = own_pass(keep, keep, xq, dkeep, dxr, stats)
-    heads = dkeep.shape[1] // HD
-    theirs = (e0, o0, late_e, late_o, se, so)
+    dq, = unpack(dq_keep, dq_got)
     got = []
-    for head in range(heads):
-        if head == 1:
-            dq, = unpack(dq_keep, dq_got)
+    for i, (run, pair) in enumerate(zip(runs, late)):
+        if i > 0:
+            sums = after(sums, *pair, flops=6e9)
+        if i == len(runs) - 1:
             sums, dq = lax.optimization_barrier((sums, dq))
-        got.append(over_x(key_pass(False, (head,), xkv, *theirs, sums)))
-    kv_keep = key_pass(True, tuple(range(heads)), keep, *theirs, own_sums)
+        for head in run:
+            piece = key_pass(False, (head,), (run,), xkv, e0, o0, se, so, sums, *pair)
+            got.append(over_x(piece))
+    every = [array for pair in late for array in pair]
+    kv_keep = key_pass(True, tuple(range(heads)), runs, keep, e0, o0, se, so, own_sums, *every)
     return (dq, *unpack(kv_keep, *got))
 
 

time: 63 us -> 65.4 us (1.038)
  waiting for transfers between devices: 17.6 us -> 19.2 us
  starting transfers between devices: 20.7 us -> 21.4 us
    ppermute x8 -> x10, starting transfers between devices: 8.64 us -> 10.4 us  [over_z(): return lax.ppermute(array, ('ctx', 'mp'), pairs)]
    ppermute x7, starting transfers between devices: 8.94 us -> 7.95 us  [over_x(): return lax.ppermute(array, 'ctx', [(i, i ^ 1) for i in range(length)])]
    ppermute x8 -> x10, waiting for transfers between devices: 8.23 us -> 9.07 us  [over_z(): return lax.ppermute(array, ('ctx', 'mp'), pairs)]
    ppermute x7, waiting for transfers between devices: 9.08 us -> 9.85 us  [over_x(): return lax.ppermute(array, 'ctx', [(i, i ^ 1) for i in range(length)])]
  transfers between devices with their start and end apart: 18 -> 20, of which waited for: 7 -> 6; matrix products, arithmetic and copies ran while one was open for 0% -> 0% of each run, Pallas kernels for 33% -> 33%
where the time goes in v13:
time: 65.4 us; the launch traced here: 65.2 us
  Pallas kernels  22.4 us (34%)
  starting transfers between devices  21.4 us (33%)
  waiting for transfers between devices  19.2 us (29%)
  local copies, waits for them, and re-layouts  1.14 us (2%)
  between operations  0.97 us (1%)
    ppermute x10, starting transfers between devices, over_z(): return lax.ppermute(array, ('ctx', 'mp'), pairs)  10.4 us
    ppermute x7, waiting for transfers between devices, over_x(): return lax.ppermute(array, 'ctx', [(i, i ^ 1) for i in range(length)])  9.85 us
    ppermute x10, waiting for transfers between devices, over_z(): return lax.ppermute(array, ('ctx', 'mp'), pairs)  9.07 us
    ppermute x7, starting transfers between devices, over_x(): return lax.ppermute(array, 'ctx', [(i, i ^ 1) for i in range(length)])  7.95 us
    pallas_call x2, Pallas kernels, query_pass(): pl.pallas_call(functools.partial(query_kernel, HD ** (-0.5), own, before...  5.94 us
    pallas_call x4, Pallas kernels, key_pass(): pl.pallas_call(functools.partial(key_kernel, HD ** (-0.5), own, heads, ru...  4.42 us
    pallas_call x1, Pallas kernels, first_piece(): pl.pallas_call(first_kernel, out_shape=(jax.ShapeDtypeStruct((rows, heads...  3.82 us
    ppermute x3, starting transfers between devices, over_mp(): return lax.ppermute(array, 'mp', [(i, i ^ flip) for i in range(lanes)])  3.12 us
  transfers between devices with their start and end apart: 20, of which 6 were waited for; matrix products, arithmetic and copies ran while one was open for 0% of the time, Pallas kernels for 33%

profile of v13, /device:TPU:0, one launch (start us, length us, event | category | flops | bytes accessed | tf_op | source)
XLA Modules:
  0.0 65.2 jit_solution(3317984286061843254)
XLA Ops:
  1.1 2.6 %collective-permute-start.4 = (bf16[256,1536]{1,0:T(8,128)(2,1)}, bf16[256,1536]{1,0:T(8,128)(2,1)S(1)}, u32[]{:S(2)}, u32[]{:S(2)}) collective-permute-start(bf16[256,1536]{1,0:T(8,128)(2,1)} %og.1), channel_id=1, source_target_pairs={{0,2},{1,3},{2,0},{3,1},{4,6},{5,7},{6,4},{7,5},{8,10},{9,11},{10,... | collective-permute-start | bytes 2359304 | tf_op jit(solution)/shard_map/ppermute | solution.py:431
  3.7 2.4 %pack.1 = (bf16[3,256,384]{2,1,0:T(8,128)(2,1)}, bf16[2,256,384]{2,1,0:T(8,128)(2,1)}, bf16[256,384]{1,0:T(8,128)(2,1)}) custom-call(bf16[256,768]{1,0:T(8,128)(2,1)} %q.1, bf16[256,768]{1,0:T(8,128)(2,1)} %k.1, bf16[256,768]{1,0:T(8,128)(2,1)} %v.1), custom_call_target="tpu_custom_call" | custom-call | flops 1 | bytes 1 | tf_op jit(solution)/shard_map/pack/pallas_call | solution.py:60
  6.1 1.6 %collective-permute-start = (bf16[2,256,384]{2,1,0:T(8,128)(2,1)}, bf16[2,256,384]{2,1,0:T(8,128)(2,1)S(1)}, u32[]{:S(2)}, u32[]{:S(2)}) collective-permute-start(bf16[2,256,384]{2,1,0:T(8,128)(2,1)} %get-tuple-element.29), channel_id=1, source_target_pairs={{0,4},{4,0},{8,12},{12,8},{16,20},{20,16},{24,28},{28,24},{1,5},{5... | collective-permute-start | bytes 1179656 | tf_op jit(solution)/shard_map/ppermute | solution.py:434
  8.2 1.6 %collective-permute-start.6 = (bf16[3,256,384]{2,1,0:T(8,128)(2,1)}, bf16[3,256,384]{2,1,0:T(8,128)(2,1)S(1)}, u32[]{:S(2)}, u32[]{:S(2)}) collective-permute-start(bf16[3,256,384]{2,1,0:T(8,128)(2,1)} %get-tuple-element.30.refs_2_.refs_0_.keep.keys.kv), channel_id=1, source_target_pairs={{0,8},{1,9},{2,10},{3,11},{4,12},{5,13},{6,14},{7,15},{8,0},{9,1},... | collective-permute-start | bytes 1769480 | tf_op jit(solution)/shard_map/ppermute | solution.py:448
  9.8 1.1 %copy-done.1 = bf16[256,1536]{1,0:T(8,128)(2,1)S(1)} copy-done((bf16[256,1536]{1,0:T(8,128)(2,1)S(1)}, bf16[256,1536]{1,0:T(8,128)(2,1)}, u32[]{:S(2)}) %copy-start.1) | copy-done | bytes 786456
  10.9 3.8 %head_grad_first.1 = (f32[256,768]{1,0:T(8,128)S(1)}, bf16[768,1536]{1,0:T(8,128)(2,1)S(1)}, bf16[768,1536]{1,0:T(8,128)(2,1)S(1)}) custom-call(bf16[256,1536]{1,0:T(8,128)(2,1)S(1)} %copy-done.1, bf16[256,1536]{1,0:T(8,128)(2,1)S(1)} %collective-permute-done.5.near, bf16[768,6144]{1,0:T(8,128)(2,1)} %w.1), custom_call_target="tpu_custom_call" | custom-call | flops 1 | bytes 1 | tf_op jit(solution)/shard_map/head_grad_first/pallas_call | solution.py:115
  14.8 7.0 %collective-permute-done.1.refs_2_.refs_0_.xq = bf16[256,384]{1,0:T(8,128)(2,1)S(1)} collective-permute-done((bf16[256,384]{1,0:T(8,128)(2,1)}, bf16[256,384]{1,0:T(8,128)(2,1)S(1)}, u32[]{:S(2)}, u32[]{:S(2)}) %collective-permute-start.1) | collective-permute-done | bytes 196640 | tf_op jit(solution)/shard_map/ppermute | solution.py:434
  22.1 1.8 %collective-permute-start.2 = (bf16[2,256,384]{2,1,0:T(8,128)(2,1)S(1)}, bf16[2,256,384]{2,1,0:T(8,128)(2,1)S(1)}, u32[]{:S(2)}, u32[]{:S(2)}) collective-permute-start(bf16[2,256,384]{2,1,0:T(8,128)(2,1)S(1)} %collective-permute-done.refs_1_.refs_3_.keys.kv), channel_id=1, source_target_pairs={{0,8},{1,9},{2,10},{3,11},{4,12},{5,13},{6,14},{7,15},{8,0},{9,1},... | collective-permute-start | bytes 1179656 | tf_op jit(solution)/shard_map/ppermute | solution.py:448
  24.1 0.8 %head_grad.2.refs_0_ = f32[256,768]{1,0:T(8,128)S(1)} custom-call(f32[256,768]{1,0:T(8,128)S(1)} %after.5.acc, bf16[256,1536]{1,0:T(8,128)(2,1)S(1)} %collective-permute-done.4.piece, bf16[768,1536]{1,0:T(8,128)(2,1)S(1)} %get-tuple-element.36.w), custom_call_target="tpu_custom_call" | custom-call | flops 1 | bytes 1 | tf_op jit(solution)/shard_map/head_grad/pallas_call | solution.py:152
  25.0 0.9 %head_grad.3 = (bf16[256,384]{1,0:T(8,128)(2,1)S(1)}, bf16[256,384]{1,0:T(8,128)(2,1)S(1)}) custom-call(f32[256,768]{1,0:T(8,128)S(1)} %after.6.acc, bf16[256,1536]{1,0:T(8,128)(2,1)S(1)} %collective-permute-done.8.piece, bf16[768,1536]{1,0:T(8,128)(2,1)S(1)} %get-tuple-element.37.w), custom_call_target="tpu_custom_call" | custom-call | flops 1 | bytes 1 | tf_op jit(solution)/shard_map/head_grad/pallas_call | solution.py:152
  25.9 1.5 %collective-permute-start.9 = (bf16[256,384]{1,0:T(8,128)(2,1)S(1)}, bf16[256,384]{1,0:T(8,128)(2,1)S(1)}, u32[]{:S(2)}, u32[]{:S(2)}) collective-permute-start(bf16[256,384]{1,0:T(8,128)(2,1)S(1)} %get-tuple-element.39), channel_id=1, source_target_pairs={{0,4},{4,0},{8,12},{12,8},{16,20},{20,16},{24,28},{28,24},{1,5},{5... | collective-permute-start | bytes 589832 | tf_op jit(solution)/shard_map/ppermute | solution.py:434
  27.4 6.3 %collective-permute-done.2.refs_4_.refs_6_ = bf16[2,256,384]{2,1,0:T(8,128)(2,1)S(1)} collective-permute-done((bf16[2,256,384]{2,1,0:T(8,128)(2,1)S(1)}, bf16[2,256,384]{2,1,0:T(8,128)(2,1)S(1)}, u32[]{:S(2)}, u32[]{:S(2)}) %collective-permute-start.2) | collective-permute-done | bytes 393248 | tf_op jit(solution)/shard_map/ppermute | solution.py:448
  33.8 2.9 %collective-permute-start.10 = (bf16[3,256,128]{2,1,0:T(8,128)(2,1)S(1)}, bf16[3,256,128]{2,1,0:T(8,128)(2,1)S(1)}, u32[]{:S(2)}, u32[]{:S(2)}) collective-permute-start(bf16[3,256,128]{2,1,0:T(8,128)(2,1)S(1)} %get-tuple-element.44), channel_id=1, source_target_pairs={{0,8},{1,9},{2,10},{3,11},{4,12},{5,13},{6,14},{7,15},{8,0},{9,1},... | collective-permute-start | bytes 589832 | tf_op jit(solution)/shard_map/ppermute | solution.py:448
  36.7 3.0 %query_pass.2 = (bf16[1,256,384]{2,1,0:T(8,128)(2,1)S(1)}, f32[8,256]{1,0:T(8,128)S(1)}) custom-call(bf16[256,384]{1,0:T(8,128)(2,1)S(1)} %collective-permute-done.1.refs_2_.refs_0_.xq, bf16[256,384]{1,0:T(8,128)(2,1)S(1)} %after.7.refs_1_.refs_2_.dxr, bf16[3,256,384]{2,1,0:T(8,128)(2,1)S(1)} %copy-done, ...), custom_call_target="tpu_custom_call" | custom-call | flops 6000000000 | bytes 1 | tf_op jit(solution)/shard_map/query_pass/pallas_call | solution.py:261
  39.7 1.6 %collective-permute-start.14 = (bf16[1,256,384]{2,1,0:T(8,128)(2,1)S(1)}, bf16[1,256,384]{2,1,0:T(8,128)(2,1)S(1)}, u32[]{:S(2)}, u32[]{:S(2)}) collective-permute-start(bf16[1,256,384]{2,1,0:T(8,128)(2,1)S(1)} %get-tuple-element.48), channel_id=1, source_target_pairs={{0,4},{4,0},{8,12},{12,8},{16,20},{20,16},{24,28},{28,24},{1,5},{5... | collective-permute-start | bytes 589832 | tf_op jit(solution)/shard_map/ppermute | solution.py:434
  41.3 2.0 %collective-permute-start.12 = (bf16[3,256,256]{2,1,0:T(8,128)(2,1)S(1)}, bf16[3,256,256]{2,1,0:T(8,128)(2,1)S(1)}, u32[]{:S(2)}, u32[]{:S(2)}) collective-permute-start(bf16[3,256,256]{2,1,0:T(8,128)(2,1)S(1)} %get-tuple-element.46), channel_id=1, source_target_pairs={{0,8},{1,9},{2,10},{3,11},{4,12},{5,13},{6,14},{7,15},{8,0},{9,1},... | collective-permute-start | bytes 1179656 | tf_op jit(solution)/shard_map/ppermute | solution.py:448
  43.3 3.0 %query_pass.3 = (bf16[1,256,384]{2,1,0:T(8,128)(2,1)S(1)}, f32[8,512]{1,0:T(8,128)S(1)}) custom-call(bf16[3,256,384]{2,1,0:T(8,128)(2,1)S(1)} %copy-done, bf16[256,384]{1,0:T(8,128)(2,1)S(1)} %get-tuple-element.38.refs_1_.dkeep, bf16[3,256,384]{2,1,0:T(8,128)(2,1)S(1)} %copy-done, bf16[2,256,384]{2,1,0:T(8,128)(2,1)S(1)} %collective-permute-done.refs_1_.refs_3_.keys.kv, ...), custom_call_target="tpu_custom_call" | custom-call | flops 1000000000 | bytes 1 | tf_op jit(solution)/shard_map/query_pass/pallas_call | solution.py:261
  46.3 1.8 %collective-permute-start.15 = (f32[8,512]{1,0:T(8,128)S(1)}, f32[8,512]{1,0:T(8,128)S(1)}, u32[]{:S(2)}, u32[]{:S(2)}) collective-permute-start(f32[8,512]{1,0:T(8,128)S(1)} %get-tuple-element.45.stats), channel_id=1, source_target_pairs={{0,8},{1,9},{2,10},{3,11},{4,12},{5,13},{6,14},{7,15},{8,0},{9,1},... | collective-permute-start | bytes 49160 | tf_op jit(solution)/shard_map/ppermute | solution.py:448
  48.1 0.8 %unpack.2 = bf16[256,768]{1,0:T(8,128)(2,1)} custom-call(bf16[1,256,384]{2,1,0:T(8,128)(2,1)S(1)} %get-tuple-element.47.kept, bf16[1,256,384]{2,1,0:T(8,128)(2,1)S(1)} %after.9.refs_0_), custom_call_target="tpu_custom_call" | custom-call | flops 1 | bytes 1 | tf_op jit(solution)/shard_map/unpack/pallas_call | solution.py:412
  48.8 1.2 %own_pass.2.refs_0_.sums = f32[2,256,384]{2,1,0:T(8,128)S(1)} custom-call(bf16[2,256,384]{2,1,0:T(8,128)(2,1)S(1)} %collective-permute-done.refs_1_.refs_3_.keys.kv, bf16[3,256,384]{2,1,0:T(8,128)(2,1)S(1)} %copy-done, bf16[256,384]{1,0:T(8,128)(2,1)S(1)} %collective-permute-done.1.refs_2_.refs_0_.xq, bf16[256,384]{1,0:T(8,128)(2,1)S(1)} %get-tuple-element.38.refs_1_.dkeep, ...), custom_call_target="tpu_custom_call" | custom-call | flops 1 | bytes 1 | tf_op jit(solution)/shard_map/own_pass/pallas_call | solution.py:311
  50.1 2.8 %collective-permute-done.15.se = f32[8,512]{1,0:T(8,128)S(1)} collective-permute-done((f32[8,512]{1,0:T(8,128)S(1)}, f32[8,512]{1,0:T(8,128)S(1)}, u32[]{:S(2)}, u32[]{:S(2)}) %collective-permute-start.15) | collective-permute-done | bytes 16416 | tf_op jit(solution)/shard_map/ppermute | solution.py:448
  52.8 0.8 %key_pass.5 = bf16[2,256,128]{2,1,0:T(8,128)(2,1)S(1)} custom-call(bf16[2,256,384]{2,1,0:T(8,128)(2,1)S(1)} %collective-permute-done.refs_1_.refs_3_.keys.kv, bf16[3,256,384]{2,1,0:T(8,128)(2,1)S(1)} %collective-permute-done.6.refs_1_.refs_6_.refs_4_.e0, bf16[3,256,384]{2,1,0:T(8,128)(2,1)S(1)} %collective-permute-done.7.refs_2_.refs_7_.refs_5_.o0, ...), custom_call_target="tpu_custom_call" | custom-call | flops 1000000000 | bytes 1 | tf_op jit(solution)/shard_map/key_pass/pallas_call | solution.py:376
  53.6 0.6 collective-permute-start.17
  54.2 0.9 %key_pass.7 = bf16[2,256,128]{2,1,0:T(8,128)(2,1)S(1)} custom-call(bf16[2,256,384]{2,1,0:T(8,128)(2,1)S(1)} %collective-permute-done.refs_1_.refs_3_.keys.kv, bf16[3,256,384]{2,1,0:T(8,128)(2,1)S(1)} %collective-permute-done.6.refs_1_.refs_6_.refs_4_.e0, bf16[3,256,384]{2,1,0:T(8,128)(2,1)S(1)} %collective-permute-done.7.refs_2_.refs_7_.refs_5_.o0, ...), custom_call_target="tpu_custom_call" | custom-call | flops 1000000000 | bytes 1 | tf_op jit(solution)/shard_map/key_pass/pallas_call | solution.py:376
  55.2 1.6 %collective-permute-start.19 = (bf16[2,256,128]{2,1,0:T(8,128)(2,1)S(1)}, bf16[2,256,128]{2,1,0:T(8,128)(2,1)S(1)}, u32[]{:S(2)}, u32[]{:S(2)}) collective-permute-start(bf16[2,256,128]{2,1,0:T(8,128)(2,1)S(1)} %key_pass.7), channel_id=1, source_target_pairs={{0,4},{4,0},{8,12},{12,8},{16,20},{20,16},{24,28},{28,24},{1,5},{5... | collective-permute-start | bytes 393224 | tf_op jit(solution)/shard_map/ppermute | solution.py:434
  56.7 0.8 %key_pass.6 = bf16[2,256,128]{2,1,0:T(8,128)(2,1)S(1)} custom-call(bf16[2,256,384]{2,1,0:T(8,128)(2,1)S(1)} %collective-permute-done.refs_1_.refs_3_.keys.kv, bf16[3,256,384]{2,1,0:T(8,128)(2,1)S(1)} %collective-permute-done.6.refs_1_.refs_6_.refs_4_.e0, bf16[3,256,384]{2,1,0:T(8,128)(2,1)S(1)} %collective-permute-done.7.refs_2_.refs_7_.refs_5_.o0, ...), custom_call_target="tpu_custom_call" | custom-call | flops 1000000000 | bytes 1 | tf_op jit(solution)/shard_map/key_pass/pallas_call | solution.py:376
  57.5 0.6 collective-permute-start.18
  58.1 1.2 %own_pass.3.sums = f32[2,256,384]{2,1,0:T(8,128)S(1)} custom-call(bf16[3,256,384]{2,1,0:T(8,128)(2,1)S(1)} %copy-done, bf16[3,256,384]{2,1,0:T(8,128)(2,1)S(1)} %copy-done, bf16[256,384]{1,0:T(8,128)(2,1)S(1)} %collective-permute-done.1.refs_2_.refs_0_.xq, bf16[256,384]{1,0:T(8,128)(2,1)S(1)} %get-tuple-element.38.refs_1_.dkeep, ...), custom_call_target="tpu_custom_call" | custom-call | flops 1 | bytes 1 | tf_op jit(solution)/shard_map/own_pass/pallas_call | solution.py:311
  59.3 2.0 %key_pass.4.kept = bf16[2,256,384]{2,1,0:T(8,128)(2,1)S(1)} custom-call(bf16[3,256,384]{2,1,0:T(8,128)(2,1)S(1)} %copy-done, bf16[3,256,384]{2,1,0:T(8,128)(2,1)S(1)} %collective-permute-done.6.refs_1_.refs_6_.refs_4_.e0, bf16[3,256,384]{2,1,0:T(8,128)(2,1)S(1)} %collective-permute-done.7.refs_2_.refs_7_.refs_5_.o0, ...), custom_call_target="tpu_custom_call" | custom-call | flops 1000000000 | bytes 1 | tf_op jit(solution)/shard_map/key_pass/pallas_call | solution.py:376
  61.3 1.4 %collective-permute-done.19.refs_2_ = bf16[2,256,128]{2,1,0:T(8,128)(2,1)S(1)} collective-permute-done((bf16[2,256,128]{2,1,0:T(8,128)(2,1)S(1)}, bf16[2,256,128]{2,1,0:T(8,128)(2,1)S(1)}, u32[]{:S(2)}, u32[]{:S(2)}) %collective-permute-start.19) | collective-permute-done | bytes 131104 | tf_op jit(solution)/shard_map/ppermute | solution.py:434
  62.7 1.4 %collective-permute-done.18.refs_1_ = bf16[2,256,128]{2,1,0:T(8,128)(2,1)S(1)} collective-permute-done((bf16[2,256,128]{2,1,0:T(8,128)(2,1)S(1)}, bf16[2,256,128]{2,1,0:T(8,128)(2,1)S(1)}, u32[]{:S(2)}, u32[]{:S(2)}) %collective-permute-start.18) | collective-permute-done | bytes 131104 | tf_op jit(solution)/shard_map/ppermute | solution.py:434
  64.1 0.9 %unpack.3 = (bf16[256,768]{1,0:T(8,128)(2,1)}, bf16[256,768]{1,0:T(8,128)(2,1)}) custom-call(bf16[2,256,384]{2,1,0:T(8,128)(2,1)S(1)} %key_pass.4.kept, bf16[2,256,128]{2,1,0:T(8,128)(2,1)S(1)} %collective-permute-done.17.refs_0_, bf16[2,256,128]{2,1,0:T(8,128)(2,1)S(1)} %collective-permute-done.18.refs_1_, ...), custom_call_target="tpu_custom_call" | custom-call | flops 1 | bytes 1 | tf_op jit(solution)/shard_map/unpack/pallas_call | solution.py:412
  (32 shorter events, 1.7 us)
Async XLA Ops:
  0.6 9.2 %collective-permute-start.5 = (bf16[256,1536]{1,0:T(8,128)(2,1)}, bf16[256,1536]{1,0:T(8,128)(2,1)S(1)}, u32[]{:S(2)}, u32[]{:S(2)}) collective-permute-start(bf16[256,1536]{1,0:T(8,128)(2,1)} %og.1), channel_id=1, source_target_pairs={{0,1},{1,0},{2,3},{3,2},{4,5},{5,4},{6,7},{7,6},{8,9},{9,8},{10,11... | collective-permute-start | bytes 2359304 | tf_op jit(solution)/shard_map/ppermute | solution.py:431
  1.1 20.9 %collective-permute-start.4 = (bf16[256,1536]{1,0:T(8,128)(2,1)}, bf16[256,1536]{1,0:T(8,128)(2,1)S(1)}, u32[]{:S(2)}, u32[]{:S(2)}) collective-permute-start(bf16[256,1536]{1,0:T(8,128)(2,1)} %og.1), channel_id=1, source_target_pairs={{0,2},{1,3},{2,0},{3,1},{4,6},{5,7},{6,4},{7,5},{8,10},{9,11},{10,... | collective-permute-start | bytes 2359304 | tf_op jit(solution)/shard_map/ppermute | solution.py:431
  6.1 15.7 %collective-permute-start = (bf16[2,256,384]{2,1,0:T(8,128)(2,1)}, bf16[2,256,384]{2,1,0:T(8,128)(2,1)S(1)}, u32[]{:S(2)}, u32[]{:S(2)}) collective-permute-start(bf16[2,256,384]{2,1,0:T(8,128)(2,1)} %get-tuple-element.29), channel_id=1, source_target_pairs={{0,4},{4,0},{8,12},{12,8},{16,20},{20,16},{24,28},{28,24},{1,5},{5... | collective-permute-start | bytes 1179656 | tf_op jit(solution)/shard_map/ppermute | solution.py:434
  7.7 14.1 %collective-permute-start.1 = (bf16[256,384]{1,0:T(8,128)(2,1)}, bf16[256,384]{1,0:T(8,128)(2,1)S(1)}, u32[]{:S(2)}, u32[]{:S(2)}) collective-permute-start(bf16[256,384]{1,0:T(8,128)(2,1)} %get-tuple-element.31), channel_id=1, source_target_pairs={{0,4},{4,0},{8,12},{12,8},{16,20},{20,16},{24,28},{28,24},{1,5},{5... | collective-permute-start | bytes 589832 | tf_op jit(solution)/shard_map/ppermute | solution.py:434
  8.2 16.7 %collective-permute-start.6 = (bf16[3,256,384]{2,1,0:T(8,128)(2,1)}, bf16[3,256,384]{2,1,0:T(8,128)(2,1)S(1)}, u32[]{:S(2)}, u32[]{:S(2)}) collective-permute-start(bf16[3,256,384]{2,1,0:T(8,128)(2,1)} %get-tuple-element.30.refs_2_.refs_0_.keep.keys.kv), channel_id=1, source_target_pairs={{0,8},{1,9},{2,10},{3,11},{4,12},{5,13},{6,14},{7,15},{8,0},{9,1},... | collective-permute-start | bytes 1769480 | tf_op jit(solution)/shard_map/ppermute | solution.py:448
  9.8 15.1 %collective-permute-start.7 = (bf16[3,256,384]{2,1,0:T(8,128)(2,1)}, bf16[3,256,384]{2,1,0:T(8,128)(2,1)S(1)}, u32[]{:S(2)}, u32[]{:S(2)}) collective-permute-start(bf16[3,256,384]{2,1,0:T(8,128)(2,1)} %get-tuple-element.30.refs_2_.refs_0_.keep.keys.kv), channel_id=1, source_target_pairs={{0,1},{1,0},{2,3},{3,2},{4,5},{5,4},{6,7},{7,6},{8,16},{9,17},{10,... | collective-permute-start | bytes 1769480 | tf_op jit(solution)/shard_map/ppermute | solution.py:448
  9.8 1.1 %copy-start.1 = (bf16[256,1536]{1,0:T(8,128)(2,1)S(1)}, bf16[256,1536]{1,0:T(8,128)(2,1)}, u32[]{:S(2)}) copy-start(bf16[256,1536]{1,0:T(8,128)(2,1)} %og.1) | copy-start | bytes 2359300
  22.1 2.9 %collective-permute-start.8 = (bf16[256,1536]{1,0:T(8,128)(2,1)S(1)}, bf16[256,1536]{1,0:T(8,128)(2,1)S(1)}, u32[]{:S(2)}, u32[]{:S(2)}) collective-permute-start(bf16[256,1536]{1,0:T(8,128)(2,1)S(1)} %collective-permute-done.4.piece), channel_id=1, source_target_pairs={{0,1},{1,0},{2,3},{3,2},{4,5},{5,4},{6,7},{7,6},{8,9},{9,8},{10,11... | collective-permute-start | bytes 2359304 | tf_op jit(solution)/shard_map/ppermute | solution.py:431
  22.1 11.6 %collective-permute-start.2 = (bf16[2,256,384]{2,1,0:T(8,128)(2,1)S(1)}, bf16[2,256,384]{2,1,0:T(8,128)(2,1)S(1)}, u32[]{:S(2)}, u32[]{:S(2)}) collective-permute-start(bf16[2,256,384]{2,1,0:T(8,128)(2,1)S(1)} %collective-permute-done.refs_1_.refs_3_.keys.kv), channel_id=1, source_target_pairs={{0,8},{1,9},{2,10},{3,11},{4,12},{5,13},{6,14},{7,15},{8,0},{9,1},... | collective-permute-start | bytes 1179656 | tf_op jit(solution)/shard_map/ppermute | solution.py:448
  23.9 9.8 %collective-permute-start.3 = (bf16[2,256,384]{2,1,0:T(8,128)(2,1)S(1)}, bf16[2,256,384]{2,1,0:T(8,128)(2,1)S(1)}, u32[]{:S(2)}, u32[]{:S(2)}) collective-permute-start(bf16[2,256,384]{2,1,0:T(8,128)(2,1)S(1)} %collective-permute-done.refs_1_.refs_3_.keys.kv), channel_id=1, source_target_pairs={{0,1},{1,0},{2,3},{3,2},{4,5},{5,4},{6,7},{7,6},{8,16},{9,17},{10,... | collective-permute-start | bytes 1179656 | tf_op jit(solution)/shard_map/ppermute | solution.py:448
  25.8 10.9 %copy-start = (bf16[3,256,384]{2,1,0:T(8,128)(2,1)S(1)}, bf16[3,256,384]{2,1,0:T(8,128)(2,1)}, u32[]{:S(2)}) copy-start(bf16[3,256,384]{2,1,0:T(8,128)(2,1)} %get-tuple-element.30.refs_2_.refs_0_.keep.keys.kv) | copy-start | bytes 1769476
  25.9 7.8 %collective-permute-start.9 = (bf16[256,384]{1,0:T(8,128)(2,1)S(1)}, bf16[256,384]{1,0:T(8,128)(2,1)S(1)}, u32[]{:S(2)}, u32[]{:S(2)}) collective-permute-start(bf16[256,384]{1,0:T(8,128)(2,1)S(1)} %get-tuple-element.39), channel_id=1, source_target_pairs={{0,4},{4,0},{8,12},{12,8},{16,20},{20,16},{24,28},{28,24},{1,5},{5... | collective-permute-start | bytes 589832 | tf_op jit(solution)/shard_map/ppermute | solution.py:434
  33.8 12.5 %collective-permute-start.10 = (bf16[3,256,128]{2,1,0:T(8,128)(2,1)S(1)}, bf16[3,256,128]{2,1,0:T(8,128)(2,1)S(1)}, u32[]{:S(2)}, u32[]{:S(2)}) collective-permute-start(bf16[3,256,128]{2,1,0:T(8,128)(2,1)S(1)} %get-tuple-element.44), channel_id=1, source_target_pairs={{0,8},{1,9},{2,10},{3,11},{4,12},{5,13},{6,14},{7,15},{8,0},{9,1},... | collective-permute-start | bytes 589832 | tf_op jit(solution)/shard_map/ppermute | solution.py:448
  36.7 9.6 %collective-permute-start.11 = (bf16[3,256,128]{2,1,0:T(8,128)(2,1)S(1)}, bf16[3,256,128]{2,1,0:T(8,128)(2,1)S(1)}, u32[]{:S(2)}, u32[]{:S(2)}) collective-permute-start(bf16[3,256,128]{2,1,0:T(8,128)(2,1)S(1)} %get-tuple-element.44), channel_id=1, source_target_pairs={{0,1},{1,0},{2,3},{3,2},{4,5},{5,4},{6,7},{7,6},{8,16},{9,17},{10,... | collective-permute-start | bytes 589832 | tf_op jit(solution)/shard_map/ppermute | solution.py:448
  39.7 8.4 %collective-permute-start.14 = (bf16[1,256,384]{2,1,0:T(8,128)(2,1)S(1)}, bf16[1,256,384]{2,1,0:T(8,128)(2,1)S(1)}, u32[]{:S(2)}, u32[]{:S(2)}) collective-permute-start(bf16[1,256,384]{2,1,0:T(8,128)(2,1)S(1)} %get-tuple-element.48), channel_id=1, source_target_pairs={{0,4},{4,0},{8,12},{12,8},{16,20},{20,16},{24,28},{28,24},{1,5},{5... | collective-permute-start | bytes 589832 | tf_op jit(solution)/shard_map/ppermute | solution.py:434
  41.3 12.9 %collective-permute-start.12 = (bf16[3,256,256]{2,1,0:T(8,128)(2,1)S(1)}, bf16[3,256,256]{2,1,0:T(8,128)(2,1)S(1)}, u32[]{:S(2)}, u32[]{:S(2)}) collective-permute-start(bf16[3,256,256]{2,1,0:T(8,128)(2,1)S(1)} %get-tuple-element.46), channel_id=1, source_target_pairs={{0,8},{1,9},{2,10},{3,11},{4,12},{5,13},{6,14},{7,15},{8,0},{9,1},... | collective-permute-start | bytes 1179656 | tf_op jit(solution)/shard_map/ppermute | solution.py:448
  43.3 10.9 %collective-permute-start.13 = (bf16[3,256,256]{2,1,0:T(8,128)(2,1)S(1)}, bf16[3,256,256]{2,1,0:T(8,128)(2,1)S(1)}, u32[]{:S(2)}, u32[]{:S(2)}) collective-permute-start(bf16[3,256,256]{2,1,0:T(8,128)(2,1)S(1)} %get-tuple-element.46), channel_id=1, source_target_pairs={{0,1},{1,0},{2,3},{3,2},{4,5},{5,4},{6,7},{7,6},{8,16},{9,17},{10,... | collective-permute-start | bytes 1179656 | tf_op jit(solution)/shard_map/ppermute | solution.py:448
  46.3 6.6 %collective-permute-start.15 = (f32[8,512]{1,0:T(8,128)S(1)}, f32[8,512]{1,0:T(8,128)S(1)}, u32[]{:S(2)}, u32[]{:S(2)}) collective-permute-start(f32[8,512]{1,0:T(8,128)S(1)} %get-tuple-element.45.stats), channel_id=1, source_target_pairs={{0,8},{1,9},{2,10},{3,11},{4,12},{5,13},{6,14},{7,15},{8,0},{9,1},... | collective-permute-start | bytes 49160 | tf_op jit(solution)/shard_map/ppermute | solution.py:448
  48.1 4.8 %collective-permute-start.16 = (f32[8,512]{1,0:T(8,128)S(1)}, f32[8,512]{1,0:T(8,128)S(1)}, u32[]{:S(2)}, u32[]{:S(2)}) collective-permute-start(f32[8,512]{1,0:T(8,128)S(1)} %get-tuple-element.45.stats), channel_id=1, source_target_pairs={{0,1},{1,0},{2,3},{3,2},{4,5},{5,4},{6,7},{7,6},{8,16},{9,17},{10,... | collective-permute-start | bytes 49160 | tf_op jit(solution)/shard_map/ppermute | solution.py:448
  53.6 7.7 %collective-permute-start.17 = (bf16[2,256,128]{2,1,0:T(8,128)(2,1)S(1)}, bf16[2,256,128]{2,1,0:T(8,128)(2,1)S(1)}, u32[]{:S(2)}, u32[]{:S(2)}) collective-permute-start(bf16[2,256,128]{2,1,0:T(8,128)(2,1)S(1)} %key_pass.5), channel_id=1, source_target_pairs={{0,4},{4,0},{8,12},{12,8},{16,20},{20,16},{24,28},{28,24},{1,5},{5... | collective-permute-start | bytes 393224 | tf_op jit(solution)/shard_map/ppermute | solution.py:434
  55.2 7.5 %collective-permute-start.19 = (bf16[2,256,128]{2,1,0:T(8,128)(2,1)S(1)}, bf16[2,256,128]{2,1,0:T(8,128)(2,1)S(1)}, u32[]{:S(2)}, u32[]{:S(2)}) collective-permute-start(bf16[2,256,128]{2,1,0:T(8,128)(2,1)S(1)} %key_pass.7), channel_id=1, source_target_pairs={{0,4},{4,0},{8,12},{12,8},{16,20},{20,16},{24,28},{28,24},{1,5},{5... | collective-permute-start | bytes 393224 | tf_op jit(solution)/shard_map/ppermute | solution.py:434
  57.5 6.6 %collective-permute-start.18 = (bf16[2,256,128]{2,1,0:T(8,128)(2,1)S(1)}, bf16[2,256,128]{2,1,0:T(8,128)(2,1)S(1)}, u32[]{:S(2)}, u32[]{:S(2)}) collective-permute-start(bf16[2,256,128]{2,1,0:T(8,128)(2,1)S(1)} %key_pass.6), channel_id=1, source_target_pairs={{0,4},{4,0},{8,12},{12,8},{16,20},{20,16},{24,28},{28,24},{1,5},{5... | collective-permute-start | bytes 393224 | tf_op jit(solution)/shard_map/ppermute | solution.py:434

commit v14 on v11

--- a/solution.py
+++ b/solution.py
@@ -405,6 +405,36 @@
     )(kept, *got)
 
 
+def finish_kernel(dk_in, dv_in, last, dk, dv, sem):
+    del dk_in, dv_in
+    width = last.shape[2]
+    half = dk.shape[1] // 2
+    x = lax.rem(lax.axis_index("ctx"), 2)
+    columns = pl.ds(pl.multiple_of((1 - x) * half + half - width, width), width)
+    copies = [
+        pltpu.make_async_copy(last.at[i], out.at[:, columns], sem.at[i])
+        for i, out in enumerate((dk, dv))
+    ]
+    for copy in copies:
+        copy.start()
+    for copy in copies:
+        copy.wait()
+
+
+def finish(dk, dv, last):
+    return pl.pallas_call(
+        finish_kernel,
+        out_shape=(jax.ShapeDtypeStruct(dk.shape, dk.dtype),) * 2,
+        in_specs=[ANY, ANY, VM],
+        out_specs=(ANY, ANY),
+        input_output_aliases={0: 0, 1: 1},
+        scratch_shapes=[pltpu.SemaphoreType.DMA((2,))],
+        compiler_params=params(16),
+        cost_estimate=cost(),
+        name="finish",
+    )(dk, dv, last)
+
+
 def body(queries, keys, values, out_grad, out_weight):
     length = lax.axis_size("ctx")
     lanes = lax.axis_size("mp")
@@ -465,7 +495,9 @@
             sums, dq = lax.optimization_barrier((sums, dq))
         got.append(over_x(key_pass(False, (head,), xkv, *theirs, sums)))
     kv_keep = key_pass(True, tuple(range(heads)), keep, *theirs, own_sums)
-    return (dq, *unpack(kv_keep, *got))
+    *early, last = got
+    dk, dv = unpack(kv_keep, *early)
+    return (dq, *finish(dk, dv, last))
 
 
 def solution(mesh):

time: 63 us -> 62.7 us (level)
  waiting for transfers between devices: 17.6 us -> 16.7 us
    ppermute x7, waiting for transfers between devices: 9.08 us -> 8.2 us  [over_x(): return lax.ppermute(array, 'ctx', [(i, i ^ 1) for i in range(length)])]
    pallas_call x0 -> x1, Pallas kernels: none -> 0.67 us  [finish(): pl.pallas_call(finish_kernel, out_shape=(jax.ShapeDtypeStruct(dk.shape, d...]
  transfers between devices with their start and end apart: 18 -> 18, of which waited for: 7 -> 7; matrix products, arithmetic and copies ran while one was open for 0% -> 0% of each run, Pallas kernels for 33% -> 34%
where the time goes in v14:
time: 62.7 us; the launch traced here: 62.5 us
  Pallas kernels  23 us (37%)
  starting transfers between devices  20.7 us (33%)
  waiting for transfers between devices  16.7 us (27%)
  local copies, waits for them, and re-layouts  1.14 us (2%)
  between operations  0.97 us (2%)
    ppermute x7, starting transfers between devices, over_x(): return lax.ppermute(array, 'ctx', [(i, i ^ 1) for i in range(length)])  8.94 us
    ppermute x8, starting transfers between devices, over_z(): return lax.ppermute(array, ('ctx', 'mp'), pairs)  8.64 us
    ppermute x8, waiting for transfers between devices, over_z(): return lax.ppermute(array, ('ctx', 'mp'), pairs)  8.23 us
    ppermute x7, waiting for transfers between devices, over_x(): return lax.ppermute(array, 'ctx', [(i, i ^ 1) for i in range(length)])  8.2 us
    pallas_call x2, Pallas kernels, query_pass(): pl.pallas_call(functools.partial(query_kernel, HD ** (-0.5), own, before...  5.94 us
    pallas_call x4, Pallas kernels, key_pass(): pl.pallas_call(functools.partial(key_kernel, HD ** (-0.5), own, heads), o...  4.39 us
    pallas_call x1, Pallas kernels, first_piece(): pl.pallas_call(first_kernel, out_shape=(jax.ShapeDtypeStruct((rows, heads...  3.82 us
    ppermute x3, starting transfers between devices, over_mp(): return lax.ppermute(array, 'mp', [(i, i ^ flip) for i in range(lanes)])  3.12 us
  transfers between devices with their start and end apart: 18, of which 7 were waited for; matrix products, arithmetic and copies ran while one was open for 0% of the time, Pallas kernels for 34%

profile of v14, /device:TPU:0, one launch (start us, length us, event | category | flops | bytes accessed | tf_op | source)
XLA Modules:
  0.0 62.5 jit_solution(9364030823855396792)
XLA Ops:
  1.1 2.6 %collective-permute-start.4 = (bf16[256,1536]{1,0:T(8,128)(2,1)}, bf16[256,1536]{1,0:T(8,128)(2,1)S(1)}, u32[]{:S(2)}, u32[]{:S(2)}) collective-permute-start(bf16[256,1536]{1,0:T(8,128)(2,1)} %og.1), channel_id=1, source_target_pairs={{0,2},{1,3},{2,0},{3,1},{4,6},{5,7},{6,4},{7,5},{8,10},{9,11},{10,... | collective-permute-start | bytes 2359304 | tf_op jit(solution)/shard_map/ppermute | solution.py:445
  3.7 2.4 %pack.1 = (bf16[3,256,384]{2,1,0:T(8,128)(2,1)}, bf16[2,256,384]{2,1,0:T(8,128)(2,1)}, bf16[256,384]{1,0:T(8,128)(2,1)}) custom-call(bf16[256,768]{1,0:T(8,128)(2,1)} %q.1, bf16[256,768]{1,0:T(8,128)(2,1)} %k.1, bf16[256,768]{1,0:T(8,128)(2,1)} %v.1), custom_call_target="tpu_custom_call" | custom-call | flops 1 | bytes 1 | tf_op jit(solution)/shard_map/pack/pallas_call | solution.py:60
  6.1 1.6 %collective-permute-start = (bf16[2,256,384]{2,1,0:T(8,128)(2,1)}, bf16[2,256,384]{2,1,0:T(8,128)(2,1)S(1)}, u32[]{:S(2)}, u32[]{:S(2)}) collective-permute-start(bf16[2,256,384]{2,1,0:T(8,128)(2,1)} %get-tuple-element.26), channel_id=1, source_target_pairs={{0,4},{4,0},{8,12},{12,8},{16,20},{20,16},{24,28},{28,24},{1,5},{5... | collective-permute-start | bytes 1179656 | tf_op jit(solution)/shard_map/ppermute | solution.py:448
  7.7 0.5 collective-permute-start.1
  8.2 1.6 %collective-permute-start.6 = (bf16[3,256,384]{2,1,0:T(8,128)(2,1)}, bf16[3,256,384]{2,1,0:T(8,128)(2,1)S(1)}, u32[]{:S(2)}, u32[]{:S(2)}) collective-permute-start(bf16[3,256,384]{2,1,0:T(8,128)(2,1)} %get-tuple-element.27.refs_2_.refs_0_.keep.keys.kv), channel_id=1, source_target_pairs={{0,8},{1,9},{2,10},{3,11},{4,12},{5,13},{6,14},{7,15},{8,0},{9,1},... | collective-permute-start | bytes 1769480 | tf_op jit(solution)/shard_map/ppermute | solution.py:462
  9.8 1.1 %copy-done.1 = bf16[256,1536]{1,0:T(8,128)(2,1)S(1)} copy-done((bf16[256,1536]{1,0:T(8,128)(2,1)S(1)}, bf16[256,1536]{1,0:T(8,128)(2,1)}, u32[]{:S(2)}) %copy-start.1) | copy-done | bytes 786456
  10.9 3.8 %head_grad_first.1 = (f32[256,768]{1,0:T(8,128)S(1)}, bf16[768,1536]{1,0:T(8,128)(2,1)S(1)}, bf16[768,1536]{1,0:T(8,128)(2,1)S(1)}) custom-call(bf16[256,1536]{1,0:T(8,128)(2,1)S(1)} %copy-done.1, bf16[256,1536]{1,0:T(8,128)(2,1)S(1)} %collective-permute-done.5.near, bf16[768,6144]{1,0:T(8,128)(2,1)} %w.1), custom_call_target="tpu_custom_call" | custom-call | flops 1 | bytes 1 | tf_op jit(solution)/shard_map/head_grad_first/pallas_call | solution.py:110
  14.8 7.0 %collective-permute-done.1.refs_2_.refs_0_.xq = bf16[256,384]{1,0:T(8,128)(2,1)S(1)} collective-permute-done((bf16[256,384]{1,0:T(8,128)(2,1)}, bf16[256,384]{1,0:T(8,128)(2,1)S(1)}, u32[]{:S(2)}, u32[]{:S(2)}) %collective-permute-start.1) | collective-permute-done | bytes 196640 | tf_op jit(solution)/shard_map/ppermute | solution.py:448
  22.1 1.8 %collective-permute-start.2 = (bf16[2,256,384]{2,1,0:T(8,128)(2,1)S(1)}, bf16[2,256,384]{2,1,0:T(8,128)(2,1)S(1)}, u32[]{:S(2)}, u32[]{:S(2)}) collective-permute-start(bf16[2,256,384]{2,1,0:T(8,128)(2,1)S(1)} %collective-permute-done.refs_1_.refs_3_.keys.kv), channel_id=1, source_target_pairs={{0,8},{1,9},{2,10},{3,11},{4,12},{5,13},{6,14},{7,15},{8,0},{9,1},... | collective-permute-start | bytes 1179656 | tf_op jit(solution)/shard_map/ppermute | solution.py:462
  24.1 0.8 %head_grad.2.refs_0_ = f32[256,768]{1,0:T(8,128)S(1)} custom-call(f32[256,768]{1,0:T(8,128)S(1)} %after.5.acc, bf16[256,1536]{1,0:T(8,128)(2,1)S(1)} %collective-permute-done.4.piece, bf16[768,1536]{1,0:T(8,128)(2,1)S(1)} %get-tuple-element.33.w), custom_call_target="tpu_custom_call" | custom-call | flops 1 | bytes 1 | tf_op jit(solution)/shard_map/head_grad/pallas_call | solution.py:147
  25.0 0.9 %head_grad.3 = (bf16[256,384]{1,0:T(8,128)(2,1)S(1)}, bf16[256,384]{1,0:T(8,128)(2,1)S(1)}) custom-call(f32[256,768]{1,0:T(8,128)S(1)} %after.6.acc, bf16[256,1536]{1,0:T(8,128)(2,1)S(1)} %collective-permute-done.8.piece, bf16[768,1536]{1,0:T(8,128)(2,1)S(1)} %get-tuple-element.34.w), custom_call_target="tpu_custom_call" | custom-call | flops 1 | bytes 1 | tf_op jit(solution)/shard_map/head_grad/pallas_call | solution.py:147
  25.9 1.5 %collective-permute-start.9 = (bf16[256,384]{1,0:T(8,128)(2,1)S(1)}, bf16[256,384]{1,0:T(8,128)(2,1)S(1)}, u32[]{:S(2)}, u32[]{:S(2)}) collective-permute-start(bf16[256,384]{1,0:T(8,128)(2,1)S(1)} %get-tuple-element.36), channel_id=1, source_target_pairs={{0,4},{4,0},{8,12},{12,8},{16,20},{20,16},{24,28},{28,24},{1,5},{5... | collective-permute-start | bytes 589832 | tf_op jit(solution)/shard_map/ppermute | solution.py:448
  27.4 6.3 %collective-permute-done.2.refs_4_.refs_6_ = bf16[2,256,384]{2,1,0:T(8,128)(2,1)S(1)} collective-permute-done((bf16[2,256,384]{2,1,0:T(8,128)(2,1)S(1)}, bf16[2,256,384]{2,1,0:T(8,128)(2,1)S(1)}, u32[]{:S(2)}, u32[]{:S(2)}) %collective-permute-start.2) | collective-permute-done | bytes 393248 | tf_op jit(solution)/shard_map/ppermute | solution.py:462
  33.8 2.9 %collective-permute-start.10 = (bf16[3,256,384]{2,1,0:T(8,128)(2,1)S(1)}, bf16[3,256,384]{2,1,0:T(8,128)(2,1)S(1)}, u32[]{:S(2)}, u32[]{:S(2)}) collective-permute-start(bf16[3,256,384]{2,1,0:T(8,128)(2,1)S(1)} %join.1), channel_id=1, source_target_pairs={{0,8},{1,9},{2,10},{3,11},{4,12},{5,13},{6,14},{7,15},{8,0},{9,1},... | collective-permute-start | bytes 1769480 | tf_op jit(solution)/shard_map/ppermute | solution.py:462
  36.7 3.0 %query_pass.2 = (bf16[1,256,384]{2,1,0:T(8,128)(2,1)S(1)}, f32[8,256]{1,0:T(8,128)S(1)}) custom-call(bf16[256,384]{1,0:T(8,128)(2,1)S(1)} %collective-permute-done.1.refs_2_.refs_0_.xq, bf16[256,384]{1,0:T(8,128)(2,1)S(1)} %after.7.refs_1_.dxr.refs_2_, bf16[3,256,384]{2,1,0:T(8,128)(2,1)S(1)} %copy-done, ...), custom_call_target="tpu_custom_call" | custom-call | flops 1 | bytes 1 | tf_op jit(solution)/shard_map/query_pass/pallas_call | solution.py:256
  39.7 1.6 %collective-permute-start.12 = (bf16[1,256,384]{2,1,0:T(8,128)(2,1)S(1)}, bf16[1,256,384]{2,1,0:T(8,128)(2,1)S(1)}, u32[]{:S(2)}, u32[]{:S(2)}) collective-permute-start(bf16[1,256,384]{2,1,0:T(8,128)(2,1)S(1)} %get-tuple-element.42), channel_id=1, source_target_pairs={{0,4},{4,0},{8,12},{12,8},{16,20},{20,16},{24,28},{28,24},{1,5},{5... | collective-permute-start | bytes 589832 | tf_op jit(solution)/shard_map/ppermute | solution.py:448
  41.2 3.0 %query_pass.3 = (bf16[1,256,384]{2,1,0:T(8,128)(2,1)S(1)}, f32[8,512]{1,0:T(8,128)S(1)}) custom-call(bf16[3,256,384]{2,1,0:T(8,128)(2,1)S(1)} %copy-done, bf16[256,384]{1,0:T(8,128)(2,1)S(1)} %get-tuple-element.35.refs_1_.dkeep, bf16[3,256,384]{2,1,0:T(8,128)(2,1)S(1)} %copy-done, bf16[2,256,384]{2,1,0:T(8,128)(2,1)S(1)} %collective-permute-done.refs_1_.refs_3_.keys.kv, ...), custom_call_target="tpu_custom_call" | custom-call | flops 6000000000 | bytes 1 | tf_op jit(solution)/shard_map/query_pass/pallas_call | solution.py:256
  44.2 2.1 %collective-permute-start.13 = (f32[8,512]{1,0:T(8,128)S(1)}, f32[8,512]{1,0:T(8,128)S(1)}, u32[]{:S(2)}, u32[]{:S(2)}) collective-permute-start(f32[8,512]{1,0:T(8,128)S(1)} %get-tuple-element.40.stats), channel_id=1, source_target_pairs={{0,8},{1,9},{2,10},{3,11},{4,12},{5,13},{6,14},{7,15},{8,0},{9,1},... | collective-permute-start | bytes 49160 | tf_op jit(solution)/shard_map/ppermute | solution.py:462
  46.3 1.2 %own_pass.2.refs_0_ = f32[2,256,384]{2,1,0:T(8,128)S(1)} custom-call(bf16[2,256,384]{2,1,0:T(8,128)(2,1)S(1)} %collective-permute-done.refs_1_.refs_3_.keys.kv, bf16[3,256,384]{2,1,0:T(8,128)(2,1)S(1)} %copy-done, bf16[256,384]{1,0:T(8,128)(2,1)S(1)} %collective-permute-done.1.refs_2_.refs_0_.xq, bf16[256,384]{1,0:T(8,128)(2,1)S(1)} %get-tuple-element.35.refs_1_.dkeep, ...), custom_call_target="tpu_custom_call" | custom-call | flops 1 | bytes 1 | tf_op jit(solution)/shard_map/own_pass/pallas_call | solution.py:306
  47.5 0.8 %unpack.2 = bf16[256,768]{1,0:T(8,128)(2,1)} custom-call(bf16[1,256,384]{2,1,0:T(8,128)(2,1)S(1)} %get-tuple-element.41.kept, bf16[1,256,384]{2,1,0:T(8,128)(2,1)S(1)} %after.9.refs_0_), custom_call_target="tpu_custom_call" | custom-call | flops 1 | bytes 1 | tf_op jit(solution)/shard_map/unpack/pallas_call | solution.py:396
  48.3 1.8 %collective-permute-done.10.refs_1_.late_e = bf16[3,256,384]{2,1,0:T(8,128)(2,1)S(1)} collective-permute-done((bf16[3,256,384]{2,1,0:T(8,128)(2,1)S(1)}, bf16[3,256,384]{2,1,0:T(8,128)(2,1)S(1)}, u32[]{:S(2)}, u32[]{:S(2)}) %collective-permute-start.10) | collective-permute-done | bytes 589856 | tf_op jit(solution)/shard_map/ppermute | solution.py:462
  50.3 0.8 %key_pass.6 = bf16[2,256,128]{2,1,0:T(8,128)(2,1)S(1)} custom-call(bf16[2,256,384]{2,1,0:T(8,128)(2,1)S(1)} %collective-permute-done.refs_1_.refs_3_.keys.kv, bf16[3,256,384]{2,1,0:T(8,128)(2,1)S(1)} %collective-permute-done.6.refs_1_.refs_6_.refs_4_.e0, bf16[3,256,384]{2,1,0:T(8,128)(2,1)S(1)} %collective-permute-done.7.refs_2_.refs_7_.refs_5_.o0, ...), custom_call_target="tpu_custom_call" | custom-call | flops 1000000000 | bytes 1 | tf_op jit(solution)/shard_map/key_pass/pallas_call | solution.py:360
  51.0 1.6 %collective-permute-start.16 = (bf16[2,256,128]{2,1,0:T(8,128)(2,1)S(1)}, bf16[2,256,128]{2,1,0:T(8,128)(2,1)S(1)}, u32[]{:S(2)}, u32[]{:S(2)}) collective-permute-start(bf16[2,256,128]{2,1,0:T(8,128)(2,1)S(1)} %key_pass.6), channel_id=1, source_target_pairs={{0,4},{4,0},{8,12},{12,8},{16,20},{20,16},{24,28},{28,24},{1,5},{5... | collective-permute-start | bytes 393224 | tf_op jit(solution)/shard_map/ppermute | solution.py:448
  52.6 0.8 %key_pass.5 = bf16[2,256,128]{2,1,0:T(8,128)(2,1)S(1)} custom-call(bf16[2,256,384]{2,1,0:T(8,128)(2,1)S(1)} %collective-permute-done.refs_1_.refs_3_.keys.kv, bf16[3,256,384]{2,1,0:T(8,128)(2,1)S(1)} %collective-permute-done.6.refs_1_.refs_6_.refs_4_.e0, bf16[3,256,384]{2,1,0:T(8,128)(2,1)S(1)} %collective-permute-done.7.refs_2_.refs_7_.refs_5_.o0, ...), custom_call_target="tpu_custom_call" | custom-call | flops 1000000000 | bytes 1 | tf_op jit(solution)/shard_map/key_pass/pallas_call | solution.py:360
  53.3 0.6 collective-permute-start.15
  53.9 0.9 %key_pass.7 = bf16[2,256,128]{2,1,0:T(8,128)(2,1)S(1)} custom-call(bf16[2,256,384]{2,1,0:T(8,128)(2,1)S(1)} %collective-permute-done.refs_1_.refs_3_.keys.kv, bf16[3,256,384]{2,1,0:T(8,128)(2,1)S(1)} %collective-permute-done.6.refs_1_.refs_6_.refs_4_.e0, bf16[3,256,384]{2,1,0:T(8,128)(2,1)S(1)} %collective-permute-done.7.refs_2_.refs_7_.refs_5_.o0, ...), custom_call_target="tpu_custom_call" | custom-call | flops 1000000000 | bytes 1 | tf_op jit(solution)/shard_map/key_pass/pallas_call | solution.py:360
  54.9 1.6 %collective-permute-start.17 = (bf16[2,256,128]{2,1,0:T(8,128)(2,1)S(1)}, bf16[2,256,128]{2,1,0:T(8,128)(2,1)S(1)}, u32[]{:S(2)}, u32[]{:S(2)}) collective-permute-start(bf16[2,256,128]{2,1,0:T(8,128)(2,1)S(1)} %key_pass.7), channel_id=1, source_target_pairs={{0,4},{4,0},{8,12},{12,8},{16,20},{20,16},{24,28},{28,24},{1,5},{5... | collective-permute-start | bytes 393224 | tf_op jit(solution)/shard_map/ppermute | solution.py:448
  56.5 1.2 %own_pass.3.sums = f32[2,256,384]{2,1,0:T(8,128)S(1)} custom-call(bf16[3,256,384]{2,1,0:T(8,128)(2,1)S(1)} %copy-done, bf16[3,256,384]{2,1,0:T(8,128)(2,1)S(1)} %copy-done, bf16[256,384]{1,0:T(8,128)(2,1)S(1)} %collective-permute-done.1.refs_2_.refs_0_.xq, bf16[256,384]{1,0:T(8,128)(2,1)S(1)} %get-tuple-element.35.refs_1_.dkeep, ...), custom_call_target="tpu_custom_call" | custom-call | flops 1 | bytes 1 | tf_op jit(solution)/shard_map/own_pass/pallas_call | solution.py:306
  57.7 1.9 %key_pass.4.kept = bf16[2,256,384]{2,1,0:T(8,128)(2,1)S(1)} custom-call(bf16[3,256,384]{2,1,0:T(8,128)(2,1)S(1)} %copy-done, bf16[3,256,384]{2,1,0:T(8,128)(2,1)S(1)} %collective-permute-done.6.refs_1_.refs_6_.refs_4_.e0, bf16[3,256,384]{2,1,0:T(8,128)(2,1)S(1)} %collective-permute-done.7.refs_2_.refs_7_.refs_5_.o0, ...), custom_call_target="tpu_custom_call" | custom-call | flops 1000000000 | bytes 1 | tf_op jit(solution)/shard_map/key_pass/pallas_call | solution.py:360
  60.0 0.9 %unpack.3 = (bf16[256,768]{1,0:T(8,128)(2,1)}, bf16[256,768]{1,0:T(8,128)(2,1)}) custom-call(bf16[2,256,384]{2,1,0:T(8,128)(2,1)S(1)} %key_pass.4.kept, bf16[2,256,128]{2,1,0:T(8,128)(2,1)S(1)} %collective-permute-done.15.refs_0_, bf16[2,256,128]{2,1,0:T(8,128)(2,1)S(1)} %collective-permute-done.16.refs_1_), custom_call_target="tpu_custom_call" | custom-call | flops 1 | bytes 1 | tf_op jit(solution)/shard_map/unpack/pallas_call | solution.py:396
  60.9 0.8 %collective-permute-done.17.last = bf16[2,256,128]{2,1,0:T(8,128)(2,1)S(1)} collective-permute-done((bf16[2,256,128]{2,1,0:T(8,128)(2,1)S(1)}, bf16[2,256,128]{2,1,0:T(8,128)(2,1)S(1)}, u32[]{:S(2)}, u32[]{:S(2)}) %collective-permute-start.17) | collective-permute-done | bytes 131104 | tf_op jit(solution)/shard_map/ppermute | solution.py:448
  61.7 0.7 %finish.1 = (bf16[256,768]{1,0:T(8,128)(2,1)}, bf16[256,768]{1,0:T(8,128)(2,1)}) custom-call(bf16[256,768]{1,0:T(8,128)(2,1)} %get-tuple-element.45.dk_in, bf16[256,768]{1,0:T(8,128)(2,1)} %get-tuple-element.46.dv_in, bf16[2,256,128]{2,1,0:T(8,128)(2,1)S(1)} %collective-permute-done.17.last), custom_call_target="tpu_custom_call", output_to_operand_aliasing={{0}: (0, {}), {1}: (1, {})} | custom-call | flops 1 | bytes 1 | tf_op jit(solution)/shard_map/finish/pallas_call | solution.py:425
  (29 shorter events, 1.7 us)
Async XLA Ops:
  0.6 9.2 %collective-permute-start.5 = (bf16[256,1536]{1,0:T(8,128)(2,1)}, bf16[256,1536]{1,0:T(8,128)(2,1)S(1)}, u32[]{:S(2)}, u32[]{:S(2)}) collective-permute-start(bf16[256,1536]{1,0:T(8,128)(2,1)} %og.1), channel_id=1, source_target_pairs={{0,1},{1,0},{2,3},{3,2},{4,5},{5,4},{6,7},{7,6},{8,9},{9,8},{10,11... | collective-permute-start | bytes 2359304 | tf_op jit(solution)/shard_map/ppermute | solution.py:445
  1.1 20.9 %collective-permute-start.4 = (bf16[256,1536]{1,0:T(8,128)(2,1)}, bf16[256,1536]{1,0:T(8,128)(2,1)S(1)}, u32[]{:S(2)}, u32[]{:S(2)}) collective-permute-start(bf16[256,1536]{1,0:T(8,128)(2,1)} %og.1), channel_id=1, source_target_pairs={{0,2},{1,3},{2,0},{3,1},{4,6},{5,7},{6,4},{7,5},{8,10},{9,11},{10,... | collective-permute-start | bytes 2359304 | tf_op jit(solution)/shard_map/ppermute | solution.py:445
  6.1 15.7 %collective-permute-start = (bf16[2,256,384]{2,1,0:T(8,128)(2,1)}, bf16[2,256,384]{2,1,0:T(8,128)(2,1)S(1)}, u32[]{:S(2)}, u32[]{:S(2)}) collective-permute-start(bf16[2,256,384]{2,1,0:T(8,128)(2,1)} %get-tuple-element.26), channel_id=1, source_target_pairs={{0,4},{4,0},{8,12},{12,8},{16,20},{20,16},{24,28},{28,24},{1,5},{5... | collective-permute-start | bytes 1179656 | tf_op jit(solution)/shard_map/ppermute | solution.py:448
  7.7 14.1 %collective-permute-start.1 = (bf16[256,384]{1,0:T(8,128)(2,1)}, bf16[256,384]{1,0:T(8,128)(2,1)S(1)}, u32[]{:S(2)}, u32[]{:S(2)}) collective-permute-start(bf16[256,384]{1,0:T(8,128)(2,1)} %get-tuple-element.28), channel_id=1, source_target_pairs={{0,4},{4,0},{8,12},{12,8},{16,20},{20,16},{24,28},{28,24},{1,5},{5... | collective-permute-start | bytes 589832 | tf_op jit(solution)/shard_map/ppermute | solution.py:448
  8.2 16.7 %collective-permute-start.6 = (bf16[3,256,384]{2,1,0:T(8,128)(2,1)}, bf16[3,256,384]{2,1,0:T(8,128)(2,1)S(1)}, u32[]{:S(2)}, u32[]{:S(2)}) collective-permute-start(bf16[3,256,384]{2,1,0:T(8,128)(2,1)} %get-tuple-element.27.refs_2_.refs_0_.keep.keys.kv), channel_id=1, source_target_pairs={{0,8},{1,9},{2,10},{3,11},{4,12},{5,13},{6,14},{7,15},{8,0},{9,1},... | collective-permute-start | bytes 1769480 | tf_op jit(solution)/shard_map/ppermute | solution.py:462
  9.8 15.1 %collective-permute-start.7 = (bf16[3,256,384]{2,1,0:T(8,128)(2,1)}, bf16[3,256,384]{2,1,0:T(8,128)(2,1)S(1)}, u32[]{:S(2)}, u32[]{:S(2)}) collective-permute-start(bf16[3,256,384]{2,1,0:T(8,128)(2,1)} %get-tuple-element.27.refs_2_.refs_0_.keep.keys.kv), channel_id=1, source_target_pairs={{0,1},{1,0},{2,3},{3,2},{4,5},{5,4},{6,7},{7,6},{8,16},{9,17},{10,... | collective-permute-start | bytes 1769480 | tf_op jit(solution)/shard_map/ppermute | solution.py:462
  9.8 1.1 %copy-start.1 = (bf16[256,1536]{1,0:T(8,128)(2,1)S(1)}, bf16[256,1536]{1,0:T(8,128)(2,1)}, u32[]{:S(2)}) copy-start(bf16[256,1536]{1,0:T(8,128)(2,1)} %og.1) | copy-start | bytes 2359300
  22.1 2.9 %collective-permute-start.8 = (bf16[256,1536]{1,0:T(8,128)(2,1)S(1)}, bf16[256,1536]{1,0:T(8,128)(2,1)S(1)}, u32[]{:S(2)}, u32[]{:S(2)}) collective-permute-start(bf16[256,1536]{1,0:T(8,128)(2,1)S(1)} %collective-permute-done.4.piece), channel_id=1, source_target_pairs={{0,1},{1,0},{2,3},{3,2},{4,5},{5,4},{6,7},{7,6},{8,9},{9,8},{10,11... | collective-permute-start | bytes 2359304 | tf_op jit(solution)/shard_map/ppermute | solution.py:445
  22.1 11.6 %collective-permute-start.2 = (bf16[2,256,384]{2,1,0:T(8,128)(2,1)S(1)}, bf16[2,256,384]{2,1,0:T(8,128)(2,1)S(1)}, u32[]{:S(2)}, u32[]{:S(2)}) collective-permute-start(bf16[2,256,384]{2,1,0:T(8,128)(2,1)S(1)} %collective-permute-done.refs_1_.refs_3_.keys.kv), channel_id=1, source_target_pairs={{0,8},{1,9},{2,10},{3,11},{4,12},{5,13},{6,14},{7,15},{8,0},{9,1},... | collective-permute-start | bytes 1179656 | tf_op jit(solution)/shard_map/ppermute | solution.py:462
  23.9 9.8 %collective-permute-start.3 = (bf16[2,256,384]{2,1,0:T(8,128)(2,1)S(1)}, bf16[2,256,384]{2,1,0:T(8,128)(2,1)S(1)}, u32[]{:S(2)}, u32[]{:S(2)}) collective-permute-start(bf16[2,256,384]{2,1,0:T(8,128)(2,1)S(1)} %collective-permute-done.refs_1_.refs_3_.keys.kv), channel_id=1, source_target_pairs={{0,1},{1,0},{2,3},{3,2},{4,5},{5,4},{6,7},{7,6},{8,16},{9,17},{10,... | collective-permute-start | bytes 1179656 | tf_op jit(solution)/shard_map/ppermute | solution.py:462
  25.8 10.9 %copy-start = (bf16[3,256,384]{2,1,0:T(8,128)(2,1)S(1)}, bf16[3,256,384]{2,1,0:T(8,128)(2,1)}, u32[]{:S(2)}) copy-start(bf16[3,256,384]{2,1,0:T(8,128)(2,1)} %get-tuple-element.27.refs_2_.refs_0_.keep.keys.kv) | copy-start | bytes 1769476
  25.9 7.8 %collective-permute-start.9 = (bf16[256,384]{1,0:T(8,128)(2,1)S(1)}, bf16[256,384]{1,0:T(8,128)(2,1)S(1)}, u32[]{:S(2)}, u32[]{:S(2)}) collective-permute-start(bf16[256,384]{1,0:T(8,128)(2,1)S(1)} %get-tuple-element.36), channel_id=1, source_target_pairs={{0,4},{4,0},{8,12},{12,8},{16,20},{20,16},{24,28},{28,24},{1,5},{5... | collective-permute-start | bytes 589832 | tf_op jit(solution)/shard_map/ppermute | solution.py:448
  33.8 16.3 %collective-permute-start.10 = (bf16[3,256,384]{2,1,0:T(8,128)(2,1)S(1)}, bf16[3,256,384]{2,1,0:T(8,128)(2,1)S(1)}, u32[]{:S(2)}, u32[]{:S(2)}) collective-permute-start(bf16[3,256,384]{2,1,0:T(8,128)(2,1)S(1)} %join.1), channel_id=1, source_target_pairs={{0,8},{1,9},{2,10},{3,11},{4,12},{5,13},{6,14},{7,15},{8,0},{9,1},... | collective-permute-start | bytes 1769480 | tf_op jit(solution)/shard_map/ppermute | solution.py:462
  36.7 13.4 %collective-permute-start.11 = (bf16[3,256,384]{2,1,0:T(8,128)(2,1)S(1)}, bf16[3,256,384]{2,1,0:T(8,128)(2,1)S(1)}, u32[]{:S(2)}, u32[]{:S(2)}) collective-permute-start(bf16[3,256,384]{2,1,0:T(8,128)(2,1)S(1)} %join.1), channel_id=1, source_target_pairs={{0,1},{1,0},{2,3},{3,2},{4,5},{5,4},{6,7},{7,6},{8,16},{9,17},{10,... | collective-permute-start | bytes 1769480 | tf_op jit(solution)/shard_map/ppermute | solution.py:462
  39.7 7.9 %collective-permute-start.12 = (bf16[1,256,384]{2,1,0:T(8,128)(2,1)S(1)}, bf16[1,256,384]{2,1,0:T(8,128)(2,1)S(1)}, u32[]{:S(2)}, u32[]{:S(2)}) collective-permute-start(bf16[1,256,384]{2,1,0:T(8,128)(2,1)S(1)} %get-tuple-element.42), channel_id=1, source_target_pairs={{0,4},{4,0},{8,12},{12,8},{16,20},{20,16},{24,28},{28,24},{1,5},{5... | collective-permute-start | bytes 589832 | tf_op jit(solution)/shard_map/ppermute | solution.py:448
  44.2 6.0 %collective-permute-start.13 = (f32[8,512]{1,0:T(8,128)S(1)}, f32[8,512]{1,0:T(8,128)S(1)}, u32[]{:S(2)}, u32[]{:S(2)}) collective-permute-start(f32[8,512]{1,0:T(8,128)S(1)} %get-tuple-element.40.stats), channel_id=1, source_target_pairs={{0,8},{1,9},{2,10},{3,11},{4,12},{5,13},{6,14},{7,15},{8,0},{9,1},... | collective-permute-start | bytes 49160 | tf_op jit(solution)/shard_map/ppermute | solution.py:462
  46.3 4.0 %collective-permute-start.14 = (f32[8,512]{1,0:T(8,128)S(1)}, f32[8,512]{1,0:T(8,128)S(1)}, u32[]{:S(2)}, u32[]{:S(2)}) collective-permute-start(f32[8,512]{1,0:T(8,128)S(1)} %get-tuple-element.40.stats), channel_id=1, source_target_pairs={{0,1},{1,0},{2,3},{3,2},{4,5},{5,4},{6,7},{7,6},{8,16},{9,17},{10,... | collective-permute-start | bytes 49160 | tf_op jit(solution)/shard_map/ppermute | solution.py:462
  51.0 8.6 %collective-permute-start.16 = (bf16[2,256,128]{2,1,0:T(8,128)(2,1)S(1)}, bf16[2,256,128]{2,1,0:T(8,128)(2,1)S(1)}, u32[]{:S(2)}, u32[]{:S(2)}) collective-permute-start(bf16[2,256,128]{2,1,0:T(8,128)(2,1)S(1)} %key_pass.6), channel_id=1, source_target_pairs={{0,4},{4,0},{8,12},{12,8},{16,20},{20,16},{24,28},{28,24},{1,5},{5... | collective-permute-start | bytes 393224 | tf_op jit(solution)/shard_map/ppermute | solution.py:448
  53.3 6.7 %collective-permute-start.15 = (bf16[2,256,128]{2,1,0:T(8,128)(2,1)S(1)}, bf16[2,256,128]{2,1,0:T(8,128)(2,1)S(1)}, u32[]{:S(2)}, u32[]{:S(2)}) collective-permute-start(bf16[2,256,128]{2,1,0:T(8,128)(2,1)S(1)} %key_pass.5), channel_id=1, source_target_pairs={{0,4},{4,0},{8,12},{12,8},{16,20},{20,16},{24,28},{28,24},{1,5},{5... | collective-permute-start | bytes 393224 | tf_op jit(solution)/shard_map/ppermute | solution.py:448
  54.9 6.8 %collective-permute-start.17 = (bf16[2,256,128]{2,1,0:T(8,128)(2,1)S(1)}, bf16[2,256,128]{2,1,0:T(8,128)(2,1)S(1)}, u32[]{:S(2)}, u32[]{:S(2)}) collective-permute-start(bf16[2,256,128]{2,1,0:T(8,128)(2,1)S(1)} %key_pass.7), channel_id=1, source_target_pairs={{0,4},{4,0},{8,12},{12,8},{16,20},{20,16},{24,28},{28,24},{1,5},{5... | collective-permute-start | bytes 393224 | tf_op jit(solution)/shard_map/ppermute | solution.py:448

commit v15 on v14

--- a/solution.py
+++ b/solution.py
@@ -314,12 +314,12 @@
     )(*operands)
 
 
-def key_kernel(scale, own, heads, kv, e0, o0, late_e, late_o, se, so, sums, out, fifth_q, fifth_d):
+def key_kernel(scale, own, heads, kv, e0, o0, qe, qo, late_e, late_o, se, so, sums, out, fifth_q, fifth_d):
     rows = kv.shape[1]
     even_ok, odd_ok, turned = place()
     from_even = turned if own else jnp.logical_not(turned)
-    even_q, odd_q = (e0.at[2], late_e.at[0]), (o0.at[2], late_o.at[0])
-    even_d, odd_d = (late_e.at[1], late_e.at[2]), (late_o.at[1], late_o.at[2])
+    even_q, odd_q = (e0.at[2], qe), (o0.at[2], qo)
+    even_d, odd_d = (late_e.at[0], late_e.at[1]), (late_o.at[0], late_o.at[1])
     same, other = (0, 1) if own else (1, 0)
     wanted = slice(heads[0] * HD, (heads[-1] + 1) * HD)
 
@@ -476,18 +476,21 @@
     dkeep, dsend = grad_piece(acc, far, wf, True)
     dxr = after(over_x(dsend), flops=6e9)
 
-    xq, e1, o1 = lax.optimization_barrier((xq, e1, o1))
-    late = join(xq, dkeep, dxr)
+    late_q, dxr = lax.optimization_barrier((xq, dxr))
+    qe, qo = over_z(late_q, 0), over_z(late_q, 1)
+    own_d, e1, o1 = lax.optimization_barrier((dkeep, e1, o1))
+    late = join(own_d, dxr)
     late_e, late_o = over_z(late, 0), over_z(late, 1)
     dq_send, marks = query_pass(False, xq, dxr, keep, xkv, e1, o1, e0, o0)
     dq_keep, stats = query_pass(True, keep, dkeep, keep, xkv, e0, o0, e1, o1, marks)
     dq_got = after(over_x(dq_send), flops=6e9)
+    stats, qe, qo = lax.optimization_barrier((stats, qe, qo))
     se, so = over_z(stats, 0), over_z(stats, 1)
     sums = own_pass(xkv, keep, xq, dkeep, dxr, stats)
     sums = after(sums, late_e, late_o, flops=3e9)
     own_sums = own_pass(keep, keep, xq, dkeep, dxr, stats)
     heads = dkeep.shape[1] // HD
-    theirs = (e0, o0, late_e, late_o, se, so)
+    theirs = (e0, o0, qe, qo, late_e, late_o, se, so)
     got = []
     for head in range(heads):
         if head == 1:

time: 62.7 us -> 63.8 us (1.018)
  starting transfers between devices: 20.7 us -> 22.4 us
    ppermute x8 -> x10, waiting for transfers between devices: 8.23 us -> 6.32 us  [over_z(): return lax.ppermute(array, ('ctx', 'mp'), pairs)]
    ppermute x8 -> x10, starting transfers between devices: 8.64 us -> 10.4 us  [over_z(): return lax.ppermute(array, ('ctx', 'mp'), pairs)]
    ppermute x7, waiting for transfers between devices: 8.2 us -> 9.46 us  [over_x(): return lax.ppermute(array, 'ctx', [(i, i ^ 1) for i in range(length)])]
  transfers between devices with their start and end apart: 18 -> 20, of which waited for: 7 -> 6; matrix products, arithmetic and copies ran while one was open for 0% -> 0% of each run, Pallas kernels for 34% -> 34%
where the time goes in v15:
time: 63.8 us; the launch traced here: 63.6 us
  Pallas kernels  23 us (36%)
  starting transfers between devices  22.4 us (35%)
  waiting for transfers between devices  16.1 us (25%)
  local copies, waits for them, and re-layouts  1.14 us (2%)
  between operations  1.01 us (2%)
    ppermute x10, starting transfers between devices, over_z(): return lax.ppermute(array, ('ctx', 'mp'), pairs)  10.4 us
    ppermute x7, waiting for transfers between devices, over_x(): return lax.ppermute(array, 'ctx', [(i, i ^ 1) for i in range(length)])  9.46 us
    ppermute x7, starting transfers between devices, over_x(): return lax.ppermute(array, 'ctx', [(i, i ^ 1) for i in range(length)])  8.91 us
    ppermute x10, waiting for transfers between devices, over_z(): return lax.ppermute(array, ('ctx', 'mp'), pairs)  6.32 us
    pallas_call x2, Pallas kernels, query_pass(): pl.pallas_call(functools.partial(query_kernel, HD ** (-0.5), own, before...  5.94 us
    pallas_call x4, Pallas kernels, key_pass(): pl.pallas_call(functools.partial(key_kernel, HD ** (-0.5), own, heads), o...  4.43 us
    pallas_call x1, Pallas kernels, first_piece(): pl.pallas_call(first_kernel, out_shape=(jax.ShapeDtypeStruct((rows, heads...  3.82 us
    ppermute x3, starting transfers between devices, over_mp(): return lax.ppermute(array, 'mp', [(i, i ^ flip) for i in range(lanes)])  3.12 us
  transfers between devices with their start and end apart: 20, of which 6 were waited for; matrix products, arithmetic and copies ran while one was open for 0% of the time, Pallas kernels for 34%

profile of v15, /device:TPU:0, one launch (start us, length us, event | category | flops | bytes accessed | tf_op | source)
XLA Modules:
  0.0 63.6 jit_solution(4121839899985581067)
XLA Ops:
  1.1 2.6 %collective-permute-start.2 = (bf16[256,1536]{1,0:T(8,128)(2,1)}, bf16[256,1536]{1,0:T(8,128)(2,1)S(1)}, u32[]{:S(2)}, u32[]{:S(2)}) collective-permute-start(bf16[256,1536]{1,0:T(8,128)(2,1)} %og.1), channel_id=1, source_target_pairs={{0,2},{1,3},{2,0},{3,1},{4,6},{5,7},{6,4},{7,5},{8,10},{9,11},{10,... | collective-permute-start | bytes 2359304 | tf_op jit(solution)/shard_map/ppermute | solution.py:445
  3.7 2.4 %pack.1 = (bf16[3,256,384]{2,1,0:T(8,128)(2,1)}, bf16[2,256,384]{2,1,0:T(8,128)(2,1)}, bf16[256,384]{1,0:T(8,128)(2,1)}) custom-call(bf16[256,768]{1,0:T(8,128)(2,1)} %q.1, bf16[256,768]{1,0:T(8,128)(2,1)} %k.1, bf16[256,768]{1,0:T(8,128)(2,1)} %v.1), custom_call_target="tpu_custom_call" | custom-call | flops 1 | bytes 1 | tf_op jit(solution)/shard_map/pack/pallas_call | solution.py:60
  6.1 1.6 %collective-permute-start = (bf16[2,256,384]{2,1,0:T(8,128)(2,1)}, bf16[2,256,384]{2,1,0:T(8,128)(2,1)S(1)}, u32[]{:S(2)}, u32[]{:S(2)}) collective-permute-start(bf16[2,256,384]{2,1,0:T(8,128)(2,1)} %get-tuple-element.31), channel_id=1, source_target_pairs={{0,4},{4,0},{8,12},{12,8},{16,20},{20,16},{24,28},{28,24},{1,5},{5... | collective-permute-start | bytes 1179656 | tf_op jit(solution)/shard_map/ppermute | solution.py:448
  8.2 1.6 %collective-permute-start.4 = (bf16[3,256,384]{2,1,0:T(8,128)(2,1)}, bf16[3,256,384]{2,1,0:T(8,128)(2,1)S(1)}, u32[]{:S(2)}, u32[]{:S(2)}) collective-permute-start(bf16[3,256,384]{2,1,0:T(8,128)(2,1)} %get-tuple-element.32.refs_2_.refs_0_.keep.keys.kv), channel_id=1, source_target_pairs={{0,8},{1,9},{2,10},{3,11},{4,12},{5,13},{6,14},{7,15},{8,0},{9,1},... | collective-permute-start | bytes 1769480 | tf_op jit(solution)/shard_map/ppermute | solution.py:462
  9.8 1.1 %copy-done.1 = bf16[256,1536]{1,0:T(8,128)(2,1)S(1)} copy-done((bf16[256,1536]{1,0:T(8,128)(2,1)S(1)}, bf16[256,1536]{1,0:T(8,128)(2,1)}, u32[]{:S(2)}) %copy-start.1) | copy-done | bytes 786456
  10.9 3.8 %head_grad_first.1 = (f32[256,768]{1,0:T(8,128)S(1)}, bf16[768,1536]{1,0:T(8,128)(2,1)S(1)}, bf16[768,1536]{1,0:T(8,128)(2,1)S(1)}) custom-call(bf16[256,1536]{1,0:T(8,128)(2,1)S(1)} %copy-done.1, bf16[256,1536]{1,0:T(8,128)(2,1)S(1)} %collective-permute-done.3.near, bf16[768,6144]{1,0:T(8,128)(2,1)} %w.1), custom_call_target="tpu_custom_call" | custom-call | flops 1 | bytes 1 | tf_op jit(solution)/shard_map/head_grad_first/pallas_call | solution.py:110
  14.8 7.0 %collective-permute-done.1.refs_2_.refs_0_.xq = bf16[256,384]{1,0:T(8,128)(2,1)S(1)} collective-permute-done((bf16[256,384]{1,0:T(8,128)(2,1)}, bf16[256,384]{1,0:T(8,128)(2,1)S(1)}, u32[]{:S(2)}, u32[]{:S(2)}) %collective-permute-start.1) | collective-permute-done | bytes 196640 | tf_op jit(solution)/shard_map/ppermute | solution.py:448
  22.1 1.8 %collective-permute-start.8 = (bf16[2,256,384]{2,1,0:T(8,128)(2,1)S(1)}, bf16[2,256,384]{2,1,0:T(8,128)(2,1)S(1)}, u32[]{:S(2)}, u32[]{:S(2)}) collective-permute-start(bf16[2,256,384]{2,1,0:T(8,128)(2,1)S(1)} %collective-permute-done.refs_1_.refs_3_.keys.kv), channel_id=1, source_target_pairs={{0,8},{1,9},{2,10},{3,11},{4,12},{5,13},{6,14},{7,15},{8,0},{9,1},... | collective-permute-start | bytes 1179656 | tf_op jit(solution)/shard_map/ppermute | solution.py:462
  24.1 0.8 %head_grad.2.refs_0_ = f32[256,768]{1,0:T(8,128)S(1)} custom-call(f32[256,768]{1,0:T(8,128)S(1)} %after.5.acc, bf16[256,1536]{1,0:T(8,128)(2,1)S(1)} %collective-permute-done.2.piece, bf16[768,1536]{1,0:T(8,128)(2,1)S(1)} %get-tuple-element.37.w), custom_call_target="tpu_custom_call" | custom-call | flops 1 | bytes 1 | tf_op jit(solution)/shard_map/head_grad/pallas_call | solution.py:147
  25.0 0.9 %head_grad.3 = (bf16[256,384]{1,0:T(8,128)(2,1)S(1)}, bf16[256,384]{1,0:T(8,128)(2,1)S(1)}) custom-call(f32[256,768]{1,0:T(8,128)S(1)} %after.6.acc, bf16[256,1536]{1,0:T(8,128)(2,1)S(1)} %collective-permute-done.6.piece, bf16[768,1536]{1,0:T(8,128)(2,1)S(1)} %get-tuple-element.38.w), custom_call_target="tpu_custom_call" | custom-call | flops 1 | bytes 1 | tf_op jit(solution)/shard_map/head_grad/pallas_call | solution.py:147
  25.8 1.5 %collective-permute-start.7 = (bf16[256,384]{1,0:T(8,128)(2,1)S(1)}, bf16[256,384]{1,0:T(8,128)(2,1)S(1)}, u32[]{:S(2)}, u32[]{:S(2)}) collective-permute-start(bf16[256,384]{1,0:T(8,128)(2,1)S(1)} %get-tuple-element.40), channel_id=1, source_target_pairs={{0,4},{4,0},{8,12},{12,8},{16,20},{20,16},{24,28},{28,24},{1,5},{5... | collective-permute-start | bytes 589832 | tf_op jit(solution)/shard_map/ppermute | solution.py:448
  27.4 6.3 %collective-permute-done.8.refs_4_.refs_6_ = bf16[2,256,384]{2,1,0:T(8,128)(2,1)S(1)} collective-permute-done((bf16[2,256,384]{2,1,0:T(8,128)(2,1)S(1)}, bf16[2,256,384]{2,1,0:T(8,128)(2,1)S(1)}, u32[]{:S(2)}, u32[]{:S(2)}) %collective-permute-start.8) | collective-permute-done | bytes 393248 | tf_op jit(solution)/shard_map/ppermute | solution.py:462
  33.7 2.9 %collective-permute-start.10 = (bf16[256,384]{1,0:T(8,128)(2,1)S(1)}, bf16[256,384]{1,0:T(8,128)(2,1)S(1)}, u32[]{:S(2)}, u32[]{:S(2)}) collective-permute-start(bf16[256,384]{1,0:T(8,128)(2,1)S(1)} %collective-permute-done.1.refs_2_.refs_0_.xq), channel_id=1, source_target_pairs={{0,8},{1,9},{2,10},{3,11},{4,12},{5,13},{6,14},{7,15},{8,0},{9,1},... | collective-permute-start | bytes 589832 | tf_op jit(solution)/shard_map/ppermute | solution.py:462
  36.6 2.2 %collective-permute-start.12 = (bf16[2,256,384]{2,1,0:T(8,128)(2,1)S(1)}, bf16[2,256,384]{2,1,0:T(8,128)(2,1)S(1)}, u32[]{:S(2)}, u32[]{:S(2)}) collective-permute-start(bf16[2,256,384]{2,1,0:T(8,128)(2,1)S(1)} %join.1), channel_id=1, source_target_pairs={{0,8},{1,9},{2,10},{3,11},{4,12},{5,13},{6,14},{7,15},{8,0},{9,1},... | collective-permute-start | bytes 1179656 | tf_op jit(solution)/shard_map/ppermute | solution.py:462
  38.8 3.0 %query_pass.2 = (bf16[1,256,384]{2,1,0:T(8,128)(2,1)S(1)}, f32[8,256]{1,0:T(8,128)S(1)}) custom-call(bf16[256,384]{1,0:T(8,128)(2,1)S(1)} %collective-permute-done.1.refs_2_.refs_0_.xq, bf16[256,384]{1,0:T(8,128)(2,1)S(1)} %after.7.refs_1_.dxr, bf16[3,256,384]{2,1,0:T(8,128)(2,1)S(1)} %copy-done, ...), custom_call_target="tpu_custom_call" | custom-call | flops 1 | bytes 1 | tf_op jit(solution)/shard_map/query_pass/pallas_call | solution.py:256
  41.8 1.6 %collective-permute-start.14 = (bf16[1,256,384]{2,1,0:T(8,128)(2,1)S(1)}, bf16[1,256,384]{2,1,0:T(8,128)(2,1)S(1)}, u32[]{:S(2)}, u32[]{:S(2)}) collective-permute-start(bf16[1,256,384]{2,1,0:T(8,128)(2,1)S(1)} %get-tuple-element.50), channel_id=1, source_target_pairs={{0,4},{4,0},{8,12},{12,8},{16,20},{20,16},{24,28},{28,24},{1,5},{5... | collective-permute-start | bytes 589832 | tf_op jit(solution)/shard_map/ppermute | solution.py:448
  43.3 3.0 %query_pass.3 = (bf16[1,256,384]{2,1,0:T(8,128)(2,1)S(1)}, f32[8,512]{1,0:T(8,128)S(1)}) custom-call(bf16[3,256,384]{2,1,0:T(8,128)(2,1)S(1)} %copy-done, bf16[256,384]{1,0:T(8,128)(2,1)S(1)} %get-tuple-element.48.refs_1_.dkeep.refs_0_, bf16[3,256,384]{2,1,0:T(8,128)(2,1)S(1)} %copy-done, ...), custom_call_target="tpu_custom_call" | custom-call | flops 6000000000 | bytes 1 | tf_op jit(solution)/shard_map/query_pass/pallas_call | solution.py:256
  46.3 1.7 %collective-permute-start.15 = (f32[8,512]{1,0:T(8,128)S(1)}, f32[8,512]{1,0:T(8,128)S(1)}, u32[]{:S(2)}, u32[]{:S(2)}) collective-permute-start(f32[8,512]{1,0:T(8,128)S(1)} %get-tuple-element.47.stats), channel_id=1, source_target_pairs={{0,8},{1,9},{2,10},{3,11},{4,12},{5,13},{6,14},{7,15},{8,0},{9,1},... | collective-permute-start | bytes 49160 | tf_op jit(solution)/shard_map/ppermute | solution.py:462
  48.0 1.1 %collective-permute-done.14.refs_0_ = bf16[1,256,384]{2,1,0:T(8,128)(2,1)S(1)} collective-permute-done((bf16[1,256,384]{2,1,0:T(8,128)(2,1)S(1)}, bf16[1,256,384]{2,1,0:T(8,128)(2,1)S(1)}, u32[]{:S(2)}, u32[]{:S(2)}) %collective-permute-start.14) | collective-permute-done | bytes 196640 | tf_op jit(solution)/shard_map/ppermute | solution.py:448
  49.1 0.8 %unpack.2 = bf16[256,768]{1,0:T(8,128)(2,1)} custom-call(bf16[1,256,384]{2,1,0:T(8,128)(2,1)S(1)} %get-tuple-element.49.kept, bf16[1,256,384]{2,1,0:T(8,128)(2,1)S(1)} %after.9.refs_0_), custom_call_target="tpu_custom_call" | custom-call | flops 1 | bytes 1 | tf_op jit(solution)/shard_map/unpack/pallas_call | solution.py:396
  49.9 1.2 %own_pass.2.refs_0_ = f32[2,256,384]{2,1,0:T(8,128)S(1)} custom-call(bf16[2,256,384]{2,1,0:T(8,128)(2,1)S(1)} %collective-permute-done.refs_1_.refs_3_.keys.kv, bf16[3,256,384]{2,1,0:T(8,128)(2,1)S(1)} %copy-done, bf16[256,384]{1,0:T(8,128)(2,1)S(1)} %collective-permute-done.1.refs_2_.refs_0_.xq, ...), custom_call_target="tpu_custom_call" | custom-call | flops 1 | bytes 1 | tf_op jit(solution)/shard_map/own_pass/pallas_call | solution.py:306
  51.2 0.8 %key_pass.5 = bf16[2,256,128]{2,1,0:T(8,128)(2,1)S(1)} custom-call(bf16[2,256,384]{2,1,0:T(8,128)(2,1)S(1)} %collective-permute-done.refs_1_.refs_3_.keys.kv, bf16[3,256,384]{2,1,0:T(8,128)(2,1)S(1)} %collective-permute-done.4.refs_1_.refs_6_.refs_4_.e0, bf16[3,256,384]{2,1,0:T(8,128)(2,1)S(1)} %collective-permute-done.5.refs_2_.refs_7_.refs_5_.o0, ...), custom_call_target="tpu_custom_call" | custom-call | flops 1000000000 | bytes 1 | tf_op jit(solution)/shard_map/key_pass/pallas_call | solution.py:360
  52.0 1.6 %collective-permute-start.17 = (bf16[2,256,128]{2,1,0:T(8,128)(2,1)S(1)}, bf16[2,256,128]{2,1,0:T(8,128)(2,1)S(1)}, u32[]{:S(2)}, u32[]{:S(2)}) collective-permute-start(bf16[2,256,128]{2,1,0:T(8,128)(2,1)S(1)} %key_pass.5), channel_id=1, source_target_pairs={{0,4},{4,0},{8,12},{12,8},{16,20},{20,16},{24,28},{28,24},{1,5},{5... | collective-permute-start | bytes 393224 | tf_op jit(solution)/shard_map/ppermute | solution.py:448
  53.5 0.9 %key_pass.6 = bf16[2,256,128]{2,1,0:T(8,128)(2,1)S(1)} custom-call(bf16[2,256,384]{2,1,0:T(8,128)(2,1)S(1)} %collective-permute-done.refs_1_.refs_3_.keys.kv, bf16[3,256,384]{2,1,0:T(8,128)(2,1)S(1)} %collective-permute-done.4.refs_1_.refs_6_.refs_4_.e0, bf16[3,256,384]{2,1,0:T(8,128)(2,1)S(1)} %collective-permute-done.5.refs_2_.refs_7_.refs_5_.o0, ...), custom_call_target="tpu_custom_call" | custom-call | flops 1000000000 | bytes 1 | tf_op jit(solution)/shard_map/key_pass/pallas_call | solution.py:360
  54.5 0.6 collective-permute-start.18
  55.1 0.8 %key_pass.7 = bf16[2,256,128]{2,1,0:T(8,128)(2,1)S(1)} custom-call(bf16[2,256,384]{2,1,0:T(8,128)(2,1)S(1)} %collective-permute-done.refs_1_.refs_3_.keys.kv, bf16[3,256,384]{2,1,0:T(8,128)(2,1)S(1)} %collective-permute-done.4.refs_1_.refs_6_.refs_4_.e0, bf16[3,256,384]{2,1,0:T(8,128)(2,1)S(1)} %collective-permute-done.5.refs_2_.refs_7_.refs_5_.o0, ...), custom_call_target="tpu_custom_call" | custom-call | flops 1000000000 | bytes 1 | tf_op jit(solution)/shard_map/key_pass/pallas_call | solution.py:360
  55.9 1.5 %collective-permute-start.19 = (bf16[2,256,128]{2,1,0:T(8,128)(2,1)S(1)}, bf16[2,256,128]{2,1,0:T(8,128)(2,1)S(1)}, u32[]{:S(2)}, u32[]{:S(2)}) collective-permute-start(bf16[2,256,128]{2,1,0:T(8,128)(2,1)S(1)} %key_pass.7), channel_id=1, source_target_pairs={{0,4},{4,0},{8,12},{12,8},{16,20},{20,16},{24,28},{28,24},{1,5},{5... | collective-permute-start | bytes 393224 | tf_op jit(solution)/shard_map/ppermute | solution.py:448
  57.4 1.2 %own_pass.3.sums = f32[2,256,384]{2,1,0:T(8,128)S(1)} custom-call(bf16[3,256,384]{2,1,0:T(8,128)(2,1)S(1)} %copy-done, bf16[3,256,384]{2,1,0:T(8,128)(2,1)S(1)} %copy-done, bf16[256,384]{1,0:T(8,128)(2,1)S(1)} %collective-permute-done.1.refs_2_.refs_0_.xq, bf16[256,384]{1,0:T(8,128)(2,1)S(1)} %get-tuple-element.48.refs_1_.dkeep.refs_0_, ...), custom_call_target="tpu_custom_call" | custom-call | flops 1 | bytes 1 | tf_op jit(solution)/shard_map/own_pass/pallas_call | solution.py:306
  58.6 1.9 %key_pass.4.kept = bf16[2,256,384]{2,1,0:T(8,128)(2,1)S(1)} custom-call(bf16[3,256,384]{2,1,0:T(8,128)(2,1)S(1)} %copy-done, bf16[3,256,384]{2,1,0:T(8,128)(2,1)S(1)} %collective-permute-done.4.refs_1_.refs_6_.refs_4_.e0, bf16[3,256,384]{2,1,0:T(8,128)(2,1)S(1)} %collective-permute-done.5.refs_2_.refs_7_.refs_5_.o0, ...), custom_call_target="tpu_custom_call" | custom-call | flops 1000000000 | bytes 1 | tf_op jit(solution)/shard_map/key_pass/pallas_call | solution.py:360
  61.0 0.9 %unpack.3 = (bf16[256,768]{1,0:T(8,128)(2,1)}, bf16[256,768]{1,0:T(8,128)(2,1)}) custom-call(bf16[2,256,384]{2,1,0:T(8,128)(2,1)S(1)} %key_pass.4.kept, bf16[2,256,128]{2,1,0:T(8,128)(2,1)S(1)} %collective-permute-done.17.refs_0_, bf16[2,256,128]{2,1,0:T(8,128)(2,1)S(1)} %collective-permute-done.18.refs_1_), custom_call_target="tpu_custom_call" | custom-call | flops 1 | bytes 1 | tf_op jit(solution)/shard_map/unpack/pallas_call | solution.py:396
  61.9 0.9 %collective-permute-done.19.last = bf16[2,256,128]{2,1,0:T(8,128)(2,1)S(1)} collective-permute-done((bf16[2,256,128]{2,1,0:T(8,128)(2,1)S(1)}, bf16[2,256,128]{2,1,0:T(8,128)(2,1)S(1)}, u32[]{:S(2)}, u32[]{:S(2)}) %collective-permute-start.19) | collective-permute-done | bytes 131104 | tf_op jit(solution)/shard_map/ppermute | solution.py:448
  62.8 0.7 %finish.1 = (bf16[256,768]{1,0:T(8,128)(2,1)}, bf16[256,768]{1,0:T(8,128)(2,1)}) custom-call(bf16[256,768]{1,0:T(8,128)(2,1)} %get-tuple-element.55.dk_in, bf16[256,768]{1,0:T(8,128)(2,1)} %get-tuple-element.56.dv_in, bf16[2,256,128]{2,1,0:T(8,128)(2,1)S(1)} %collective-permute-done.19.last), custom_call_target="tpu_custom_call", output_to_operand_aliasing={{0}: (0, {}), {1}: (1, {})} | custom-call | flops 1 | bytes 1 | tf_op jit(solution)/shard_map/finish/pallas_call | solution.py:425
  (33 shorter events, 2.0 us)
Async XLA Ops:
  0.6 9.2 %collective-permute-start.3 = (bf16[256,1536]{1,0:T(8,128)(2,1)}, bf16[256,1536]{1,0:T(8,128)(2,1)S(1)}, u32[]{:S(2)}, u32[]{:S(2)}) collective-permute-start(bf16[256,1536]{1,0:T(8,128)(2,1)} %og.1), channel_id=1, source_target_pairs={{0,1},{1,0},{2,3},{3,2},{4,5},{5,4},{6,7},{7,6},{8,9},{9,8},{10,11... | collective-permute-start | bytes 2359304 | tf_op jit(solution)/shard_map/ppermute | solution.py:445
  1.1 20.9 %collective-permute-start.2 = (bf16[256,1536]{1,0:T(8,128)(2,1)}, bf16[256,1536]{1,0:T(8,128)(2,1)S(1)}, u32[]{:S(2)}, u32[]{:S(2)}) collective-permute-start(bf16[256,1536]{1,0:T(8,128)(2,1)} %og.1), channel_id=1, source_target_pairs={{0,2},{1,3},{2,0},{3,1},{4,6},{5,7},{6,4},{7,5},{8,10},{9,11},{10,... | collective-permute-start | bytes 2359304 | tf_op jit(solution)/shard_map/ppermute | solution.py:445
  6.1 15.7 %collective-permute-start = (bf16[2,256,384]{2,1,0:T(8,128)(2,1)}, bf16[2,256,384]{2,1,0:T(8,128)(2,1)S(1)}, u32[]{:S(2)}, u32[]{:S(2)}) collective-permute-start(bf16[2,256,384]{2,1,0:T(8,128)(2,1)} %get-tuple-element.31), channel_id=1, source_target_pairs={{0,4},{4,0},{8,12},{12,8},{16,20},{20,16},{24,28},{28,24},{1,5},{5... | collective-permute-start | bytes 1179656 | tf_op jit(solution)/shard_map/ppermute | solution.py:448
  7.7 14.1 %collective-permute-start.1 = (bf16[256,384]{1,0:T(8,128)(2,1)}, bf16[256,384]{1,0:T(8,128)(2,1)S(1)}, u32[]{:S(2)}, u32[]{:S(2)}) collective-permute-start(bf16[256,384]{1,0:T(8,128)(2,1)} %get-tuple-element.33), channel_id=1, source_target_pairs={{0,4},{4,0},{8,12},{12,8},{16,20},{20,16},{24,28},{28,24},{1,5},{5... | collective-permute-start | bytes 589832 | tf_op jit(solution)/shard_map/ppermute | solution.py:448
  8.2 16.7 %collective-permute-start.4 = (bf16[3,256,384]{2,1,0:T(8,128)(2,1)}, bf16[3,256,384]{2,1,0:T(8,128)(2,1)S(1)}, u32[]{:S(2)}, u32[]{:S(2)}) collective-permute-start(bf16[3,256,384]{2,1,0:T(8,128)(2,1)} %get-tuple-element.32.refs_2_.refs_0_.keep.keys.kv), channel_id=1, source_target_pairs={{0,8},{1,9},{2,10},{3,11},{4,12},{5,13},{6,14},{7,15},{8,0},{9,1},... | collective-permute-start | bytes 1769480 | tf_op jit(solution)/shard_map/ppermute | solution.py:462
  9.8 15.1 %collective-permute-start.5 = (bf16[3,256,384]{2,1,0:T(8,128)(2,1)}, bf16[3,256,384]{2,1,0:T(8,128)(2,1)S(1)}, u32[]{:S(2)}, u32[]{:S(2)}) collective-permute-start(bf16[3,256,384]{2,1,0:T(8,128)(2,1)} %get-tuple-element.32.refs_2_.refs_0_.keep.keys.kv), channel_id=1, source_target_pairs={{0,1},{1,0},{2,3},{3,2},{4,5},{5,4},{6,7},{7,6},{8,16},{9,17},{10,... | collective-permute-start | bytes 1769480 | tf_op jit(solution)/shard_map/ppermute | solution.py:462
  9.8 1.1 %copy-start.1 = (bf16[256,1536]{1,0:T(8,128)(2,1)S(1)}, bf16[256,1536]{1,0:T(8,128)(2,1)}, u32[]{:S(2)}) copy-start(bf16[256,1536]{1,0:T(8,128)(2,1)} %og.1) | copy-start | bytes 2359300
  22.1 2.9 %collective-permute-start.6 = (bf16[256,1536]{1,0:T(8,128)(2,1)S(1)}, bf16[256,1536]{1,0:T(8,128)(2,1)S(1)}, u32[]{:S(2)}, u32[]{:S(2)}) collective-permute-start(bf16[256,1536]{1,0:T(8,128)(2,1)S(1)} %collective-permute-done.2.piece), channel_id=1, source_target_pairs={{0,1},{1,0},{2,3},{3,2},{4,5},{5,4},{6,7},{7,6},{8,9},{9,8},{10,11... | collective-permute-start | bytes 2359304 | tf_op jit(solution)/shard_map/ppermute | solution.py:445
  22.1 11.6 %collective-permute-start.8 = (bf16[2,256,384]{2,1,0:T(8,128)(2,1)S(1)}, bf16[2,256,384]{2,1,0:T(8,128)(2,1)S(1)}, u32[]{:S(2)}, u32[]{:S(2)}) collective-permute-start(bf16[2,256,384]{2,1,0:T(8,128)(2,1)S(1)} %collective-permute-done.refs_1_.refs_3_.keys.kv), channel_id=1, source_target_pairs={{0,8},{1,9},{2,10},{3,11},{4,12},{5,13},{6,14},{7,15},{8,0},{9,1},... | collective-permute-start | bytes 1179656 | tf_op jit(solution)/shard_map/ppermute | solution.py:462
  23.9 9.8 %collective-permute-start.9 = (bf16[2,256,384]{2,1,0:T(8,128)(2,1)S(1)}, bf16[2,256,384]{2,1,0:T(8,128)(2,1)S(1)}, u32[]{:S(2)}, u32[]{:S(2)}) collective-permute-start(bf16[2,256,384]{2,1,0:T(8,128)(2,1)S(1)} %collective-permute-done.refs_1_.refs_3_.keys.kv), channel_id=1, source_target_pairs={{0,1},{1,0},{2,3},{3,2},{4,5},{5,4},{6,7},{7,6},{8,16},{9,17},{10,... | collective-permute-start | bytes 1179656 | tf_op jit(solution)/shard_map/ppermute | solution.py:462
  25.8 7.9 %collective-permute-start.7 = (bf16[256,384]{1,0:T(8,128)(2,1)S(1)}, bf16[256,384]{1,0:T(8,128)(2,1)S(1)}, u32[]{:S(2)}, u32[]{:S(2)}) collective-permute-start(bf16[256,384]{1,0:T(8,128)(2,1)S(1)} %get-tuple-element.40), channel_id=1, source_target_pairs={{0,4},{4,0},{8,12},{12,8},{16,20},{20,16},{24,28},{28,24},{1,5},{5... | collective-permute-start | bytes 589832 | tf_op jit(solution)/shard_map/ppermute | solution.py:448
  33.7 5.1 %copy-start = (bf16[3,256,384]{2,1,0:T(8,128)(2,1)S(1)}, bf16[3,256,384]{2,1,0:T(8,128)(2,1)}, u32[]{:S(2)}) copy-start(bf16[3,256,384]{2,1,0:T(8,128)(2,1)} %get-tuple-element.32.refs_2_.refs_0_.keep.keys.kv) | copy-start | bytes 1769476
  33.7 12.6 %collective-permute-start.10 = (bf16[256,384]{1,0:T(8,128)(2,1)S(1)}, bf16[256,384]{1,0:T(8,128)(2,1)S(1)}, u32[]{:S(2)}, u32[]{:S(2)}) collective-permute-start(bf16[256,384]{1,0:T(8,128)(2,1)S(1)} %collective-permute-done.1.refs_2_.refs_0_.xq), channel_id=1, source_target_pairs={{0,8},{1,9},{2,10},{3,11},{4,12},{5,13},{6,14},{7,15},{8,0},{9,1},... | collective-permute-start | bytes 589832 | tf_op jit(solution)/shard_map/ppermute | solution.py:462
  36.6 9.7 %collective-permute-start.11 = (bf16[256,384]{1,0:T(8,128)(2,1)S(1)}, bf16[256,384]{1,0:T(8,128)(2,1)S(1)}, u32[]{:S(2)}, u32[]{:S(2)}) collective-permute-start(bf16[256,384]{1,0:T(8,128)(2,1)S(1)} %collective-permute-done.1.refs_2_.refs_0_.xq), channel_id=1, source_target_pairs={{0,1},{1,0},{2,3},{3,2},{4,5},{5,4},{6,7},{7,6},{8,16},{9,17},{10,... | collective-permute-start | bytes 589832 | tf_op jit(solution)/shard_map/ppermute | solution.py:462
  36.6 14.5 %collective-permute-start.12 = (bf16[2,256,384]{2,1,0:T(8,128)(2,1)S(1)}, bf16[2,256,384]{2,1,0:T(8,128)(2,1)S(1)}, u32[]{:S(2)}, u32[]{:S(2)}) collective-permute-start(bf16[2,256,384]{2,1,0:T(8,128)(2,1)S(1)} %join.1), channel_id=1, source_target_pairs={{0,8},{1,9},{2,10},{3,11},{4,12},{5,13},{6,14},{7,15},{8,0},{9,1},... | collective-permute-start | bytes 1179656 | tf_op jit(solution)/shard_map/ppermute | solution.py:462
  38.8 12.4 %collective-permute-start.13 = (bf16[2,256,384]{2,1,0:T(8,128)(2,1)S(1)}, bf16[2,256,384]{2,1,0:T(8,128)(2,1)S(1)}, u32[]{:S(2)}, u32[]{:S(2)}) collective-permute-start(bf16[2,256,384]{2,1,0:T(8,128)(2,1)S(1)} %join.1), channel_id=1, source_target_pairs={{0,1},{1,0},{2,3},{3,2},{4,5},{5,4},{6,7},{7,6},{8,16},{9,17},{10,... | collective-permute-start | bytes 1179656 | tf_op jit(solution)/shard_map/ppermute | solution.py:462
  41.8 7.4 %collective-permute-start.14 = (bf16[1,256,384]{2,1,0:T(8,128)(2,1)S(1)}, bf16[1,256,384]{2,1,0:T(8,128)(2,1)S(1)}, u32[]{:S(2)}, u32[]{:S(2)}) collective-permute-start(bf16[1,256,384]{2,1,0:T(8,128)(2,1)S(1)} %get-tuple-element.50), channel_id=1, source_target_pairs={{0,4},{4,0},{8,12},{12,8},{16,20},{20,16},{24,28},{28,24},{1,5},{5... | collective-permute-start | bytes 589832 | tf_op jit(solution)/shard_map/ppermute | solution.py:448
  46.3 4.9 %collective-permute-start.15 = (f32[8,512]{1,0:T(8,128)S(1)}, f32[8,512]{1,0:T(8,128)S(1)}, u32[]{:S(2)}, u32[]{:S(2)}) collective-permute-start(f32[8,512]{1,0:T(8,128)S(1)} %get-tuple-element.47.stats), channel_id=1, source_target_pairs={{0,8},{1,9},{2,10},{3,11},{4,12},{5,13},{6,14},{7,15},{8,0},{9,1},... | collective-permute-start | bytes 49160 | tf_op jit(solution)/shard_map/ppermute | solution.py:462
  48.0 3.1 %collective-permute-start.16 = (f32[8,512]{1,0:T(8,128)S(1)}, f32[8,512]{1,0:T(8,128)S(1)}, u32[]{:S(2)}, u32[]{:S(2)}) collective-permute-start(f32[8,512]{1,0:T(8,128)S(1)} %get-tuple-element.47.stats), channel_id=1, source_target_pairs={{0,1},{1,0},{2,3},{3,2},{4,5},{5,4},{6,7},{7,6},{8,16},{9,17},{10,... | collective-permute-start | bytes 49160 | tf_op jit(solution)/shard_map/ppermute | solution.py:462
  52.0 8.6 %collective-permute-start.17 = (bf16[2,256,128]{2,1,0:T(8,128)(2,1)S(1)}, bf16[2,256,128]{2,1,0:T(8,128)(2,1)S(1)}, u32[]{:S(2)}, u32[]{:S(2)}) collective-permute-start(bf16[2,256,128]{2,1,0:T(8,128)(2,1)S(1)} %key_pass.5), channel_id=1, source_target_pairs={{0,4},{4,0},{8,12},{12,8},{16,20},{20,16},{24,28},{28,24},{1,5},{5... | collective-permute-start | bytes 393224 | tf_op jit(solution)/shard_map/ppermute | solution.py:448
  54.5 6.5 %collective-permute-start.18 = (bf16[2,256,128]{2,1,0:T(8,128)(2,1)S(1)}, bf16[2,256,128]{2,1,0:T(8,128)(2,1)S(1)}, u32[]{:S(2)}, u32[]{:S(2)}) collective-permute-start(bf16[2,256,128]{2,1,0:T(8,128)(2,1)S(1)} %key_pass.6), channel_id=1, source_target_pairs={{0,4},{4,0},{8,12},{12,8},{16,20},{20,16},{24,28},{28,24},{1,5},{5... | collective-permute-start | bytes 393224 | tf_op jit(solution)/shard_map/ppermute | solution.py:448
  55.9 6.9 %collective-permute-start.19 = (bf16[2,256,128]{2,1,0:T(8,128)(2,1)S(1)}, bf16[2,256,128]{2,1,0:T(8,128)(2,1)S(1)}, u32[]{:S(2)}, u32[]{:S(2)}) collective-permute-start(bf16[2,256,128]{2,1,0:T(8,128)(2,1)S(1)} %key_pass.7), channel_id=1, source_target_pairs={{0,4},{4,0},{8,12},{12,8},{16,20},{20,16},{24,28},{28,24},{1,5},{5... | collective-permute-start | bytes 393224 | tf_op jit(solution)/shard_map/ppermute | solution.py:448

commit v16 on v14

--- a/solution.py
+++ b/solution.py
@@ -410,7 +410,7 @@
     width = last.shape[2]
     half = dk.shape[1] // 2
     x = lax.rem(lax.axis_index("ctx"), 2)
-    columns = pl.ds(pl.multiple_of((1 - x) * half + half - width, width), width)
+    columns = pl.ds(pl.multiple_of((1 - x) * half + half - width, HD), width)
     copies = [
         pltpu.make_async_copy(last.at[i], out.at[:, columns], sem.at[i])
         for i, out in enumerate((dk, dv))
@@ -489,11 +489,11 @@
     heads = dkeep.shape[1] // HD
     theirs = (e0, o0, late_e, late_o, se, so)
     got = []
-    for head in range(heads):
-        if head == 1:
+    for group in ((0,), tuple(range(1, heads))):
+        if group[0] == 1:
             dq, = unpack(dq_keep, dq_got)
             sums, dq = lax.optimization_barrier((sums, dq))
-        got.append(over_x(key_pass(False, (head,), xkv, *theirs, sums)))
+        got.append(over_x(key_pass(False, group, xkv, *theirs, sums)))
     kv_keep = key_pass(True, tuple(range(heads)), keep, *theirs, own_sums)
     *early, last = got
     dk, dv = unpack(kv_keep, *early)

time: 62.7 us -> 63.7 us (1.016)
  waiting for transfers between devices: 16.7 us -> 19.5 us
  starting transfers between devices: 20.7 us -> 19.1 us
    ppermute x7 -> x6, waiting for transfers between devices: 8.2 us -> 11 us  [over_x(): return lax.ppermute(array, 'ctx', [(i, i ^ 1) for i in range(length)])]
    ppermute x7 -> x6, starting transfers between devices: 8.94 us -> 7.38 us  [over_x(): return lax.ppermute(array, 'ctx', [(i, i ^ 1) for i in range(length)])]
    pallas_call x4 -> x3, Pallas kernels: 4.39 us -> 4.21 us  [key_pass(): pl.pallas_call(functools.partial(key_kernel, HD ** (-0.5), own, heads), o...]
  transfers between devices with their start and end apart: 18 -> 17, of which waited for: 7 -> 6; matrix products, arithmetic and copies ran while one was open for 0% -> 0% of each run, Pallas kernels for 34% -> 33%
where the time goes in v16:
time: 63.7 us; the launch traced here: 63.6 us
  Pallas kernels  22.8 us (36%)
  waiting for transfers between devices  19.5 us (31%)
  starting transfers between devices  19.1 us (30%)
  local copies, waits for them, and re-layouts  1.14 us (2%)
  between operations  0.97 us (2%)
    ppermute x6, waiting for transfers between devices, over_x(): return lax.ppermute(array, 'ctx', [(i, i ^ 1) for i in range(length)])  11 us
    ppermute x8, starting transfers between devices, over_z(): return lax.ppermute(array, ('ctx', 'mp'), pairs)  8.64 us
    ppermute x8, waiting for transfers between devices, over_z(): return lax.ppermute(array, ('ctx', 'mp'), pairs)  8.23 us
    ppermute x6, starting transfers between devices, over_x(): return lax.ppermute(array, 'ctx', [(i, i ^ 1) for i in range(length)])  7.38 us
    pallas_call x2, Pallas kernels, query_pass(): pl.pallas_call(functools.partial(query_kernel, HD ** (-0.5), own, before...  5.94 us
    pallas_call x3, Pallas kernels, key_pass(): pl.pallas_call(functools.partial(key_kernel, HD ** (-0.5), own, heads), o...  4.21 us
    pallas_call x1, Pallas kernels, first_piece(): pl.pallas_call(first_kernel, out_shape=(jax.ShapeDtypeStruct((rows, heads...  3.82 us
    ppermute x3, starting transfers between devices, over_mp(): return lax.ppermute(array, 'mp', [(i, i ^ flip) for i in range(lanes)])  3.12 us
  transfers between devices with their start and end apart: 17, of which 6 were waited for; matrix products, arithmetic and copies ran while one was open for 0% of the time, Pallas kernels for 33%

profile of v16, /device:TPU:0, one launch (start us, length us, event | category | flops | bytes accessed | tf_op | source)
XLA Modules:
  0.0 63.6 jit_solution(9196829278568730835)
XLA Ops:
  0.6 0.5 collective-permute-start.5
  1.1 2.6 %collective-permute-start.4 = (bf16[256,1536]{1,0:T(8,128)(2,1)}, bf16[256,1536]{1,0:T(8,128)(2,1)S(1)}, u32[]{:S(2)}, u32[]{:S(2)}) collective-permute-start(bf16[256,1536]{1,0:T(8,128)(2,1)} %og.1), channel_id=1, source_target_pairs={{0,2},{1,3},{2,0},{3,1},{4,6},{5,7},{6,4},{7,5},{8,10},{9,11},{10,... | collective-permute-start | bytes 2359304 | tf_op jit(solution)/shard_map/ppermute | solution.py:445
  3.7 2.4 %pack.1 = (bf16[3,256,384]{2,1,0:T(8,128)(2,1)}, bf16[2,256,384]{2,1,0:T(8,128)(2,1)}, bf16[256,384]{1,0:T(8,128)(2,1)}) custom-call(bf16[256,768]{1,0:T(8,128)(2,1)} %q.1, bf16[256,768]{1,0:T(8,128)(2,1)} %k.1, bf16[256,768]{1,0:T(8,128)(2,1)} %v.1), custom_call_target="tpu_custom_call" | custom-call | flops 1 | bytes 1 | tf_op jit(solution)/shard_map/pack/pallas_call | solution.py:60
  6.1 1.6 %collective-permute-start = (bf16[2,256,384]{2,1,0:T(8,128)(2,1)}, bf16[2,256,384]{2,1,0:T(8,128)(2,1)S(1)}, u32[]{:S(2)}, u32[]{:S(2)}) collective-permute-start(bf16[2,256,384]{2,1,0:T(8,128)(2,1)} %get-tuple-element.26), channel_id=1, source_target_pairs={{0,4},{4,0},{8,12},{12,8},{16,20},{20,16},{24,28},{28,24},{1,5},{5... | collective-permute-start | bytes 1179656 | tf_op jit(solution)/shard_map/ppermute | solution.py:448
  7.7 0.5 collective-permute-start.1
  8.2 1.6 %collective-permute-start.6 = (bf16[3,256,384]{2,1,0:T(8,128)(2,1)}, bf16[3,256,384]{2,1,0:T(8,128)(2,1)S(1)}, u32[]{:S(2)}, u32[]{:S(2)}) collective-permute-start(bf16[3,256,384]{2,1,0:T(8,128)(2,1)} %get-tuple-element.27.refs_2_.refs_0_.keep.keys.kv), channel_id=1, source_target_pairs={{0,8},{1,9},{2,10},{3,11},{4,12},{5,13},{6,14},{7,15},{8,0},{9,1},... | collective-permute-start | bytes 1769480 | tf_op jit(solution)/shard_map/ppermute | solution.py:462
  9.8 1.1 %copy-done.1 = bf16[256,1536]{1,0:T(8,128)(2,1)S(1)} copy-done((bf16[256,1536]{1,0:T(8,128)(2,1)S(1)}, bf16[256,1536]{1,0:T(8,128)(2,1)}, u32[]{:S(2)}) %copy-start.1) | copy-done | bytes 786456
  10.9 3.8 %head_grad_first.1 = (f32[256,768]{1,0:T(8,128)S(1)}, bf16[768,1536]{1,0:T(8,128)(2,1)S(1)}, bf16[768,1536]{1,0:T(8,128)(2,1)S(1)}) custom-call(bf16[256,1536]{1,0:T(8,128)(2,1)S(1)} %copy-done.1, bf16[256,1536]{1,0:T(8,128)(2,1)S(1)} %collective-permute-done.5.near, bf16[768,6144]{1,0:T(8,128)(2,1)} %w.1), custom_call_target="tpu_custom_call" | custom-call | flops 1 | bytes 1 | tf_op jit(solution)/shard_map/head_grad_first/pallas_call | solution.py:110
  14.8 7.0 %collective-permute-done.1.refs_2_.refs_0_.xq = bf16[256,384]{1,0:T(8,128)(2,1)S(1)} collective-permute-done((bf16[256,384]{1,0:T(8,128)(2,1)}, bf16[256,384]{1,0:T(8,128)(2,1)S(1)}, u32[]{:S(2)}, u32[]{:S(2)}) %collective-permute-start.1) | collective-permute-done | bytes 196640 | tf_op jit(solution)/shard_map/ppermute | solution.py:448
  21.8 0.3 collective-permute-done.4.piece
  22.1 1.8 %collective-permute-start.2 = (bf16[2,256,384]{2,1,0:T(8,128)(2,1)S(1)}, bf16[2,256,384]{2,1,0:T(8,128)(2,1)S(1)}, u32[]{:S(2)}, u32[]{:S(2)}) collective-permute-start(bf16[2,256,384]{2,1,0:T(8,128)(2,1)S(1)} %collective-permute-done.refs_1_.refs_3_.keys.kv), channel_id=1, source_target_pairs={{0,8},{1,9},{2,10},{3,11},{4,12},{5,13},{6,14},{7,15},{8,0},{9,1},... | collective-permute-start | bytes 1179656 | tf_op jit(solution)/shard_map/ppermute | solution.py:462
  24.1 0.8 %head_grad.2.refs_0_ = f32[256,768]{1,0:T(8,128)S(1)} custom-call(f32[256,768]{1,0:T(8,128)S(1)} %after.5.acc, bf16[256,1536]{1,0:T(8,128)(2,1)S(1)} %collective-permute-done.4.piece, bf16[768,1536]{1,0:T(8,128)(2,1)S(1)} %get-tuple-element.33.w), custom_call_target="tpu_custom_call" | custom-call | flops 1 | bytes 1 | tf_op jit(solution)/shard_map/head_grad/pallas_call | solution.py:147
  25.0 0.9 %head_grad.3 = (bf16[256,384]{1,0:T(8,128)(2,1)S(1)}, bf16[256,384]{1,0:T(8,128)(2,1)S(1)}) custom-call(f32[256,768]{1,0:T(8,128)S(1)} %after.6.acc, bf16[256,1536]{1,0:T(8,128)(2,1)S(1)} %collective-permute-done.8.piece, bf16[768,1536]{1,0:T(8,128)(2,1)S(1)} %get-tuple-element.34.w), custom_call_target="tpu_custom_call" | custom-call | flops 1 | bytes 1 | tf_op jit(solution)/shard_map/head_grad/pallas_call | solution.py:147
  25.9 1.5 %collective-permute-start.9 = (bf16[256,384]{1,0:T(8,128)(2,1)S(1)}, bf16[256,384]{1,0:T(8,128)(2,1)S(1)}, u32[]{:S(2)}, u32[]{:S(2)}) collective-permute-start(bf16[256,384]{1,0:T(8,128)(2,1)S(1)} %get-tuple-element.36), channel_id=1, source_target_pairs={{0,4},{4,0},{8,12},{12,8},{16,20},{20,16},{24,28},{28,24},{1,5},{5... | collective-permute-start | bytes 589832 | tf_op jit(solution)/shard_map/ppermute | solution.py:448
  27.4 6.3 %collective-permute-done.2.refs_4_.refs_6_ = bf16[2,256,384]{2,1,0:T(8,128)(2,1)S(1)} collective-permute-done((bf16[2,256,384]{2,1,0:T(8,128)(2,1)S(1)}, bf16[2,256,384]{2,1,0:T(8,128)(2,1)S(1)}, u32[]{:S(2)}, u32[]{:S(2)}) %collective-permute-start.2) | collective-permute-done | bytes 393248 | tf_op jit(solution)/shard_map/ppermute | solution.py:462
  33.8 2.9 %collective-permute-start.10 = (bf16[3,256,384]{2,1,0:T(8,128)(2,1)S(1)}, bf16[3,256,384]{2,1,0:T(8,128)(2,1)S(1)}, u32[]{:S(2)}, u32[]{:S(2)}) collective-permute-start(bf16[3,256,384]{2,1,0:T(8,128)(2,1)S(1)} %join.1), channel_id=1, source_target_pairs={{0,8},{1,9},{2,10},{3,11},{4,12},{5,13},{6,14},{7,15},{8,0},{9,1},... | collective-permute-start | bytes 1769480 | tf_op jit(solution)/shard_map/ppermute | solution.py:462
  36.7 3.0 %query_pass.2 = (bf16[1,256,384]{2,1,0:T(8,128)(2,1)S(1)}, f32[8,256]{1,0:T(8,128)S(1)}) custom-call(bf16[256,384]{1,0:T(8,128)(2,1)S(1)} %collective-permute-done.1.refs_2_.refs_0_.xq, bf16[256,384]{1,0:T(8,128)(2,1)S(1)} %after.7.refs_1_.dxr.refs_2_, bf16[3,256,384]{2,1,0:T(8,128)(2,1)S(1)} %copy-done, ...), custom_call_target="tpu_custom_call" | custom-call | flops 1 | bytes 1 | tf_op jit(solution)/shard_map/query_pass/pallas_call | solution.py:256
  39.7 1.6 %collective-permute-start.12 = (bf16[1,256,384]{2,1,0:T(8,128)(2,1)S(1)}, bf16[1,256,384]{2,1,0:T(8,128)(2,1)S(1)}, u32[]{:S(2)}, u32[]{:S(2)}) collective-permute-start(bf16[1,256,384]{2,1,0:T(8,128)(2,1)S(1)} %get-tuple-element.42), channel_id=1, source_target_pairs={{0,4},{4,0},{8,12},{12,8},{16,20},{20,16},{24,28},{28,24},{1,5},{5... | collective-permute-start | bytes 589832 | tf_op jit(solution)/shard_map/ppermute | solution.py:448
  41.2 3.0 %query_pass.3 = (bf16[1,256,384]{2,1,0:T(8,128)(2,1)S(1)}, f32[8,512]{1,0:T(8,128)S(1)}) custom-call(bf16[3,256,384]{2,1,0:T(8,128)(2,1)S(1)} %copy-done, bf16[256,384]{1,0:T(8,128)(2,1)S(1)} %get-tuple-element.35.refs_1_.dkeep, bf16[3,256,384]{2,1,0:T(8,128)(2,1)S(1)} %copy-done, bf16[2,256,384]{2,1,0:T(8,128)(2,1)S(1)} %collective-permute-done.refs_1_.refs_3_.keys.kv, ...), custom_call_target="tpu_custom_call" | custom-call | flops 6000000000 | bytes 1 | tf_op jit(solution)/shard_map/query_pass/pallas_call | solution.py:256
  44.2 2.1 %collective-permute-start.13 = (f32[8,512]{1,0:T(8,128)S(1)}, f32[8,512]{1,0:T(8,128)S(1)}, u32[]{:S(2)}, u32[]{:S(2)}) collective-permute-start(f32[8,512]{1,0:T(8,128)S(1)} %get-tuple-element.40.stats), channel_id=1, source_target_pairs={{0,8},{1,9},{2,10},{3,11},{4,12},{5,13},{6,14},{7,15},{8,0},{9,1},... | collective-permute-start | bytes 49160 | tf_op jit(solution)/shard_map/ppermute | solution.py:462
  46.3 1.2 %own_pass.2.refs_0_ = f32[2,256,384]{2,1,0:T(8,128)S(1)} custom-call(bf16[2,256,384]{2,1,0:T(8,128)(2,1)S(1)} %collective-permute-done.refs_1_.refs_3_.keys.kv, bf16[3,256,384]{2,1,0:T(8,128)(2,1)S(1)} %copy-done, bf16[256,384]{1,0:T(8,128)(2,1)S(1)} %collective-permute-done.1.refs_2_.refs_0_.xq, bf16[256,384]{1,0:T(8,128)(2,1)S(1)} %get-tuple-element.35.refs_1_.dkeep, ...), custom_call_target="tpu_custom_call" | custom-call | flops 1 | bytes 1 | tf_op jit(solution)/shard_map/own_pass/pallas_call | solution.py:306
  47.5 0.8 %unpack.2 = bf16[256,768]{1,0:T(8,128)(2,1)} custom-call(bf16[1,256,384]{2,1,0:T(8,128)(2,1)S(1)} %get-tuple-element.41.kept, bf16[1,256,384]{2,1,0:T(8,128)(2,1)S(1)} %after.9.refs_0_), custom_call_target="tpu_custom_call" | custom-call | flops 1 | bytes 1 | tf_op jit(solution)/shard_map/unpack/pallas_call | solution.py:396
  48.3 1.8 %collective-permute-done.10.refs_1_.late_e = bf16[3,256,384]{2,1,0:T(8,128)(2,1)S(1)} collective-permute-done((bf16[3,256,384]{2,1,0:T(8,128)(2,1)S(1)}, bf16[3,256,384]{2,1,0:T(8,128)(2,1)S(1)}, u32[]{:S(2)}, u32[]{:S(2)}) %collective-permute-start.10) | collective-permute-done | bytes 589856 | tf_op jit(solution)/shard_map/ppermute | solution.py:462
  50.3 1.3 %key_pass.5 = bf16[2,256,256]{2,1,0:T(8,128)(2,1)S(1)} custom-call(bf16[2,256,384]{2,1,0:T(8,128)(2,1)S(1)} %collective-permute-done.refs_1_.refs_3_.keys.kv, bf16[3,256,384]{2,1,0:T(8,128)(2,1)S(1)} %collective-permute-done.6.refs_1_.refs_6_.refs_4_.e0, bf16[3,256,384]{2,1,0:T(8,128)(2,1)S(1)} %collective-permute-done.7.refs_2_.refs_7_.refs_5_.o0, ...), custom_call_target="tpu_custom_call" | custom-call | flops 1000000000 | bytes 1 | tf_op jit(solution)/shard_map/key_pass/pallas_call | solution.py:360
  51.6 1.6 %collective-permute-start.16 = (bf16[2,256,256]{2,1,0:T(8,128)(2,1)S(1)}, bf16[2,256,256]{2,1,0:T(8,128)(2,1)S(1)}, u32[]{:S(2)}, u32[]{:S(2)}) collective-permute-start(bf16[2,256,256]{2,1,0:T(8,128)(2,1)S(1)} %key_pass.5), channel_id=1, source_target_pairs={{0,4},{4,0},{8,12},{12,8},{16,20},{20,16},{24,28},{28,24},{1,5},{5... | collective-permute-start | bytes 786440 | tf_op jit(solution)/shard_map/ppermute | solution.py:448
  53.2 0.9 %key_pass.4 = bf16[2,256,128]{2,1,0:T(8,128)(2,1)S(1)} custom-call(bf16[2,256,384]{2,1,0:T(8,128)(2,1)S(1)} %collective-permute-done.refs_1_.refs_3_.keys.kv, bf16[3,256,384]{2,1,0:T(8,128)(2,1)S(1)} %collective-permute-done.6.refs_1_.refs_6_.refs_4_.e0, bf16[3,256,384]{2,1,0:T(8,128)(2,1)S(1)} %collective-permute-done.7.refs_2_.refs_7_.refs_5_.o0, ...), custom_call_target="tpu_custom_call" | custom-call | flops 1000000000 | bytes 1 | tf_op jit(solution)/shard_map/key_pass/pallas_call | solution.py:360
  54.1 0.6 collective-permute-start.15
  54.7 1.2 %own_pass.3.sums = f32[2,256,384]{2,1,0:T(8,128)S(1)} custom-call(bf16[3,256,384]{2,1,0:T(8,128)(2,1)S(1)} %copy-done, bf16[3,256,384]{2,1,0:T(8,128)(2,1)S(1)} %copy-done, bf16[256,384]{1,0:T(8,128)(2,1)S(1)} %collective-permute-done.1.refs_2_.refs_0_.xq, bf16[256,384]{1,0:T(8,128)(2,1)S(1)} %get-tuple-element.35.refs_1_.dkeep, ...), custom_call_target="tpu_custom_call" | custom-call | flops 1 | bytes 1 | tf_op jit(solution)/shard_map/own_pass/pallas_call | solution.py:306
  55.9 1.9 %key_pass.3.kept = bf16[2,256,384]{2,1,0:T(8,128)(2,1)S(1)} custom-call(bf16[3,256,384]{2,1,0:T(8,128)(2,1)S(1)} %copy-done, bf16[3,256,384]{2,1,0:T(8,128)(2,1)S(1)} %collective-permute-done.6.refs_1_.refs_6_.refs_4_.e0, bf16[3,256,384]{2,1,0:T(8,128)(2,1)S(1)} %collective-permute-done.7.refs_2_.refs_7_.refs_5_.o0, ...), custom_call_target="tpu_custom_call" | custom-call | flops 1000000000 | bytes 1 | tf_op jit(solution)/shard_map/key_pass/pallas_call | solution.py:360
  57.9 4.0 %collective-permute-done.15.refs_0_ = bf16[2,256,128]{2,1,0:T(8,128)(2,1)S(1)} collective-permute-done((bf16[2,256,128]{2,1,0:T(8,128)(2,1)S(1)}, bf16[2,256,128]{2,1,0:T(8,128)(2,1)S(1)}, u32[]{:S(2)}, u32[]{:S(2)}) %collective-permute-start.15) | collective-permute-done | bytes 131104 | tf_op jit(solution)/shard_map/ppermute | solution.py:448
  61.8 0.8 %unpack.3 = (bf16[256,768]{1,0:T(8,128)(2,1)}, bf16[256,768]{1,0:T(8,128)(2,1)}) custom-call(bf16[2,256,384]{2,1,0:T(8,128)(2,1)S(1)} %key_pass.3.kept, bf16[2,256,128]{2,1,0:T(8,128)(2,1)S(1)} %collective-permute-done.15.refs_0_), custom_call_target="tpu_custom_call" | custom-call | flops 1 | bytes 1 | tf_op jit(solution)/shard_map/unpack/pallas_call | solution.py:396
  62.7 0.7 %finish.1 = (bf16[256,768]{1,0:T(8,128)(2,1)}, bf16[256,768]{1,0:T(8,128)(2,1)}) custom-call(bf16[256,768]{1,0:T(8,128)(2,1)} %get-tuple-element.44.dk_in, bf16[256,768]{1,0:T(8,128)(2,1)} %get-tuple-element.45.dv_in, bf16[2,256,256]{2,1,0:T(8,128)(2,1)S(1)} %collective-permute-done.16.last), custom_call_target="tpu_custom_call", output_to_operand_aliasing={{0}: (0, {}), {1}: (1, {})} | custom-call | flops 1 | bytes 1 | tf_op jit(solution)/shard_map/finish/pallas_call | solution.py:425
  (26 shorter events, 0.5 us)
Async XLA Ops:
  0.6 9.2 %collective-permute-start.5 = (bf16[256,1536]{1,0:T(8,128)(2,1)}, bf16[256,1536]{1,0:T(8,128)(2,1)S(1)}, u32[]{:S(2)}, u32[]{:S(2)}) collective-permute-start(bf16[256,1536]{1,0:T(8,128)(2,1)} %og.1), channel_id=1, source_target_pairs={{0,1},{1,0},{2,3},{3,2},{4,5},{5,4},{6,7},{7,6},{8,9},{9,8},{10,11... | collective-permute-start | bytes 2359304 | tf_op jit(solution)/shard_map/ppermute | solution.py:445
  1.1 20.9 %collective-permute-start.4 = (bf16[256,1536]{1,0:T(8,128)(2,1)}, bf16[256,1536]{1,0:T(8,128)(2,1)S(1)}, u32[]{:S(2)}, u32[]{:S(2)}) collective-permute-start(bf16[256,1536]{1,0:T(8,128)(2,1)} %og.1), channel_id=1, source_target_pairs={{0,2},{1,3},{2,0},{3,1},{4,6},{5,7},{6,4},{7,5},{8,10},{9,11},{10,... | collective-permute-start | bytes 2359304 | tf_op jit(solution)/shard_map/ppermute | solution.py:445
  6.1 15.7 %collective-permute-start = (bf16[2,256,384]{2,1,0:T(8,128)(2,1)}, bf16[2,256,384]{2,1,0:T(8,128)(2,1)S(1)}, u32[]{:S(2)}, u32[]{:S(2)}) collective-permute-start(bf16[2,256,384]{2,1,0:T(8,128)(2,1)} %get-tuple-element.26), channel_id=1, source_target_pairs={{0,4},{4,0},{8,12},{12,8},{16,20},{20,16},{24,28},{28,24},{1,5},{5... | collective-permute-start | bytes 1179656 | tf_op jit(solution)/shard_map/ppermute | solution.py:448
  7.7 14.1 %collective-permute-start.1 = (bf16[256,384]{1,0:T(8,128)(2,1)}, bf16[256,384]{1,0:T(8,128)(2,1)S(1)}, u32[]{:S(2)}, u32[]{:S(2)}) collective-permute-start(bf16[256,384]{1,0:T(8,128)(2,1)} %get-tuple-element.28), channel_id=1, source_target_pairs={{0,4},{4,0},{8,12},{12,8},{16,20},{20,16},{24,28},{28,24},{1,5},{5... | collective-permute-start | bytes 589832 | tf_op jit(solution)/shard_map/ppermute | solution.py:448
  8.2 16.7 %collective-permute-start.6 = (bf16[3,256,384]{2,1,0:T(8,128)(2,1)}, bf16[3,256,384]{2,1,0:T(8,128)(2,1)S(1)}, u32[]{:S(2)}, u32[]{:S(2)}) collective-permute-start(bf16[3,256,384]{2,1,0:T(8,128)(2,1)} %get-tuple-element.27.refs_2_.refs_0_.keep.keys.kv), channel_id=1, source_target_pairs={{0,8},{1,9},{2,10},{3,11},{4,12},{5,13},{6,14},{7,15},{8,0},{9,1},... | collective-permute-start | bytes 1769480 | tf_op jit(solution)/shard_map/ppermute | solution.py:462
  9.8 15.1 %collective-permute-start.7 = (bf16[3,256,384]{2,1,0:T(8,128)(2,1)}, bf16[3,256,384]{2,1,0:T(8,128)(2,1)S(1)}, u32[]{:S(2)}, u32[]{:S(2)}) collective-permute-start(bf16[3,256,384]{2,1,0:T(8,128)(2,1)} %get-tuple-element.27.refs_2_.refs_0_.keep.keys.kv), channel_id=1, source_target_pairs={{0,1},{1,0},{2,3},{3,2},{4,5},{5,4},{6,7},{7,6},{8,16},{9,17},{10,... | collective-permute-start | bytes 1769480 | tf_op jit(solution)/shard_map/ppermute | solution.py:462
  9.8 1.1 %copy-start.1 = (bf16[256,1536]{1,0:T(8,128)(2,1)S(1)}, bf16[256,1536]{1,0:T(8,128)(2,1)}, u32[]{:S(2)}) copy-start(bf16[256,1536]{1,0:T(8,128)(2,1)} %og.1) | copy-start | bytes 2359300
  22.1 2.9 %collective-permute-start.8 = (bf16[256,1536]{1,0:T(8,128)(2,1)S(1)}, bf16[256,1536]{1,0:T(8,128)(2,1)S(1)}, u32[]{:S(2)}, u32[]{:S(2)}) collective-permute-start(bf16[256,1536]{1,0:T(8,128)(2,1)S(1)} %collective-permute-done.4.piece), channel_id=1, source_target_pairs={{0,1},{1,0},{2,3},{3,2},{4,5},{5,4},{6,7},{7,6},{8,9},{9,8},{10,11... | collective-permute-start | bytes 2359304 | tf_op jit(solution)/shard_map/ppermute | solution.py:445
  22.1 11.6 %collective-permute-start.2 = (bf16[2,256,384]{2,1,0:T(8,128)(2,1)S(1)}, bf16[2,256,384]{2,1,0:T(8,128)(2,1)S(1)}, u32[]{:S(2)}, u32[]{:S(2)}) collective-permute-start(bf16[2,256,384]{2,1,0:T(8,128)(2,1)S(1)} %collective-permute-done.refs_1_.refs_3_.keys.kv), channel_id=1, source_target_pairs={{0,8},{1,9},{2,10},{3,11},{4,12},{5,13},{6,14},{7,15},{8,0},{9,1},... | collective-permute-start | bytes 1179656 | tf_op jit(solution)/shard_map/ppermute | solution.py:462
  23.9 9.8 %collective-permute-start.3 = (bf16[2,256,384]{2,1,0:T(8,128)(2,1)S(1)}, bf16[2,256,384]{2,1,0:T(8,128)(2,1)S(1)}, u32[]{:S(2)}, u32[]{:S(2)}) collective-permute-start(bf16[2,256,384]{2,1,0:T(8,128)(2,1)S(1)} %collective-permute-done.refs_1_.refs_3_.keys.kv), channel_id=1, source_target_pairs={{0,1},{1,0},{2,3},{3,2},{4,5},{5,4},{6,7},{7,6},{8,16},{9,17},{10,... | collective-permute-start | bytes 1179656 | tf_op jit(solution)/shard_map/ppermute | solution.py:462
  25.8 10.9 %copy-start = (bf16[3,256,384]{2,1,0:T(8,128)(2,1)S(1)}, bf16[3,256,384]{2,1,0:T(8,128)(2,1)}, u32[]{:S(2)}) copy-start(bf16[3,256,384]{2,1,0:T(8,128)(2,1)} %get-tuple-element.27.refs_2_.refs_0_.keep.keys.kv) | copy-start | bytes 1769476
  25.9 7.8 %collective-permute-start.9 = (bf16[256,384]{1,0:T(8,128)(2,1)S(1)}, bf16[256,384]{1,0:T(8,128)(2,1)S(1)}, u32[]{:S(2)}, u32[]{:S(2)}) collective-permute-start(bf16[256,384]{1,0:T(8,128)(2,1)S(1)} %get-tuple-element.36), channel_id=1, source_target_pairs={{0,4},{4,0},{8,12},{12,8},{16,20},{20,16},{24,28},{28,24},{1,5},{5... | collective-permute-start | bytes 589832 | tf_op jit(solution)/shard_map/ppermute | solution.py:448
  33.8 16.3 %collective-permute-start.10 = (bf16[3,256,384]{2,1,0:T(8,128)(2,1)S(1)}, bf16[3,256,384]{2,1,0:T(8,128)(2,1)S(1)}, u32[]{:S(2)}, u32[]{:S(2)}) collective-permute-start(bf16[3,256,384]{2,1,0:T(8,128)(2,1)S(1)} %join.1), channel_id=1, source_target_pairs={{0,8},{1,9},{2,10},{3,11},{4,12},{5,13},{6,14},{7,15},{8,0},{9,1},... | collective-permute-start | bytes 1769480 | tf_op jit(solution)/shard_map/ppermute | solution.py:462
  36.7 13.4 %collective-permute-start.11 = (bf16[3,256,384]{2,1,0:T(8,128)(2,1)S(1)}, bf16[3,256,384]{2,1,0:T(8,128)(2,1)S(1)}, u32[]{:S(2)}, u32[]{:S(2)}) collective-permute-start(bf16[3,256,384]{2,1,0:T(8,128)(2,1)S(1)} %join.1), channel_id=1, source_target_pairs={{0,1},{1,0},{2,3},{3,2},{4,5},{5,4},{6,7},{7,6},{8,16},{9,17},{10,... | collective-permute-start | bytes 1769480 | tf_op jit(solution)/shard_map/ppermute | solution.py:462
  39.7 7.9 %collective-permute-start.12 = (bf16[1,256,384]{2,1,0:T(8,128)(2,1)S(1)}, bf16[1,256,384]{2,1,0:T(8,128)(2,1)S(1)}, u32[]{:S(2)}, u32[]{:S(2)}) collective-permute-start(bf16[1,256,384]{2,1,0:T(8,128)(2,1)S(1)} %get-tuple-element.42), channel_id=1, source_target_pairs={{0,4},{4,0},{8,12},{12,8},{16,20},{20,16},{24,28},{28,24},{1,5},{5... | collective-permute-start | bytes 589832 | tf_op jit(solution)/shard_map/ppermute | solution.py:448
  44.2 6.0 %collective-permute-start.13 = (f32[8,512]{1,0:T(8,128)S(1)}, f32[8,512]{1,0:T(8,128)S(1)}, u32[]{:S(2)}, u32[]{:S(2)}) collective-permute-start(f32[8,512]{1,0:T(8,128)S(1)} %get-tuple-element.40.stats), channel_id=1, source_target_pairs={{0,8},{1,9},{2,10},{3,11},{4,12},{5,13},{6,14},{7,15},{8,0},{9,1},... | collective-permute-start | bytes 49160 | tf_op jit(solution)/shard_map/ppermute | solution.py:462
  46.3 4.0 %collective-permute-start.14 = (f32[8,512]{1,0:T(8,128)S(1)}, f32[8,512]{1,0:T(8,128)S(1)}, u32[]{:S(2)}, u32[]{:S(2)}) collective-permute-start(f32[8,512]{1,0:T(8,128)S(1)} %get-tuple-element.40.stats), channel_id=1, source_target_pairs={{0,1},{1,0},{2,3},{3,2},{4,5},{5,4},{6,7},{7,6},{8,16},{9,17},{10,... | collective-permute-start | bytes 49160 | tf_op jit(solution)/shard_map/ppermute | solution.py:462
  51.6 11.1 %collective-permute-start.16 = (bf16[2,256,256]{2,1,0:T(8,128)(2,1)S(1)}, bf16[2,256,256]{2,1,0:T(8,128)(2,1)S(1)}, u32[]{:S(2)}, u32[]{:S(2)}) collective-permute-start(bf16[2,256,256]{2,1,0:T(8,128)(2,1)S(1)} %key_pass.5), channel_id=1, source_target_pairs={{0,4},{4,0},{8,12},{12,8},{16,20},{20,16},{24,28},{28,24},{1,5},{5... | collective-permute-start | bytes 786440 | tf_op jit(solution)/shard_map/ppermute | solution.py:448
  54.1 7.7 %collective-permute-start.15 = (bf16[2,256,128]{2,1,0:T(8,128)(2,1)S(1)}, bf16[2,256,128]{2,1,0:T(8,128)(2,1)S(1)}, u32[]{:S(2)}, u32[]{:S(2)}) collective-permute-start(bf16[2,256,128]{2,1,0:T(8,128)(2,1)S(1)} %key_pass.4), channel_id=1, source_target_pairs={{0,4},{4,0},{8,12},{12,8},{16,20},{20,16},{24,28},{28,24},{1,5},{5... | collective-permute-start | bytes 393224 | tf_op jit(solution)/shard_map/ppermute | solution.py:448
